TPU v7x, 32 devices: a whole 2x2x4 slice. The times are simulated.
32 devices in a mesh: seq: 4 (over x, core), fsdp: 8 (over z, y).
Axes of the slice: x: 2, y: 2, z: 4, core: 2. Of those that a mesh axis runs over, the one named last changes fastest.
Arguments:
- tokens: bfloat16 [8, 1024, 2048], P('fsdp', 'seq'), may hold values from -6 to 6
- positions: int32 [8, 1024], P('fsdp', 'seq'), may hold values from 0 to 4092, as said below
- attn_gain: bfloat16 [2048], P('fsdp'), may hold values from 0.099609375 to 1.8984375
- w_q: bfloat16 [2048, 2048], P('fsdp'), may hold values from -0.125 to 0.125
- w_k: bfloat16 [2048, 512], P('fsdp'), may hold values from -0.125 to 0.125
- w_v: bfloat16 [2048, 512], P('fsdp'), may hold values from -0.125 to 0.125
- w_o: bfloat16 [2048, 2048], P('fsdp'), may hold values from -1 to 1
- mlp_gain: bfloat16 [2048], P('fsdp'), may hold values from 0.099609375 to 1.8984375
- w_gate: bfloat16 [2048, 8192], P('fsdp'), may hold values from -0.125 to 0.125
- w_up: bfloat16 [2048, 8192], P('fsdp'), may hold values from -0.125 to 0.125
- w_down: bfloat16 [8192, 2048], P('fsdp'), may hold values from -0.0625 to 0.0625
- cotangent: bfloat16 [8, 1024, 2048], P('fsdp', 'seq'), may hold values from -6 to 6
Outputs:
- output: bfloat16 [8, 1024, 2048], P('fsdp', 'seq')
- tokens_grad: bfloat16 [8, 1024, 2048], P('fsdp', 'seq')
- attn_gain_grad: float32 [2048], P(('seq', 'fsdp'))
- w_q_grad: float32 [2048, 2048], P(('seq', 'fsdp'))
- w_k_grad: float32 [2048, 512], P(('seq', 'fsdp'))
- w_v_grad: float32 [2048, 512], P(('seq', 'fsdp'))
- w_o_grad: float32 [2048, 2048], P(('seq', 'fsdp'))
- mlp_gain_grad: float32 [2048], P(('seq', 'fsdp'))
- w_gate_grad: float32 [2048, 8192], P(('seq', 'fsdp'))
- w_up_grad: float32 [2048, 8192], P(('seq', 'fsdp'))
- w_down_grad: float32 [8192, 2048], P(('seq', 'fsdp'))
Inputs may be any that keep to these rules, and one draw needn't show every extreme that they name: Each sequence's positions start at 0 and rise by 1 to 4 from one token to the next; in one sequence they rise by 4 at every token.
All inputs are finite; a program needn't handle non-finite values.
Results may differ from a plain program's by a relative error of at most 0.02.
Values may be sent and summed in bfloat16 or wider, within the bound.
No kernel may reach another device: no remote copies, remote signals or barrier semaphores. Data moves between devices by JAX's collectives and lax.ppermute only.
A program may use at most 704 MiB of HBM per device.

v0:
```python
import math

import jax
import jax.numpy as jnp
from jax import lax
from jax.sharding import PartitionSpec as P

H = 32
KVH = 8
HD = 64


EPSILON = 1e-05
ROPE_BASE = 500000.0


def rotate(values, places, direction):
    half_size = values.shape[-1] // 2
    index_f = jnp.arange(half_size).astype(jnp.float32)
    freqs_all = jnp.exp(index_f * (-2.0 * math.log(ROPE_BASE) / values.shape[-1]))
    angles = places.astype(jnp.float32)[..., None] * freqs_all
    cosine = jnp.cos(angles)[..., None, :]
    sine = jnp.sin(angles)[..., None, :] * direction
    first = values[..., :half_size]
    second = values[..., half_size:]
    return jnp.concatenate(
        [first * cosine - second * sine, second * cosine + first * sine], axis=-1
    )


def scores_of(q_block, k_seq, offset, scaling):
    scores = (
        jnp.einsum("qgrd,kgd->grqk", q_block, k_seq, preferred_element_type=jnp.float32) * scaling
    )
    rows_at = offset + jnp.arange(q_block.shape[0], dtype=jnp.int32)
    cols_at = jnp.arange(k_seq.shape[0], dtype=jnp.int32)
    return jnp.where(rows_at[:, None] >= cols_at[None, :], scores, -1e30)


def attend_forward(q_heads, k_heads, v_heads):
    seq_count, length, groups_q, head_size = q_heads.shape
    groups_kv = k_heads.shape[2]
    ratio_kv = groups_q // groups_kv
    block_rows = min(512, length)
    blocks = length // block_rows
    scaling = 1.0 / math.sqrt(head_size)
    offsets = jnp.arange(blocks, dtype=jnp.int32) * block_rows

    def per_sequence(inputs):
        q_seq, k_seq, v_seq = inputs
        q_blocks = q_seq.reshape(blocks, block_rows, groups_kv, ratio_kv, head_size)

        def one_block(parts):
            q_block, offset = parts
            scores = scores_of(q_block, k_seq, offset, scaling)
            highest = jnp.max(scores, axis=-1, keepdims=True)
            exponent = jnp.exp(scores - highest)
            totals = jnp.sum(exponent, axis=-1, keepdims=True)
            probabilities = (exponent / totals).astype(jnp.bfloat16)
            mixed_out = jnp.einsum(
                "grqk,kgd->qgrd", probabilities, v_seq, preferred_element_type=jnp.float32
            )
            return (mixed_out.astype(jnp.bfloat16), (highest + jnp.log(totals))[..., 0])

        return lax.map(one_block, (q_blocks, offsets))

    mixed_out, log_sums = lax.map(per_sequence, (q_heads, k_heads, v_heads))
    return (mixed_out.reshape(seq_count, length, 1, groups_q * head_size), log_sums)


def attend_backward(q_heads, k_heads, v_heads, d_heads, log_sums):
    seq_count, length, groups_q, head_size = q_heads.shape
    groups_kv = k_heads.shape[2]
    ratio_kv = groups_q // groups_kv
    block_rows = min(512, length)
    blocks = length // block_rows
    scaling = 1.0 / math.sqrt(head_size)
    offsets = jnp.arange(blocks, dtype=jnp.int32) * block_rows

    def per_sequence(inputs):
        q_seq, k_seq, v_seq, d_seq, lse_seq = inputs
        q_blocks = q_seq.reshape(blocks, block_rows, groups_kv, ratio_kv, head_size)
        d_blocks = d_seq.reshape(blocks, block_rows, groups_kv, ratio_kv, head_size)

        def one_block(carry, parts):
            grad_k, grad_v = carry
            q_block, d_block, lse_block, offset = parts
            scores = scores_of(q_block, k_seq, offset, scaling)
            probabilities = jnp.exp(scores - lse_block[..., None])
            grad_prob = jnp.einsum(
                "qgrd,kgd->grqk", d_block, v_seq, preferred_element_type=jnp.float32
            )
            inner = jnp.sum(grad_prob * probabilities, axis=-1, keepdims=True)
            grad_score = (probabilities * (grad_prob - inner)).astype(jnp.bfloat16)
            grad_q = (
                jnp.einsum("grqk,kgd->qgrd", grad_score, k_seq, preferred_element_type=jnp.float32)
                * scaling
            )
            grad_k = (
                grad_k
                + jnp.einsum(
                    "grqk,qgrd->kgd", grad_score, q_block, preferred_element_type=jnp.float32
                )
                * scaling
            )
            grad_v = grad_v + jnp.einsum(
                "grqk,qgrd->kgd",
                probabilities.astype(jnp.bfloat16),
                d_block,
                preferred_element_type=jnp.float32,
            )
            return ((grad_k, grad_v), grad_q)

        zeros_kv = jnp.zeros((length, groups_kv, head_size), jnp.float32)
        (grad_k, grad_v), grad_q = lax.scan(
            one_block, (zeros_kv, zeros_kv), (q_blocks, d_blocks, lse_seq, offsets)
        )
        return (grad_q, grad_k, grad_v)

    grad_q, grad_k, grad_v = lax.map(per_sequence, (q_heads, k_heads, v_heads, d_heads, log_sums))
    return (
        grad_q.reshape(seq_count, length, 1, groups_q * head_size),
        grad_k.reshape(seq_count, length, 1, groups_kv * head_size),
        grad_v.reshape(seq_count, length, 1, groups_kv * head_size),
    )


def contract_rows(left, right):
    return lax.dot_general(
        left, right, (((0,), (0,)), ((), ())), preferred_element_type=jnp.float32
    )


def contract_cols(left, right):
    return lax.dot_general(
        left, right, (((1,), (1,)), ((), ())), preferred_element_type=jnp.float32
    )


def shards(
    tokens, positions, attn_gain, w_q, w_k, w_v, w_o, mlp_gain, w_gate, w_up, w_down, cotangent
):
    seq_count, part_len, width = tokens.shape
    n_seq = lax.axis_size("seq")
    n_fsdp = lax.axis_size("fsdp")
    n_all = n_seq * n_fsdp
    row_total = seq_count * part_len
    length = part_len * n_seq
    x_rows = tokens.reshape(row_total, width).astype(jnp.float32)
    gain_one, wq_full, wk_full, wv_full, wo_full = (
        lax.all_gather(attn_gain, "fsdp", axis=0, tiled=True),
        lax.all_gather(w_q, "fsdp", axis=0, tiled=True),
        lax.all_gather(w_k, "fsdp", axis=0, tiled=True),
        lax.all_gather(w_v, "fsdp", axis=0, tiled=True),
        lax.all_gather(w_o, "fsdp", axis=0, tiled=True),
    )
    q_width = wq_full.shape[1]
    kv_width = wk_full.shape[1]
    ff_width = w_gate.shape[1]
    gain_one_f = gain_one.astype(jnp.float32)
    inv_one = lax.rsqrt(jnp.mean(x_rows * x_rows, axis=-1, keepdims=True) + EPSILON)
    norm_one = x_rows * inv_one
    normed = (norm_one * gain_one_f).astype(jnp.bfloat16)
    query_proj = jnp.dot(normed, wq_full, preferred_element_type=jnp.float32)
    key_proj = jnp.dot(normed, wk_full, preferred_element_type=jnp.float32)
    value_proj = jnp.dot(normed, wv_full, preferred_element_type=jnp.float32)
    turned_q = rotate(query_proj.reshape(seq_count, part_len, H, HD), positions, 1.0).astype(
        jnp.bfloat16
    )
    turned_k = rotate(key_proj.reshape(seq_count, part_len, KVH, HD), positions, 1.0).astype(
        jnp.bfloat16
    )
    turned_q = turned_q.reshape(seq_count, part_len, n_seq, q_width // n_seq)
    turned_k = turned_k.reshape(seq_count, part_len, n_seq, kv_width // n_seq)
    value_rows = value_proj.astype(jnp.bfloat16).reshape(
        seq_count, part_len, n_seq, kv_width // n_seq
    )
    q_heads, k_heads, v_heads = (
        lax.all_to_all(turned_q, "seq", split_axis=2, concat_axis=1, tiled=True),
        lax.all_to_all(turned_k, "seq", split_axis=2, concat_axis=1, tiled=True),
        lax.all_to_all(value_rows, "seq", split_axis=2, concat_axis=1, tiled=True),
    )
    q_heads = q_heads.reshape(seq_count, length, H // n_seq, HD)
    k_heads = k_heads.reshape(seq_count, length, KVH // n_seq, HD)
    v_heads = v_heads.reshape(seq_count, length, KVH // n_seq, HD)
    mixed_out, log_sums = attend_forward(q_heads, k_heads, v_heads)
    back_rows = lax.all_to_all(mixed_out, "seq", split_axis=1, concat_axis=2, tiled=True)
    attn_rows = back_rows.reshape(row_total, q_width)
    residual = x_rows + jnp.dot(attn_rows, wo_full, preferred_element_type=jnp.float32)
    inv_two = lax.rsqrt(jnp.mean(residual * residual, axis=-1, keepdims=True) + EPSILON)
    norm_two = residual * inv_two
    gain_p = lax.all_gather(mlp_gain, "fsdp", axis=0, tiled=True)
    gate_p = lax.all_gather(w_gate, "fsdp", axis=0, tiled=True)
    up_p = lax.all_gather(w_up, "fsdp", axis=0, tiled=True)
    piece_n = (norm_two * gain_p.astype(jnp.float32)).astype(jnp.bfloat16)
    gate_sum = jnp.dot(piece_n, gate_p, preferred_element_type=jnp.float32)
    up_sum = jnp.dot(piece_n, up_p, preferred_element_type=jnp.float32)
    sigmoid_g = jax.nn.sigmoid(gate_sum)
    active = gate_sum * sigmoid_g
    mlp_mid = (active * up_sum).astype(jnp.bfloat16)
    branch_two = jnp.dot(
        mlp_mid,
        lax.all_gather(w_down, "fsdp", axis=0, tiled=True),
        preferred_element_type=jnp.float32,
    )
    output = (residual + branch_two).astype(jnp.bfloat16).reshape(tokens.shape)
    grad_b = cotangent.reshape(row_total, width)
    grad_f = grad_b.astype(jnp.float32)
    grad_mid = contract_cols(grad_b, lax.all_gather(w_down, "fsdp", axis=0, tiled=True))
    grad_gate = (grad_mid * up_sum * sigmoid_g * (1.0 + gate_sum * (1.0 - sigmoid_g))).astype(
        jnp.bfloat16
    )
    grad_up = (grad_mid * active).astype(jnp.bfloat16)
    gain_p, gate_p, up_p = lax.all_gather((mlp_gain, w_gate, w_up), "fsdp", axis=0, tiled=True)
    back_part = contract_cols(grad_gate, gate_p) + contract_cols(grad_up, up_p)
    both_parts = jnp.stack([back_part, back_part * gain_p.astype(jnp.float32)])
    grad_hn = both_parts[0]
    grad_z2 = both_parts[1]
    term_two = grad_hn * norm_two
    grad_res = grad_f + inv_two * (
        grad_z2 - norm_two * jnp.mean(grad_z2 * norm_two, axis=-1, keepdims=True)
    )
    grad_branch = grad_res.astype(jnp.bfloat16)
    grad_attn = contract_cols(grad_branch, wo_full).astype(jnp.bfloat16)
    grad_attn = grad_attn.reshape(seq_count, part_len, n_seq, q_width // n_seq)
    d_heads = lax.all_to_all(grad_attn, "seq", split_axis=2, concat_axis=1, tiled=True)
    d_heads = d_heads.reshape(seq_count, length, H // n_seq, HD)
    grad_q, grad_k, grad_v = attend_backward(q_heads, k_heads, v_heads, d_heads, log_sums)
    token_q, token_k, token_v = (
        lax.all_to_all(
            grad_q.astype(jnp.bfloat16), "seq", split_axis=1, concat_axis=2, tiled=True
        ).astype(grad_q.dtype),
        lax.all_to_all(
            grad_k.astype(jnp.bfloat16), "seq", split_axis=1, concat_axis=2, tiled=True
        ).astype(grad_k.dtype),
        lax.all_to_all(
            grad_v.astype(jnp.bfloat16), "seq", split_axis=1, concat_axis=2, tiled=True
        ).astype(grad_v.dtype),
    )
    grad_q_rows = (
        rotate(token_q.reshape(seq_count, part_len, H, HD), positions, -1.0)
        .astype(jnp.bfloat16)
        .reshape(row_total, q_width)
    )
    grad_k_rows = (
        rotate(token_k.reshape(seq_count, part_len, KVH, HD), positions, -1.0)
        .astype(jnp.bfloat16)
        .reshape(row_total, kv_width)
    )
    grad_v_rows = token_v.astype(jnp.bfloat16).reshape(row_total, kv_width)
    grad_normed = (
        contract_cols(grad_q_rows, wq_full)
        + contract_cols(grad_k_rows, wk_full)
        + contract_cols(grad_v_rows, wv_full)
    )
    grad_z1 = grad_normed * gain_one_f
    term_one = grad_normed * norm_one
    grad_x = grad_res + inv_one * (
        grad_z1 - norm_one * jnp.mean(grad_z1 * norm_one, axis=-1, keepdims=True)
    )
    tokens_grad = grad_x.astype(jnp.bfloat16).reshape(tokens.shape)
    grad_qkv = jnp.concatenate([grad_q_rows, grad_k_rows, grad_v_rows], axis=1)
    grad_gu = jnp.concatenate([grad_gate, grad_up], axis=1)
    o_rows = q_width // n_all
    d_rows = ff_width // n_all
    per_block = o_rows + d_rows
    col_gate = q_width + 2 * kv_width
    col_gain = col_gate + 2 * ff_width
    quarter_in = width // n_seq
    quarter_q = q_width // n_seq
    quarter_f = ff_width // n_seq

    def split_cols(values, cols):
        return values.astype(jnp.float32).reshape(row_total, n_seq, cols)

    x_part, h_part, a_part, m_part, one_part, two_part = (
        lax.all_to_all(
            split_cols(normed, quarter_in).astype(jnp.bfloat16),
            "seq",
            split_axis=1,
            concat_axis=0,
            tiled=True,
        ).astype(jnp.float32),
        lax.all_to_all(
            split_cols(piece_n, quarter_in).astype(jnp.bfloat16),
            "seq",
            split_axis=1,
            concat_axis=0,
            tiled=True,
        ).astype(jnp.float32),
        lax.all_to_all(
            split_cols(attn_rows, quarter_q).astype(jnp.bfloat16),
            "seq",
            split_axis=1,
            concat_axis=0,
            tiled=True,
        ).astype(jnp.float32),
        lax.all_to_all(
            split_cols(mlp_mid, quarter_f).astype(jnp.bfloat16),
            "seq",
            split_axis=1,
            concat_axis=0,
            tiled=True,
        ).astype(jnp.float32),
        lax.all_to_all(
            split_cols(term_one, quarter_in).astype(jnp.bfloat16),
            "seq",
            split_axis=1,
            concat_axis=0,
            tiled=True,
        ).astype(jnp.float32),
        lax.all_to_all(
            split_cols(term_two, quarter_in).astype(jnp.bfloat16),
            "seq",
            split_axis=1,
            concat_axis=0,
            tiled=True,
        ).astype(jnp.float32),
    )
    all_rows = n_seq * row_total
    x_part = x_part.reshape(all_rows, quarter_in).astype(jnp.bfloat16)
    h_part = h_part.reshape(all_rows, quarter_in).astype(jnp.bfloat16)
    a_part = a_part.reshape(all_rows, quarter_q).astype(jnp.bfloat16)
    m_part = m_part.reshape(all_rows, quarter_f).astype(jnp.bfloat16)
    gain_cols = jnp.stack(
        [
            jnp.sum(one_part.reshape(all_rows, quarter_in), axis=0),
            jnp.sum(two_part.reshape(all_rows, quarter_in), axis=0),
        ],
        axis=1,
    )
    seq_qkv, seq_gu, seq_branch, seq_cot = (
        lax.all_gather(grad_qkv, "seq", axis=0, tiled=True),
        lax.all_gather(grad_gu, "seq", axis=0, tiled=True),
        lax.all_gather(grad_branch, "seq", axis=0, tiled=True),
        lax.all_gather(grad_b, "seq", axis=0, tiled=True),
    )
    in_part = jnp.concatenate(
        [contract_rows(x_part, seq_qkv), contract_rows(h_part, seq_gu)], axis=1
    )
    o_part = contract_rows(a_part, seq_branch).reshape(n_fsdp, o_rows, width)
    d_part = contract_rows(m_part, seq_cot).reshape(n_fsdp, d_rows, width)
    out_part = jnp.concatenate([o_part, d_part], axis=1).reshape(n_fsdp * per_block, width)
    in_sum, out_sum, gain_sum = (
        lax.psum_scatter(
            in_part.astype(jnp.bfloat16), "fsdp", scatter_dimension=0, tiled=True
        ).astype(jnp.float32),
        lax.psum_scatter(
            out_part.astype(jnp.bfloat16), "fsdp", scatter_dimension=0, tiled=True
        ).astype(jnp.float32),
        lax.psum_scatter(
            gain_cols.astype(jnp.bfloat16), "fsdp", scatter_dimension=0, tiled=True
        ).astype(jnp.float32),
    )
    attn_gain_grad = gain_sum[:, 0]
    mlp_gain_grad = gain_sum[:, 1]
    w_q_grad = in_sum[:, :q_width]
    w_k_grad = in_sum[:, q_width : q_width + kv_width]
    w_v_grad = in_sum[:, q_width + kv_width : col_gate]
    w_gate_grad = in_sum[:, col_gate : col_gate + ff_width]
    w_up_grad = in_sum[:, col_gate + ff_width : col_gain]
    w_o_grad = out_sum[:o_rows]
    w_down_grad = out_sum[o_rows:]
    return (
        output,
        tokens_grad,
        attn_gain_grad,
        w_q_grad,
        w_k_grad,
        w_v_grad,
        w_o_grad,
        mlp_gain_grad,
        w_gate_grad,
        w_up_grad,
        w_down_grad,
    )


def solution(mesh):
    placed = (
        P("fsdp", "seq", None),
        P("fsdp", "seq"),
        P("fsdp"),
        P("fsdp", None),
        P("fsdp", None),
        P("fsdp", None),
        P("fsdp", None),
        P("fsdp"),
        P("fsdp", None),
        P("fsdp", None),
        P("fsdp", None),
        P("fsdp", "seq", None),
    )
    return jax.shard_map(
        shards,
        mesh=mesh,
        in_specs=placed,
        out_specs=(
            P("fsdp", "seq", None),
            P("fsdp", "seq", None),
            P(("seq", "fsdp")),
            P(("seq", "fsdp"), None),
            P(("seq", "fsdp"), None),
            P(("seq", "fsdp"), None),
            P(("seq", "fsdp"), None),
            P(("seq", "fsdp")),
            P(("seq", "fsdp"), None),
            P(("seq", "fsdp"), None),
            P(("seq", "fsdp"), None),
        ),
        check_vma=False,
    )
```

profile of v0, /device:TPU:11, one launch (start us, length us, event | category | flops | bytes accessed | tf_op | source)
XLA Modules:
  0.0 3462.3 jit_solution(11746547101020020471)
XLA Ops:
  11.9 14.7 all-gather.1
  28.4 31.4 all-gather.17.cloned.1.call-done
  69.4 40.3 %all-gather.19.cloned.1.call-done = bf16[2048,512]{1,0:T(8,128)(2,1)} async-done(((bf16[256,512]{1,0:T(8,128)(2,1)}), bf16[2048,512]{1,0:T(8,128)(2,1)}) %all-gather.19.cloned.1.call-update) | async-done | bytes 2097168 | tf_op jit(solution)/shard_map/all_gather | solution.py:154
  112.9 121.0 %all-gather.15.cloned.1.call-done = bf16[2048,2048]{1,0:T(8,128)(2,1)} async-done(((bf16[256,2048]{1,0:T(8,128)(2,1)}), bf16[2048,2048]{1,0:T(8,128)(2,1)}) %all-gather.15.cloned.1.call-update) | async-done | bytes 8388624 | tf_op jit(solution)/shard_map/all_gather | solution.py:152
  233.9 12.4 copy.135
  269.1 10.8 all-to-all-done
  282.5 33.1 while.47
  319.8 7.5 reshape.521
  327.8 8.0 reduce.10
  346.5 13.7 all-gather.2
  366.6 7.3 multiply_reduce_fusion.1
  375.4 623.4 %all-gather.23.cloned.1.call-done = bf16[2048,8192]{1,0:T(8,128)(2,1)} async-done(((bf16[256,8192]{1,0:T(8,128)(2,1)}), bf16[2048,8192]{1,0:T(8,128)(2,1)}) %all-gather.23.cloned.1.call-update) | async-done | bytes 33554448 | tf_op jit(solution)/shard_map/all_gather | solution.py:193
  998.8 18.7 fusion.89
  1017.6 620.4 %all-gather.25.cloned.1.call-done = bf16[2048,8192]{1,0:T(8,128)(2,1)} async-done(((bf16[256,8192]{1,0:T(8,128)(2,1)}), bf16[2048,8192]{1,0:T(8,128)(2,1)}) %all-gather.25.cloned.1.call-update) | async-done | bytes 33554448 | tf_op jit(solution)/shard_map/all_gather | solution.py:194
  1638.0 18.6 fusion.90
  1656.6 620.7 %all-gather.27.cloned.1.call-done = bf16[8192,2048]{1,0:T(8,128)(2,1)} async-done(((bf16[1024,2048]{1,0:T(8,128)(2,1)}), bf16[8192,2048]{1,0:T(8,128)(2,1)}) %all-gather.27.cloned.1.call-update) | async-done | bytes 33554448 | tf_op jit(solution)/shard_map/all_gather | solution.py:203
  2277.2 24.8 multiply_convert_fusion
  2302.1 17.0 fusion.91
  2319.1 17.9 multiply_reduce_fusion
  2352.6 12.5 all-to-all-done.4
  2367.8 101.2 %while.48 = (s32[]{:T(128)}, f32[1024,2,64]{0,2,1:T(8,128)}, f32[1024,2,64]{0,2,1:T(8,128)}, bf16[2,512,2,4,64]{1,4,3,2,0:T(8,128)(2,1)}, bf16[2,512,2,4,64]{1,4...) while((s32[]{:T(128)}, f32[1024,2,64]{0,2,1:T(8,128)}, ...), condition=%wide.region_9.10_spmd.clone, body=%wide.region_7.9_spmd.clone.sunk | while | flops 2748707328 | bytes 213834096 | solution.py:115
  2375.5 11.1 fusion.154
  2386.6 10.7 fusion.155
  2409.6 8.2 fusion.157
  2425.8 11.1 fusion.154
  2437.0 10.7 fusion.155
  2447.7 6.9 fusion.158
  2459.9 8.2 fusion.157
  2493.8 7.0 reshape.522
  2500.8 7.0 reduce.11
  2516.6 9.5 all-to-all-done.5
  2532.7 7.7 pad_maximum_fusion.2
  2561.4 9.7 all-to-all-done.12
  2579.8 19.7 all-to-all-done.8
  2610.2 7.7 all-to-all-done.9
  2617.9 7.1 all-to-all-start.13
  2631.5 84.9 %all-to-all-done.13 = bf16[256,4,2048]{2,0,1:T(8,128)(2,1)} async-done(((bf16[256,4,2048]{2,0,1:T(8,128)(2,1)}), bf16[256,4,2048]{2,0,1:T(8,128)(2,1)}, u32[]{:S(2)}, u32[]{:S(2)}) %all-to-all-start.13) | async-done | bytes 4194336 | tf_op jit(solution)/shard_map/all_to_all | solution.py:298
  2723.2 13.9 convolution_convert_fusion.1
  2742.2 7.6 pad_maximum_fusion.1
  2763.3 22.9 all-to-all-done.10
  2791.8 8.4 convolution_convert_fusion.2
  2800.2 15.6 all-to-all-done.11
  2815.8 56.9 %all-gather.31.cloned.1.call-done = bf16[1024,16384]{1,0:T(8,128)(2,1)} async-done(((bf16[256,16384]{1,0:T(8,128)(2,1)}), bf16[1024,16384]{1,0:T(8,128)(2,1)}) %all-gather.31.cloned.1.call-update) | async-done | bytes 33554448 | tf_op jit(solution)/shard_map/all_gather | solution.py:334
  2872.7 32.2 convolution_convert_fusion
  2904.9 15.3 pad_maximum_fusion
  2920.2 17.1 fusion.60
  2938.6 178.2 %reduce-scatter.8.cloned.1.call-done = bf16[320,2048]{1,0:T(8,128)(2,1)} async-done(((bf16[2560,2048]{1,0:T(8,128)(2,1)}), bf16[320,2048]{1,0:T(8,128)(2,1)}) %reduce-scatter.8.cloned.1.call-update) | async-done | bytes 1310736 | tf_op jit(solution)/shard_map/reduce_scatter | solution.py:348
  3121.4 326.9 %reduce-scatter.6.cloned.1.call-done = bf16[64,19456]{1,0:T(8,128)(2,1)} async-done(((bf16[512,19456]{1,0:T(8,128)(2,1)}), bf16[64,19456]{1,0:T(8,128)(2,1)}) %reduce-scatter.6.cloned.1.call-update) | async-done | bytes 2490384 | tf_op jit(solution)/shard_map/reduce_scatter | solution.py:345
  (284 shorter events, 283.2 us)
Async XLA Ops:
  7.2 52.6 %all-gather.17.cloned.1.call-start = ((), (), s32[]{:S(2)}) async-start(), calls=%async_computation.18 | async-start | bytes 2359296 | tf_op jit(solution)/shard_map/all_gather | solution.py:153
  7.9 101.8 %all-gather.19.cloned.1.call-start = ((), (), s32[]{:S(2)}) async-start(), calls=%async_computation.19 | async-start | bytes 2359296 | tf_op jit(solution)/shard_map/all_gather | solution.py:154
  8.7 225.2 %all-gather.15.cloned.1.call-start = ((), (), s32[]{:S(2)}) async-start(), calls=%async_computation.17 | async-start | bytes 9437184 | tf_op jit(solution)/shard_map/all_gather | solution.py:152
  9.4 357.2 %all-gather.21.cloned.1.call-start = ((), (), s32[]{:S(2)}) async-start(), calls=%async_computation.20 | async-start | bytes 9437184 | tf_op jit(solution)/shard_map/all_gather | solution.py:155
  10.0 988.9 %all-gather.23.cloned.1.call-start = ((), (), s32[]{:S(2)}) async-start(), calls=%async_computation.21 | async-start | bytes 37748736 | tf_op jit(solution)/shard_map/all_gather | solution.py:193
  10.6 16.6 copy-start.37
  10.6 16.7 copy-start.5
  10.6 1627.4 %all-gather.25.cloned.1.call-start = ((), (), s32[]{:S(2)}) async-start(), calls=%async_computation.22 | async-start | bytes 37748736 | tf_op jit(solution)/shard_map/all_gather | solution.py:194
  11.2 2266.1 %all-gather.27.cloned.1.call-start = ((), (), s32[]{:S(2)}) async-start(), calls=%async_computation.23 | async-start | bytes 37748736 | tf_op jit(solution)/shard_map/all_gather | solution.py:203
  27.2 219.0 %copy-start.29 = (f32[8,1,256]{2,1,0:T(1,128)}, f32[8,1,256]{2,1,0:T(1,128)S(1)}, u32[]{:S(2)}) copy-start(f32[8,1,256]{2,1,0:T(1,128)S(1)} %convert_element_type.361) | copy-start | bytes 24580
  27.5 218.7 %copy-start.31 = (f32[256]{0:T(256)}, f32[256]{0:T(256)S(1)}, u32[]{:S(2)}) copy-start(f32[256]{0:T(256)S(1)} %add_rsqrt_fusion.1) | copy-start | bytes 3076
  28.4 228.4 %copy-start.20 = (f32[256,32]{0,1:T(8,128)}, f32[256,32]{0,1:T(8,128)S(1)}, u32[]{:S(2)}) copy-start(f32[256,32]{0,1:T(8,128)S(1)} %get-tuple-element.335) | copy-start | bytes 98308
  64.3 188.1 %all-to-all-start.1 = ((bf16[1,256,4,128]{1,3,0,2:T(8,128)(2,1)}), bf16[1,256,4,128]{1,3,0,2:T(8,128)(2,1)S(1)}, u32[]{:S(2)}, u32[]{:S(2)}) async-start(bf16[1,256,4,128]{1,3,0,2:T(8,128)(2,1)} %bitcast.26), calls=%async_computation.1 | async-start | bytes 524288 | tf_op jit(solution)/shard_map/all_to_all | solution.py:180
  252.4 8.6 all-to-all-start.2
  261.7 18.1 all-to-all-start
  327.8 18.7 copy-start.39
  339.6 20.7 all-to-all-start.3
  345.7 2377.5 %all-gather.35.cloned.1.call-start = ((), (), s32[]{:S(2)}) async-start(), calls=%async_computation.29 | async-start | bytes 5242880 | tf_op jit(solution)/shard_map/all_gather | solution.py:336
  360.2 1976.8 %copy-start.25 = (f32[8,1,256]{2,1,0:T(1,128)}, f32[8,1,256]{2,1,0:T(1,128)S(1)}, u32[]{:S(2)}) copy-start(f32[8,1,256]{2,1,0:T(1,128)S(1)} %convert_element_type.362) | copy-start | bytes 24580
  373.9 1963.1 %copy-start.3 = (f32[256,2048]{1,0:T(8,128)}, f32[256,2048]{1,0:T(8,128)S(1)}, u32[]{:S(2)}) copy-start(f32[256,2048]{1,0:T(8,128)S(1)} %get-tuple-element.339) | copy-start | bytes 6291460
  374.0 1963.1 %copy-start.33 = (f32[256]{0:T(256)}, f32[256]{0:T(256)S(1)}, u32[]{:S(2)}) copy-start(f32[256]{0:T(256)S(1)} %add_rsqrt_fusion) | copy-start | bytes 3076
  2337.0 9.5 copy-start.35
  2347.9 17.2 all-to-all-start.4
  2351.9 385.3 %all-gather.33.cloned.1.call-start = ((), (), s32[]{:S(2)}) async-start(), calls=%async_computation.27 | async-start | bytes 5242880 | tf_op jit(solution)/shard_map/all_gather | solution.py:335
  2371.7 14.9 copy-start
  2397.3 6.9 copy-start.1
  2409.5 8.3 copy-start.2
  2422.0 14.9 copy-start
  2447.7 6.9 copy-start.1
  2459.9 8.3 copy-start.2
  2473.6 10.5 all-to-all-start.6
  2484.1 25.7 all-to-all-start.7
  2509.9 16.2 all-to-all-start.5
  2513.5 278.3 %all-gather.29.cloned.1.call-start = ((), (), s32[]{:S(2)}) async-start(), calls=%async_computation.24 | async-start | bytes 7864320 | tf_op jit(solution)/shard_map/all_gather | solution.py:333
  2532.6 340.1 %all-gather.31.cloned.1.call-start = ((), (), s32[]{:S(2)}) async-start(), calls=%async_computation.25 | async-start | bytes 41943040 | tf_op jit(solution)/shard_map/all_gather | solution.py:334
  2540.4 30.8 all-to-all-start.12
  2547.1 6.1 copy-start.9
  2547.1 6.1 copy-start.15
  2571.1 28.3 all-to-all-start.8
  2599.5 18.5 all-to-all-start.9
  2617.9 98.5 %all-to-all-start.13 = ((bf16[256,4,2048]{2,0,1:T(8,128)(2,1)}), bf16[256,4,2048]{2,0,1:T(8,128)(2,1)}, u32[]{:S(2)}, u32[]{:S(2)}) async-start(bf16[256,4,2048]{2,0,1:T(8,128)(2,1)} %bitcast.390), calls=%async_computation.14 | async-start | bytes 8388608 | tf_op jit(solution)/shard_map/all_to_all | solution.py:298
  2625.0 312.3 %reduce-scatter.10.cloned.1.call-start = ((), (), s32[]{:S(2)}) async-start(), calls=%async_computation.30 | async-start | bytes 147456
  2631.5 485.3 %reduce-scatter.8.cloned.1.call-start = ((), (), s32[]{:S(2)}) async-start(), calls=%async_computation.28 | async-start | bytes 11796480 | tf_op jit(solution)/shard_map/reduce_scatter | solution.py:348
  2752.4 9.8 copy-start.11
  2755.8 30.3 all-to-all-start.10
  2786.2 29.6 all-to-all-start.11
  2791.8 656.5 %reduce-scatter.6.cloned.1.call-start = ((), (), s32[]{:S(2)}) async-start(), calls=%async_computation.26 | async-start | bytes 22413312 | tf_op jit(solution)/shard_map/reduce_scatter | solution.py:345
  2872.7 32.2 copy-start.13
  (31 other events, 95.5 us)
Sparse Core Ops, SparseCore 0:
  10.1 49.5 all-gather.16
  61.9 47.7 all-gather.18
  111.8 122.0 all-gather.14
  235.9 123.1 all-gather.20
  360.4 638.3 all-gather.22
  1000.2 637.6 all-gather.24
  1639.5 637.6 all-gather.26
  2278.8 33.7 all-gather.34
  2354.3 34.5 all-gather.32
  2532.7 67.4 all-gather.28
  2601.8 270.7 all-gather.30
  2876.4 59.2 reduce-scatter.9
  2939.3 177.4 reduce-scatter.7
  3120.6 327.6 reduce-scatter.5
where the time goes:
time: 3470 us; the launch traced here: 3460 us
  waiting for transfers between devices  2820 us (81%)
  matrix products  292 us (8%)
  local copies, waits for them, and re-layouts  117 us (3%)
  other arithmetic  109 us (3%)
  starting transfers between devices  78.8 us (2%)
    all_gather x1, waiting for transfers between devices, shards(): gate_p = lax.all_gather(w_gate, 'fsdp', axis=0, tiled=True)  623 us
    all_gather x1, waiting for transfers between devices, shards(): lax.all_gather(w_down, 'fsdp', axis=0, tiled=True)  621 us
    all_gather x1, waiting for transfers between devices, shards(): up_p = lax.all_gather(w_up, 'fsdp', axis=0, tiled=True)  620 us
    reduce_scatter x1, waiting for transfers between devices, shards(): lax.psum_scatter(in_part.astype(jnp.bfloat16), 'fsdp', scatter_dimension=...  327 us
    reduce_scatter x1, waiting for transfers between devices, shards(): lax.psum_scatter(out_part.astype(jnp.bfloat16), 'fsdp', scatter_dimension...  178 us
    all_gather x1, waiting for transfers between devices, shards(): lax.all_gather(w_q, 'fsdp', axis=0, tiled=True)  121 us
    all_to_all x1, waiting for transfers between devices, shards(): lax.all_to_all(split_cols(mlp_mid, quarter_f).astype(jnp.bfloat16), 'seq'...  84.9 us
    dot_general x7, matrix products, contract_cols(): lax.dot_general(left, right, (((1,), (1,)), ((), ())), preferred_element_...  73.9 us
  transfers between devices with their start and end apart: 28, of which 19 were waited for; matrix products, arithmetic and copies ran while one was open for 15% of the time, Pallas kernels for 0%

commit v1 on v0

v1 whole, which is shorter than its diff:
```python
import math

import jax
import jax.numpy as jnp
from jax import lax
from jax.sharding import PartitionSpec as P

H = 32
KVH = 8
HD = 64
NY = 2


EPSILON = 1e-05
ROPE_BASE = 500000.0

F32 = jnp.float32
BF16 = jnp.bfloat16


def turn(values, cosine, sine):
    first, second = jnp.split(values, 2, axis=-1)
    return jnp.concatenate([first * cosine - second * sine, second * cosine + first * sine], axis=-1)


def scores_of(q_block, k_seq, offset, scaling):
    scores = jnp.einsum("qgrd,kgd->grqk", q_block, k_seq, preferred_element_type=F32) * scaling
    rows_at = offset + jnp.arange(q_block.shape[0], dtype=jnp.int32)
    cols_at = jnp.arange(k_seq.shape[0], dtype=jnp.int32)
    return jnp.where(rows_at[:, None] >= cols_at[None, :], scores, -1e30)


def attend_forward(q_heads, k_heads, v_heads):
    seq_count, length, groups_q, head_size = q_heads.shape
    groups_kv = k_heads.shape[2]
    ratio_kv = groups_q // groups_kv
    block_rows = min(512, length)
    blocks = length // block_rows
    scaling = 1.0 / math.sqrt(head_size)
    offsets = jnp.arange(blocks, dtype=jnp.int32) * block_rows

    def per_sequence(inputs):
        q_seq, k_seq, v_seq = inputs
        q_blocks = q_seq.reshape(blocks, block_rows, groups_kv, ratio_kv, head_size)

        def one_block(parts):
            q_block, offset = parts
            scores = scores_of(q_block, k_seq, offset, scaling)
            highest = jnp.max(scores, axis=-1, keepdims=True)
            exponent = jnp.exp(scores - highest)
            totals = jnp.sum(exponent, axis=-1, keepdims=True)
            probabilities = (exponent / totals).astype(BF16)
            mixed_out = jnp.einsum("grqk,kgd->qgrd", probabilities, v_seq, preferred_element_type=F32)
            return (mixed_out.astype(BF16), (highest + jnp.log(totals))[..., 0])

        return lax.map(one_block, (q_blocks, offsets))

    mixed_out, log_sums = lax.map(per_sequence, (q_heads, k_heads, v_heads))
    return (mixed_out.reshape(seq_count, length, groups_q * head_size), log_sums)


def attend_backward(q_heads, k_heads, v_heads, d_heads, log_sums):
    seq_count, length, groups_q, head_size = q_heads.shape
    groups_kv = k_heads.shape[2]
    ratio_kv = groups_q // groups_kv
    block_rows = min(512, length)
    blocks = length // block_rows
    scaling = 1.0 / math.sqrt(head_size)
    offsets = jnp.arange(blocks, dtype=jnp.int32) * block_rows

    def per_sequence(inputs):
        q_seq, k_seq, v_seq, d_seq, lse_seq = inputs
        q_blocks = q_seq.reshape(blocks, block_rows, groups_kv, ratio_kv, head_size)
        d_blocks = d_seq.reshape(blocks, block_rows, groups_kv, ratio_kv, head_size)

        def one_block(carry, parts):
            grad_k, grad_v = carry
            q_block, d_block, lse_block, offset = parts
            scores = scores_of(q_block, k_seq, offset, scaling)
            probabilities = jnp.exp(scores - lse_block[..., None])
            grad_prob = jnp.einsum("qgrd,kgd->grqk", d_block, v_seq, preferred_element_type=F32)
            inner = jnp.sum(grad_prob * probabilities, axis=-1, keepdims=True)
            grad_score = (probabilities * (grad_prob - inner)).astype(BF16)
            grad_q = jnp.einsum("grqk,kgd->qgrd", grad_score, k_seq, preferred_element_type=F32) * scaling
            grad_k = (
                grad_k
                + jnp.einsum("grqk,qgrd->kgd", grad_score, q_block, preferred_element_type=F32) * scaling
            )
            grad_v = grad_v + jnp.einsum(
                "grqk,qgrd->kgd", probabilities.astype(BF16), d_block, preferred_element_type=F32
            )
            return ((grad_k, grad_v), grad_q)

        zeros_kv = jnp.zeros((length, groups_kv, head_size), F32)
        (grad_k, grad_v), grad_q = lax.scan(
            one_block, (zeros_kv, zeros_kv), (q_blocks, d_blocks, lse_seq, offsets)
        )
        return (grad_q, grad_k, grad_v)

    grad_q, grad_k, grad_v = lax.map(per_sequence, (q_heads, k_heads, v_heads, d_heads, log_sums))
    return (
        grad_q.reshape(seq_count, length, groups_q * head_size),
        grad_k.reshape(seq_count, length, groups_kv * head_size),
        grad_v.reshape(seq_count, length, groups_kv * head_size),
    )


def dot_rows(left, right):
    return lax.dot_general(left, right, (((0,), (0,)), ((), ())), preferred_element_type=F32)


def dot_cols(left, right):
    return lax.dot_general(left, right, (((1,), (1,)), ((), ())), preferred_element_type=F32)


def dot(left, right):
    return jnp.dot(left, right, preferred_element_type=F32)


def swap_core(value):
    return lax.ppermute(value, "seq", [(i, i ^ 1) for i in range(lax.axis_size("seq"))])


def swap_x(value):
    return lax.ppermute(value, "seq", [(i, i ^ 2) for i in range(lax.axis_size("seq"))])


def swap_y(value):
    return lax.ppermute(value, "fsdp", [(i, i ^ 1) for i in range(lax.axis_size("fsdp"))])


def gather_plane(own):
    half = own.shape[0] // 2
    x_part = swap_x(own)
    y_part = swap_y(own)
    core = swap_core(own)
    xy_up = swap_y(x_part[:half])
    xy_low = swap_x(y_part[half:])
    others = jnp.concatenate([x_part, y_part, xy_up, xy_low])
    return jnp.concatenate([own, others, core, swap_core(others)])


def scatter_plane(make):
    sent = swap_core(make(1).astype(BF16))
    mine = (make(0) + sent.astype(F32)).astype(BF16)
    rows = mine.shape[0] // 4
    half = rows // 2
    own, x_part, y_part, xy_part = (mine[i * rows : (i + 1) * rows].astype(F32) for i in range(4))
    from_x = swap_x(mine[3 * rows : 3 * rows + half]).astype(F32)
    from_y = swap_y(mine[3 * rows + half :]).astype(F32)
    x_sum = jnp.concatenate([x_part[:half], x_part[half:] + from_y])
    y_sum = jnp.concatenate([y_part[:half] + from_x, y_part[half:]])
    return own + swap_x(x_sum.astype(BF16)).astype(F32) + swap_y(y_sum.astype(BF16)).astype(F32)


def planes():
    return lax.axis_size("fsdp") // NY


def z_groups():
    return [[z * NY + y for z in range(planes())] for y in range(NY)]


def plane_groups():
    n_fsdp = lax.axis_size("fsdp")
    return [
        [s * n_fsdp + z * NY + y for s in range(lax.axis_size("seq")) for y in range(NY)]
        for z in range(planes())
    ]


def gather_z(own):
    return lax.all_gather(own, "fsdp", axis=0, tiled=True, axis_index_groups=z_groups())


def scatter_z(terms):
    return lax.psum_scatter(
        terms, "fsdp", scatter_dimension=0, tiled=True, axis_index_groups=z_groups()
    )


def pick(values, index, axis):
    return lax.dynamic_index_in_dim(values, index, axis, keepdims=False)


def shards(
    tokens, positions, attn_gain, w_q, w_k, w_v, w_o, mlp_gain, w_gate, w_up, w_down, cotangent
):
    seq_count, part_len, width = tokens.shape
    n_seq = lax.axis_size("seq")
    n_fsdp = lax.axis_size("fsdp")
    n_all = n_seq * n_fsdp
    n_z = planes()
    n_team = n_seq * NY
    s = lax.axis_index("seq")
    f = lax.axis_index("fsdp")
    z, y = f // NY, lax.rem(f, NY)
    length = part_len * n_seq
    w_rows = w_q.shape[0]
    q_width, kv_width, ff_width = w_q.shape[1], w_k.shape[1], w_gate.shape[1]
    q_cols, kv_cols, ff_cols = q_width // n_team, kv_width // n_team, ff_width // n_team
    ff_block = ff_cols // n_z

    x_own = tokens.reshape(part_len, width)
    cot_own = cotangent.reshape(part_len, width)
    x_all = gather_plane(x_own)

    gains = jnp.stack([attn_gain, mlp_gain])
    gains = lax.all_to_all(
        jnp.broadcast_to(gains, (n_fsdp, *gains.shape)), "fsdp", split_axis=0, concat_axis=0, tiled=True
    )
    gains = gains.transpose(1, 0, 2).reshape(2, width).astype(F32)
    gain_one, gain_two = gains[0], gains[1]
    places = lax.all_to_all(
        jnp.broadcast_to(positions.reshape(part_len), (n_seq, part_len)),
        "seq",
        split_axis=0,
        concat_axis=0,
        tiled=True,
    ).reshape(length)
    places = jnp.stack([places, swap_y(places)])

    def cols_qkv(y_of):
        team = s * NY + y_of
        return jnp.concatenate(
            [
                lax.dynamic_slice_in_dim(w_q, team * q_cols, q_cols, 1),
                lax.dynamic_slice_in_dim(w_k, team * kv_cols, kv_cols, 1),
                lax.dynamic_slice_in_dim(w_v, team * kv_cols, kv_cols, 1),
            ],
            axis=1,
        )

    def cols_ff(weight, y_of):
        return jnp.concatenate(
            [
                lax.dynamic_slice_in_dim(weight, ((at * NY + y_of) * n_seq + s) * ff_block, ff_block, 1)
                for at in range(n_z)
            ],
            axis=1,
        )

    def both_rows(cols_of):
        ours = cols_of(y)
        others = swap_y(cols_of(1 - y))
        rows = jnp.where(y == 0, jnp.stack([ours, others]), jnp.stack([others, ours]))
        return gather_z(rows.reshape(NY * w_rows, -1))

    def rows_o(weight):
        sub = weight.shape[0] // n_seq
        mine = lax.dynamic_slice_in_dim(weight, s * sub, sub, 0)
        pairs = []
        for block in range(n_all):
            team, z_to = block // n_z, block % n_z
            source = (block % n_seq) * n_fsdp + block // n_seq
            target = (team // NY) * n_fsdp + z_to * NY + team % NY
            pairs.append((source, target))
        return lax.ppermute(mine, ("seq", "fsdp"), pairs)

    wqkv = both_rows(cols_qkv)
    wo = gather_z(rows_o(w_o))
    wg = both_rows(lambda y_of: cols_ff(w_gate, y_of))
    wu = both_rows(lambda y_of: cols_ff(w_up, y_of))
    wd = gather_z(lax.dynamic_slice_in_dim(w_down, s * ff_block, ff_block, 0))
    cot_all = gather_plane(cot_own)

    def normed(rows):
        rows = rows.astype(F32)
        inv = lax.rsqrt(jnp.mean(rows * rows, axis=-1, keepdims=True) + EPSILON)
        return rows * inv, inv

    xn = (normed(x_all)[0] * gain_one).astype(BF16)
    z_one, inv_one = normed(x_own)

    def in_order(values):
        blocks = values.reshape(2, NY, 2, part_len, *values.shape[1:])
        found = []
        for at in range(n_seq):
            relative = jnp.bitwise_xor(s, at)
            found.append(pick(pick(blocks, relative % 2, 0), relative // 2, 1))
        return jnp.concatenate(found, axis=1)

    def out_of_order(values):
        blocks = values.reshape(NY, n_seq, part_len, *values.shape[2:])
        found = []
        for core in range(2):
            for y_at in range(NY):
                for x_at in range(2):
                    found.append(pick(blocks[y_at], jnp.bitwise_xor(s, x_at * 2 + core), 0))
        return jnp.concatenate(found)

    half_head = HD // 2
    freqs = jnp.exp(jnp.arange(half_head).astype(F32) * (-2.0 * math.log(ROPE_BASE) / HD))
    angles = places.astype(F32)[..., None] * freqs
    cosine, sine = jnp.cos(angles)[:, :, None, :], jnp.sin(angles)[:, :, None, :]
    qkv = in_order(dot(xn, wqkv))
    q_heads = qkv[..., :q_cols].reshape(NY, length, q_cols // HD, HD)
    k_heads = qkv[..., q_cols : q_cols + kv_cols].reshape(NY, length, kv_cols // HD, HD)
    v_heads = qkv[..., q_cols + kv_cols :].reshape(NY, length, kv_cols // HD, HD).astype(BF16)
    q_heads = turn(q_heads, cosine, sine).astype(BF16)
    k_heads = turn(k_heads, cosine, sine).astype(BF16)
    mixed, log_sums = attend_forward(q_heads, k_heads, v_heads)
    attn_rows = out_of_order(mixed)
    side = attn_rows.shape[0] // 2
    residual = x_own.astype(F32) + scatter_plane(
        lambda core: dot(attn_rows[core * side : (core + 1) * side], wo)
    )

    z_two, inv_two = normed(residual)
    hn = gather_plane((z_two * gain_two).astype(BF16))
    gate = dot(hn, wg)
    up = dot(hn, wu)
    sigmoid_g = jax.nn.sigmoid(gate)
    active = gate * sigmoid_g
    mid = (active * up).astype(BF16)
    branch = scatter_plane(lambda core: dot(mid[core * side : (core + 1) * side], wd))
    output = (residual + branch).astype(BF16).reshape(tokens.shape)

    grad_mid = dot_cols(cot_all, wd)
    grad_gate = (grad_mid * up * sigmoid_g * (1.0 + gate * (1.0 - sigmoid_g))).astype(BF16)
    grad_up = (grad_mid * active).astype(BF16)

    def ff_back(core):
        at = slice(core * side, (core + 1) * side)
        return dot_cols(grad_gate[at], wg) + dot_cols(grad_up[at], wu)

    grad_hn = scatter_plane(ff_back)
    grad_z2 = grad_hn * gain_two
    grad_res = cot_own.astype(F32) + inv_two * (
        grad_z2 - z_two * jnp.mean(grad_z2 * z_two, axis=-1, keepdims=True)
    )
    da = gather_plane(grad_res.astype(BF16))
    d_heads = in_order(dot_cols(da, wo).astype(BF16)).reshape(NY, length, q_cols // HD, HD)
    grad_q, grad_k, grad_v = attend_backward(q_heads, k_heads, v_heads, d_heads, log_sums)
    grad_q = turn(grad_q.reshape(q_heads.shape), cosine, -sine).astype(BF16)
    grad_k = turn(grad_k.reshape(k_heads.shape), cosine, -sine).astype(BF16)
    grad_qkv = out_of_order(
        jnp.concatenate(
            [
                grad_q.reshape(NY, length, q_cols),
                grad_k.reshape(NY, length, kv_cols),
                grad_v.astype(BF16),
            ],
            axis=-1,
        )
    )
    grad_xn = scatter_plane(lambda core: dot_cols(grad_qkv[core * side : (core + 1) * side], wqkv))
    grad_z1 = grad_xn * gain_one
    grad_x = grad_res + inv_one * (
        grad_z1 - z_one * jnp.mean(grad_z1 * z_one, axis=-1, keepdims=True)
    )
    tokens_grad = grad_x.astype(BF16).reshape(tokens.shape)

    out_rows = width // n_all

    def to_owners(grad):
        blocks = grad.reshape(n_seq, n_z, NY * out_rows, grad.shape[1]).transpose(1, 0, 2, 3)
        summed = scatter_z(blocks.reshape(grad.shape))
        spread = lax.all_to_all(
            summed, ("seq", "fsdp"), split_axis=0, concat_axis=0, tiled=True, axis_index_groups=plane_groups()
        )
        return spread.reshape(n_team, out_rows, -1).astype(F32)

    def rows_to_owners(grad, block_of):
        summed = scatter_z(grad)
        pairs = [
            (si * n_fsdp + zi * NY + yi, block_of(si, zi, yi))
            for si in range(n_seq)
            for zi in range(n_z)
            for yi in range(NY)
        ]
        return lax.ppermute(summed, ("seq", "fsdp"), pairs).astype(F32)

    w_down_grad = rows_to_owners(
        dot_rows(mid, cot_all).astype(BF16), lambda si, zi, yi: (zi * NY + yi) * n_seq + si
    )

    def ff_columns(grad):
        spread = to_owners(dot_rows(hn, grad).astype(BF16))
        spread = spread.reshape(n_seq, NY, out_rows, n_z, ff_block)
        return spread.transpose(2, 3, 1, 0, 4).reshape(out_rows, ff_width)

    w_gate_grad = ff_columns(grad_gate)
    w_up_grad = ff_columns(grad_up)
    w_o_grad = rows_to_owners(
        dot_rows(attn_rows, da).astype(BF16), lambda si, zi, yi: (si * NY + yi) * n_z + zi
    )
    spread = to_owners(dot_rows(xn, grad_qkv).astype(BF16)).transpose(1, 0, 2)
    w_q_grad = spread[..., :q_cols].reshape(out_rows, q_width)
    w_k_grad = spread[..., q_cols : q_cols + kv_cols].reshape(out_rows, kv_width)
    w_v_grad = spread[..., q_cols + kv_cols :].reshape(out_rows, kv_width)

    gain_terms = jnp.stack([jnp.sum(grad_xn * z_one, axis=0), jnp.sum(grad_hn * z_two, axis=0)])
    gain_terms = gain_terms.reshape(2, n_all, out_rows).transpose(1, 0, 2)
    gain_sums = jnp.sum(
        lax.all_to_all(gain_terms, ("seq", "fsdp"), split_axis=0, concat_axis=0, tiled=True), axis=0
    )
    return (
        output,
        tokens_grad,
        gain_sums[0],
        w_q_grad,
        w_k_grad,
        w_v_grad,
        w_o_grad,
        gain_sums[1],
        w_gate_grad,
        w_up_grad,
        w_down_grad,
    )


def solution(mesh):
    by_both = P("fsdp", "seq", None)
    by_rows = P("fsdp", None)
    spread = P(("seq", "fsdp"), None)
    return jax.shard_map(
        shards,
        mesh=mesh,
        in_specs=(
            by_both,
            P("fsdp", "seq"),
            P("fsdp"),
            by_rows,
            by_rows,
            by_rows,
            by_rows,
            P("fsdp"),
            by_rows,
            by_rows,
            by_rows,
            by_both,
        ),
        out_specs=(
            by_both,
            by_both,
            P(("seq", "fsdp")),
            spread,
            spread,
            spread,
            spread,
            P(("seq", "fsdp")),
            spread,
            spread,
            spread,
        ),
        check_vma=False,
    )
```

time: 3470 us -> 896 us (0.26)
  waiting for transfers between devices: 2820 us -> 248 us
  starting transfers between devices: 78.8 us -> 130 us
    all_gather x11 -> x5, waiting for transfers between devices: 2110 us -> 20.6 us  [gather_z(): lax.all_gather(own, 'fsdp', axis=0, tiled=True, axis_index_groups=z_group...]
    reduce_scatter x2 -> x5, waiting for transfers between devices: 505 us -> 7.3 us  [scatter_z(): lax.psum_scatter(terms, 'fsdp', scatter_dimension=0, tiled=True, axis_ind...]
    ppermute x0 -> x51, waiting for transfers between devices: none -> 205 us  [the longest x16 146 us: swap_x(): lax.ppermute(value, 'seq', [(i, i ^ 2) for i in range(lax.axis_size('seq'...]
    all_to_all x14 -> x6, waiting for transfers between devices: 196 us -> 15.3 us  [the longest x3 15 us: to_owners(): lax.all_to_all(summed, ('seq', 'fsdp'), split_axis=0, concat_axis=0, tile...]
    ppermute x0 -> x51, starting transfers between devices: none -> 94.2 us  [the longest x2 25.8 us: rows_to_owners(): return lax.ppermute(summed, ('seq', 'fsdp'), pairs).astype(F32)]
    all_to_all x14 -> x6, starting transfers between devices: 78.4 us -> 35.3 us  [the longest x3 18.1 us: to_owners(): lax.all_to_all(summed, ('seq', 'fsdp'), split_axis=0, concat_axis=0, tile...]
    dot_general x28 -> x40, matrix products: 271 us -> 237 us  [the longest x8 71.9 us: dot_cols(): lax.dot_general(left, right, (((1,), (1,)), ((), ())), preferred_element_...]
  transfers between devices with their start and end apart: 28 -> 67, of which waited for: 19 -> 26; matrix products, arithmetic and copies ran while one was open for 15% -> 48% of each run, Pallas kernels for 0% -> 0%
where the time goes in v1:
time: 896 us; the launch traced here: 886 us
  matrix products  262 us (29%)
  waiting for transfers between devices  248 us (28%)
  local copies, waits for them, and re-layouts  138 us (15%)
  starting transfers between devices  130 us (15%)
  other arithmetic  89.5 us (10%)
  between operations  16.2 us (2%)
    ppermute x16, waiting for transfers between devices, swap_x(): lax.ppermute(value, 'seq', [(i, i ^ 2) for i in range(lax.axis_size('seq'...  146 us
    dot_general x8, matrix products, dot_cols(): lax.dot_general(left, right, (((1,), (1,)), ((), ())), preferred_element_...  71.9 us
    dot_general x7, matrix products, dot(): return jnp.dot(left, right, preferred_element_type=F32)  60.9 us
    ppermute x20, waiting for transfers between devices, swap_y(): lax.ppermute(value, 'fsdp', [(i, i ^ 1) for i in range(lax.axis_size('fsd...  58.8 us
    dot_general x5, matrix products, dot_rows(): lax.dot_general(left, right, (((0,), (0,)), ((), ())), preferred_element_...  49.8 us
    unnamed x224, local copies, waits for them, and re-layouts  36.1 us
    ppermute x2, starting transfers between devices, rows_to_owners(): return lax.ppermute(summed, ('seq', 'fsdp'), pairs).astype(F32)  25.8 us
    ppermute x12, starting transfers between devices, swap_core(): lax.ppermute(value, 'seq', [(i, i ^ 1) for i in range(lax.axis_size('seq'...  22.1 us
  transfers between devices with their start and end apart: 67, of which 26 were waited for; matrix products, arithmetic and copies ran while one was open for 48% of the time, Pallas kernels for 0%

profile of v1, /device:TPU:11, one launch (start us, length us, event | category | flops | bytes accessed | tf_op | source)
XLA Modules:
  0.0 885.6 jit_solution(18251063941823556918)
XLA Ops:
  18.0 22.3 %collective-permute-done = bf16[256,2048]{1,0:T(8,128)(2,1)S(1)} collective-permute-done((bf16[256,2048]{1,0:T(8,128)(2,1)}, bf16[256,2048]{1,0:T(8,128)(2,1)S(1)}, u32[]{:S(2)}, u32[]{:S(2)}) %collective-permute-start) | collective-permute-done | bytes 1048608 | tf_op jit(solution)/shard_map/ppermute | solution.py:125
  58.5 5.7 pad_maximum_fusion
  74.4 5.4 collective-permute-done.7
  97.6 5.1 fusion.66
  102.8 7.8 fusion.74
  117.0 40.1 %while.58 = (s32[]{:T(128)}, bf16[2,2,512,1,4,64]{2,5,4,1,3,0:T(8,128)(2,1)}, f32[2,2,1,4,512]{4,3,1,2,0:T(4,128)S(1)}, bf16[2,1024,4,64]{1,3,2,0:T(8,128)(2,1)S...) while((s32[]{:T(128)}, ...), condition=%wide.region_6.7_spmd.clone, body=%wide.region_1.6_spmd.clone.sunk | while | flops 562690560 | bytes 32871208 | solution.py:58
  118.5 17.6 %while.61 = (s32[]{:T(128)}, bf16[2,512,1,4,64]{1,4,3,2,0:T(8,128)(2,1)S(1)}, f32[2,1,4,512]{3,2,1,0:T(4,128)S(1)}, s32[2]{0:T(128)S(1)}, bf16[2,512,1,4,64]{1,4...) while((s32[]{:T(128)}, ...), condition=%wide.region_5.5_spmd, body=%wide.region_2.4_spmd.sunk | while | flops 562690560 | bytes 28119152 | solution.py:56
  138.4 17.6 %while.61 = (s32[]{:T(128)}, bf16[2,512,1,4,64]{1,4,3,2,0:T(8,128)(2,1)S(1)}, f32[2,1,4,512]{3,2,1,0:T(4,128)S(1)}, s32[2]{0:T(128)S(1)}, bf16[2,512,1,4,64]{1,4...) while((s32[]{:T(128)}, ...), condition=%wide.region_5.5_spmd, body=%wide.region_2.4_spmd.sunk | while | flops 562690560 | bytes 28119152 | solution.py:56
  170.5 13.4 %collective-permute-done.20 = bf16[256,1024]{1,0:T(8,128)(2,1)S(1)} collective-permute-done((bf16[256,1024]{1,0:T(8,128)(2,1)S(1)}, bf16[256,1024]{1,0:T(8,128)(2,1)S(1)}, u32[]{:S(2)}, u32[]{:S(2)}) %collective-permute-start.20) | collective-permute-done | bytes 524320 | tf_op jit(solution)/shard_map/ppermute | solution.py:129
  192.5 9.7 %collective-permute-done.10 = bf16[128,2048]{1,0:T(8,128)(2,1)S(1)} collective-permute-done((bf16[128,2048]{1,0:T(8,128)(2,1)S(1)}, bf16[128,2048]{1,0:T(8,128)(2,1)S(1)}, u32[]{:S(2)}, u32[]{:S(2)}) %collective-permute-start.10) | collective-permute-done | bytes 524320 | tf_op jit(solution)/shard_map/ppermute | solution.py:129
  204.4 20.3 %collective-permute-done.27 = bf16[256,2048]{1,0:T(8,128)(2,1)S(1)} collective-permute-done((bf16[256,2048]{1,0:T(8,128)(2,1)}, bf16[256,2048]{1,0:T(8,128)(2,1)S(1)}, u32[]{:S(2)}, u32[]{:S(2)}) %collective-permute-start.27) | collective-permute-done | bytes 1048608 | tf_op jit(solution)/shard_map/ppermute | solution.py:125
  226.3 20.7 %collective-permute-done.11 = bf16[256,2048]{1,0:T(8,128)(2,1)S(1)} collective-permute-done((bf16[256,2048]{1,0:T(8,128)(2,1)S(1)}, bf16[256,2048]{1,0:T(8,128)(2,1)S(1)}, u32[]{:S(2)}, u32[]{:S(2)}) %collective-permute-start.11) | collective-permute-done | bytes 1048608 | tf_op jit(solution)/shard_map/ppermute | solution.py:125
  252.7 5.6 collective-permute-done.29
  263.6 17.1 %collective-permute-done.14 = bf16[256,2048]{1,0:T(8,128)(2,1)S(1)} collective-permute-done((bf16[256,2048]{1,0:T(8,128)(2,1)S(1)}, bf16[256,2048]{1,0:T(8,128)(2,1)S(1)}, u32[]{:S(2)}, u32[]{:S(2)}) %collective-permute-start.14) | collective-permute-done | bytes 1048608 | tf_op jit(solution)/shard_map/ppermute | solution.py:125
  317.3 14.5 %fusion.162 = f32[2048,1024]{1,0:T(8,128)} fusion(bf16[2048,2048]{1,0:T(8,128)(2,1)} %constant_dynamic-update-slice_fusion.7, bf16[2048,1024]{1,0:T(8,128)(2,1)} %all-gather.12.cloned.1.call-done), kind=kOutput, calls=%fused_computation.355 | convolution fusion | flops 8589934592 | bytes 20971520 | tf_op jit(solution)/shard_map/dot_general | solution.py:117
  331.8 14.5 %fusion.161 = f32[2048,1024]{1,0:T(8,128)} fusion(bf16[2048,2048]{1,0:T(8,128)(2,1)} %constant_dynamic-update-slice_fusion.7, bf16[2048,1024]{1,0:T(8,128)(2,1)} %all-gather.10.cloned.1.call-done), kind=kOutput, calls=%fused_computation.354 | convolution fusion | flops 8589934592 | bytes 20971520 | tf_op jit(solution)/shard_map/dot_general | solution.py:117
  346.4 20.5 %all-gather.14.cloned.1.call-done = bf16[1024,2048]{1,0:T(8,128)(2,1)} async-done(((bf16[256,2048]{1,0:T(8,128)(2,1)}), bf16[1024,2048]{1,0:T(8,128)(2,1)}) %all-gather.14.cloned.1.call-update) | async-done | bytes 4194320 | tf_op jit(solution)/shard_map/all_gather | solution.py:173
  366.9 23.6 %multiply_convert_fusion = (bf16[2048,1024]{1,0:T(8,128)(2,1)}, bf16[2048,1024]{1,0:T(8,128)(2,1)}, bf16[2048,1024]{1,0:T(8,128)(2,1)}) fusion(f32[2048,1024]{1,0:T(8,128)} %fusion.161, f32[2048,1024]{1,0:T(8,128)} %fusion.162, bf16[2048,2048]{1,0:T(8,128)(2,1)} %copy-done.65, bf16[1024,2048]{1,0:T(8,128)(2,1)} %all-gather.14.cloned.1.call-done), kind=kOutput, calls=%fused_computation.90 | convolution fusion | flops 8621391872 | bytes 41943040 | tf_op jit(solution)/shard_map/dot_general | solution.py:113
  390.5 12.7 %convolution_convert_fusion.5 = bf16[2048,1024]{1,0:T(8,128)(2,1)S(1)} fusion(bf16[2048,2048]{1,0:T(8,128)(2,1)} %constant_dynamic-update-slice_fusion.7, bf16[2048,1024]{1,0:T(8,128)(2,1)} %get-tuple-element.493), kind=kOutput, calls=%fused_computation.102 | convolution fusion | flops 8592031744 | bytes 16777216 | tf_op jit(solution)/shard_map/dot_general | solution.py:109
  405.9 9.4 %convolution_convert_fusion.3 = bf16[1024,2048]{1,0:T(8,128)(2,1)} fusion(bf16[1024,2048]{1,0:T(8,128)(2,1)} %all-gather.14.cloned.1.call-done, bf16[2048,1024]{1,0:T(8,128)(2,1)} %get-tuple-element.494), kind=kOutput, calls=%fused_computation.100 | convolution fusion | flops 4297064448 | bytes 10485760 | tf_op jit(solution)/shard_map/dot_general | solution.py:117
  420.6 6.6 add_convert_fusion.2
  427.2 11.5 %convolution_convert_fusion.4 = bf16[2048,1024]{1,0:T(8,128)(2,1)S(1)} fusion(bf16[2048,2048]{1,0:T(8,128)(2,1)} %constant_dynamic-update-slice_fusion.7, bf16[2048,1024]{1,0:T(8,128)(2,1)S(1)} %copy-done.89), kind=kOutput, calls=%fused_computation.101 | convolution fusion | flops 8592031744 | bytes 16777216 | tf_op jit(solution)/shard_map/dot_general | solution.py:109
  441.3 10.9 %fusion.87 = f32[1024,2048]{1,0:T(8,128)} fusion(bf16[2048,1024]{1,0:T(8,128)(2,1)} %all-gather.10.cloned.1.call-done, bf16[2048,1024]{1,0:T(8,128)(2,1)} %get-tuple-element.493), kind=kOutput, calls=%fused_computation.129 | convolution fusion | flops 4294967296 | bytes 14680064 | tf_op jit(solution)/shard_map/dot_general | solution.py:113
  452.2 6.5 add_convert_fusion.3
  460.5 11.0 %add_convert_fusion.1 = bf16[1024,2048]{1,0:T(8,128)(2,1)S(1)} fusion(bf16[1024,2048]{1,0:T(8,128)(2,1)} %collective-permute-done.33, f32[1024,2048]{1,0:T(8,128)} %fusion.87, bf16[2048,1024]{1,0:T(8,128)(2,1)} %all-gather.12.cloned.1.call-done, bf16[2048,1024]{1,0:T(8,128)(2,1)} %get-tuple-element.492), kind=kOutput, calls=%fused_computation.88 | convolution fusion | flops 4303355904 | bytes 23068672 | tf_op jit(solution)/shard_map/dot_general | solution.py:113
  475.5 8.5 collective-permute-done.34
  487.2 19.3 %collective-permute-done.24 = bf16[256,2048]{1,0:T(8,128)(2,1)S(1)} collective-permute-done((bf16[256,2048]{1,0:T(8,128)(2,1)S(1)}, bf16[256,2048]{1,0:T(8,128)(2,1)S(1)}, u32[]{:S(2)}, u32[]{:S(2)}) %collective-permute-start.24) | collective-permute-done | bytes 1048608 | tf_op jit(solution)/shard_map/ppermute | solution.py:125
  506.6 22.3 %collective-permute-done.35 = bf16[256,2048]{1,0:T(8,128)(2,1)S(1)} collective-permute-done((bf16[256,2048]{1,0:T(8,128)(2,1)S(1)}, bf16[256,2048]{1,0:T(8,128)(2,1)S(1)}, u32[]{:S(2)}, u32[]{:S(2)}) %collective-permute-start.35) | collective-permute-done | bytes 1048608 | tf_op jit(solution)/shard_map/ppermute | solution.py:125
  538.8 20.2 %collective-permute-done.38 = bf16[256,2048]{1,0:T(8,128)(2,1)S(1)} collective-permute-done((bf16[256,2048]{1,0:T(8,128)(2,1)S(1)}, bf16[256,2048]{1,0:T(8,128)(2,1)S(1)}, u32[]{:S(2)}, u32[]{:S(2)}) %collective-permute-start.38) | collective-permute-done | bytes 1048608 | tf_op jit(solution)/shard_map/ppermute | solution.py:125
  578.0 13.3 %convolution_convert_fusion.1 = bf16[1024,2048]{1,0:T(8,128)(2,1)} fusion(bf16[2048,1024]{1,0:T(8,128)(2,1)S(1)} %copy-done.88, bf16[2048,2048]{1,0:T(8,128)(2,1)} %copy-done.65), kind=kOutput, calls=%fused_computation.98 | convolution fusion | flops 8592031744 | bytes 16777216 | tf_op jit(solution)/shard_map/dot_general | solution.py:109
  602.3 5.8 convolution_convert_fusion.8
  609.9 100.7 %while.60 = (s32[]{:T(128)}, f32[2,2,512,1,4,64]{2,1,5,4,0,3:T(2,128)}, f32[2,1024,1,64]{1,3,2,0:T(8,128)}, bf16[2,1024,1,64]{1,3,2,0:T(8,128)(2,1)}, bf16[2,102...) while((s32[]{:T(128)}, ...), condition=%wide.region_14.15_spmd.clone, body=%wide.region_10.14_spmd.clone.sunk | while | flops 1374616064 | bytes 128415704 | solution.py:100
  613.4 42.5 %while.62 = (s32[]{:T(128)}, f32[1024,1,64]{0,2,1:T(8,128)S(1)}, f32[1024,1,64]{0,2,1:T(8,128)}, f32[2,512,1,4,64]{1,4,3,2,0:T(8,128)}, bf16[2,512,1,4,64]{1,4,3...) while((s32[]{:T(128)}, f32[1024,1,64]{0,2,1:T(8,128)S(1)}, ...), condition=%wide.region_13.13_spmd.clone, body=%wide.region_11.12_spmd.clone.sunk | while | flops 1374616064 | bytes 118420184 | solution.py:95
  629.1 5.5 fusion.224
  650.2 5.6 fusion.224
  663.6 42.3 %while.62 = (s32[]{:T(128)}, f32[1024,1,64]{0,2,1:T(8,128)S(1)}, f32[1024,1,64]{0,2,1:T(8,128)}, f32[2,512,1,4,64]{1,4,3,2,0:T(8,128)}, bf16[2,512,1,4,64]{1,4,3...) while((s32[]{:T(128)}, f32[1024,1,64]{0,2,1:T(8,128)S(1)}, ...), condition=%wide.region_13.13_spmd.clone, body=%wide.region_11.12_spmd.clone.sunk | while | flops 1374616064 | bytes 118420184 | solution.py:95
  679.3 5.4 fusion.224
  700.4 5.5 fusion.224
  723.1 5.3 convolution_convert_fusion.6
  734.9 7.0 convolution_convert_fusion.7
  741.9 5.1 add_convert_fusion
  751.6 5.5 all-to-all-start.5
  768.5 12.8 %collective-permute-start.46 = (bf16[256,2048]{1,0:T(8,128)(2,1)}, bf16[256,2048]{1,0:T(8,128)(2,1)}, u32[]{:S(2)}, u32[]{:S(2)}) collective-permute-start(bf16[256,2048]{1,0:T(8,128)(2,1)} %pad_maximum_fusion.15), channel_id=1, source_target_pairs={{0,16},{8,24},{16,0},{24,8},{1,17},{9,25},{17,1},{25,9},{2,18},{10... | collective-permute-start | bytes 3145736 | tf_op jit(solution)/shard_map/ppermute | solution.py:125
  781.3 15.0 %all-to-all-done.5 = bf16[8,64,1024]{2,1,0:T(8,128)(2,1)S(1)} async-done(((bf16[8,64,1024]{2,1,0:T(8,128)(2,1)}), bf16[8,64,1024]{2,1,0:T(8,128)(2,1)S(1)}, u32[]{:S(2)}, u32[]{:S(2)}) %all-to-all-start.5) | async-done | bytes 1048608 | tf_op jit(solution)/shard_map/all_to_all | solution.py:359
  796.3 8.0 all-to-all-start.3
  806.5 7.3 reduce-scatter.8.cloned.1.call-done
  813.8 22.6 %collective-permute-start.49 = (bf16[64,2048]{1,0:T(8,128)(2,1)}, bf16[64,2048]{1,0:T(8,128)(2,1)}, u32[]{:S(2)}, u32[]{:S(2)}) collective-permute-start(bf16[64,2048]{1,0:T(8,128)(2,1)} %reduce-scatter.8.cloned.1.call-done), channel_id=1, source_target_pairs={{0,0},{1,4},{2,1},{3,5},{4,2},{5,6},{6,3},{7,7},{8,8},{9,12},{10,9... | collective-permute-start | bytes 786440 | tf_op jit(solution)/shard_map/ppermute | solution.py:372
  863.6 8.2 all-to-all-start.2
  (617 shorter events, 385.0 us)
Async XLA Ops:
  7.2 95.5 %all-gather.6.cloned.1.call-start = ((), (), s32[]{:S(2)}) async-start(), calls=%async_computation.11 | async-start | bytes 1966080 | tf_op jit(solution)/shard_map/all_gather | solution.py:173
  16.7 23.7 %collective-permute-start = (bf16[256,2048]{1,0:T(8,128)(2,1)}, bf16[256,2048]{1,0:T(8,128)(2,1)S(1)}, u32[]{:S(2)}, u32[]{:S(2)}) collective-permute-start(bf16[256,2048]{1,0:T(8,128)(2,1)} %bitcast.454), channel_id=1, source_target_pairs={{0,16},{8,24},{16,0},{24,8},{1,17},{9,25},{17,1},{25,9},{2,18},{10... | collective-permute-start | bytes 3145736 | tf_op jit(solution)/shard_map/ppermute | solution.py:125
  16.8 25.6 %collective-permute-start.1 = (bf16[256,2048]{1,0:T(8,128)(2,1)}, bf16[256,2048]{1,0:T(8,128)(2,1)S(1)}, u32[]{:S(2)}, u32[]{:S(2)}) collective-permute-start(bf16[256,2048]{1,0:T(8,128)(2,1)} %bitcast.455), channel_id=1, source_target_pairs={{0,1},{1,0},{2,3},{3,2},{4,5},{5,4},{6,7},{7,6},{8,9},{9,8},{10,11... | collective-permute-start | bytes 3145736 | tf_op jit(solution)/shard_map/ppermute | solution.py:129
  41.1 17.3 %collective-permute-start.2 = (bf16[128,2048]{1,0:T(8,128)(2,1)}, bf16[128,2048]{1,0:T(8,128)(2,1)}, u32[]{:S(2)}, u32[]{:S(2)}) collective-permute-start(bf16[128,2048]{1,0:T(8,128)(2,1)} %slice.315), channel_id=1, source_target_pairs={{0,1},{1,0},{2,3},{3,2},{4,5},{5,4},{6,7},{7,6},{8,9},{9,8},{10,11... | collective-permute-start | bytes 1572872 | tf_op jit(solution)/shard_map/ppermute | solution.py:129
  43.5 47.6 %collective-permute-start.4 = (bf16[256,2048]{1,0:T(8,128)(2,1)S(1)}, bf16[256,2048]{1,0:T(8,128)(2,1)}, u32[]{:S(2)}, u32[]{:S(2)}) collective-permute-start(bf16[256,2048]{1,0:T(8,128)(2,1)S(1)} %bitcast.456), channel_id=1, source_target_pairs={{0,8},{8,0},{16,24},{24,16},{1,9},{9,1},{17,25},{25,17},{2,10},{10... | collective-permute-start | bytes 3145736 | tf_op jit(solution)/shard_map/ppermute | solution.py:121
  46.9 21.2 %all-to-all-start.1 = ((s32[4,1,256]{2,1,0:T(1,128)}), s32[4,1,256]{2,1,0:T(1,128)S(1)}, u32[]{:S(2)}, u32[]{:S(2)}) async-start(s32[4,1,256]{2,1,0:T(1,128)} %broadcast_in_dim.78), calls=%async_computation.1 | async-start | bytes 8192 | tf_op jit(solution)/shard_map/all_to_all | solution.py:214
  51.5 112.5 %all-gather.8.cloned.1.call-start = ((), (), s32[]{:S(2)}) async-start(), calls=%async_computation.12 | async-start | bytes 1310720 | tf_op jit(solution)/shard_map/all_gather | solution.py:173
  51.5 15.5 %collective-permute-start.8 = (bf16[64,2048]{1,0:T(8,128)(2,1)S(1)}, bf16[64,2048]{1,0:T(8,128)(2,1)}, u32[]{:S(2)}, u32[]{:S(2)}) collective-permute-start(bf16[64,2048]{1,0:T(8,128)(2,1)S(1)} %constant_dynamic-slice_fusion.28), channel_id=1, source_target_pairs={{0,0},{8,2},{16,4},{24,6},{1,1},{9,3},{17,5},{25,7},{2,8},{10,10},... | collective-permute-start | bytes 786440 | tf_op jit(solution)/shard_map/ppermute | solution.py:258
  64.2 29.3 %collective-permute-start.5 = (bf16[768,2048]{1,0:T(8,128)(2,1)}, bf16[768,2048]{1,0:T(8,128)(2,1)}, u32[]{:S(2)}, u32[]{:S(2)}) collective-permute-start(bf16[768,2048]{1,0:T(8,128)(2,1)} %pad_maximum_fusion), channel_id=1, source_target_pairs={{0,8},{8,0},{16,24},{24,16},{1,9},{9,1},{17,25},{25,17},{2,10},{10... | collective-permute-start | bytes 9437192 | tf_op jit(solution)/shard_map/ppermute | solution.py:121
  65.8 16.5 %collective-permute-start.21 = (bf16[256,1024]{1,0:T(8,128)(2,1)}, bf16[256,1024]{1,0:T(8,128)(2,1)}, u32[]{:S(2)}, u32[]{:S(2)}) collective-permute-start(bf16[256,1024]{1,0:T(8,128)(2,1)} %pad_maximum_fusion.18), channel_id=1, source_target_pairs={{0,1},{1,0},{2,3},{3,2},{4,5},{5,4},{6,7},{7,6},{8,9},{9,8},{10,11... | collective-permute-start | bytes 1572872 | tf_op jit(solution)/shard_map/ppermute | solution.py:129
  73.2 244.1 %all-gather.12.cloned.1.call-start = ((), (), s32[]{:S(2)}) async-start(), calls=%async_computation.14 | async-start | bytes 5242880 | tf_op jit(solution)/shard_map/all_gather | solution.py:173
  85.0 246.8 %all-gather.10.cloned.1.call-start = ((), (), s32[]{:S(2)}) async-start(), calls=%async_computation.13 | async-start | bytes 5242880 | tf_op jit(solution)/shard_map/all_gather | solution.py:173
  169.2 16.5 %collective-permute-start.9 = (bf16[1024,2048]{1,0:T(8,128)(2,1)}, bf16[1024,2048]{1,0:T(8,128)(2,1)}, u32[]{:S(2)}, u32[]{:S(2)}) collective-permute-start(bf16[1024,2048]{1,0:T(8,128)(2,1)} %convolution_convert_fusion.2), channel_id=1, source_target_pairs={{0,8},{8,0},{16,24},{24,16},{1,9},{9,1},{17,25},{25,17},{2,10},{10... | collective-permute-start | bytes 12582920 | tf_op jit(solution)/shard_map/ppermute | solution.py:121
  185.0 181.9 %all-gather.14.cloned.1.call-start = ((), (), s32[]{:S(2)}) async-start(), calls=%async_computation.15 | async-start | bytes 5242880 | tf_op jit(solution)/shard_map/all_gather | solution.py:173
  189.7 34.9 %collective-permute-start.27 = (bf16[256,2048]{1,0:T(8,128)(2,1)}, bf16[256,2048]{1,0:T(8,128)(2,1)S(1)}, u32[]{:S(2)}, u32[]{:S(2)}) collective-permute-start(bf16[256,2048]{1,0:T(8,128)(2,1)} %bitcast.51), channel_id=1, source_target_pairs={{0,16},{8,24},{16,0},{24,8},{1,17},{9,25},{17,1},{25,9},{2,18},{10... | collective-permute-start | bytes 3145736 | tf_op jit(solution)/shard_map/ppermute | solution.py:125
  191.2 34.8 %collective-permute-start.28 = (bf16[256,2048]{1,0:T(8,128)(2,1)}, bf16[256,2048]{1,0:T(8,128)(2,1)S(1)}, u32[]{:S(2)}, u32[]{:S(2)}) collective-permute-start(bf16[256,2048]{1,0:T(8,128)(2,1)} %bitcast.51), channel_id=1, source_target_pairs={{0,1},{1,0},{2,3},{3,2},{4,5},{5,4},{6,7},{7,6},{8,9},{9,8},{10,11... | collective-permute-start | bytes 3145736 | tf_op jit(solution)/shard_map/ppermute | solution.py:129
  202.7 44.4 %collective-permute-start.11 = (bf16[256,2048]{1,0:T(8,128)(2,1)S(1)}, bf16[256,2048]{1,0:T(8,128)(2,1)S(1)}, u32[]{:S(2)}, u32[]{:S(2)}) collective-permute-start(bf16[256,2048]{1,0:T(8,128)(2,1)S(1)} %pad_maximum_fusion.7), channel_id=1, source_target_pairs={{0,16},{8,24},{16,0},{24,8},{1,17},{9,25},{17,1},{25,9},{2,18},{10... | collective-permute-start | bytes 3145736 | tf_op jit(solution)/shard_map/ppermute | solution.py:125
  203.1 44.0 %collective-permute-start.13 = (bf16[256,2048]{1,0:T(8,128)(2,1)S(1)}, bf16[256,2048]{1,0:T(8,128)(2,1)S(1)}, u32[]{:S(2)}, u32[]{:S(2)}) collective-permute-start(bf16[256,2048]{1,0:T(8,128)(2,1)S(1)} %pad_maximum_fusion.8), channel_id=1, source_target_pairs={{0,1},{1,0},{2,3},{3,2},{4,5},{5,4},{6,7},{7,6},{8,9},{9,8},{10,11... | collective-permute-start | bytes 3145736 | tf_op jit(solution)/shard_map/ppermute | solution.py:129
  224.7 33.7 %collective-permute-start.29 = (bf16[128,2048]{1,0:T(8,128)(2,1)S(1)}, bf16[128,2048]{1,0:T(8,128)(2,1)S(1)}, u32[]{:S(2)}, u32[]{:S(2)}) collective-permute-start(bf16[128,2048]{1,0:T(8,128)(2,1)S(1)} %slice.340), channel_id=1, source_target_pairs={{0,1},{1,0},{2,3},{3,2},{4,5},{5,4},{6,7},{7,6},{8,9},{9,8},{10,11... | collective-permute-start | bytes 1572872 | tf_op jit(solution)/shard_map/ppermute | solution.py:129
  226.0 32.4 %collective-permute-start.30 = (bf16[128,2048]{1,0:T(8,128)(2,1)S(1)}, bf16[128,2048]{1,0:T(8,128)(2,1)S(1)}, u32[]{:S(2)}, u32[]{:S(2)}) collective-permute-start(bf16[128,2048]{1,0:T(8,128)(2,1)S(1)} %slice.341), channel_id=1, source_target_pairs={{0,16},{8,24},{16,0},{24,8},{1,17},{9,25},{17,1},{25,9},{2,18},{10... | collective-permute-start | bytes 1572872 | tf_op jit(solution)/shard_map/ppermute | solution.py:125
  251.3 29.5 %collective-permute-start.14 = (bf16[256,2048]{1,0:T(8,128)(2,1)S(1)}, bf16[256,2048]{1,0:T(8,128)(2,1)S(1)}, u32[]{:S(2)}, u32[]{:S(2)}) collective-permute-start(bf16[256,2048]{1,0:T(8,128)(2,1)S(1)} %get-tuple-element.481), channel_id=1, source_target_pairs={{0,16},{8,24},{16,0},{24,8},{1,17},{9,25},{17,1},{25,9},{2,18},{10... | collective-permute-start | bytes 3145736 | tf_op jit(solution)/shard_map/ppermute | solution.py:125
  251.5 31.3 %collective-permute-start.15 = (bf16[256,2048]{1,0:T(8,128)(2,1)S(1)}, bf16[256,2048]{1,0:T(8,128)(2,1)S(1)}, u32[]{:S(2)}, u32[]{:S(2)}) collective-permute-start(bf16[256,2048]{1,0:T(8,128)(2,1)S(1)} %get-tuple-element.481), channel_id=1, source_target_pairs={{0,1},{1,0},{2,3},{3,2},{4,5},{5,4},{6,7},{7,6},{8,9},{9,8},{10,11... | collective-permute-start | bytes 3145736 | tf_op jit(solution)/shard_map/ppermute | solution.py:129
  260.4 44.3 %collective-permute-start.32 = (bf16[768,2048]{1,0:T(8,128)(2,1)}, bf16[768,2048]{1,0:T(8,128)(2,1)}, u32[]{:S(2)}, u32[]{:S(2)}) collective-permute-start(bf16[768,2048]{1,0:T(8,128)(2,1)} %pad_maximum_fusion.3), channel_id=1, source_target_pairs={{0,8},{8,0},{16,24},{24,16},{1,9},{9,1},{17,25},{25,17},{2,10},{10... | collective-permute-start | bytes 9437192 | tf_op jit(solution)/shard_map/ppermute | solution.py:121
  285.0 18.2 %collective-permute-start.31 = (bf16[256,2048]{1,0:T(8,128)(2,1)}, bf16[256,2048]{1,0:T(8,128)(2,1)}, u32[]{:S(2)}, u32[]{:S(2)}) collective-permute-start(bf16[256,2048]{1,0:T(8,128)(2,1)} %bitcast.51), channel_id=1, source_target_pairs={{0,8},{8,0},{16,24},{24,16},{1,9},{9,1},{17,25},{25,17},{2,10},{10... | collective-permute-start | bytes 3145736 | tf_op jit(solution)/shard_map/ppermute | solution.py:121
  289.6 440.5 %reduce-scatter.10.cloned.1.call-start = ((), (), s32[]{:S(2)}) async-start(), calls=%async_computation.18 | async-start | bytes 5242880 | tf_op jit(solution)/shard_map/reduce_scatter | solution.py:177
  298.4 16.8 %collective-permute-start.19 = (bf16[768,2048]{1,0:T(8,128)(2,1)S(1)}, bf16[768,2048]{1,0:T(8,128)(2,1)S(1)}, u32[]{:S(2)}, u32[]{:S(2)}) collective-permute-start(bf16[768,2048]{1,0:T(8,128)(2,1)S(1)} %pad_maximum_fusion.2), channel_id=1, source_target_pairs={{0,8},{8,0},{16,24},{24,16},{1,9},{9,1},{17,25},{25,17},{2,10},{10... | collective-permute-start | bytes 9437192 | tf_op jit(solution)/shard_map/ppermute | solution.py:121
  405.6 346.1 %reduce-scatter.12.cloned.1.call-start = ((), (), s32[]{:S(2)}) async-start(), calls=%async_computation.19 | async-start | bytes 5242880 | tf_op jit(solution)/shard_map/reduce_scatter | solution.py:177
  415.3 36.9 %collective-permute-start.22 = (bf16[1024,2048]{1,0:T(8,128)(2,1)}, bf16[1024,2048]{1,0:T(8,128)(2,1)}, u32[]{:S(2)}, u32[]{:S(2)}) collective-permute-start(bf16[1024,2048]{1,0:T(8,128)(2,1)} %convolution_convert_fusion.3), channel_id=1, source_target_pairs={{0,8},{8,0},{16,24},{24,16},{1,9},{9,1},{17,25},{25,17},{2,10},{10... | collective-permute-start | bytes 12582920 | tf_op jit(solution)/shard_map/ppermute | solution.py:121
  427.2 33.3 %collective-permute-start.33 = (bf16[1024,2048]{1,0:T(8,128)(2,1)}, bf16[1024,2048]{1,0:T(8,128)(2,1)}, u32[]{:S(2)}, u32[]{:S(2)}) collective-permute-start(bf16[1024,2048]{1,0:T(8,128)(2,1)} %add_convert_fusion.2), channel_id=1, source_target_pairs={{0,8},{8,0},{16,24},{24,16},{1,9},{9,1},{17,25},{25,17},{2,10},{10... | collective-permute-start | bytes 12582920 | tf_op jit(solution)/shard_map/ppermute | solution.py:121
  441.3 315.9 %reduce-scatter.14.cloned.1.call-start = ((), (), s32[]{:S(2)}) async-start(), calls=%async_computation.20 | async-start | bytes 5242880 | tf_op jit(solution)/shard_map/reduce_scatter | solution.py:177
  473.8 32.7 %collective-permute-start.24 = (bf16[256,2048]{1,0:T(8,128)(2,1)S(1)}, bf16[256,2048]{1,0:T(8,128)(2,1)S(1)}, u32[]{:S(2)}, u32[]{:S(2)}) collective-permute-start(bf16[256,2048]{1,0:T(8,128)(2,1)S(1)} %pad_maximum_fusion.9), channel_id=1, source_target_pairs={{0,16},{8,24},{16,0},{24,8},{1,17},{9,25},{17,1},{25,9},{2,18},{10... | collective-permute-start | bytes 3145736 | tf_op jit(solution)/shard_map/ppermute | solution.py:125
  474.1 32.5 %collective-permute-start.26 = (bf16[256,2048]{1,0:T(8,128)(2,1)S(1)}, bf16[256,2048]{1,0:T(8,128)(2,1)S(1)}, u32[]{:S(2)}, u32[]{:S(2)}) collective-permute-start(bf16[256,2048]{1,0:T(8,128)(2,1)S(1)} %pad_maximum_fusion.10), channel_id=1, source_target_pairs={{0,1},{1,0},{2,3},{3,2},{4,5},{5,4},{6,7},{7,6},{8,9},{9,8},{10,11... | collective-permute-start | bytes 3145736 | tf_op jit(solution)/shard_map/ppermute | solution.py:129
  484.5 44.4 %collective-permute-start.35 = (bf16[256,2048]{1,0:T(8,128)(2,1)S(1)}, bf16[256,2048]{1,0:T(8,128)(2,1)S(1)}, u32[]{:S(2)}, u32[]{:S(2)}) collective-permute-start(bf16[256,2048]{1,0:T(8,128)(2,1)S(1)} %pad_maximum_fusion.11), channel_id=1, source_target_pairs={{0,16},{8,24},{16,0},{24,8},{1,17},{9,25},{17,1},{25,9},{2,18},{10... | collective-permute-start | bytes 3145736 | tf_op jit(solution)/shard_map/ppermute | solution.py:125
  485.9 43.1 %collective-permute-start.37 = (bf16[256,2048]{1,0:T(8,128)(2,1)S(1)}, bf16[256,2048]{1,0:T(8,128)(2,1)S(1)}, u32[]{:S(2)}, u32[]{:S(2)}) collective-permute-start(bf16[256,2048]{1,0:T(8,128)(2,1)S(1)} %pad_maximum_fusion.12), channel_id=1, source_target_pairs={{0,1},{1,0},{2,3},{3,2},{4,5},{5,4},{6,7},{7,6},{8,9},{9,8},{10,11... | collective-permute-start | bytes 3145736 | tf_op jit(solution)/shard_map/ppermute | solution.py:129
  536.3 22.6 %collective-permute-start.38 = (bf16[256,2048]{1,0:T(8,128)(2,1)S(1)}, bf16[256,2048]{1,0:T(8,128)(2,1)S(1)}, u32[]{:S(2)}, u32[]{:S(2)}) collective-permute-start(bf16[256,2048]{1,0:T(8,128)(2,1)S(1)} %get-tuple-element.478), channel_id=1, source_target_pairs={{0,16},{8,24},{16,0},{24,8},{1,17},{9,25},{17,1},{25,9},{2,18},{10... | collective-permute-start | bytes 3145736 | tf_op jit(solution)/shard_map/ppermute | solution.py:125
  537.6 23.2 %collective-permute-start.39 = (bf16[256,2048]{1,0:T(8,128)(2,1)S(1)}, bf16[256,2048]{1,0:T(8,128)(2,1)S(1)}, u32[]{:S(2)}, u32[]{:S(2)}) collective-permute-start(bf16[256,2048]{1,0:T(8,128)(2,1)S(1)} %get-tuple-element.478), channel_id=1, source_target_pairs={{0,1},{1,0},{2,3},{3,2},{4,5},{5,4},{6,7},{7,6},{8,9},{9,8},{10,11... | collective-permute-start | bytes 3145736 | tf_op jit(solution)/shard_map/ppermute | solution.py:129
  562.9 32.4 %collective-permute-start.42 = (bf16[256,2048]{1,0:T(8,128)(2,1)}, bf16[256,2048]{1,0:T(8,128)(2,1)}, u32[]{:S(2)}, u32[]{:S(2)}) collective-permute-start(bf16[256,2048]{1,0:T(8,128)(2,1)} %copy-done.48), channel_id=1, source_target_pairs={{0,8},{8,0},{16,24},{24,16},{1,9},{9,1},{17,25},{25,17},{2,10},{10... | collective-permute-start | bytes 3145736 | tf_op jit(solution)/shard_map/ppermute | solution.py:121
  573.7 24.0 %collective-permute-start.43 = (bf16[768,2048]{1,0:T(8,128)(2,1)}, bf16[768,2048]{1,0:T(8,128)(2,1)}, u32[]{:S(2)}, u32[]{:S(2)}) collective-permute-start(bf16[768,2048]{1,0:T(8,128)(2,1)} %pad_maximum_fusion.4), channel_id=1, source_target_pairs={{0,8},{8,0},{16,24},{24,16},{1,9},{9,1},{17,25},{25,17},{2,10},{10... | collective-permute-start | bytes 9437192 | tf_op jit(solution)/shard_map/ppermute | solution.py:121
  591.4 204.9 %reduce-scatter.6.cloned.1.call-start = ((), (), s32[]{:S(2)}) async-start(), calls=%async_computation.16 | async-start | bytes 1966080 | tf_op jit(solution)/shard_map/reduce_scatter | solution.py:177
  723.0 19.0 %collective-permute-start.44 = (bf16[1024,2048]{1,0:T(8,128)(2,1)}, bf16[1024,2048]{1,0:T(8,128)(2,1)}, u32[]{:S(2)}, u32[]{:S(2)}) collective-permute-start(bf16[1024,2048]{1,0:T(8,128)(2,1)} %convolution_convert_fusion), channel_id=1, source_target_pairs={{0,8},{8,0},{16,24},{24,16},{1,9},{9,1},{17,25},{25,17},{2,10},{10... | collective-permute-start | bytes 12582920 | tf_op jit(solution)/shard_map/ppermute | solution.py:121
  730.1 21.5 %all-to-all-start.4 = ((bf16[8,64,1024]{2,1,0:T(8,128)(2,1)}), bf16[8,64,1024]{2,1,0:T(8,128)(2,1)S(1)}, u32[]{:S(2)}, u32[]{:S(2)}) async-start(bf16[8,64,1024]{2,1,0:T(8,128)(2,1)} %bitcast.492), calls=%async_computation.7 | async-start | bytes 2097152 | tf_op jit(solution)/shard_map/all_to_all | solution.py:359
  734.7 79.1 %reduce-scatter.8.cloned.1.call-start = ((), (), s32[]{:S(2)}) async-start(), calls=%async_computation.17 | async-start | bytes 1310720 | tf_op jit(solution)/shard_map/reduce_scatter | solution.py:177
  751.6 44.7 %all-to-all-start.5 = ((bf16[8,64,1024]{2,1,0:T(8,128)(2,1)}), bf16[8,64,1024]{2,1,0:T(8,128)(2,1)S(1)}, u32[]{:S(2)}, u32[]{:S(2)}) async-start(bf16[8,64,1024]{2,1,0:T(8,128)(2,1)} %bitcast.491), calls=%async_computation.9 | async-start | bytes 2097152 | tf_op jit(solution)/shard_map/all_to_all | solution.py:359
  757.2 95.1 %collective-permute-start.50 = (bf16[256,2048]{1,0:T(8,128)(2,1)}, bf16[256,2048]{1,0:T(8,128)(2,1)}, u32[]{:S(2)}, u32[]{:S(2)}) collective-permute-start(bf16[256,2048]{1,0:T(8,128)(2,1)} %reduce-scatter.14.cloned.1.call-done), channel_id=1, source_target_pairs={{0,0},{1,4},{2,8},{3,12},{4,16},{5,20},{6,24},{7,28},{8,1},{9,5},{... | collective-permute-start | bytes 3145736 | tf_op jit(solution)/shard_map/ppermute | solution.py:372
  768.5 91.3 %collective-permute-start.46 = (bf16[256,2048]{1,0:T(8,128)(2,1)}, bf16[256,2048]{1,0:T(8,128)(2,1)}, u32[]{:S(2)}, u32[]{:S(2)}) collective-permute-start(bf16[256,2048]{1,0:T(8,128)(2,1)} %pad_maximum_fusion.15), channel_id=1, source_target_pairs={{0,16},{8,24},{16,0},{24,8},{1,17},{9,25},{17,1},{25,9},{2,18},{10... | collective-permute-start | bytes 3145736 | tf_op jit(solution)/shard_map/ppermute | solution.py:125
  796.3 60.6 %all-to-all-start.3 = ((bf16[8,64,384]{2,1,0:T(8,128)(2,1)}), bf16[8,64,384]{2,1,0:T(8,128)(2,1)S(1)}, u32[]{:S(2)}, u32[]{:S(2)}) async-start(bf16[8,64,384]{2,1,0:T(8,128)(2,1)} %bitcast.501), calls=%async_computation.4 | async-start | bytes 786432 | tf_op jit(solution)/shard_map/all_to_all | solution.py:359
  805.3 54.5 %collective-permute-start.48 = (bf16[256,2048]{1,0:T(8,128)(2,1)}, bf16[256,2048]{1,0:T(8,128)(2,1)}, u32[]{:S(2)}, u32[]{:S(2)}) collective-permute-start(bf16[256,2048]{1,0:T(8,128)(2,1)} %pad_maximum_fusion.16), channel_id=1, source_target_pairs={{0,1},{1,0},{2,3},{3,2},{4,5},{5,4},{6,7},{7,6},{8,9},{9,8},{10,11... | collective-permute-start | bytes 3145736 | tf_op jit(solution)/shard_map/ppermute | solution.py:129
  813.8 41.2 %collective-permute-start.49 = (bf16[64,2048]{1,0:T(8,128)(2,1)}, bf16[64,2048]{1,0:T(8,128)(2,1)}, u32[]{:S(2)}, u32[]{:S(2)}) collective-permute-start(bf16[64,2048]{1,0:T(8,128)(2,1)} %reduce-scatter.8.cloned.1.call-done), channel_id=1, source_target_pairs={{0,0},{1,4},{2,1},{3,5},{4,2},{5,6},{6,3},{7,7},{8,8},{9,12},{10,9... | collective-permute-start | bytes 786440 | tf_op jit(solution)/shard_map/ppermute | solution.py:372
  (117 other events, 1335.9 us)
Sparse Core Ops, SparseCore 0:
  16.8 37.6 all-gather.5
  67.2 28.0 all-gather.7
  97.4 78.0 all-gather.11
  185.1 77.5 all-gather.9
  289.7 77.1 all-gather.13
  405.7 77.7 reduce-scatter.9
  485.9 77.2 reduce-scatter.11
  591.5 77.0 reduce-scatter.13
  730.0 33.8 reduce-scatter.5
  766.7 47.0 reduce-scatter.7

commit v2 on v1

v2 whole, which is shorter than its diff:
```python
import functools
import math

import jax
import jax.numpy as jnp
from jax import lax
from jax.experimental import pallas as pl
from jax.experimental.pallas import tpu as pltpu
from jax.sharding import PartitionSpec as P

H = 32
KVH = 8
HD = 64
NY = 2
VMEM_BYTES = 48 << 20


EPSILON = 1e-05
ROPE_BASE = 500000.0

F32 = jnp.float32
BF16 = jnp.bfloat16


def dot_rows(left, right):
    return lax.dot_general(left, right, (((0,), (0,)), ((), ())), preferred_element_type=F32)


def dot_cols(left, right):
    return lax.dot_general(left, right, (((1,), (1,)), ((), ())), preferred_element_type=F32)


def dot(left, right):
    return jnp.dot(left, right, preferred_element_type=F32)


def swap_core(value):
    return lax.ppermute(value, "seq", [(i, i ^ 1) for i in range(lax.axis_size("seq"))])


def swap_x(value):
    return lax.ppermute(value, "seq", [(i, i ^ 2) for i in range(lax.axis_size("seq"))])


def swap_y(value):
    return lax.ppermute(value, "fsdp", [(i, i ^ 1) for i in range(lax.axis_size("fsdp"))])


def gather_plane(own):
    half = own.shape[0] // 2
    x_part = swap_x(own)
    y_part = swap_y(own)
    core = swap_core(own)
    xy_up = swap_y(x_part[:half])
    xy_low = swap_x(y_part[half:])
    others = jnp.concatenate([x_part, y_part, xy_up, xy_low])
    return own, others, core, swap_core(others)


def scatter_plane(make):
    sent = swap_core(make(1).astype(BF16))
    mine = (make(0) + sent.astype(F32)).astype(BF16)
    rows = mine.shape[0] // 4
    half = rows // 2
    own, x_part, y_part, xy_part = (mine[i * rows : (i + 1) * rows].astype(F32) for i in range(4))
    from_x = swap_x(mine[3 * rows : 3 * rows + half]).astype(F32)
    from_y = swap_y(mine[3 * rows + half :]).astype(F32)
    x_sum = jnp.concatenate([x_part[:half], x_part[half:] + from_y])
    y_sum = jnp.concatenate([y_part[:half] + from_x, y_part[half:]])
    return own + swap_x(x_sum.astype(BF16)).astype(F32) + swap_y(y_sum.astype(BF16)).astype(F32)


def planes():
    return lax.axis_size("fsdp") // NY


def z_groups():
    return [[z * NY + y for z in range(planes())] for y in range(NY)]


def plane_groups():
    n_fsdp = lax.axis_size("fsdp")
    return [
        [s * n_fsdp + z * NY + y for s in range(lax.axis_size("seq")) for y in range(NY)]
        for z in range(planes())
    ]


def gather_z(own):
    return lax.all_gather(own, "fsdp", axis=0, tiled=True, axis_index_groups=z_groups())


def scatter_z(terms):
    return lax.psum_scatter(
        terms, "fsdp", scatter_dimension=0, tiled=True, axis_index_groups=z_groups()
    )


def lanes_of(shape):
    return lax.broadcasted_iota(jnp.int32, shape, len(shape) - 1)


def turn_lanes(values, cosine, sine):
    width = values.shape[-1]
    half = HD // 2
    lower = lanes_of(values.shape) % HD < half
    partner = jnp.where(lower, pltpu.roll(values, width - half, 1), pltpu.roll(values, half, 1))
    repeats = width // cosine.shape[-1]
    return values * jnp.tile(cosine, (1, repeats)) + partner * jnp.tile(sine, (1, repeats))


def load_heads(blocks, cos_ref, sin_ref, q_at, k_at, v_at):
    rows = blocks[0].shape[0]
    for j, block in enumerate(blocks):
        at = pl.ds(j * rows, rows)
        cosine, sine = cos_ref[at, :], sin_ref[at, :]
        q_width = q_at.shape[1]
        turned = turn_lanes(block[:, :q_width], cosine, sine).astype(BF16)
        q_at[at, :] = (turned.astype(F32) * (1.0 / math.sqrt(HD))).astype(BF16)
        both = block[:, q_width:]
        swapped = pltpu.roll(both, HD, 1)
        low = lanes_of(both.shape) < HD
        keys = turn_lanes(jnp.where(low, both, swapped), cosine, sine).astype(BF16)
        values = jnp.where(low, swapped, both).astype(BF16)
        k_at[at, :] = jnp.tile(keys, (1, q_width // keys.shape[1]))
        v_at[at, :] = jnp.tile(values, (1, q_width // values.shape[1]))


def dot_nt(left, right):
    return lax.dot_general(left, right, (((1,), (1,)), ((), ())), preferred_element_type=F32)


def dot_tn(left, right):
    return lax.dot_general(left, right, (((0,), (0,)), ((), ())), preferred_element_type=F32)


def causal(scores):
    rows = lax.broadcasted_iota(jnp.int32, scores.shape, 0)
    cols = lax.broadcasted_iota(jnp.int32, scores.shape, 1)
    return jnp.where(rows >= cols, scores, -1e30)


def scores_at(q_head, k_at, i, rows):
    found = []
    for j in range(i + 1):
        scores = dot_nt(q_head, k_at[j * rows : (j + 1) * rows, :])
        found.append(causal(scores) if j == i else scores)
    return found


def attend_kernel(n_parts, member, *refs):
    blocks = refs[:n_parts]
    cos_ref, sin_ref, o_ref, lse_ref, q_at, k_at, v_at, o_at, lse_at = refs[n_parts:]
    rows = blocks[0].shape[0]
    step = pl.program_id(1)

    @pl.when(step == 0)
    def _():
        load_heads(blocks, cos_ref, sin_ref, q_at, k_at, v_at)
        o_at[...] = jnp.zeros_like(o_at)
        lse_at[...] = jnp.zeros_like(lse_at)

        def one_head(h, carry):
            for i in range(n_parts):
                at = slice(i * rows, (i + 1) * rows)
                mask = lanes_of((rows, q_at.shape[1])) // HD == h
                q_head = jnp.where(mask, q_at[at, :], 0)
                scores = scores_at(q_head, k_at, i, rows)
                top = scores[0].max(axis=-1, keepdims=True)
                for part in scores[1:]:
                    top = jnp.maximum(top, part.max(axis=-1, keepdims=True))
                terms = [jnp.exp(part - top) for part in scores]
                total = terms[0].sum(axis=-1, keepdims=True)
                for part in terms[1:]:
                    total = total + part.sum(axis=-1, keepdims=True)
                scale = 1.0 / total
                mixed = jnp.zeros((rows, q_at.shape[1]), F32)
                for j, part in enumerate(terms):
                    mixed = mixed + jnp.dot(
                        (part * scale).astype(BF16),
                        v_at[j * rows : (j + 1) * rows, :],
                        preferred_element_type=F32,
                    )
                o_at[at, :] = jnp.where(mask, mixed, o_at[at, :])
                lse_at[at, :] = jnp.where(
                    lanes_of((rows, lse_at.shape[1])) == h, top + jnp.log(total), lse_at[at, :]
                )
            return carry

        lax.fori_loop(0, q_at.shape[1] // HD, one_head, 0)

    here = pl.ds(pl.multiple_of(step * rows, rows), rows)
    o_ref[...] = o_at[here, :].astype(BF16)
    lse_ref[...] = lse_at[here, :]


def attend_back_kernel(n_parts, member, *refs):
    blocks, d_blocks, l_blocks = refs[:n_parts], refs[n_parts : 2 * n_parts], refs[2 * n_parts : 3 * n_parts]
    cos_ref, sin_ref, g_ref, q_at, k_at, v_at, dq_at, dk_at, dv_at = refs[3 * n_parts :]
    rows = blocks[0].shape[0]
    width = q_at.shape[1]
    step = pl.program_id(1)

    @pl.when(step == 0)
    def _():
        load_heads(blocks, cos_ref, sin_ref, q_at, k_at, v_at)
        dq_at[...] = jnp.zeros_like(dq_at)
        dk_at[...] = jnp.zeros_like(dk_at)
        dv_at[...] = jnp.zeros_like(dv_at)

        def one_head(h, carry):
            for i in range(n_parts):
                at = slice(i * rows, (i + 1) * rows)
                mask = lanes_of((rows, width)) // HD == h
                q_head = jnp.where(mask, q_at[at, :], 0)
                d_head = jnp.where(mask, d_blocks[i][...], 0)
                lse = jnp.sum(
                    jnp.where(lanes_of(l_blocks[i].shape) == h, l_blocks[i][...], 0.0),
                    axis=-1,
                    keepdims=True,
                )
                scores = scores_at(q_head, k_at, i, rows)
                probs = [jnp.exp(part - lse) for part in scores]
                grads = [dot_nt(d_head, v_at[j * rows : (j + 1) * rows, :]) for j in range(i + 1)]
                inner = jnp.zeros((rows, 1), F32)
                for prob, grad in zip(probs, grads):
                    inner = inner + jnp.sum(prob * grad, axis=-1, keepdims=True)
                dq = jnp.zeros((rows, width), F32)
                for j, (prob, grad) in enumerate(zip(probs, grads)):
                    there = slice(j * rows, (j + 1) * rows)
                    d_score = (prob * (grad - inner)).astype(BF16)
                    dq = dq + jnp.dot(d_score, k_at[there, :], preferred_element_type=F32)
                    dk_at[there, :] += dot_tn(d_score, q_head)
                    dv_at[there, :] += dot_tn(prob.astype(BF16), d_head)
                dq_at[at, :] = jnp.where(mask, dq, dq_at[at, :])
            return carry

        lax.fori_loop(0, width // HD, one_head, 0)

    here = pl.ds(pl.multiple_of(step * rows, rows), rows)
    cosine, sine = cos_ref[here, :], -sin_ref[here, :]
    dq = turn_lanes(dq_at[here, :] * (1.0 / math.sqrt(HD)), cosine, sine)
    span = cos_ref.shape[1]

    def fold(values):
        total = values[:, :span]
        for at in range(span, width, span):
            total = total + values[:, at : at + span]
        shift = HD
        while shift < span:
            total = total + pltpu.roll(total, shift, 1)
            shift *= 2
        return total

    dk = turn_lanes(fold(dk_at[here, :]), cosine, sine)
    dv = fold(dv_at[here, :])
    dkv = jnp.where(lanes_of(dk.shape) < HD, dk, dv)
    g_ref[:, :width] = dq.astype(BF16)
    g_ref[:, width:] = dkv.astype(BF16)


def place_of(member, y_at, part):
    relative = jnp.bitwise_xor(member[0], part)
    return (relative % 2) * 4 + y_at * 2 + relative // 2


def attend(member, qkv, cosine, sine, q_width, n_parts):
    rows = qkv.shape[0] // (NY * n_parts)
    length = rows * n_parts
    span = cosine.shape[-1]

    def part_spec(width, part):
        return pl.BlockSpec((rows, width), lambda y, i, member: (place_of(member, y, part), 0))

    def own_spec(width):
        return pl.BlockSpec((rows, width), lambda y, i, member: (place_of(member, y, i), 0))

    table = pl.BlockSpec((length, span), lambda y, i, member: (y, 0))
    tiles = NY * (q_width // HD) * length * length
    return pl.pallas_call(
        functools.partial(attend_kernel, n_parts),
        out_shape=(
            jax.ShapeDtypeStruct((qkv.shape[0], q_width), BF16),
            jax.ShapeDtypeStruct((qkv.shape[0], span), F32),
        ),
        grid_spec=pltpu.PrefetchScalarGridSpec(
            num_scalar_prefetch=1,
            grid=(NY, n_parts),
            in_specs=[part_spec(qkv.shape[1], j) for j in range(n_parts)] + [table, table],
            out_specs=(own_spec(q_width), own_spec(span)),
            scratch_shapes=[pltpu.VMEM((length, q_width), BF16)] * 3
            + [pltpu.VMEM((length, q_width), F32), pltpu.VMEM((length, span), F32)],
        ),
        compiler_params=pltpu.CompilerParams(vmem_limit_bytes=VMEM_BYTES),
        cost_estimate=pl.CostEstimate(
            flops=8 * tiles * HD, bytes_accessed=8 * qkv.size, transcendentals=tiles // 2
        ),
        name="attend",
    )(member, *([qkv] * n_parts), cosine, sine)


def attend_back(member, qkv, d_out, log_sums, cosine, sine, n_parts):
    rows = qkv.shape[0] // (NY * n_parts)
    length = rows * n_parts
    span = cosine.shape[-1]
    q_width = d_out.shape[1]

    def part_spec(width, part):
        return pl.BlockSpec((rows, width), lambda y, i, member: (place_of(member, y, part), 0))

    table = pl.BlockSpec((length, span), lambda y, i, member: (y, 0))
    tiles = NY * (q_width // HD) * length * length
    return pl.pallas_call(
        functools.partial(attend_back_kernel, n_parts),
        out_shape=jax.ShapeDtypeStruct(qkv.shape, BF16),
        grid_spec=pltpu.PrefetchScalarGridSpec(
            num_scalar_prefetch=1,
            grid=(NY, n_parts),
            in_specs=[part_spec(qkv.shape[1], j) for j in range(n_parts)]
            + [part_spec(q_width, j) for j in range(n_parts)]
            + [part_spec(span, j) for j in range(n_parts)]
            + [table, table],
            out_specs=pl.BlockSpec((rows, qkv.shape[1]), lambda y, i, member: (place_of(member, y, i), 0)),
            scratch_shapes=[pltpu.VMEM((length, q_width), BF16)] * 3
            + [pltpu.VMEM((length, q_width), F32)] * 3,
        ),
        compiler_params=pltpu.CompilerParams(vmem_limit_bytes=VMEM_BYTES),
        cost_estimate=pl.CostEstimate(
            flops=20 * tiles * HD, bytes_accessed=10 * qkv.size, transcendentals=tiles // 2
        ),
        name="attend_back",
    )(member, *([qkv] * n_parts), *([d_out] * n_parts), *([log_sums] * n_parts), cosine, sine)

def piece_specs(pieces):
    rows, width = pieces[0].shape
    specs, first = [], 0
    for piece in pieces:
        count = piece.shape[0] // rows
        specs.append(
            pl.BlockSpec(
                (rows, width),
                functools.partial(lambda i, lo, n: (jnp.clip(i - lo, 0, n - 1), 0), lo=first, n=count),
            )
        )
        first += count
    return specs, first


def on_pieces(counts, refs, body):
    step, first = pl.program_id(0), 0
    for count, ref in zip(counts, refs):
        pl.when((step >= first) & (step < first + count))(functools.partial(body, ref))
        first += count


def pieces_call(name, body, pieces, fixed, by_rows, outs, flops):
    specs, blocks = piece_specs(pieces)
    rows = pieces[0].shape[0]
    counts = [piece.shape[0] // rows for piece in pieces]
    n_pieces = len(pieces)

    def kernel(*refs):
        on_pieces(counts, refs[:n_pieces], lambda ref: body(ref, *refs[n_pieces:]))

    def row_spec(width):
        return pl.BlockSpec((rows, width), lambda i: (i, 0))

    fixed_specs = [
        pl.BlockSpec(shape, lambda i: (0, 0), pipeline_mode=pl.Buffered(1)) for _, shape in fixed
    ]
    moved = sum(a.size * a.dtype.itemsize for a in (*pieces, *by_rows, *(f for f, _ in fixed)))
    moved += sum(blocks * rows * w * jnp.dtype(t).itemsize for w, t in outs)
    return pl.pallas_call(
        kernel,
        out_shape=tuple(jax.ShapeDtypeStruct((blocks * rows, w), t) for w, t in outs),
        grid=(blocks,),
        in_specs=specs + fixed_specs + [row_spec(a.shape[1]) for a in by_rows],
        out_specs=tuple(row_spec(w) for w, _ in outs),
        compiler_params=pltpu.CompilerParams(vmem_limit_bytes=VMEM_BYTES),
        cost_estimate=pl.CostEstimate(flops=flops, bytes_accessed=moved, transcendentals=0),
        name=name,
    )(*pieces, *(f for f, _ in fixed), *by_rows)


def project(pieces, gain, weight, cols):
    width = pieces[0].shape[1]

    def body(x_ref, gain_ref, w_ref, xn_ref, out_ref):
        x = x_ref[...].astype(F32)
        inv = lax.rsqrt(jnp.mean(x * x, axis=-1, keepdims=True) + EPSILON)
        xn = (x * inv * gain_ref[...]).astype(BF16)
        xn_ref[...] = xn
        out_ref[...] = dot(xn, w_ref[...])

    rows = sum(p.shape[0] for p in pieces)
    return pieces_call(
        "project",
        body,
        pieces,
        [(gain, (1, width)), (weight, (width, cols))],
        [],
        [(width, BF16), (cols, F32)],
        2 * rows * width * cols,
    )


def feed(pieces, w_both):
    width, cols = w_both.shape[0], w_both.shape[1] // 2

    def body(h_ref, w_ref, hn_ref, mid_ref, by_gate_ref, by_up_ref):
        hn = h_ref[...]
        hn_ref[...] = hn
        chunk = min(256, cols)
        for at in range(0, cols, chunk):
            gate = dot(hn, w_ref[:, at : at + chunk])
            up = dot(hn, w_ref[:, cols + at : cols + at + chunk])
            sigma = jax.nn.sigmoid(gate)
            active = gate * sigma
            mid_ref[:, at : at + chunk] = (active * up).astype(BF16)
            by_up_ref[:, at : at + chunk] = active.astype(BF16)
            by_gate_ref[:, at : at + chunk] = (up * sigma * (1.0 + gate * (1.0 - sigma))).astype(BF16)

    rows = sum(p.shape[0] for p in pieces)
    return pieces_call(
        "feed",
        body,
        pieces,
        [(w_both, w_both.shape)],
        [],
        [(width, BF16)] + [(cols, BF16)] * 3,
        4 * rows * width * cols,
    )


def feed_back(pieces, w_down, by_gate, by_up):
    cols, width = w_down.shape

    def body(c_ref, w_ref, by_gate_ref, by_up_ref, cot_ref, grad_ref):
        cot = c_ref[...]
        cot_ref[...] = cot
        chunk = min(256, cols)
        for at in range(0, cols, chunk):
            grad = dot_nt(cot, w_ref[at : at + chunk, :])
            here = slice(at, at + chunk)
            grad_ref[:, here] = (grad * by_gate_ref[:, here].astype(F32)).astype(BF16)
            grad_ref[:, cols + at : cols + at + chunk] = (grad * by_up_ref[:, here].astype(F32)).astype(BF16)

    rows = sum(p.shape[0] for p in pieces)
    return pieces_call(
        "feed_back",
        body,
        pieces,
        [(w_down, w_down.shape)],
        [by_gate, by_up],
        [(width, BF16), (2 * cols, BF16)],
        2 * rows * width * cols,
    )


def out_back(pieces, w_o):
    cols, width = w_o.shape

    def body(a_ref, w_ref, da_ref, out_ref):
        da = a_ref[...]
        da_ref[...] = da
        out_ref[...] = dot_nt(da, w_ref[...]).astype(BF16)

    rows = sum(p.shape[0] for p in pieces)
    return pieces_call(
        "out_back",
        body,
        pieces,
        [(w_o, w_o.shape)],
        [],
        [(width, BF16), (cols, BF16)],
        2 * rows * width * cols,
    )


def shards(
    tokens, positions, attn_gain, w_q, w_k, w_v, w_o, mlp_gain, w_gate, w_up, w_down, cotangent
):
    seq_count, part_len, width = tokens.shape
    n_seq = lax.axis_size("seq")
    n_fsdp = lax.axis_size("fsdp")
    n_all = n_seq * n_fsdp
    n_z = planes()
    n_team = n_seq * NY
    s = lax.axis_index("seq")
    f = lax.axis_index("fsdp")
    y = lax.rem(f, NY)
    length = part_len * n_seq
    w_rows = w_q.shape[0]
    q_width, kv_width, ff_width = w_q.shape[1], w_k.shape[1], w_gate.shape[1]
    q_cols, kv_cols, ff_cols = q_width // n_team, kv_width // n_team, ff_width // n_team
    ff_block = ff_cols // n_z

    x_own = tokens.reshape(part_len, width)
    cot_own = cotangent.reshape(part_len, width)
    x_pieces = gather_plane(x_own)

    gains = jnp.stack([attn_gain, mlp_gain])
    gains = lax.all_to_all(
        jnp.broadcast_to(gains, (n_fsdp, *gains.shape)), "fsdp", split_axis=0, concat_axis=0, tiled=True
    )
    gains = gains.transpose(1, 0, 2).reshape(2, width).astype(F32)
    gain_one, gain_two = gains[:1], gains[1:]
    places = lax.all_to_all(
        jnp.broadcast_to(positions.reshape(part_len), (n_seq, part_len)),
        "seq",
        split_axis=0,
        concat_axis=0,
        tiled=True,
    ).reshape(length)
    places = jnp.concatenate([places, swap_y(places)])

    def cols_qkv(y_of):
        team = s * NY + y_of
        return jnp.concatenate(
            [
                lax.dynamic_slice_in_dim(w_q, team * q_cols, q_cols, 1),
                lax.dynamic_slice_in_dim(w_k, team * kv_cols, kv_cols, 1),
                lax.dynamic_slice_in_dim(w_v, team * kv_cols, kv_cols, 1),
            ],
            axis=1,
        )

    def cols_ff(y_of):
        return jnp.concatenate(
            [
                lax.dynamic_slice_in_dim(weight, ((at * NY + y_of) * n_seq + s) * ff_block, ff_block, 1)
                for weight in (w_gate, w_up)
                for at in range(n_z)
            ],
            axis=1,
        )

    def both_rows(cols_of):
        ours = cols_of(y)
        others = swap_y(cols_of(1 - y))
        rows = jnp.where(y == 0, jnp.stack([ours, others]), jnp.stack([others, ours]))
        return rows.reshape(NY * w_rows, -1)

    def rows_o():
        sub = w_o.shape[0] // n_seq
        mine = lax.dynamic_slice_in_dim(w_o, s * sub, sub, 0)
        pairs = []
        for block in range(n_all):
            team, z_to = block // n_z, block % n_z
            source = (block % n_seq) * n_fsdp + block // n_seq
            target = (team // NY) * n_fsdp + z_to * NY + team % NY
            pairs.append((source, target))
        return lax.ppermute(mine, ("seq", "fsdp"), pairs)

    head_cols = q_cols + 2 * kv_cols
    w_heads = gather_z(
        jnp.concatenate([both_rows(cols_qkv), rows_o().reshape(NY * w_rows, -1)], axis=1)
    )
    wqkv = w_heads[:, :head_cols]
    wo = w_heads[:, head_cols:].reshape(q_cols, width)
    w_both = gather_z(both_rows(cols_ff))
    wd = gather_z(lax.dynamic_slice_in_dim(w_down, s * ff_block, ff_block, 0))
    cot_pieces = gather_plane(cot_own)

    def normed(rows):
        rows = rows.astype(F32)
        inv = lax.rsqrt(jnp.mean(rows * rows, axis=-1, keepdims=True) + EPSILON)
        return rows * inv, inv

    z_one, inv_one = normed(x_own)
    freqs = jnp.exp(jnp.arange(HD // 2).astype(F32) * (-2.0 * math.log(ROPE_BASE) / HD))
    angles = places.astype(F32)[:, None] * freqs
    cosine, sine = jnp.cos(angles), jnp.sin(angles)
    cosine = jnp.tile(cosine, (1, 4))
    sine = jnp.concatenate([-sine, sine, -sine, sine], axis=1)
    member = s.astype(jnp.int32).reshape(1)

    xn, qkv = project(x_pieces, gain_one, w_heads, head_cols)
    attn_rows, log_sums = attend(member, qkv, cosine, sine, q_cols, n_seq)
    side = attn_rows.shape[0] // 2
    residual = x_own.astype(F32) + scatter_plane(
        lambda core: dot(attn_rows[core * side : (core + 1) * side], wo)
    )

    z_two, inv_two = normed(residual)
    hn, mid, by_gate, by_up = feed(gather_plane((z_two * gain_two).astype(BF16)), w_both)
    branch = scatter_plane(lambda core: dot(mid[core * side : (core + 1) * side], wd))
    output = (residual + branch).astype(BF16).reshape(tokens.shape)

    cot_all, grad_both = feed_back(cot_pieces, wd, by_gate, by_up)
    grad_hn = scatter_plane(lambda core: dot_cols(grad_both[core * side : (core + 1) * side], w_both))
    grad_z2 = grad_hn * gain_two
    grad_res = cot_own.astype(F32) + inv_two * (
        grad_z2 - z_two * jnp.mean(grad_z2 * z_two, axis=-1, keepdims=True)
    )
    da, d_out = out_back(gather_plane(grad_res.astype(BF16)), wo)
    grad_qkv = attend_back(member, qkv, d_out, log_sums, cosine, sine, n_seq)
    grad_xn = scatter_plane(lambda core: dot_cols(grad_qkv[core * side : (core + 1) * side], wqkv))
    grad_z1 = grad_xn * gain_one
    grad_x = grad_res + inv_one * (
        grad_z1 - z_one * jnp.mean(grad_z1 * z_one, axis=-1, keepdims=True)
    )
    tokens_grad = grad_x.astype(BF16).reshape(tokens.shape)

    out_rows = width // n_all

    def by_plane(grad):
        blocks = grad.astype(BF16).reshape(n_seq, n_z, NY * out_rows, grad.shape[1])
        return blocks.transpose(1, 0, 2, 3).reshape(grad.shape)

    def to_team(summed):
        spread = lax.all_to_all(
            summed, ("seq", "fsdp"), split_axis=0, concat_axis=0, tiled=True, axis_index_groups=plane_groups()
        )
        return spread.reshape(n_team, out_rows, -1).astype(F32)

    def to_owner(summed, block_of):
        pairs = [
            (si * n_fsdp + zi * NY + yi, block_of(si, zi, yi))
            for si in range(n_seq)
            for zi in range(n_z)
            for yi in range(NY)
        ]
        return lax.ppermute(summed, ("seq", "fsdp"), pairs).astype(F32)

    w_down_grad = to_owner(
        scatter_z(dot_rows(mid, cot_all).astype(BF16)),
        lambda si, zi, yi: (zi * NY + yi) * n_seq + si,
    )
    spread = to_team(scatter_z(by_plane(dot_rows(hn, grad_both))))
    spread = spread.reshape(n_seq, NY, out_rows, 2, n_z, ff_block).transpose(3, 2, 4, 1, 0, 5)
    w_gate_grad = spread[0].reshape(out_rows, ff_width)
    w_up_grad = spread[1].reshape(out_rows, ff_width)

    summed = scatter_z(
        jnp.concatenate(
            [
                by_plane(dot_rows(xn, grad_qkv)),
                dot_rows(attn_rows, da).astype(BF16).reshape(w_q.shape[1], -1),
            ],
            axis=1,
        )
    )
    w_o_grad = to_owner(
        summed[:, head_cols:].reshape(-1, width), lambda si, zi, yi: (si * NY + yi) * n_z + zi
    )
    spread = to_team(summed[:, :head_cols]).transpose(1, 0, 2)
    w_q_grad = spread[..., :q_cols].reshape(out_rows, q_width)
    w_k_grad = spread[..., q_cols : q_cols + kv_cols].reshape(out_rows, kv_width)
    w_v_grad = spread[..., q_cols + kv_cols :].reshape(out_rows, kv_width)

    gain_terms = jnp.stack([jnp.sum(grad_xn * z_one, axis=0), jnp.sum(grad_hn * z_two, axis=0)])
    gain_terms = gain_terms.reshape(2, n_all, out_rows).transpose(1, 0, 2)
    gain_sums = jnp.sum(
        lax.all_to_all(gain_terms, ("seq", "fsdp"), split_axis=0, concat_axis=0, tiled=True), axis=0
    )
    return (
        output,
        tokens_grad,
        gain_sums[0],
        w_q_grad,
        w_k_grad,
        w_v_grad,
        w_o_grad,
        gain_sums[1],
        w_gate_grad,
        w_up_grad,
        w_down_grad,
    )


def solution(mesh):
    by_both = P("fsdp", "seq", None)
    by_rows = P("fsdp", None)
    spread = P(("seq", "fsdp"), None)
    return jax.shard_map(
        shards,
        mesh=mesh,
        in_specs=(
            by_both,
            P("fsdp", "seq"),
            P("fsdp"),
            by_rows,
            by_rows,
            by_rows,
            by_rows,
            P("fsdp"),
            by_rows,
            by_rows,
            by_rows,
            by_both,
        ),
        out_specs=(
            by_both,
            by_both,
            P(("seq", "fsdp")),
            spread,
            spread,
            spread,
            spread,
            P(("seq", "fsdp")),
            spread,
            spread,
            spread,
        ),
        check_vma=False,
    )
```

time: 896 us -> 899 us (level)
  matrix products: 262 us -> 97.2 us
  Pallas kernels: 0 us -> 123 us
  waiting for transfers between devices: 248 us -> 332 us
  blocking collectives: 0 us -> 69.7 us
  local copies, waits for them, and re-layouts: 138 us -> 92 us
  other arithmetic: 89.5 us -> 45.7 us
  starting transfers between devices: 130 us -> 112 us
    pallas_call x0 -> x6, Pallas kernels: none -> 123 us  [the longest x4 68 us: pieces_call(): pl.pallas_call(kernel, out_shape=tuple((jax.ShapeDtypeStruct((blocks * ro...]
    dot_general x28 -> x0, matrix products: 78.9 us -> none  [the longest x4 22 us: one_block(): jnp.einsum('grqk,qgrd->kgd', probabilities.astype(BF16), d_block, preferr...]
    all_to_all x0 -> x1, blocking collectives: none -> 69.7 us  [shards(): lax.all_to_all(gain_terms, ('seq', 'fsdp'), split_axis=0, concat_axis=0,...]
    reduce_scatter x5 -> x3, waiting for transfers between devices: 7.3 us -> 53.5 us  [scatter_z(): lax.psum_scatter(terms, 'fsdp', scatter_dimension=0, tiled=True, axis_ind...]
    dot_general x7 -> x4, matrix products: 60.9 us -> 19 us  [dot(): return jnp.dot(left, right, preferred_element_type=F32)]
    dot_general x8 -> x4, matrix products: 71.9 us -> 31.9 us  [dot_cols(): lax.dot_general(left, right, (((1,), (1,)), ((), ())), preferred_element_...]
    all_to_all x4 -> x2, waiting for transfers between devices: 15.3 us -> 40.6 us  [to_team(): lax.all_to_all(summed, ('seq', 'fsdp'), split_axis=0, concat_axis=0, tile...]
    ppermute x12, waiting for transfers between devices: 0.03 us -> 20.3 us  [swap_core(): lax.ppermute(value, 'seq', [(i, i ^ 1) for i in range(lax.axis_size('seq'...]
  transfers between devices with their start and end apart: 67 -> 60, of which waited for: 26 -> 33; matrix products, arithmetic and copies ran while one was open for 48% -> 23% of each run, Pallas kernels for 0% -> 14%
where the time goes in v2:
time: 899 us; the launch traced here: 887 us
  waiting for transfers between devices  332 us (37%)
  Pallas kernels  123 us (14%)
  starting transfers between devices  112 us (12%)
  matrix products  97.2 us (11%)
  local copies, waits for them, and re-layouts  92 us (10%)
  blocking collectives  69.7 us (8%)
  other arithmetic  45.7 us (5%)
  between operations  15.2 us (2%)
    ppermute x16, waiting for transfers between devices, swap_x(): lax.ppermute(value, 'seq', [(i, i ^ 2) for i in range(lax.axis_size('seq'...  135 us
    ppermute x19, waiting for transfers between devices, swap_y(): lax.ppermute(value, 'fsdp', [(i, i ^ 1) for i in range(lax.axis_size('fsd...  69.8 us
    all_to_all x1, blocking collectives, shards(): lax.all_to_all(gain_terms, ('seq', 'fsdp'), split_axis=0, concat_axis=0,...  69.7 us
    pallas_call x4, Pallas kernels, pieces_call(): pl.pallas_call(kernel, out_shape=tuple((jax.ShapeDtypeStruct((blocks * ro...  68 us
    reduce_scatter x3, waiting for transfers between devices, scatter_z(): lax.psum_scatter(terms, 'fsdp', scatter_dimension=0, tiled=True, axis_ind...  53.5 us
    dot_general x4, matrix products, dot_rows(): lax.dot_general(left, right, (((0,), (0,)), ((), ())), preferred_element_...  46.4 us
    all_to_all x2, waiting for transfers between devices, to_team(): lax.all_to_all(summed, ('seq', 'fsdp'), split_axis=0, concat_axis=0, tile...  40.6 us
    pallas_call x1, Pallas kernels, attend_back(): pl.pallas_call(functools.partial(attend_back_kernel, n_parts), out_shape=...  33.5 us
  transfers between devices with their start and end apart: 60, of which 33 were waited for; matrix products, arithmetic and copies ran while one was open for 23% of the time, Pallas kernels for 14%

profile of v2, /device:TPU:11, one launch (start us, length us, event | category | flops | bytes accessed | tf_op | source)
XLA Modules:
  0.0 887.1 jit_solution(8373838188037186023)
XLA Ops:
  10.9 4.2 collective-permute-start.7
  15.5 10.9 %collective-permute-done.7 = bf16[64,2048]{1,0:T(8,128)(2,1)S(1)} collective-permute-done((bf16[64,2048]{1,0:T(8,128)(2,1)S(1)}, bf16[64,2048]{1,0:T(8,128)(2,1)S(1)}, u32[]{:S(2)}, u32[]{:S(2)}) %collective-permute-start.7) | collective-permute-done | bytes 262176 | tf_op jit(solution)/shard_map/ppermute | solution.py:553
  37.6 12.3 %collective-permute-done = bf16[256,2048]{1,0:T(8,128)(2,1)S(1)} collective-permute-done((bf16[256,2048]{1,0:T(8,128)(2,1)S(1)}, bf16[256,2048]{1,0:T(8,128)(2,1)S(1)}, u32[]{:S(2)}, u32[]{:S(2)}) %collective-permute-start) | collective-permute-done | bytes 1048608 | tf_op jit(solution)/shard_map/ppermute | solution.py:42
  55.0 5.4 collective-permute-done.2
  63.1 6.7 collective-permute-start.5
  69.8 13.1 %collective-permute-done.20 = bf16[256,2048]{1,0:T(8,128)(2,1)S(1)} collective-permute-done((bf16[256,2048]{1,0:T(8,128)(2,1)S(1)}, bf16[256,2048]{1,0:T(8,128)(2,1)S(1)}, u32[]{:S(2)}, u32[]{:S(2)}) %collective-permute-start.20) | collective-permute-done | bytes 1048608 | tf_op jit(solution)/shard_map/ppermute | solution.py:46
  84.6 4.1 collective-permute-start.4
  89.3 4.5 all-to-all-start.1
  96.0 6.3 all-to-all-start
  118.7 12.5 %project.1 = (bf16[2048,2048]{1,0:T(8,128)(2,1)}, f32[2048,384]{1,0:T(8,128)}) custom-call(bf16[256,2048]{1,0:T(8,128)(2,1)S(1)} %bitcast.69, bf16[768,2048]{1,0:T(8,128)(2,1)} %constant_dynamic-update-slice_fusion.refs_1_, bf16[256,2048]{1,0:T(8,128)(2,1)S(1)} %collective-permute-done.4.refs_2_, bf16[768,2048]{1,0:T(8,128)(2,1)} %collective-permute-done.5.refs_3_, ...), custom_call_target="tpu_custom_call" | custom-call | flops 3221225472 | bytes 22552576 | tf_op jit(solution)/shard_map/project/pallas_call | solution.py:373
  131.2 21.9 %attend.1 = (bf16[2048,256]{1,0:T(8,128)(2,1)S(1)}, f32[2048,128]{1,0:T(8,128)S(1)}) custom-call(s32[1]{0:T(128)} %bitcast.1.member, f32[2048,384]{1,0:T(8,128)} %get-tuple-element.23.refs_0_.refs_1_.refs_2_.refs_3_, f32[2048,384]{1,0:T(8,128)} %get-tuple-element.23.refs_0_.refs_1_.refs_2_.refs_3_, ...), custom_call_target="tpu_custom_call" | custom-call | flops 4294967296 | bytes 6291456 | tf_op jit(solution)/shard_map/attend/pallas_call | solution.py:280
  156.4 6.8 collective-permute-done.9
  167.7 10.3 %collective-permute-done.10 = bf16[128,2048]{1,0:T(8,128)(2,1)S(1)} collective-permute-done((bf16[128,2048]{1,0:T(8,128)(2,1)S(1)}, bf16[128,2048]{1,0:T(8,128)(2,1)S(1)}, u32[]{:S(2)}, u32[]{:S(2)}) %collective-permute-start.10) | collective-permute-done | bytes 524320 | tf_op jit(solution)/shard_map/ppermute | solution.py:46
  181.6 21.9 %collective-permute-done.11 = bf16[256,2048]{1,0:T(8,128)(2,1)S(1)} collective-permute-done((bf16[256,2048]{1,0:T(8,128)(2,1)S(1)}, bf16[256,2048]{1,0:T(8,128)(2,1)S(1)}, u32[]{:S(2)}, u32[]{:S(2)}) %collective-permute-start.11) | collective-permute-done | bytes 1048608 | tf_op jit(solution)/shard_map/ppermute | solution.py:42
  210.4 18.8 %collective-permute-done.14 = bf16[256,2048]{1,0:T(8,128)(2,1)} collective-permute-done((bf16[256,2048]{1,0:T(8,128)(2,1)S(1)}, bf16[256,2048]{1,0:T(8,128)(2,1)}, u32[]{:S(2)}, u32[]{:S(2)}) %collective-permute-start.14) | collective-permute-done | bytes 1048608 | tf_op jit(solution)/shard_map/ppermute | solution.py:42
  242.8 4.6 collective-permute-start.19
  249.2 23.1 %collective-permute-done.26 = bf16[256,2048]{1,0:T(8,128)(2,1)S(1)} collective-permute-done((bf16[256,2048]{1,0:T(8,128)(2,1)S(1)}, bf16[256,2048]{1,0:T(8,128)(2,1)S(1)}, u32[]{:S(2)}, u32[]{:S(2)}) %collective-permute-start.26) | collective-permute-done | bytes 1048608 | tf_op jit(solution)/shard_map/ppermute | solution.py:42
  277.7 7.5 collective-permute-done.28
  292.0 26.1 %feed.1 = (bf16[2048,2048]{1,0:T(8,128)(2,1)}, bf16[2048,1024]{1,0:T(8,128)(2,1)}, bf16[2048,1024]{1,0:T(8,128)(2,1)}, bf16[2048,1024]{1,0:T(8,128)(2,1)}) custom-call(bf16[256,2048]{1,0:T(8,128)(2,1)S(1)} %copy-done.11, bf16[768,2048]{1,0:T(8,128)(2,1)} %constant_dynamic-update-slice_fusion.4.refs_1_, bf16[256,2048]{1,0:T(8,128)(2,1)S(1)} %copy-done.15, ...), custom_call_target="tpu_custom_call" | custom-call | flops 17179869184 | bytes 37748736 | tf_op jit(solution)/shard_map/feed/pallas_call | solution.py:373
  318.5 9.5 %convolution_convert_fusion.4 = bf16[1024,2048]{1,0:T(8,128)(2,1)} fusion(bf16[1024,2048]{1,0:T(8,128)(2,1)} %all-gather.8.cloned.1.call-done.refs_4_, bf16[2048,1024]{1,0:T(8,128)(2,1)} %get-tuple-element.25), kind=kOutput, calls=%fused_computation.13 | convolution fusion | flops 4297064448 | bytes 10485760 | tf_op jit(solution)/shard_map/dot_general | solution.py:34
  328.7 19.3 %feed_back.1 = (bf16[2048,2048]{1,0:T(8,128)(2,1)}, bf16[2048,2048]{1,0:T(8,128)(2,1)}) custom-call(bf16[256,2048]{1,0:T(8,128)(2,1)S(1)} %bitcast.73, bf16[768,2048]{1,0:T(8,128)(2,1)} %constant_dynamic-update-slice_fusion.8.refs_1_, bf16[256,2048]{1,0:T(8,128)(2,1)} %collective-permute-done.30.refs_2_, bf16[768,2048]{1,0:T(8,128)(2,1)} %collective-permute-done.31.refs_3_, ...), custom_call_target="tpu_custom_call" | custom-call | flops 8589934592 | bytes 37748736 | tf_op jit(solution)/shard_map/feed_back/pallas_call | solution.py:373
  348.0 12.2 %fusion.4 = bf16[1024,2048]{1,0:T(8,128)(2,1)} fusion(bf16[2048,2048]{1,0:T(8,128)(2,1)S(1)} %bitcast.97, bf16[2048,2048]{1,0:T(8,128)(2,1)} %get-tuple-element.28), kind=kOutput, calls=%fused_computation.10 | convolution fusion | flops 8592031744 | bytes 16777216 | tf_op jit(solution)/shard_map/dot_general | solution.py:30
  360.2 7.0 add_convert_fusion.2
  369.0 13.4 %add_convert_fusion.1 = bf16[1024,2048]{1,0:T(8,128)(2,1)S(1)} fusion(bf16[1024,2048]{1,0:T(8,128)(2,1)} %collective-permute-done.32, bf16[2048,2048]{1,0:T(8,128)(2,1)} %all-gather.6.cloned.1.call-done.refs_4_, bf16[2048,2048]{1,0:T(8,128)(2,1)} %get-tuple-element.28), kind=kOutput, calls=%fused_computation.1 | convolution fusion | flops 8596226048 | bytes 20971520 | tf_op jit(solution)/shard_map/dot_general | solution.py:30
  388.2 6.9 collective-permute-done.33
  400.0 11.0 %convolution_convert_fusion.2 = bf16[1024,2048]{1,0:T(8,128)(2,1)} fusion(bf16[2048,1024]{1,0:T(8,128)(2,1)S(1)} %copy-done.37, bf16[2048,2048]{1,0:T(8,128)(2,1)S(1)} %bitcast.99), kind=kOutput, calls=%fused_computation.11 | convolution fusion | flops 8592031744 | bytes 16777216 | tf_op jit(solution)/shard_map/dot_general | solution.py:26
  411.3 29.4 %collective-permute-done.34 = bf16[256,2048]{1,0:T(8,128)(2,1)} collective-permute-done((bf16[256,2048]{1,0:T(8,128)(2,1)}, bf16[256,2048]{1,0:T(8,128)(2,1)}, u32[]{:S(2)}, u32[]{:S(2)}) %collective-permute-start.34) | collective-permute-done | bytes 1048608 | tf_op jit(solution)/shard_map/ppermute | solution.py:42
  444.2 6.4 fusion.33
  452.4 21.0 %collective-permute-done.37 = bf16[256,2048]{1,0:T(8,128)(2,1)S(1)} collective-permute-done((bf16[256,2048]{1,0:T(8,128)(2,1)S(1)}, bf16[256,2048]{1,0:T(8,128)(2,1)S(1)}, u32[]{:S(2)}, u32[]{:S(2)}) %collective-permute-start.37) | collective-permute-done | bytes 1048608 | tf_op jit(solution)/shard_map/ppermute | solution.py:42
  475.4 9.2 %collective-permute-done.39 = bf16[128,2048]{1,0:T(8,128)(2,1)S(1)} collective-permute-done((bf16[128,2048]{1,0:T(8,128)(2,1)S(1)}, bf16[128,2048]{1,0:T(8,128)(2,1)S(1)}, u32[]{:S(2)}, u32[]{:S(2)}) %collective-permute-start.39) | collective-permute-done | bytes 524320 | tf_op jit(solution)/shard_map/ppermute | solution.py:46
  488.7 6.7 collective-permute-done.41.refs_2_
  497.1 10.1 %out_back.1 = (bf16[2048,2048]{1,0:T(8,128)(2,1)}, bf16[2048,256]{1,0:T(8,128)(2,1)S(1)}) custom-call(bf16[256,2048]{1,0:T(8,128)(2,1)S(1)} %get-tuple-element.39.refs_0_, bf16[768,2048]{1,0:T(8,128)(2,1)} %copy-done.24, bf16[256,2048]{1,0:T(8,128)(2,1)S(1)} %collective-permute-done.41.refs_2_, bf16[768,2048]{1,0:T(8,128)(2,1)} %copy-done.28, ...), custom_call_target="tpu_custom_call" | custom-call | flops 2147483648 | bytes 18874368 | tf_op jit(solution)/shard_map/out_back/pallas_call | solution.py:373
  507.1 33.5 %attend_back.1 = bf16[2048,384]{1,0:T(8,128)(2,1)S(1)} custom-call(s32[1]{0:T(128)} %bitcast.1.member, f32[2048,384]{1,0:T(8,128)} %get-tuple-element.23.refs_0_.refs_1_.refs_2_.refs_3_, f32[2048,384]{1,0:T(8,128)} %get-tuple-element.23.refs_0_.refs_1_.refs_2_.refs_3_, f32[2048,384]{1,0:T(8,128)} %get-tuple-element.23.refs_0_.refs_1_.refs_2_.refs_3_, ...), custom_call_target="tpu_custom_call" | custom-call | flops 10737418240 | bytes 7864320 | tf_op jit(solution)/shard_map/attend_back/pallas_call | solution.py:313
  540.7 8.1 convolution_convert_fusion.5
  558.3 24.0 %convolution_convert_fusion = bf16[2048,2048]{1,0:T(8,128)(2,1)} fusion(bf16[2048,2048]{1,0:T(8,128)(2,1)} %get-tuple-element.33, bf16[2048,2048]{1,0:T(8,128)(2,1)} %get-tuple-element.28), kind=kOutput, calls=%fused_computation.4 | convolution fusion | flops 17184063488 | bytes 25165824 | tf_op jit(solution)/shard_map/dot_general | solution.py:26
  582.2 8.4 copy.60
  595.0 6.8 collective-permute-done.43
  605.9 11.7 %collective-permute-done.44 = bf16[128,2048]{1,0:T(8,128)(2,1)S(1)} collective-permute-done((bf16[128,2048]{1,0:T(8,128)(2,1)S(1)}, bf16[128,2048]{1,0:T(8,128)(2,1)S(1)}, u32[]{:S(2)}, u32[]{:S(2)}) %collective-permute-start.44) | collective-permute-done | bytes 524320 | tf_op jit(solution)/shard_map/ppermute | solution.py:46
  628.5 5.8 all-to-all-start.3
  637.7 11.9 %collective-permute-start.48 = (bf16[64,2048]{1,0:T(8,128)(2,1)}, bf16[64,2048]{1,0:T(8,128)(2,1)}, u32[]{:S(2)}, u32[]{:S(2)}) collective-permute-start(bf16[64,2048]{1,0:T(8,128)(2,1)} %reshape.201), channel_id=1, source_target_pairs={{0,0},{1,4},{2,1},{3,5},{4,2},{5,6},{6,3},{7,7},{8,8},{9,12},{10,9... | collective-permute-start | bytes 786440 | tf_op jit(solution)/shard_map/ppermute | solution.py:624
  660.1 30.6 %all-to-all-done.3 = bf16[8,64,384]{2,1,0:T(8,128)(2,1)S(1)} async-done(((bf16[8,64,384]{2,1,0:T(8,128)(2,1)}), bf16[8,64,384]{2,1,0:T(8,128)(2,1)S(1)}, u32[]{:S(2)}, u32[]{:S(2)}) %all-to-all-start.3) | async-done | bytes 393248 | tf_op jit(solution)/shard_map/all_to_all | solution.py:612
  690.7 69.7 %all_to_all.34 = f32[32,1,128]{2,1,0:T(1,128)} all-to-all(f32[32,1,128]{2,1,0:T(1,128)} %reshape.205), channel_id=1, replica_groups=mesh['seq'=4,'fsdp'=8] {'seq','fsdp'}, dimensions={0} | all-to-all | bytes 32768 | tf_op jit(solution)/shard_map/all_to_all | solution.py:655
  760.3 53.4 %reduce-scatter.6.cloned.1.call-done = bf16[512,2048]{1,0:T(8,128)(2,1)} async-done(((bf16[2048,2048]{1,0:T(8,128)(2,1)}), bf16[512,2048]{1,0:T(8,128)(2,1)}) %reduce-scatter.6.cloned.1.call-update) | async-done | bytes 2097168 | tf_op jit(solution)/shard_map/reduce_scatter | solution.py:94
  813.8 22.4 %all-to-all-start.4 = ((bf16[8,64,2048]{2,1,0:T(8,128)(2,1)}), bf16[8,64,2048]{2,1,0:T(8,128)(2,1)}, u32[]{:S(2)}, u32[]{:S(2)}) async-start(bf16[8,64,2048]{2,1,0:T(8,128)(2,1)} %bitcast.83), calls=%async_computation.6 | async-start | bytes 4194304 | tf_op jit(solution)/shard_map/all_to_all | solution.py:612
  845.4 3.9 fusion.24
  851.2 10.0 %all-to-all-done.4 = bf16[8,64,2048]{2,1,0:T(8,128)(2,1)} async-done(((bf16[8,64,2048]{2,1,0:T(8,128)(2,1)}), bf16[8,64,2048]{2,1,0:T(8,128)(2,1)}, u32[]{:S(2)}, u32[]{:S(2)}) %all-to-all-start.4) | async-done | bytes 2097184 | tf_op jit(solution)/shard_map/all_to_all | solution.py:612
  861.2 6.0 reshape.204
  867.3 4.3 fusion.34
  (302 shorter events, 178.4 us)
Async XLA Ops:
  7.2 105.4 %all-gather.4.cloned.1.call-start = ((), (), s32[]{:S(2)}) async-start(), calls=%async_computation.8 | async-start | bytes 3276800 | tf_op jit(solution)/shard_map/all_gather | solution.py:90
  10.9 15.5 %collective-permute-start.7 = (bf16[64,2048]{1,0:T(8,128)(2,1)S(1)}, bf16[64,2048]{1,0:T(8,128)(2,1)S(1)}, u32[]{:S(2)}, u32[]{:S(2)}) collective-permute-start(bf16[64,2048]{1,0:T(8,128)(2,1)S(1)} %constant_dynamic-slice_fusion.1), channel_id=1, source_target_pairs={{0,0},{8,2},{16,4},{24,6},{1,1},{9,3},{17,5},{25,7},{2,8},{10,10},... | collective-permute-start | bytes 786440 | tf_op jit(solution)/shard_map/ppermute | solution.py:553
  27.5 262.1 %all-gather.6.cloned.1.call-start = ((), (), s32[]{:S(2)}) async-start(), calls=%async_computation.9 | async-start | bytes 10485760 | tf_op jit(solution)/shard_map/all_gather | solution.py:90
  27.5 22.4 %collective-permute-start = (bf16[256,2048]{1,0:T(8,128)(2,1)S(1)}, bf16[256,2048]{1,0:T(8,128)(2,1)S(1)}, u32[]{:S(2)}, u32[]{:S(2)}) collective-permute-start(bf16[256,2048]{1,0:T(8,128)(2,1)S(1)} %bitcast.66), channel_id=1, source_target_pairs={{0,16},{8,24},{16,0},{24,8},{1,17},{9,25},{17,1},{25,9},{2,18},{10... | collective-permute-start | bytes 3145736 | tf_op jit(solution)/shard_map/ppermute | solution.py:42
  27.6 24.9 %collective-permute-start.1 = (bf16[256,2048]{1,0:T(8,128)(2,1)S(1)}, bf16[256,2048]{1,0:T(8,128)(2,1)S(1)}, u32[]{:S(2)}, u32[]{:S(2)}) collective-permute-start(bf16[256,2048]{1,0:T(8,128)(2,1)S(1)} %bitcast.67), channel_id=1, source_target_pairs={{0,1},{1,0},{2,3},{3,2},{4,5},{5,4},{6,7},{7,6},{8,9},{9,8},{10,11... | collective-permute-start | bytes 3145736 | tf_op jit(solution)/shard_map/ppermute | solution.py:46
  51.1 31.7 %collective-permute-start.20 = (bf16[256,2048]{1,0:T(8,128)(2,1)S(1)}, bf16[256,2048]{1,0:T(8,128)(2,1)S(1)}, u32[]{:S(2)}, u32[]{:S(2)}) collective-permute-start(bf16[256,2048]{1,0:T(8,128)(2,1)S(1)} %dynamic-slice_dynamic-update-slice_fusion), channel_id=1, source_target_pairs={{0,1},{1,0},{2,3},{3,2},{4,5},{5,4},{6,7},{7,6},{8,9},{9,8},{10,11... | collective-permute-start | bytes 3145736 | tf_op jit(solution)/shard_map/ppermute | solution.py:46
  63.1 53.8 %collective-permute-start.5 = (bf16[768,2048]{1,0:T(8,128)(2,1)}, bf16[768,2048]{1,0:T(8,128)(2,1)}, u32[]{:S(2)}, u32[]{:S(2)}) collective-permute-start(bf16[768,2048]{1,0:T(8,128)(2,1)} %constant_dynamic-update-slice_fusion.refs_1_), channel_id=1, source_target_pairs={{0,8},{8,0},{16,24},{24,16},{1,9},{9,1},{17,25},{25,17},{2,10},{10... | collective-permute-start | bytes 9437192 | tf_op jit(solution)/shard_map/ppermute | solution.py:38
  84.6 32.3 %collective-permute-start.4 = (bf16[256,2048]{1,0:T(8,128)(2,1)S(1)}, bf16[256,2048]{1,0:T(8,128)(2,1)S(1)}, u32[]{:S(2)}, u32[]{:S(2)}) collective-permute-start(bf16[256,2048]{1,0:T(8,128)(2,1)S(1)} %bitcast.68), channel_id=1, source_target_pairs={{0,8},{8,0},{16,24},{24,16},{1,9},{9,1},{17,25},{25,17},{2,10},{10... | collective-permute-start | bytes 3145736 | tf_op jit(solution)/shard_map/ppermute | solution.py:38
  96.0 16.5 %all-to-all-start = ((bf16[8,2,256]{2,1,0:T(2,128)(2,1)}), bf16[8,2,256]{2,1,0:T(2,128)(2,1)S(1)}, u32[]{:S(2)}, u32[]{:S(2)}) async-start(bf16[8,2,256]{2,1,0:T(2,128)(2,1)} %broadcast_in_dim.4), calls=%async_computation | async-start | bytes 16384 | tf_op jit(solution)/shard_map/all_to_all | solution.py:503
  102.3 216.2 %all-gather.8.cloned.1.call-start = ((), (), s32[]{:S(2)}) async-start(), calls=%async_computation.10 | async-start | bytes 5242880 | tf_op jit(solution)/shard_map/all_gather | solution.py:90
  164.7 13.3 %collective-permute-start.10 = (bf16[128,2048]{1,0:T(8,128)(2,1)S(1)}, bf16[128,2048]{1,0:T(8,128)(2,1)S(1)}, u32[]{:S(2)}, u32[]{:S(2)}) collective-permute-start(bf16[128,2048]{1,0:T(8,128)(2,1)S(1)} %get-tuple-element.74), channel_id=1, source_target_pairs={{0,1},{1,0},{2,3},{3,2},{4,5},{5,4},{6,7},{7,6},{8,9},{9,8},{10,11... | collective-permute-start | bytes 1572872 | tf_op jit(solution)/shard_map/ppermute | solution.py:46
  165.9 13.5 %collective-permute-start.12 = (bf16[128,2048]{1,0:T(8,128)(2,1)S(1)}, bf16[128,2048]{1,0:T(8,128)(2,1)S(1)}, u32[]{:S(2)}, u32[]{:S(2)}) collective-permute-start(bf16[128,2048]{1,0:T(8,128)(2,1)S(1)} %get-tuple-element.73), channel_id=1, source_target_pairs={{0,16},{8,24},{16,0},{24,8},{1,17},{9,25},{17,1},{25,9},{2,18},{10... | collective-permute-start | bytes 1572872 | tf_op jit(solution)/shard_map/ppermute | solution.py:42
  179.9 23.6 %collective-permute-start.11 = (bf16[256,2048]{1,0:T(8,128)(2,1)S(1)}, bf16[256,2048]{1,0:T(8,128)(2,1)S(1)}, u32[]{:S(2)}, u32[]{:S(2)}) collective-permute-start(bf16[256,2048]{1,0:T(8,128)(2,1)S(1)} %pad_maximum_fusion.2), channel_id=1, source_target_pairs={{0,16},{8,24},{16,0},{24,8},{1,17},{9,25},{17,1},{25,9},{2,18},{10... | collective-permute-start | bytes 3145736 | tf_op jit(solution)/shard_map/ppermute | solution.py:42
  181.2 23.0 %collective-permute-start.13 = (bf16[256,2048]{1,0:T(8,128)(2,1)S(1)}, bf16[256,2048]{1,0:T(8,128)(2,1)S(1)}, u32[]{:S(2)}, u32[]{:S(2)}) collective-permute-start(bf16[256,2048]{1,0:T(8,128)(2,1)S(1)} %pad_maximum_fusion.3), channel_id=1, source_target_pairs={{0,1},{1,0},{2,3},{3,2},{4,5},{5,4},{6,7},{7,6},{8,9},{9,8},{10,11... | collective-permute-start | bytes 3145736 | tf_op jit(solution)/shard_map/ppermute | solution.py:46
  207.1 22.1 %collective-permute-start.14 = (bf16[256,2048]{1,0:T(8,128)(2,1)S(1)}, bf16[256,2048]{1,0:T(8,128)(2,1)}, u32[]{:S(2)}, u32[]{:S(2)}) collective-permute-start(bf16[256,2048]{1,0:T(8,128)(2,1)S(1)} %multiply_convert_fusion.refs_0_), channel_id=1, source_target_pairs={{0,16},{8,24},{16,0},{24,8},{1,17},{9,25},{17,1},{25,9},{2,18},{10... | collective-permute-start | bytes 3145736 | tf_op jit(solution)/shard_map/ppermute | solution.py:42
  207.8 23.3 %collective-permute-start.15 = (bf16[256,2048]{1,0:T(8,128)(2,1)S(1)}, bf16[256,2048]{1,0:T(8,128)(2,1)}, u32[]{:S(2)}, u32[]{:S(2)}) collective-permute-start(bf16[256,2048]{1,0:T(8,128)(2,1)S(1)} %multiply_convert_fusion.refs_0_), channel_id=1, source_target_pairs={{0,1},{1,0},{2,3},{3,2},{4,5},{5,4},{6,7},{7,6},{8,9},{9,8},{10,11... | collective-permute-start | bytes 3145736 | tf_op jit(solution)/shard_map/ppermute | solution.py:46
  210.4 412.0 %reduce-scatter.8.cloned.1.call-start = ((), (), s32[]{:S(2)}) async-start(), calls=%async_computation.13 | async-start | bytes 5242880 | tf_op jit(solution)/shard_map/reduce_scatter | solution.py:94
  242.8 46.7 %collective-permute-start.19 = (bf16[768,2048]{1,0:T(8,128)(2,1)}, bf16[768,2048]{1,0:T(8,128)(2,1)}, u32[]{:S(2)}, u32[]{:S(2)}) collective-permute-start(bf16[768,2048]{1,0:T(8,128)(2,1)} %constant_dynamic-update-slice_fusion.4.refs_1_), channel_id=1, source_target_pairs={{0,8},{8,0},{16,24},{24,16},{1,9},{9,1},{17,25},{25,17},{2,10},{10... | collective-permute-start | bytes 9437192 | tf_op jit(solution)/shard_map/ppermute | solution.py:38
  247.4 24.9 %collective-permute-start.26 = (bf16[256,2048]{1,0:T(8,128)(2,1)S(1)}, bf16[256,2048]{1,0:T(8,128)(2,1)S(1)}, u32[]{:S(2)}, u32[]{:S(2)}) collective-permute-start(bf16[256,2048]{1,0:T(8,128)(2,1)S(1)} %bitcast.70), channel_id=1, source_target_pairs={{0,16},{8,24},{16,0},{24,8},{1,17},{9,25},{17,1},{25,9},{2,18},{10... | collective-permute-start | bytes 3145736 | tf_op jit(solution)/shard_map/ppermute | solution.py:42
  248.0 25.2 %collective-permute-start.27 = (bf16[256,2048]{1,0:T(8,128)(2,1)S(1)}, bf16[256,2048]{1,0:T(8,128)(2,1)S(1)}, u32[]{:S(2)}, u32[]{:S(2)}) collective-permute-start(bf16[256,2048]{1,0:T(8,128)(2,1)S(1)} %bitcast.71), channel_id=1, source_target_pairs={{0,1},{1,0},{2,3},{3,2},{4,5},{5,4},{6,7},{7,6},{8,9},{9,8},{10,11... | collective-permute-start | bytes 3145736 | tf_op jit(solution)/shard_map/ppermute | solution.py:46
  272.3 12.9 %collective-permute-start.28 = (bf16[128,2048]{1,0:T(8,128)(2,1)S(1)}, bf16[128,2048]{1,0:T(8,128)(2,1)S(1)}, u32[]{:S(2)}, u32[]{:S(2)}) collective-permute-start(bf16[128,2048]{1,0:T(8,128)(2,1)S(1)} %slice.318), channel_id=1, source_target_pairs={{0,1},{1,0},{2,3},{3,2},{4,5},{5,4},{6,7},{7,6},{8,9},{9,8},{10,11... | collective-permute-start | bytes 1572872 | tf_op jit(solution)/shard_map/ppermute | solution.py:46
  273.3 12.8 %collective-permute-start.29 = (bf16[128,2048]{1,0:T(8,128)(2,1)S(1)}, bf16[128,2048]{1,0:T(8,128)(2,1)S(1)}, u32[]{:S(2)}, u32[]{:S(2)}) collective-permute-start(bf16[128,2048]{1,0:T(8,128)(2,1)S(1)} %slice.319), channel_id=1, source_target_pairs={{0,16},{8,24},{16,0},{24,8},{1,17},{9,25},{17,1},{25,9},{2,18},{10... | collective-permute-start | bytes 1572872 | tf_op jit(solution)/shard_map/ppermute | solution.py:42
  275.5 13.1 %collective-permute-start.18 = (bf16[256,2048]{1,0:T(8,128)(2,1)S(1)}, bf16[256,2048]{1,0:T(8,128)(2,1)S(1)}, u32[]{:S(2)}, u32[]{:S(2)}) collective-permute-start(bf16[256,2048]{1,0:T(8,128)(2,1)S(1)} %copy-done.10), channel_id=1, source_target_pairs={{0,8},{8,0},{16,24},{24,16},{1,9},{9,1},{17,25},{25,17},{2,10},{10... | collective-permute-start | bytes 3145736 | tf_op jit(solution)/shard_map/ppermute | solution.py:38
  286.9 41.8 %collective-permute-start.31 = (bf16[768,2048]{1,0:T(8,128)(2,1)}, bf16[768,2048]{1,0:T(8,128)(2,1)}, u32[]{:S(2)}, u32[]{:S(2)}) collective-permute-start(bf16[768,2048]{1,0:T(8,128)(2,1)} %constant_dynamic-update-slice_fusion.8.refs_1_), channel_id=1, source_target_pairs={{0,8},{8,0},{16,24},{24,16},{1,9},{9,1},{17,25},{25,17},{2,10},{10... | collective-permute-start | bytes 9437192 | tf_op jit(solution)/shard_map/ppermute | solution.py:38
  288.5 40.1 %collective-permute-start.30 = (bf16[256,2048]{1,0:T(8,128)(2,1)S(1)}, bf16[256,2048]{1,0:T(8,128)(2,1)}, u32[]{:S(2)}, u32[]{:S(2)}) collective-permute-start(bf16[256,2048]{1,0:T(8,128)(2,1)S(1)} %bitcast.72), channel_id=1, source_target_pairs={{0,8},{8,0},{16,24},{24,16},{1,9},{9,1},{17,25},{25,17},{2,10},{10... | collective-permute-start | bytes 3145736 | tf_op jit(solution)/shard_map/ppermute | solution.py:38
  328.0 32.2 %collective-permute-start.21 = (bf16[1024,2048]{1,0:T(8,128)(2,1)}, bf16[1024,2048]{1,0:T(8,128)(2,1)}, u32[]{:S(2)}, u32[]{:S(2)}) collective-permute-start(bf16[1024,2048]{1,0:T(8,128)(2,1)} %convolution_convert_fusion.4), channel_id=1, source_target_pairs={{0,8},{8,0},{16,24},{24,16},{1,9},{9,1},{17,25},{25,17},{2,10},{10... | collective-permute-start | bytes 12582920 | tf_op jit(solution)/shard_map/ppermute | solution.py:38
  367.5 16.8 %collective-permute-start.22 = (bf16[128,2048]{1,0:T(8,128)(2,1)S(1)}, bf16[128,2048]{1,0:T(8,128)(2,1)S(1)}, u32[]{:S(2)}, u32[]{:S(2)}) collective-permute-start(bf16[128,2048]{1,0:T(8,128)(2,1)S(1)} %get-tuple-element.60), channel_id=1, source_target_pairs={{0,1},{1,0},{2,3},{3,2},{4,5},{5,4},{6,7},{7,6},{8,9},{9,8},{10,11... | collective-permute-start | bytes 1572872 | tf_op jit(solution)/shard_map/ppermute | solution.py:46
  368.7 15.5 %collective-permute-start.24 = (bf16[128,2048]{1,0:T(8,128)(2,1)S(1)}, bf16[128,2048]{1,0:T(8,128)(2,1)S(1)}, u32[]{:S(2)}, u32[]{:S(2)}) collective-permute-start(bf16[128,2048]{1,0:T(8,128)(2,1)S(1)} %get-tuple-element.59), channel_id=1, source_target_pairs={{0,16},{8,24},{16,0},{24,8},{1,17},{9,25},{17,1},{25,9},{2,18},{10... | collective-permute-start | bytes 1572872 | tf_op jit(solution)/shard_map/ppermute | solution.py:42
  382.7 12.4 %collective-permute-start.33 = (bf16[128,2048]{1,0:T(8,128)(2,1)S(1)}, bf16[128,2048]{1,0:T(8,128)(2,1)S(1)}, u32[]{:S(2)}, u32[]{:S(2)}) collective-permute-start(bf16[128,2048]{1,0:T(8,128)(2,1)S(1)} %get-tuple-element.54), channel_id=1, source_target_pairs={{0,1},{1,0},{2,3},{3,2},{4,5},{5,4},{6,7},{7,6},{8,9},{9,8},{10,11... | collective-permute-start | bytes 1572872 | tf_op jit(solution)/shard_map/ppermute | solution.py:46
  383.3 12.3 %collective-permute-start.35 = (bf16[128,2048]{1,0:T(8,128)(2,1)S(1)}, bf16[128,2048]{1,0:T(8,128)(2,1)S(1)}, u32[]{:S(2)}, u32[]{:S(2)}) collective-permute-start(bf16[128,2048]{1,0:T(8,128)(2,1)S(1)} %get-tuple-element.53), channel_id=1, source_target_pairs={{0,16},{8,24},{16,0},{24,8},{1,17},{9,25},{17,1},{25,9},{2,18},{10... | collective-permute-start | bytes 1572872 | tf_op jit(solution)/shard_map/ppermute | solution.py:42
  385.7 58.5 %collective-permute-start.23 = (bf16[256,2048]{1,0:T(8,128)(2,1)}, bf16[256,2048]{1,0:T(8,128)(2,1)}, u32[]{:S(2)}, u32[]{:S(2)}) collective-permute-start(bf16[256,2048]{1,0:T(8,128)(2,1)} %pad_maximum_fusion.4), channel_id=1, source_target_pairs={{0,16},{8,24},{16,0},{24,8},{1,17},{9,25},{17,1},{25,9},{2,18},{10... | collective-permute-start | bytes 3145736 | tf_op jit(solution)/shard_map/ppermute | solution.py:42
  387.3 56.9 %collective-permute-start.25 = (bf16[256,2048]{1,0:T(8,128)(2,1)}, bf16[256,2048]{1,0:T(8,128)(2,1)}, u32[]{:S(2)}, u32[]{:S(2)}) collective-permute-start(bf16[256,2048]{1,0:T(8,128)(2,1)} %pad_maximum_fusion.5), channel_id=1, source_target_pairs={{0,1},{1,0},{2,3},{3,2},{4,5},{5,4},{6,7},{7,6},{8,9},{9,8},{10,11... | collective-permute-start | bytes 3145736 | tf_op jit(solution)/shard_map/ppermute | solution.py:46
  397.1 43.6 %collective-permute-start.34 = (bf16[256,2048]{1,0:T(8,128)(2,1)}, bf16[256,2048]{1,0:T(8,128)(2,1)}, u32[]{:S(2)}, u32[]{:S(2)}) collective-permute-start(bf16[256,2048]{1,0:T(8,128)(2,1)} %pad_maximum_fusion.6), channel_id=1, source_target_pairs={{0,16},{8,24},{16,0},{24,8},{1,17},{9,25},{17,1},{25,9},{2,18},{10... | collective-permute-start | bytes 3145736 | tf_op jit(solution)/shard_map/ppermute | solution.py:42
  398.8 41.9 %collective-permute-start.36 = (bf16[256,2048]{1,0:T(8,128)(2,1)}, bf16[256,2048]{1,0:T(8,128)(2,1)}, u32[]{:S(2)}, u32[]{:S(2)}) collective-permute-start(bf16[256,2048]{1,0:T(8,128)(2,1)} %pad_maximum_fusion.7), channel_id=1, source_target_pairs={{0,1},{1,0},{2,3},{3,2},{4,5},{5,4},{6,7},{7,6},{8,9},{9,8},{10,11... | collective-permute-start | bytes 3145736 | tf_op jit(solution)/shard_map/ppermute | solution.py:46
  411.0 215.7 %reduce-scatter.4.cloned.1.call-start = ((), (), s32[]{:S(2)}) async-start(), calls=%async_computation.11 | async-start | bytes 3276800 | tf_op jit(solution)/shard_map/reduce_scatter | solution.py:94
  450.6 22.8 %collective-permute-start.37 = (bf16[256,2048]{1,0:T(8,128)(2,1)S(1)}, bf16[256,2048]{1,0:T(8,128)(2,1)S(1)}, u32[]{:S(2)}, u32[]{:S(2)}) collective-permute-start(bf16[256,2048]{1,0:T(8,128)(2,1)S(1)} %get-tuple-element.39.refs_0_), channel_id=1, source_target_pairs={{0,16},{8,24},{16,0},{24,8},{1,17},{9,25},{17,1},{25,9},{2,18},{10... | collective-permute-start | bytes 3145736 | tf_op jit(solution)/shard_map/ppermute | solution.py:42
  451.3 22.8 %collective-permute-start.38 = (bf16[256,2048]{1,0:T(8,128)(2,1)S(1)}, bf16[256,2048]{1,0:T(8,128)(2,1)S(1)}, u32[]{:S(2)}, u32[]{:S(2)}) collective-permute-start(bf16[256,2048]{1,0:T(8,128)(2,1)S(1)} %get-tuple-element.39.refs_0_), channel_id=1, source_target_pairs={{0,1},{1,0},{2,3},{3,2},{4,5},{5,4},{6,7},{7,6},{8,9},{9,8},{10,11... | collective-permute-start | bytes 3145736 | tf_op jit(solution)/shard_map/ppermute | solution.py:46
  473.5 11.2 %collective-permute-start.39 = (bf16[128,2048]{1,0:T(8,128)(2,1)S(1)}, bf16[128,2048]{1,0:T(8,128)(2,1)S(1)}, u32[]{:S(2)}, u32[]{:S(2)}) collective-permute-start(bf16[128,2048]{1,0:T(8,128)(2,1)S(1)} %slice.327), channel_id=1, source_target_pairs={{0,1},{1,0},{2,3},{3,2},{4,5},{5,4},{6,7},{7,6},{8,9},{9,8},{10,11... | collective-permute-start | bytes 1572872 | tf_op jit(solution)/shard_map/ppermute | solution.py:46
  474.1 10.6 %collective-permute-start.40 = (bf16[128,2048]{1,0:T(8,128)(2,1)S(1)}, bf16[128,2048]{1,0:T(8,128)(2,1)S(1)}, u32[]{:S(2)}, u32[]{:S(2)}) collective-permute-start(bf16[128,2048]{1,0:T(8,128)(2,1)S(1)} %slice.328), channel_id=1, source_target_pairs={{0,16},{8,24},{16,0},{24,8},{1,17},{9,25},{17,1},{25,9},{2,18},{10... | collective-permute-start | bytes 1572872 | tf_op jit(solution)/shard_map/ppermute | solution.py:42
  558.2 255.6 %reduce-scatter.6.cloned.1.call-start = ((), (), s32[]{:S(2)}) async-start(), calls=%async_computation.12 | async-start | bytes 10485760 | tf_op jit(solution)/shard_map/reduce_scatter | solution.py:94
  604.4 13.2 %collective-permute-start.44 = (bf16[128,2048]{1,0:T(8,128)(2,1)S(1)}, bf16[128,2048]{1,0:T(8,128)(2,1)S(1)}, u32[]{:S(2)}, u32[]{:S(2)}) collective-permute-start(bf16[128,2048]{1,0:T(8,128)(2,1)S(1)} %get-tuple-element.48), channel_id=1, source_target_pairs={{0,1},{1,0},{2,3},{3,2},{4,5},{5,4},{6,7},{7,6},{8,9},{9,8},{10,11... | collective-permute-start | bytes 1572872 | tf_op jit(solution)/shard_map/ppermute | solution.py:46
  605.5 12.8 %collective-permute-start.46 = (bf16[128,2048]{1,0:T(8,128)(2,1)S(1)}, bf16[128,2048]{1,0:T(8,128)(2,1)S(1)}, u32[]{:S(2)}, u32[]{:S(2)}) collective-permute-start(bf16[128,2048]{1,0:T(8,128)(2,1)S(1)} %get-tuple-element.47), channel_id=1, source_target_pairs={{0,16},{8,24},{16,0},{24,8},{1,17},{9,25},{17,1},{25,9},{2,18},{10... | collective-permute-start | bytes 1572872 | tf_op jit(solution)/shard_map/ppermute | solution.py:42
  619.8 33.3 %collective-permute-start.45 = (bf16[256,2048]{1,0:T(8,128)(2,1)}, bf16[256,2048]{1,0:T(8,128)(2,1)S(1)}, u32[]{:S(2)}, u32[]{:S(2)}) collective-permute-start(bf16[256,2048]{1,0:T(8,128)(2,1)} %pad_maximum_fusion.8), channel_id=1, source_target_pairs={{0,16},{8,24},{16,0},{24,8},{1,17},{9,25},{17,1},{25,9},{2,18},{10... | collective-permute-start | bytes 3145736 | tf_op jit(solution)/shard_map/ppermute | solution.py:42
  621.3 32.1 %collective-permute-start.47 = (bf16[256,2048]{1,0:T(8,128)(2,1)}, bf16[256,2048]{1,0:T(8,128)(2,1)S(1)}, u32[]{:S(2)}, u32[]{:S(2)}) collective-permute-start(bf16[256,2048]{1,0:T(8,128)(2,1)} %pad_maximum_fusion.9), channel_id=1, source_target_pairs={{0,1},{1,0},{2,3},{3,2},{4,5},{5,4},{6,7},{7,6},{8,9},{9,8},{10,11... | collective-permute-start | bytes 3145736 | tf_op jit(solution)/shard_map/ppermute | solution.py:46
  622.4 213.8 %collective-permute-start.49 = (bf16[256,2048]{1,0:T(8,128)(2,1)}, bf16[256,2048]{1,0:T(8,128)(2,1)}, u32[]{:S(2)}, u32[]{:S(2)}) collective-permute-start(bf16[256,2048]{1,0:T(8,128)(2,1)} %reduce-scatter.8.cloned.1.call-done), channel_id=1, source_target_pairs={{0,0},{1,4},{2,8},{3,12},{4,16},{5,20},{6,24},{7,28},{8,1},{9,5},{... | collective-permute-start | bytes 3145736 | tf_op jit(solution)/shard_map/ppermute | solution.py:624
  628.5 62.2 %all-to-all-start.3 = ((bf16[8,64,384]{2,1,0:T(8,128)(2,1)}), bf16[8,64,384]{2,1,0:T(8,128)(2,1)S(1)}, u32[]{:S(2)}, u32[]{:S(2)}) async-start(bf16[8,64,384]{2,1,0:T(8,128)(2,1)} %bitcast.23), calls=%async_computation.4 | async-start | bytes 786432 | tf_op jit(solution)/shard_map/all_to_all | solution.py:612
  637.7 201.3 %collective-permute-start.48 = (bf16[64,2048]{1,0:T(8,128)(2,1)}, bf16[64,2048]{1,0:T(8,128)(2,1)}, u32[]{:S(2)}, u32[]{:S(2)}) collective-permute-start(bf16[64,2048]{1,0:T(8,128)(2,1)} %reshape.201), channel_id=1, source_target_pairs={{0,0},{1,4},{2,1},{3,5},{4,2},{5,6},{6,3},{7,7},{8,8},{9,12},{10,9... | collective-permute-start | bytes 786440 | tf_op jit(solution)/shard_map/ppermute | solution.py:624
  813.8 47.5 %all-to-all-start.4 = ((bf16[8,64,2048]{2,1,0:T(8,128)(2,1)}), bf16[8,64,2048]{2,1,0:T(8,128)(2,1)}, u32[]{:S(2)}, u32[]{:S(2)}) async-start(bf16[8,64,2048]{2,1,0:T(8,128)(2,1)} %bitcast.83), calls=%async_computation.6 | async-start | bytes 4194304 | tf_op jit(solution)/shard_map/all_to_all | solution.py:612
  (54 other events, 940.5 us)
Sparse Core Ops, SparseCore 0:
  27.6 52.9 all-gather.3
  84.7 152.3 all-gather.5
  239.2 79.2 all-gather.7
  411.1 80.8 reduce-scatter.7
  558.3 51.6 reduce-scatter.3
  612.4 201.3 reduce-scatter.5

commit v3 on v2

--- a/solution.py
+++ b/solution.py
@@ -46,28 +46,44 @@
     return lax.ppermute(value, "fsdp", [(i, i ^ 1) for i in range(lax.axis_size("fsdp"))])
 
 
-def gather_plane(own):
+def after(value, *others):
+    return lax.optimization_barrier((value, *others))[0]
+
+
+def gather_plane(own, *others, x_part=None):
     half = own.shape[0] // 2
-    x_part = swap_x(own)
+    x_part = swap_x(own) if x_part is None else x_part
     y_part = swap_y(own)
     core = swap_core(own)
+    x_part, y_part = lax.optimization_barrier((x_part, y_part, *others))[:2]
     xy_up = swap_y(x_part[:half])
     xy_low = swap_x(y_part[half:])
     others = jnp.concatenate([x_part, y_part, xy_up, xy_low])
-    return own, others, core, swap_core(others)
-
-
-def scatter_plane(make):
+    return y_part, (own, others, core, swap_core(others))
+
+
+def halve_core(make):
     sent = swap_core(make(1).astype(BF16))
-    mine = (make(0) + sent.astype(F32)).astype(BF16)
+    return (make(0) + sent.astype(F32)).astype(BF16)
+
+
+def fold_corner(mine):
     rows = mine.shape[0] // 4
     half = rows // 2
-    own, x_part, y_part, xy_part = (mine[i * rows : (i + 1) * rows].astype(F32) for i in range(4))
-    from_x = swap_x(mine[3 * rows : 3 * rows + half]).astype(F32)
-    from_y = swap_y(mine[3 * rows + half :]).astype(F32)
-    x_sum = jnp.concatenate([x_part[:half], x_part[half:] + from_y])
-    y_sum = jnp.concatenate([y_part[:half] + from_x, y_part[half:]])
-    return own + swap_x(x_sum.astype(BF16)).astype(F32) + swap_y(y_sum.astype(BF16)).astype(F32)
+    own, x_part, y_part, corner = (mine[i * rows : (i + 1) * rows] for i in range(4))
+    from_x = swap_x(corner[:half]).astype(F32)
+    from_y = swap_y(corner[half:]).astype(F32)
+    x_sum = jnp.concatenate([x_part[:half], (x_part[half:].astype(F32) + from_y).astype(BF16)])
+    y_sum = jnp.concatenate([(y_part[:half].astype(F32) + from_x).astype(BF16), y_part[half:]])
+    return own, x_sum, y_sum
+
+
+def fold_sides(own, x_sum, y_sum):
+    return own.astype(F32) + swap_x(x_sum).astype(F32) + swap_y(y_sum).astype(F32)
+
+
+def scatter_plane(make):
+    return fold_sides(*fold_corner(halve_core(make)))
 
 
 def planes():
@@ -346,21 +362,22 @@
     return specs, first
 
 
-def on_pieces(counts, refs, body):
-    step, first = pl.program_id(0), 0
-    for count, ref in zip(counts, refs):
-        pl.when((step >= first) & (step < first + count))(functools.partial(body, ref))
-        first += count
-
-
 def pieces_call(name, body, pieces, fixed, by_rows, outs, flops):
-    specs, blocks = piece_specs(pieces)
-    rows = pieces[0].shape[0]
-    counts = [piece.shape[0] // rows for piece in pieces]
-    n_pieces = len(pieces)
+    specs, blocks = piece_specs(pieces[0])
+    specs = specs * len(pieces)
+    rows = pieces[0][0].shape[0]
+    counts = [piece.shape[0] // rows for piece in pieces[0]]
+    n_pieces = len(specs)
+    pieces = [piece for group in pieces for piece in group]
 
     def kernel(*refs):
-        on_pieces(counts, refs[:n_pieces], lambda ref: body(ref, *refs[n_pieces:]))
+        step, first = pl.program_id(0), 0
+        for at, count in enumerate(counts):
+            chosen = refs[at : n_pieces : len(counts)]
+            pl.when((step >= first) & (step < first + count))(
+                functools.partial(body, *chosen, *refs[n_pieces:])
+            )
+            first += count
 
     def row_spec(width):
         return pl.BlockSpec((rows, width), lambda i: (i, 0))
@@ -396,7 +413,7 @@
     return pieces_call(
         "project",
         body,
-        pieces,
+        [pieces],
         [(gain, (1, width)), (weight, (width, cols))],
         [],
         [(width, BF16), (cols, F32)],
@@ -404,12 +421,13 @@
     )
 
 
-def feed(pieces, w_both):
+def feed(pieces, cot_pieces, w_both):
     width, cols = w_both.shape[0], w_both.shape[1] // 2
 
-    def body(h_ref, w_ref, hn_ref, mid_ref, by_gate_ref, by_up_ref):
+    def body(h_ref, c_ref, w_ref, hn_ref, cot_ref, mid_ref, by_gate_ref, by_up_ref):
         hn = h_ref[...]
         hn_ref[...] = hn
+        cot_ref[...] = c_ref[...]
         chunk = min(256, cols)
         for at in range(0, cols, chunk):
             gate = dot(hn, w_ref[:, at : at + chunk])
@@ -424,37 +442,53 @@
     return pieces_call(
         "feed",
         body,
-        pieces,
+        [pieces, cot_pieces],
         [(w_both, w_both.shape)],
         [],
-        [(width, BF16)] + [(cols, BF16)] * 3,
+        [(width, BF16)] * 2 + [(cols, BF16)] * 3,
         4 * rows * width * cols,
     )
 
 
-def feed_back(pieces, w_down, by_gate, by_up):
+def feed_back(cot, w_down, by_gate, by_up, places):
     cols, width = w_down.shape
-
-    def body(c_ref, w_ref, by_gate_ref, by_up_ref, cot_ref, grad_ref):
+    chunk = cols // places.shape[0]
+
+    def body(places_ref, c_ref, w_ref, by_gate_ref, by_up_ref, grad_ref):
         cot = c_ref[...]
-        cot_ref[...] = cot
-        chunk = min(256, cols)
-        for at in range(0, cols, chunk):
-            grad = dot_nt(cot, w_ref[at : at + chunk, :])
+        for q in range(places.shape[0]):
+            at = q * chunk
+            grad = dot_nt(cot, w_ref[pl.ds(pl.multiple_of(places_ref[q] * chunk, chunk), chunk), :])
             here = slice(at, at + chunk)
             grad_ref[:, here] = (grad * by_gate_ref[:, here].astype(F32)).astype(BF16)
             grad_ref[:, cols + at : cols + at + chunk] = (grad * by_up_ref[:, here].astype(F32)).astype(BF16)
 
-    rows = sum(p.shape[0] for p in pieces)
-    return pieces_call(
-        "feed_back",
+    rows = cot.shape[0]
+    block = rows // 8
+
+    def row_spec(width):
+        return pl.BlockSpec((block, width), lambda i: (i, 0))
+
+    return pl.pallas_call(
         body,
-        pieces,
-        [(w_down, w_down.shape)],
-        [by_gate, by_up],
-        [(width, BF16), (2 * cols, BF16)],
-        2 * rows * width * cols,
-    )
+        out_shape=jax.ShapeDtypeStruct((rows, 2 * cols), BF16),
+        grid=(rows // block,),
+        in_specs=[
+            pl.BlockSpec(memory_space=pltpu.SMEM),
+            row_spec(width),
+            pl.BlockSpec(w_down.shape, lambda i: (0, 0), pipeline_mode=pl.Buffered(1)),
+            row_spec(cols),
+            row_spec(cols),
+        ],
+        out_specs=row_spec(2 * cols),
+        compiler_params=pltpu.CompilerParams(vmem_limit_bytes=VMEM_BYTES),
+        cost_estimate=pl.CostEstimate(
+            flops=2 * rows * width * cols,
+            bytes_accessed=2 * (rows * width + 4 * rows * cols + cols * width),
+            transcendentals=0,
+        ),
+        name="feed_back",
+    )(places, cot, w_down, by_gate, by_up)
 
 
 def out_back(pieces, w_o):
@@ -469,12 +503,103 @@
     return pieces_call(
         "out_back",
         body,
-        pieces,
+        [pieces],
         [(w_o, w_o.shape)],
         [],
         [(width, BF16), (cols, BF16)],
         2 * rows * width * cols,
     )
+
+
+def row_terms(left, right, n_blocks, n_planes):
+    tokens, width = left.shape
+    cols = right.shape[1]
+    rows = width // n_blocks
+    part = rows // n_planes
+    chunk = min(512, cols)
+
+    def kernel(left_ref, right_ref, out_ref):
+        for at in range(0, cols, chunk):
+            here = slice(at, min(at + chunk, cols))
+            terms = dot_tn(left_ref[...], right_ref[:, here]).astype(BF16)
+            out_ref[:, 0, :, here] = terms.reshape(n_planes, part, terms.shape[1])
+
+    return pl.pallas_call(
+        kernel,
+        out_shape=jax.ShapeDtypeStruct((n_planes, n_blocks, part, cols), BF16),
+        grid=(n_blocks,),
+        in_specs=[
+            pl.BlockSpec((tokens, rows), lambda i: (0, i)),
+            pl.BlockSpec((tokens, cols), lambda i: (0, 0), pipeline_mode=pl.Buffered(1)),
+        ],
+        out_specs=pl.BlockSpec((n_planes, 1, part, cols), lambda i: (0, i, 0, 0)),
+        compiler_params=pltpu.CompilerParams(vmem_limit_bytes=VMEM_BYTES),
+        cost_estimate=pl.CostEstimate(
+            flops=2 * tokens * width * cols,
+            bytes_accessed=2 * (left.size + right.size + width * cols),
+            transcendentals=0,
+        ),
+        name="row_terms",
+    )(left, right).reshape(width, cols)
+
+
+def take_columns(weights, firsts, block):
+    rows = weights[0].shape[0]
+    n_arrays, n_blocks = firsts.shape
+    width = len(weights) * n_blocks * block
+
+    def kernel(firsts_ref, *refs):
+        sources, targets, sems = refs[: len(weights)], refs[len(weights) : -1], refs[-1]
+        copies = []
+        for side, target in enumerate(targets):
+            for k, source in enumerate(sources):
+                for at in range(n_blocks):
+                    first = pl.multiple_of(firsts_ref[side, at], block)
+                    copies.append(
+                        pltpu.make_async_copy(
+                            source.at[:, pl.ds(first, block)],
+                            target.at[:, pl.ds((k * n_blocks + at) * block, block)],
+                            sems.at[len(copies)],
+                        )
+                    )
+        for copy in copies:
+            copy.start()
+        for copy in copies:
+            copy.wait()
+
+    return pl.pallas_call(
+        kernel,
+        out_shape=(jax.ShapeDtypeStruct((rows, width), BF16),) * n_arrays,
+        in_specs=[pl.BlockSpec(memory_space=pltpu.SMEM)]
+        + [pl.BlockSpec(memory_space=pl.ANY)] * len(weights),
+        out_specs=(pl.BlockSpec(memory_space=pltpu.VMEM),) * n_arrays,
+        scratch_shapes=[pltpu.SemaphoreType.DMA((n_arrays * len(weights) * n_blocks,))],
+        compiler_params=pltpu.CompilerParams(vmem_limit_bytes=VMEM_BYTES),
+        cost_estimate=pl.CostEstimate(
+            flops=0, bytes_accessed=4 * n_arrays * rows * width, transcendentals=0
+        ),
+        name="take_columns",
+    )(firsts, *weights)
+
+
+def deal(spread, places, block):
+    _, rows, cols = spread.shape
+    width = len(places) * block
+
+    def kernel(in_ref, gate_ref, up_ref):
+        for at, (member, own) in enumerate(places):
+            here = slice(at * block, (at + 1) * block)
+            gate_ref[:, here] = in_ref[member, :, own * block : (own + 1) * block].astype(F32)
+            first = cols // 2 + own * block
+            up_ref[:, here] = in_ref[member, :, first : first + block].astype(F32)
+
+    return pl.pallas_call(
+        kernel,
+        out_shape=(jax.ShapeDtypeStruct((rows, width), F32),) * 2,
+        compiler_params=pltpu.CompilerParams(vmem_limit_bytes=VMEM_BYTES),
+        cost_estimate=pl.CostEstimate(flops=0, bytes_accessed=10 * rows * width, transcendentals=0),
+        name="deal",
+    )(spread)
 
 
 def shards(
@@ -497,23 +622,6 @@
 
     x_own = tokens.reshape(part_len, width)
     cot_own = cotangent.reshape(part_len, width)
-    x_pieces = gather_plane(x_own)
-
-    gains = jnp.stack([attn_gain, mlp_gain])
-    gains = lax.all_to_all(
-        jnp.broadcast_to(gains, (n_fsdp, *gains.shape)), "fsdp", split_axis=0, concat_axis=0, tiled=True
-    )
-    gains = gains.transpose(1, 0, 2).reshape(2, width).astype(F32)
-    gain_one, gain_two = gains[:1], gains[1:]
-    places = lax.all_to_all(
-        jnp.broadcast_to(positions.reshape(part_len), (n_seq, part_len)),
-        "seq",
-        split_axis=0,
-        concat_axis=0,
-        tiled=True,
-    ).reshape(length)
-    places = jnp.concatenate([places, swap_y(places)])
-
     def cols_qkv(y_of):
         team = s * NY + y_of
         return jnp.concatenate(
@@ -525,19 +633,42 @@
             axis=1,
         )
 
-    def cols_ff(y_of):
-        return jnp.concatenate(
-            [
-                lax.dynamic_slice_in_dim(weight, ((at * NY + y_of) * n_seq + s) * ff_block, ff_block, 1)
-                for weight in (w_gate, w_up)
-                for at in range(n_z)
-            ],
-            axis=1,
-        )
-
-    def both_rows(cols_of):
-        ours = cols_of(y)
-        others = swap_y(cols_of(1 - y))
+    lines = n_z // n_seq
+
+    def hidden_plane(q, s_of):
+        return lax.rem(q % n_seq - s_of + n_seq, n_seq) * lines + q // n_seq
+
+    def cols_ff(w_gate, w_up):
+        firsts = [
+            [(n_team * hidden_plane(q, s) + NY * (q % n_seq) + y_of) * ff_block for q in range(n_z)]
+            for y_of in (y, 1 - y)
+        ]
+        if ff_block % 128 == 0:
+            firsts = jnp.stack([jnp.stack(row) for row in firsts]).astype(jnp.int32)
+            return take_columns((w_gate, w_up), firsts, ff_block)
+        return [
+            jnp.concatenate(
+                [lax.dynamic_slice_in_dim(w, first, ff_block, 1) for w in (w_gate, w_up) for first in row], axis=1
+            )
+            for row in firsts
+        ]
+
+    def rows_down(w_down):
+        turn = lax.rem(f // NY // lines + s, n_seq)
+        blocks = w_down.reshape(n_seq, ff_block, width)
+        mine = lax.dynamic_index_in_dim(blocks, lax.rem(NY * turn + y, n_seq), 0, keepdims=False)
+        theirs = lax.dynamic_index_in_dim(blocks, lax.rem(NY * turn + 1 - y, n_seq), 0, keepdims=False)
+        pairs = []
+        for si in range(n_seq):
+            for zi in range(n_z):
+                holder = NY * ((zi // lines + si) % n_seq) // n_seq
+                base = si * n_fsdp + zi * NY
+                pairs.append((base + holder, base + 1 - holder))
+        sent = lax.ppermute(theirs, ("seq", "fsdp"), pairs)
+        return jnp.where(NY * turn // n_seq == y, mine, sent)
+
+    def both_rows(ours, theirs):
+        others = swap_y(theirs)
         rows = jnp.where(y == 0, jnp.stack([ours, others]), jnp.stack([others, ours]))
         return rows.reshape(NY * w_rows, -1)
 
@@ -553,66 +684,100 @@
         return lax.ppermute(mine, ("seq", "fsdp"), pairs)
 
     head_cols = q_cols + 2 * kv_cols
-    w_heads = gather_z(
-        jnp.concatenate([both_rows(cols_qkv), rows_o().reshape(NY * w_rows, -1)], axis=1)
-    )
-    wqkv = w_heads[:, :head_cols]
-    wo = w_heads[:, head_cols:].reshape(q_cols, width)
-    w_both = gather_z(both_rows(cols_ff))
-    wd = gather_z(lax.dynamic_slice_in_dim(w_down, s * ff_block, ff_block, 0))
-    cot_pieces = gather_plane(cot_own)
+    side = NY * n_seq * part_len // 2
+    out_rows = width // n_all
+    member = s.astype(jnp.int32).reshape(1)
+    flag = positions[0, 0] >= 0
+
+    def stage(work, *given):
+        kinds = jax.eval_shape(work, *given)
+        return lax.cond(
+            flag, work, lambda *_: jax.tree.map(lambda k: jnp.zeros(k.shape, k.dtype), kinds), *given
+        )
+
+    def halves(values, weight, over_rows):
+        product = dot_cols if over_rows else dot
+        return lambda core: product(values[core * side : (core + 1) * side], weight)
 
     def normed(rows):
         rows = rows.astype(F32)
         inv = lax.rsqrt(jnp.mean(rows * rows, axis=-1, keepdims=True) + EPSILON)
         return rows * inv, inv
 
-    z_one, inv_one = normed(x_own)
-    freqs = jnp.exp(jnp.arange(HD // 2).astype(F32) * (-2.0 * math.log(ROPE_BASE) / HD))
-    angles = places.astype(F32)[:, None] * freqs
-    cosine, sine = jnp.cos(angles), jnp.sin(angles)
-    cosine = jnp.tile(cosine, (1, 4))
-    sine = jnp.concatenate([-sine, sine, -sine, sine], axis=1)
-    member = s.astype(jnp.int32).reshape(1)
-
-    xn, qkv = project(x_pieces, gain_one, w_heads, head_cols)
-    attn_rows, log_sums = attend(member, qkv, cosine, sine, q_cols, n_seq)
-    side = attn_rows.shape[0] // 2
-    residual = x_own.astype(F32) + scatter_plane(
-        lambda core: dot(attn_rows[core * side : (core + 1) * side], wo)
-    )
-
-    z_two, inv_two = normed(residual)
-    hn, mid, by_gate, by_up = feed(gather_plane((z_two * gain_two).astype(BF16)), w_both)
-    branch = scatter_plane(lambda core: dot(mid[core * side : (core + 1) * side], wd))
-    output = (residual + branch).astype(BF16).reshape(tokens.shape)
-
-    cot_all, grad_both = feed_back(cot_pieces, wd, by_gate, by_up)
-    grad_hn = scatter_plane(lambda core: dot_cols(grad_both[core * side : (core + 1) * side], w_both))
-    grad_z2 = grad_hn * gain_two
-    grad_res = cot_own.astype(F32) + inv_two * (
-        grad_z2 - z_two * jnp.mean(grad_z2 * z_two, axis=-1, keepdims=True)
-    )
-    da, d_out = out_back(gather_plane(grad_res.astype(BF16)), wo)
-    grad_qkv = attend_back(member, qkv, d_out, log_sums, cosine, sine, n_seq)
-    grad_xn = scatter_plane(lambda core: dot_cols(grad_qkv[core * side : (core + 1) * side], wqkv))
-    grad_z1 = grad_xn * gain_one
-    grad_x = grad_res + inv_one * (
-        grad_z1 - z_one * jnp.mean(grad_z1 * z_one, axis=-1, keepdims=True)
-    )
-    tokens_grad = grad_x.astype(BF16).reshape(tokens.shape)
-
-    out_rows = width // n_all
-
-    def by_plane(grad):
-        blocks = grad.astype(BF16).reshape(n_seq, n_z, NY * out_rows, grad.shape[1])
-        return blocks.transpose(1, 0, 2, 3).reshape(grad.shape)
-
-    def to_team(summed):
-        spread = lax.all_to_all(
-            summed, ("seq", "fsdp"), split_axis=0, concat_axis=0, tiled=True, axis_index_groups=plane_groups()
+    def with_gains(rows, gains):
+        extra = jnp.pad(gains, ((0, 16 - gains.shape[0]), (0, rows.shape[1] - gains.shape[1])))
+        return jnp.concatenate([rows, extra])
+
+    gains_own = jnp.stack([attn_gain, mlp_gain])
+    mine, others = with_gains(cols_qkv(y), gains_own), with_gains(cols_qkv(1 - y), gains_own)
+    others = swap_y(others)
+    first = jnp.where(y == 0, mine, others)
+    second = jnp.where(y == 0, others, mine)
+    gains_both = jnp.concatenate([first[w_rows : w_rows + 2, :w_rows], second[w_rows : w_rows + 2, :w_rows]])
+    head_rows = jnp.concatenate(
+        [jnp.concatenate([first[:w_rows], second[:w_rows]]), rows_o().reshape(NY * w_rows, -1)], axis=1
+    )
+    w_heads = gather_z(with_gains(head_rows, gains_both)).reshape(n_z, -1, head_rows.shape[1])
+
+    def first_moves(x_own, w_gate, w_up, positions, ready):
+        ours, theirs = cols_ff(w_gate, w_up)
+        both = both_rows(ours, theirs)
+        places = lax.all_to_all(
+            jnp.broadcast_to(positions.reshape(part_len), (n_seq, part_len)),
+            "seq",
+            split_axis=0,
+            concat_axis=0,
+            tiled=True,
+        ).reshape(length)
+        x_pieces = gather_plane(after(x_own, theirs), places)[1]
+        places = jnp.concatenate([places, swap_y(places)])
+        freqs = jnp.exp(jnp.arange(HD // 2).astype(F32) * (-2.0 * math.log(ROPE_BASE) / HD))
+        angles = places.astype(F32)[:, None] * freqs
+        cosine, sine = jnp.cos(angles), jnp.sin(angles)
+        cosine = jnp.tile(cosine, (1, 4))
+        sine = jnp.concatenate([-sine, sine, -sine, sine], axis=1)
+        return both, x_pieces, cosine, sine
+
+    both, x_pieces, cosine, sine = stage(first_moves, x_own, w_gate, w_up, positions, head_rows)
+    w_both = gather_z(after(both, w_heads))
+
+    def attention(x_own, x_pieces, cot_own, w_heads, w_down, cosine, sine):
+        gains = w_heads[:, NY * w_rows : NY * w_rows + 4, :w_rows].reshape(n_z, NY, 2, w_rows)
+        gains = gains.transpose(2, 0, 1, 3).reshape(2, width).astype(F32)
+        gain_one, gain_two = gains[:1], gains[1:]
+        wqkv = w_heads[:, : NY * w_rows, :head_cols].reshape(width, head_cols)
+        wo = w_heads[:, : NY * w_rows, head_cols:].reshape(q_cols, width)
+        cot_hop, cot_pieces = gather_plane(cot_own)
+        xn, qkv = project(x_pieces, gain_one, wqkv, head_cols)
+        attn_rows, log_sums = attend(member, after(qkv, cot_hop), cosine, sine, q_cols, n_seq)
+        residual = x_own.astype(F32) + scatter_plane(halves(attn_rows, wo, False))
+        hn_own = (normed(residual)[0] * gain_two).astype(BF16)
+        hn_pieces = gather_plane(after(hn_own, *cot_pieces))[1]
+        return xn, qkv, attn_rows, log_sums, wqkv, wo, gain_one, gain_two, residual, rows_down(w_down), hn_pieces, cot_pieces
+
+    xn, qkv, attn_rows, log_sums, wqkv, wo, gain_one, gain_two, residual, down_own, hn_pieces, cot_pieces = stage(
+        attention, x_own, x_pieces, cot_own, w_heads, w_down, cosine, sine
+    )
+    wd = gather_z(down_own)
+    down_places = jnp.stack([hidden_plane(q, s) for q in range(n_z)]).astype(jnp.int32)
+
+    hn, cot_all, mid, by_gate, by_up = feed(hn_pieces, cot_pieces, w_both)
+    down_summed = scatter_z(dot_rows(mid, cot_all).astype(BF16))
+
+    def feed_backward(cot_all, cot_own, wd, by_gate, by_up, hn, w_both, residual, gain_two):
+        z_two, inv_two = normed(residual)
+        grad_both = feed_back(cot_all, wd, by_gate, by_up, down_places)
+        grad_hn = scatter_plane(halves(grad_both, w_both, True))
+        grad_z2 = grad_hn * gain_two
+        grad_res = cot_own.astype(F32) + inv_two * (
+            grad_z2 - z_two * jnp.mean(grad_z2 * z_two, axis=-1, keepdims=True)
         )
-        return spread.reshape(n_team, out_rows, -1).astype(F32)
+        return row_terms(hn, grad_both, n_seq, n_z), grad_res, jnp.sum(grad_hn * z_two, axis=0)
+
+    both_terms, grad_res, gain_two_terms = stage(
+        feed_backward, cot_all, cot_own, wd, by_gate, by_up, hn, w_both, residual, gain_two
+    )
+    both_summed = scatter_z(both_terms)
 
     def to_owner(summed, block_of):
         pairs = [
@@ -623,33 +788,71 @@
         ]
         return lax.ppermute(summed, ("seq", "fsdp"), pairs).astype(F32)
 
-    w_down_grad = to_owner(
-        scatter_z(dot_rows(mid, cot_all).astype(BF16)),
-        lambda si, zi, yi: (zi * NY + yi) * n_seq + si,
-    )
-    spread = to_team(scatter_z(by_plane(dot_rows(hn, grad_both))))
-    spread = spread.reshape(n_seq, NY, out_rows, 2, n_z, ff_block).transpose(3, 2, 4, 1, 0, 5)
-    w_gate_grad = spread[0].reshape(out_rows, ff_width)
-    w_up_grad = spread[1].reshape(out_rows, ff_width)
-
-    summed = scatter_z(
-        jnp.concatenate(
+    def attention_backward(grad_res, wo, wqkv, xn, qkv, cosine, sine, attn_rows, log_sums, x_own, gain_one):
+        da, d_out = out_back(gather_plane(grad_res.astype(BF16))[1], wo)
+        grad_qkv = attend_back(member, qkv, d_out, log_sums, cosine, sine, n_seq)
+        z_one, inv_one = normed(x_own)
+        grad_xn = scatter_plane(halves(grad_qkv, wqkv, True))
+        grad_z1 = grad_xn * gain_one
+        grad_x = grad_res + inv_one * (
+            grad_z1 - z_one * jnp.mean(grad_z1 * z_one, axis=-1, keepdims=True)
+        )
+        head_terms = jnp.concatenate(
             [
-                by_plane(dot_rows(xn, grad_qkv)),
-                dot_rows(attn_rows, da).astype(BF16).reshape(w_q.shape[1], -1),
+                row_terms(xn, grad_qkv, n_seq, n_z),
+                dot_rows(attn_rows, da).astype(BF16).reshape(w_rows * n_fsdp, -1),
             ],
             axis=1,
         )
-    )
+        return head_terms, grad_x.astype(BF16), jnp.sum(grad_xn * z_one, axis=0)
+
+    head_terms, grad_x, gain_one_terms = stage(
+        attention_backward,
+        *(after(grad_res, down_summed), wo, wqkv, xn, qkv, cosine, sine, attn_rows, log_sums, x_own, gain_one),
+    )
+    tokens_grad = grad_x.reshape(tokens.shape)
+    head_summed = scatter_z(after(head_terms, both_summed))
+
+    def to_team(summed):
+        spread = lax.all_to_all(
+            summed, ("seq", "fsdp"), split_axis=0, concat_axis=0, tiled=True, axis_index_groups=plane_groups()
+        )
+        return spread.reshape(n_team, out_rows, -1)
+
+    places_of = []
+    for block in range(n_all):
+        plane, rest = divmod(block, n_team)
+        turn = rest // NY
+        places_of.append(
+            ((turn - plane // lines) % n_seq * NY + rest % NY, plane % lines * n_seq + turn)
+        )
+
+    def outputs(mid, wd, residual, down_summed, both_summed):
+        spread = to_team(both_summed)
+        blocks = [
+            lax.dynamic_slice_in_dim(wd, down_places[q] * ff_block, ff_block, 0) for q in range(n_z)
+        ]
+        branch = scatter_plane(halves(mid, jnp.concatenate(blocks), False))
+        output = (residual + branch).astype(BF16)
+        w_down_grad = to_owner(
+            down_summed, lambda si, zi, yi: (zi - si) % n_seq * n_fsdp + zi * NY + yi
+        )
+        return output, w_down_grad, *deal(spread, places_of, ff_block)
+
+    output, w_down_grad, w_gate_grad, w_up_grad = stage(
+        outputs, mid, wd, residual, down_summed, both_summed
+    )
+    output = output.reshape(tokens.shape)
+
     w_o_grad = to_owner(
-        summed[:, head_cols:].reshape(-1, width), lambda si, zi, yi: (si * NY + yi) * n_z + zi
-    )
-    spread = to_team(summed[:, :head_cols]).transpose(1, 0, 2)
+        head_summed[:, head_cols:].reshape(-1, width), lambda si, zi, yi: (si * NY + yi) * n_z + zi
+    )
+    spread = to_team(head_summed[:, :head_cols]).astype(F32).transpose(1, 0, 2)
     w_q_grad = spread[..., :q_cols].reshape(out_rows, q_width)
     w_k_grad = spread[..., q_cols : q_cols + kv_cols].reshape(out_rows, kv_width)
     w_v_grad = spread[..., q_cols + kv_cols :].reshape(out_rows, kv_width)
 
-    gain_terms = jnp.stack([jnp.sum(grad_xn * z_one, axis=0), jnp.sum(grad_hn * z_two, axis=0)])
+    gain_terms = after(jnp.stack([gain_one_terms, gain_two_terms]), head_summed)
     gain_terms = gain_terms.reshape(2, n_all, out_rows).transpose(1, 0, 2)
     gain_sums = jnp.sum(
         lax.all_to_all(gain_terms, ("seq", "fsdp"), split_axis=0, concat_axis=0, tiled=True), axis=0

time: 899 us -> 781 us (0.87)
  blocking collectives: 69.7 us -> 25 us
  Pallas kernels: 123 us -> 163 us
  waiting for transfers between devices: 332 us -> 293 us
  matrix products: 97.2 us -> 61.8 us
  local copies, waits for them, and re-layouts: 92 us -> 68 us
  starting transfers between devices: 112 us -> 96 us
    reduce_scatter x3, waiting for transfers between devices: 53.5 us -> 0.04 us  [scatter_z(): lax.psum_scatter(terms, 'fsdp', scatter_dimension=0, tiled=True, axis_ind...]
    pallas_call x0 -> x5, Pallas kernels: none -> 53 us  [the longest x2 31 us: row_terms(): pl.pallas_call(kernel, out_shape=jax.ShapeDtypeStruct((n_planes, n_blocks...]
    all_gather x3, waiting for transfers between devices: 0.5 us -> 48.2 us  [gather_z(): lax.all_gather(own, 'fsdp', axis=0, tiled=True, axis_index_groups=z_group...]
    ppermute x16, waiting for transfers between devices: 135 us -> 87.4 us  [swap_x(): lax.ppermute(value, 'seq', [(i, i ^ 2) for i in range(lax.axis_size('seq'...]
    all_to_all x1, blocking collectives: 69.7 us -> 25 us  [first_moves(): lax.all_to_all(jnp.broadcast_to(positions.reshape(part_len), (n_seq, part...]
    dot_general x4 -> x2, matrix products: 46.4 us -> 15.9 us  [dot_rows(): lax.dot_general(left, right, (((0,), (0,)), ((), ())), preferred_element_...]
    all_to_all x2, waiting for transfers between devices: 40.6 us -> 16 us  [to_team(): lax.all_to_all(summed, ('seq', 'fsdp'), split_axis=0, concat_axis=0, tile...]
    unnamed x108 -> x17, local copies, waits for them, and re-layouts: 30 us -> 5.44 us
  transfers between devices with their start and end apart: 60 -> 60, of which waited for: 33 -> 35; matrix products, arithmetic and copies ran while one was open for 23% -> 21% of each run, Pallas kernels for 14% -> 21%
where the time goes in v3:
time: 781 us; the launch traced here: 772 us
  waiting for transfers between devices  293 us (38%)
  Pallas kernels  163 us (21%)
  starting transfers between devices  96 us (12%)
  local copies, waits for them, and re-layouts  68 us (9%)
  matrix products  61.8 us (8%)
  other arithmetic  48.1 us (6%)
  blocking collectives  25 us (3%)
  between operations  15.3 us (2%)
    ppermute x16, waiting for transfers between devices, swap_x(): lax.ppermute(value, 'seq', [(i, i ^ 2) for i in range(lax.axis_size('seq'...  87.4 us
    ppermute x19, waiting for transfers between devices, swap_y(): lax.ppermute(value, 'fsdp', [(i, i ^ 1) for i in range(lax.axis_size('fsd...  85.5 us
    pallas_call x3, Pallas kernels, pieces_call(): pl.pallas_call(kernel, out_shape=tuple((jax.ShapeDtypeStruct((blocks * ro...  52.5 us
    all_gather x3, waiting for transfers between devices, gather_z(): lax.all_gather(own, 'fsdp', axis=0, tiled=True, axis_index_groups=z_group...  48.2 us
    pallas_call x1, Pallas kernels, attend_back(): pl.pallas_call(functools.partial(attend_back_kernel, n_parts), out_shape=...  34.3 us
    pallas_call x2, Pallas kernels, row_terms(): pl.pallas_call(kernel, out_shape=jax.ShapeDtypeStruct((n_planes, n_blocks...  31 us
    dot_general x4, matrix products, dot_cols(): lax.dot_general(left, right, (((1,), (1,)), ((), ())), preferred_element_...  29.8 us
    all_to_all x1, starting transfers between devices, shards(): lax.all_to_all(gain_terms, ('seq', 'fsdp'), split_axis=0, concat_axis=0,...  28.8 us
  transfers between devices with their start and end apart: 60, of which 35 were waited for; matrix products, arithmetic and copies ran while one was open for 21% of the time, Pallas kernels for 21%

profile of v3, /device:TPU:11, one launch (start us, length us, event | category | flops | bytes accessed | tf_op | source)
XLA Modules:
  0.0 772.1 jit_solution(8394978691912720477)
XLA Ops:
  12.3 4.2 collective-permute-start.49
  17.3 10.5 %collective-permute-done.49 = bf16[64,2048]{1,0:T(8,128)(2,1)S(1)} collective-permute-done((bf16[64,2048]{1,0:T(8,128)(2,1)S(1)}, bf16[64,2048]{1,0:T(8,128)(2,1)S(1)}, u32[]{:S(2)}, u32[]{:S(2)}) %collective-permute-start.49) | collective-permute-done | bytes 262176 | tf_op jit(solution)/shard_map/ppermute | solution.py:684
  30.1 75.3 %conditional.5 = (bf16[512,2048]{1,0:T(8,128)(2,1)}, bf16[256,2048]{1,0:T(8,128)(2,1)}, bf16[768,2048]{1,0:T(8,128)(2,1)}, bf16[256,2048]{1,0:T(8,128)(2,1)}, bf...) conditional(s32[]{:T(128)} %bitcast.33, () %tuple.69, (s32[]{:T(128)}, s32[]{:T(128)}, ...), branch_computations={%region_0.1_spmd, %region_1.2_spmd} | conditional | flops 4067477 | bytes 56154448 | solution.py:694
  32.9 25.0 %all_to_all.26 = s32[4,1,256]{2,1,0:T(1,128)S(1)} all-to-all(s32[4,1,256]{2,1,0:T(1,128)S(1)} %broadcast_in_dim.0), channel_id=1, replica_groups=mesh['seq'=4,'fsdp'=8] {'seq'}, dimensions={0} | all-to-all | bytes 8192 | tf_op jit(solution)/shard_map/cond/branch_1_fun/all_to_all | solution.py:725
  60.5 10.7 %collective-permute-done.3 = bf16[128,2048]{1,0:T(8,128)(2,1)S(1)} collective-permute-done((bf16[128,2048]{1,0:T(8,128)(2,1)S(1)}, bf16[128,2048]{1,0:T(8,128)(2,1)S(1)}, u32[]{:S(2)}, u32[]{:S(2)}) %collective-permute-start.3) | collective-permute-done | bytes 524320 | tf_op jit(solution)/shard_map/cond/branch_1_fun/ppermute | solution.py:46
  76.8 22.3 %collective-permute-done.7 = s32[1024]{0:T(1024)S(1)} collective-permute-done((s32[1024]{0:T(1024)S(1)}, s32[1024]{0:T(1024)S(1)}, u32[]{:S(2)}, u32[]{:S(2)}) %collective-permute-start.7) | collective-permute-done | bytes 4128 | tf_op jit(solution)/shard_map/cond/branch_1_fun/ppermute | solution.py:46
  105.4 169.2 %conditional.6 = (bf16[2048,2048]{1,0:T(8,128)(2,1)}, f32[2048,384]{1,0:T(8,128)}, bf16[2048,256]{1,0:T(8,128)(2,1)}, f32[2048,128]{1,0:T(8,128)}, bf16[2048,384...) conditional(s32[]{:T(128)} %bitcast.33, () %tuple.68, ...), branch_computations={%region_2.3_spmd, %region_3.5_spmd} | conditional | flops 9685176320 | bytes 196875824 | solution.py:694
  118.1 14.0 %project.1 = (bf16[2048,2048]{1,0:T(8,128)(2,1)}, f32[2048,384]{1,0:T(8,128)}) custom-call(bf16[256,2048]{1,0:T(8,128)(2,1)} %get-tuple-element.117.refs_0_, bf16[768,2048]{1,0:T(8,128)(2,1)} %get-tuple-element.118.refs_1_, bf16[256,2048]{1,0:T(8,128)(2,1)} %get-tuple-element.119.refs_2_, bf16[768,2048]{1,0:T(8,128)(2,1)} %get-tuple-element.120.refs_3_, ...), custom_call_target="tpu_custom_call" | custom-call | flops 3221225472 | bytes 21504000 | tf_op jit(solution)/shard_map/cond/branch_1_fun/project/pallas_call | solution.py:390
  132.1 23.7 %attend.1 = (bf16[2048,256]{1,0:T(8,128)(2,1)}, f32[2048,128]{1,0:T(8,128)}) custom-call(s32[1]{0:T(128)} %get-tuple-element.124.member, f32[2048,384]{1,0:T(8,128)} %get-tuple-element.127.refs_0_.refs_1_.refs_2_.refs_3_, f32[2048,384]{1,0:T(8,128)} %get-tuple-element.127.refs_0_.refs_1_.refs_2_.refs_3_, ...), custom_call_target="tpu_custom_call" | custom-call | flops 4294967296 | bytes 6291456 | tf_op jit(solution)/shard_map/cond/branch_1_fun/attend/pallas_call | solution.py:296
  178.7 8.1 %collective-permute-done.17 = bf16[128,2048]{1,0:T(8,128)(2,1)S(1)} collective-permute-done((bf16[128,2048]{1,0:T(8,128)(2,1)S(1)}, bf16[128,2048]{1,0:T(8,128)(2,1)S(1)}, u32[]{:S(2)}, u32[]{:S(2)}) %collective-permute-start.17) | collective-permute-done | bytes 524320 | tf_op jit(solution)/shard_map/cond/branch_1_fun/ppermute | solution.py:46
  191.3 20.1 %collective-permute-done.18 = bf16[256,2048]{1,0:T(8,128)(2,1)S(1)} collective-permute-done((bf16[256,2048]{1,0:T(8,128)(2,1)S(1)}, bf16[256,2048]{1,0:T(8,128)(2,1)S(1)}, u32[]{:S(2)}, u32[]{:S(2)}) %collective-permute-start.18) | collective-permute-done | bytes 1048608 | tf_op jit(solution)/shard_map/cond/branch_1_fun/ppermute | solution.py:42
  218.2 22.1 %collective-permute-done.26 = bf16[256,2048]{1,0:T(8,128)(2,1)S(1)} collective-permute-done((bf16[256,2048]{1,0:T(8,128)(2,1)}, bf16[256,2048]{1,0:T(8,128)(2,1)S(1)}, u32[]{:S(2)}, u32[]{:S(2)}) %collective-permute-start.26) | collective-permute-done | bytes 1048608 | tf_op jit(solution)/shard_map/cond/branch_1_fun/ppermute | solution.py:42
  244.0 6.8 collective-permute-done.28
  262.5 9.6 %collective-permute-done.21 = bf16[256,2048]{1,0:T(8,128)(2,1)} collective-permute-done((bf16[256,2048]{1,0:T(8,128)(2,1)S(1)}, bf16[256,2048]{1,0:T(8,128)(2,1)}, u32[]{:S(2)}, u32[]{:S(2)}) %collective-permute-start.21) | collective-permute-done | bytes 1048608 | tf_op jit(solution)/shard_map/cond/branch_1_fun/ppermute | solution.py:667
  274.8 28.1 %feed.1 = (bf16[2048,2048]{1,0:T(8,128)(2,1)}, bf16[2048,2048]{1,0:T(8,128)(2,1)S(1)}, bf16[2048,1024]{1,0:T(8,128)(2,1)S(1)}, bf16[2048,1024]{1,0:T(8,128)(2,1)}, bf16[2048,1024]{1,0:T(8,128)(2,1)}) custom-call(bf16[256,2048]{1,0:T(8,128)(2,1)} %get-tuple-element.239.refs_0_, bf16[768,2048]{1,0:T(8,128)(2,1)} %get-tuple-element.240.refs_1_, ...), custom_call_target="tpu_custom_call" | custom-call | flops 17179869184 | bytes 54525952 | tf_op jit(solution)/shard_map/feed/pallas_call | solution.py:390
  307.5 11.0 %convolution_convert_fusion.3 = bf16[1024,2048]{1,0:T(8,128)(2,1)} fusion(bf16[2048,1024]{1,0:T(8,128)(2,1)S(1)} %get-tuple-element.249, bf16[2048,2048]{1,0:T(8,128)(2,1)S(1)} %get-tuple-element.250), kind=kOutput, calls=%fused_computation.106 | convolution fusion | flops 8592031744 | bytes 16777216 | tf_op jit(solution)/shard_map/dot_general | solution.py:26
  318.8 48.2 %all-gather.8.cloned.1.call-done = bf16[1024,2048]{1,0:T(8,128)(2,1)} async-done(((bf16[256,2048]{1,0:T(8,128)(2,1)}), bf16[1024,2048]{1,0:T(8,128)(2,1)}) %all-gather.8.cloned.1.call-update) | async-done | bytes 4194320 | tf_op jit(solution)/shard_map/all_gather | solution.py:106
  366.9 93.4 %conditional.7 = (bf16[2048,2048]{1,0:T(8,128)(2,1)}, f32[256,2048]{1,0:T(8,128)}, f32[1,2048]{1,0:T(1,128)S(1)}) conditional(s32[]{:T(128)} %bitcast.33, () %tuple.73, (s32[4]{0:T(128)S(1)}, bf16[2048,2048]{1,0:T(8,128)(2,1)}, bf16[1024,2048]{1,0:T(8,128)(2,1)}, bf16[2048,1024]{1,0:T(8,128)(2,1)}, bf16[2048,1024]{1,0:T(8,128)(2,1)}, ...), branch_computations={%region_5.6_spmd, %region_6.10_spmd} | conditional | flops 42977456128 | bytes 182486240 | solution.py:694
  366.9 17.4 %feed_back.1.right_ref = bf16[2048,2048]{1,0:T(8,128)(2,1)} custom-call(s32[4]{0:T(128)S(1)} %get-tuple-element.142.places_ref, bf16[2048,2048]{1,0:T(8,128)(2,1)} %get-tuple-element.143.c_ref, bf16[1024,2048]{1,0:T(8,128)(2,1)} %get-tuple-element.144.w_ref, bf16[2048,1024]{1,0:T(8,128)(2,1)} %get-tuple-element.145.by_gate_ref, ...), custom_call_target="tpu_custom_call" | custom-call | flops 8589934592 | bytes 29360128 | tf_op jit(solution)/shard_map/cond/branch_1_fun/feed_back/pallas_call | solution.py:472
  384.3 10.7 %fusion.10 = bf16[1024,2048]{1,0:T(8,128)(2,1)S(1)} fusion(bf16[2048,2048]{1,0:T(8,128)(2,1)S(1)} %copy-done.14, bf16[2048,2048]{1,0:T(8,128)(2,1)} %feed_back.1.right_ref), kind=kOutput, calls=%fused_computation.45 | convolution fusion | flops 8592031744 | bytes 16777216 | tf_op jit(solution)/shard_map/cond/branch_1_fun/dot_general | solution.py:30
  396.1 6.9 collective-permute-done.32
  403.0 11.3 %add_convert_fusion.4 = bf16[1024,2048]{1,0:T(8,128)(2,1)S(1)} fusion(bf16[1024,2048]{1,0:T(8,128)(2,1)} %collective-permute-done.32, bf16[2048,2048]{1,0:T(8,128)(2,1)S(1)} %copy-done.14, bf16[2048,2048]{1,0:T(8,128)(2,1)} %feed_back.1.right_ref), kind=kOutput, calls=%fused_computation.40 | convolution fusion | flops 8596226048 | bytes 20971520 | tf_op jit(solution)/shard_map/cond/branch_1_fun/dot_general | solution.py:30
  417.8 10.0 %collective-permute-done.33 = bf16[128,2048]{1,0:T(8,128)(2,1)S(1)} collective-permute-done((bf16[128,2048]{1,0:T(8,128)(2,1)S(1)}, bf16[128,2048]{1,0:T(8,128)(2,1)S(1)}, u32[]{:S(2)}, u32[]{:S(2)}) %collective-permute-start.33) | collective-permute-done | bytes 524320 | tf_op jit(solution)/shard_map/cond/branch_1_fun/ppermute | solution.py:46
  430.0 23.7 %row_terms.2 = bf16[4,4,128,2048]{3,2,1,0:T(8,128)(2,1)} custom-call(bf16[2048,2048]{1,0:T(8,128)(2,1)} %get-tuple-element.141.left_ref, bf16[2048,2048]{1,0:T(8,128)(2,1)} %feed_back.1.right_ref), custom_call_target="tpu_custom_call" | custom-call | flops 17179869184 | bytes 25165824 | tf_op jit(solution)/shard_map/cond/branch_1_fun/row_terms/pallas_call | solution.py:527
  460.5 156.1 %conditional.9 = (bf16[2048,640]{1,0:T(8,128)(2,1)}, bf16[1,256,2048]{2,1,0:T(8,128)(2,1)}, f32[1,2048]{1,0:T(1,128)S(1)}) conditional(s32[]{:T(128)} %bitcast.33, () %tuple.76, (f32[256,2048]{1,0:T(8,128)}, bf16[256,2048]{1,0:T(8,128)(2,1)}, s32[1]{0:T(128)}, f32[2048,384]{1,0:T(8,128)}, f32[2048,128]{1,0:T(8,128)}, ...), branch_computations={%region_14.15_spmd, %region_15.19_spmd} | conditional | flops 21510486016 | bytes 249595552 | solution.py:694
  465.0 20.8 %collective-permute-done.37 = bf16[256,2048]{1,0:T(8,128)(2,1)S(1)} collective-permute-done((bf16[256,2048]{1,0:T(8,128)(2,1)S(1)}, bf16[256,2048]{1,0:T(8,128)(2,1)S(1)}, u32[]{:S(2)}, u32[]{:S(2)}) %collective-permute-start.37) | collective-permute-done | bytes 1048608 | tf_op jit(solution)/shard_map/cond/branch_1_fun/ppermute | solution.py:42
  490.1 6.7 collective-permute-done.39
  498.6 4.2 collective-permute-start.42
  510.0 10.3 %out_back.1 = (bf16[2048,2048]{1,0:T(8,128)(2,1)}, bf16[2048,256]{1,0:T(8,128)(2,1)S(1)}) custom-call(bf16[256,2048]{1,0:T(8,128)(2,1)S(1)} %convert_element_type.202.refs_0_, bf16[768,2048]{1,0:T(8,128)(2,1)} %constant_dynamic-update-slice_fusion.12.refs_1_, bf16[256,2048]{1,0:T(8,128)(2,1)S(1)} %collective-permute-done.41.refs_2_, ...), custom_call_target="tpu_custom_call" | custom-call | flops 2147483648 | bytes 18874368 | tf_op jit(solution)/shard_map/cond/branch_1_fun/out_back/pallas_call | solution.py:390
  520.3 34.3 %attend_back.1.right_ref = bf16[2048,384]{1,0:T(8,128)(2,1)S(1)} custom-call(s32[1]{0:T(128)} %get-tuple-element.163.member, f32[2048,384]{1,0:T(8,128)} %get-tuple-element.164.refs_0_.refs_1_.refs_2_.refs_3_, f32[2048,384]{1,0:T(8,128)} %get-tuple-element.164.refs_0_.refs_1_.refs_2_.refs_3_, f32[2048,384]{1,0:T(8,128)} %get-tuple-element.164.refs_0_.refs_1_.refs_2_.refs_3_, ...), custom_call_target="tpu_custom_call" | custom-call | flops 10737418240 | bytes 7864320 | tf_op jit(solution)/shard_map/cond/branch_1_fun/attend_back/pallas_call | solution.py:329
  558.8 6.8 collective-permute-done.43
  565.6 3.9 add_convert_fusion.10
  571.9 11.3 %collective-permute-done.44 = bf16[128,2048]{1,0:T(8,128)(2,1)S(1)} collective-permute-done((bf16[128,2048]{1,0:T(8,128)(2,1)S(1)}, bf16[128,2048]{1,0:T(8,128)(2,1)S(1)}, u32[]{:S(2)}, u32[]{:S(2)}) %collective-permute-start.44) | collective-permute-done | bytes 524320 | tf_op jit(solution)/shard_map/cond/branch_1_fun/ppermute | solution.py:46
  587.3 4.8 fusion.24
  596.7 7.3 row_terms.3
  612.2 4.2 fusion.32
  616.7 89.1 %conditional.8 = (f32[256,2048]{1,0:T(8,128)}, f32[64,8192]{1,0:T(8,128)}, f32[64,8192]{1,0:T(8,128)}, bf16[1,256,2048]{2,1,0:T(8,128)(2,1)}) conditional(s32[]{:T(128)} %bitcast.33, () %tuple.67, (bf16[256,2048]{1,0:T(8,128)(2,1)}, bf16[512,2048]{1,0:T(8,128)(2,1)}, s32[]{:T(128)}, bf16[1024,2048]{1,0:T(8,128)(2,1)}, s32[]{:T(128)}, ...), branch_computations={%region_12.13_spmd, %region_13.14_spmd} | conditional | flops 8642363392 | bytes 116392464 | solution.py:694
  620.2 4.7 convert_bitcast_fusion
  627.5 6.8 collective-permute-done.9
  634.3 6.1 fusion.15
  645.0 4.8 all-to-all-start.1
  652.0 4.6 collective-permute-done.10
  664.5 16.0 %all-to-all-done.1.in_ref = bf16[8,64,2048]{2,1,0:T(8,128)(2,1)S(1)} async-done(((bf16[8,64,2048]{2,1,0:T(8,128)(2,1)}), bf16[8,64,2048]{2,1,0:T(8,128)(2,1)S(1)}, u32[]{:S(2)}, u32[]{:S(2)}) %all-to-all-start.1) | async-done | bytes 2097184 | tf_op jit(solution)/shard_map/cond/branch_1_fun/all_to_all | solution.py:817
  682.8 19.2 %collective-permute-done.11 = bf16[256,2048]{1,0:T(8,128)(2,1)} collective-permute-done((bf16[256,2048]{1,0:T(8,128)(2,1)}, bf16[256,2048]{1,0:T(8,128)(2,1)}, u32[]{:S(2)}, u32[]{:S(2)}) %collective-permute-start.11) | collective-permute-done | bytes 1048608 | tf_op jit(solution)/shard_map/cond/branch_1_fun/ppermute | solution.py:42
  706.6 28.8 %all-to-all-start.2 = ((f32[32,1,128]{2,1,0:T(1,128)}), f32[32,1,128]{2,1,0:T(1,128)S(1)}, u32[]{:S(2)}, u32[]{:S(2)}) async-start(f32[32,1,128]{2,1,0:T(1,128)} %reshape.218), calls=%async_computation.5 | async-start | bytes 32768 | tf_op jit(solution)/shard_map/all_to_all | solution.py:858
  740.1 5.0 all-to-all-start.3
  746.3 4.0 collective-permute-start.50
  752.2 9.1 %collective-permute-done.50 = bf16[64,2048]{1,0:T(8,128)(2,1)S(1)} collective-permute-done((bf16[64,2048]{1,0:T(8,128)(2,1)S(1)}, bf16[64,2048]{1,0:T(8,128)(2,1)S(1)}, u32[]{:S(2)}, u32[]{:S(2)}) %collective-permute-start.50) | collective-permute-done | bytes 262176 | tf_op jit(solution)/shard_map/ppermute | solution.py:789
  (270 shorter events, 187.2 us)
Async XLA Ops:
  7.2 98.2 %all-gather.4.cloned.1.call-start = ((), (), s32[]{:S(2)}) async-start(), calls=%async_computation.7 | async-start | bytes 3379200 | tf_op jit(solution)/shard_map/all_gather | solution.py:106
  12.3 15.5 %collective-permute-start.49 = (bf16[64,2048]{1,0:T(8,128)(2,1)S(1)}, bf16[64,2048]{1,0:T(8,128)(2,1)S(1)}, u32[]{:S(2)}, u32[]{:S(2)}) collective-permute-start(bf16[64,2048]{1,0:T(8,128)(2,1)S(1)} %constant_dynamic-slice_fusion.4), channel_id=1, source_target_pairs={{0,0},{8,2},{16,4},{24,6},{1,1},{9,3},{17,5},{25,7},{2,8},{10,10},... | collective-permute-start | bytes 786440 | tf_op jit(solution)/shard_map/ppermute | solution.py:684
  28.8 245.9 %all-gather.6.cloned.1.call-start = ((), (), s32[]{:S(2)}) async-start(), calls=%async_computation.8 | async-start | bytes 10485760 | tf_op jit(solution)/shard_map/all_gather | solution.py:106
  32.5 25.3 %collective-permute-start.1 = (bf16[256,2048]{1,0:T(8,128)(2,1)S(1)}, bf16[256,2048]{1,0:T(8,128)(2,1)S(1)}, u32[]{:S(2)}, u32[]{:S(2)}) collective-permute-start(bf16[256,2048]{1,0:T(8,128)(2,1)S(1)} %get-tuple-element.425), channel_id=1, source_target_pairs={{0,16},{8,24},{16,0},{24,8},{1,17},{9,25},{17,1},{25,9},{2,18},{10... | collective-permute-start | bytes 3145736 | tf_op jit(solution)/shard_map/cond/branch_1_fun/ppermute | solution.py:42
  32.6 25.3 %collective-permute-start.2 = (bf16[256,2048]{1,0:T(8,128)(2,1)S(1)}, bf16[256,2048]{1,0:T(8,128)(2,1)S(1)}, u32[]{:S(2)}, u32[]{:S(2)}) collective-permute-start(bf16[256,2048]{1,0:T(8,128)(2,1)S(1)} %get-tuple-element.425), channel_id=1, source_target_pairs={{0,1},{1,0},{2,3},{3,2},{4,5},{5,4},{6,7},{7,6},{8,9},{9,8},{10,11... | collective-permute-start | bytes 3145736 | tf_op jit(solution)/shard_map/cond/branch_1_fun/ppermute | solution.py:46
  57.9 13.3 %collective-permute-start.3 = (bf16[128,2048]{1,0:T(8,128)(2,1)S(1)}, bf16[128,2048]{1,0:T(8,128)(2,1)S(1)}, u32[]{:S(2)}, u32[]{:S(2)}) collective-permute-start(bf16[128,2048]{1,0:T(8,128)(2,1)S(1)} %slice.162), channel_id=1, source_target_pairs={{0,1},{1,0},{2,3},{3,2},{4,5},{5,4},{6,7},{7,6},{8,9},{9,8},{10,11... | collective-permute-start | bytes 1572872 | tf_op jit(solution)/shard_map/cond/branch_1_fun/ppermute | solution.py:46
  58.3 13.7 %collective-permute-start.4 = (bf16[128,2048]{1,0:T(8,128)(2,1)S(1)}, bf16[128,2048]{1,0:T(8,128)(2,1)S(1)}, u32[]{:S(2)}, u32[]{:S(2)}) collective-permute-start(bf16[128,2048]{1,0:T(8,128)(2,1)S(1)} %slice.163), channel_id=1, source_target_pairs={{0,16},{8,24},{16,0},{24,8},{1,17},{9,25},{17,1},{25,9},{2,18},{10... | collective-permute-start | bytes 1572872 | tf_op jit(solution)/shard_map/cond/branch_1_fun/ppermute | solution.py:42
  72.9 31.4 %collective-permute-start.6 = (bf16[768,2048]{1,0:T(8,128)(2,1)}, bf16[768,2048]{1,0:T(8,128)(2,1)}, u32[]{:S(2)}, u32[]{:S(2)}) collective-permute-start(bf16[768,2048]{1,0:T(8,128)(2,1)} %constant_dynamic-update-slice_fusion), channel_id=1, source_target_pairs={{0,8},{8,0},{16,24},{24,16},{1,9},{9,1},{17,25},{25,17},{2,10},{10... | collective-permute-start | bytes 9437192 | tf_op jit(solution)/shard_map/cond/branch_1_fun/ppermute | solution.py:38
  74.0 27.1 %collective-permute-start = (bf16[256,2048]{1,0:T(8,128)(2,1)S(1)}, bf16[256,2048]{1,0:T(8,128)(2,1)}, u32[]{:S(2)}, u32[]{:S(2)}) collective-permute-start(bf16[256,2048]{1,0:T(8,128)(2,1)S(1)} %get-tuple-element.111), channel_id=1, source_target_pairs={{0,1},{1,0},{2,3},{3,2},{4,5},{5,4},{6,7},{7,6},{8,9},{9,8},{10,11... | collective-permute-start | bytes 3145736 | tf_op jit(solution)/shard_map/cond/branch_1_fun/ppermute | solution.py:46
  74.8 29.5 %collective-permute-start.5 = (bf16[256,2048]{1,0:T(8,128)(2,1)S(1)}, bf16[256,2048]{1,0:T(8,128)(2,1)}, u32[]{:S(2)}, u32[]{:S(2)}) collective-permute-start(bf16[256,2048]{1,0:T(8,128)(2,1)S(1)} %get-tuple-element.425), channel_id=1, source_target_pairs={{0,8},{8,0},{16,24},{24,16},{1,9},{9,1},{17,25},{25,17},{2,10},{10... | collective-permute-start | bytes 3145736 | tf_op jit(solution)/shard_map/cond/branch_1_fun/ppermute | solution.py:38
  75.1 24.0 %collective-permute-start.7 = (s32[1024]{0:T(1024)S(1)}, s32[1024]{0:T(1024)S(1)}, u32[]{:S(2)}, u32[]{:S(2)}) collective-permute-start(s32[1024]{0:T(1024)S(1)} %bitcast.100), channel_id=1, source_target_pairs={{0,1},{1,0},{2,3},{3,2},{4,5},{5,4},{6,7},{7,6},{8,9},{9,8},{10,11... | collective-permute-start | bytes 12296 | tf_op jit(solution)/shard_map/cond/branch_1_fun/ppermute | solution.py:46
  105.4 261.5 %all-gather.8.cloned.1.call-start = ((), (), s32[]{:S(2)}) async-start(), calls=%async_computation.10 | async-start | bytes 5242880 | tf_op jit(solution)/shard_map/all_gather | solution.py:106
  105.6 26.5 %collective-permute-start.14 = (bf16[256,2048]{1,0:T(8,128)(2,1)}, bf16[256,2048]{1,0:T(8,128)(2,1)}, u32[]{:S(2)}, u32[]{:S(2)}) collective-permute-start(bf16[256,2048]{1,0:T(8,128)(2,1)} %get-tuple-element.463), channel_id=1, source_target_pairs={{0,16},{8,24},{16,0},{24,8},{1,17},{9,25},{17,1},{25,9},{2,18},{10... | collective-permute-start | bytes 3145736 | tf_op jit(solution)/shard_map/cond/branch_1_fun/ppermute | solution.py:42
  105.8 26.3 %collective-permute-start.15 = (bf16[256,2048]{1,0:T(8,128)(2,1)}, bf16[256,2048]{1,0:T(8,128)(2,1)}, u32[]{:S(2)}, u32[]{:S(2)}) collective-permute-start(bf16[256,2048]{1,0:T(8,128)(2,1)} %get-tuple-element.463), channel_id=1, source_target_pairs={{0,1},{1,0},{2,3},{3,2},{4,5},{5,4},{6,7},{7,6},{8,9},{9,8},{10,11... | collective-permute-start | bytes 3145736 | tf_op jit(solution)/shard_map/cond/branch_1_fun/ppermute | solution.py:46
  161.9 13.6 %collective-permute-start.22 = (bf16[128,2048]{1,0:T(8,128)(2,1)S(1)}, bf16[128,2048]{1,0:T(8,128)(2,1)S(1)}, u32[]{:S(2)}, u32[]{:S(2)}) collective-permute-start(bf16[128,2048]{1,0:T(8,128)(2,1)S(1)} %slice.180), channel_id=1, source_target_pairs={{0,1},{1,0},{2,3},{3,2},{4,5},{5,4},{6,7},{7,6},{8,9},{9,8},{10,11... | collective-permute-start | bytes 1572872 | tf_op jit(solution)/shard_map/cond/branch_1_fun/ppermute | solution.py:46
  162.8 13.5 %collective-permute-start.23 = (bf16[128,2048]{1,0:T(8,128)(2,1)S(1)}, bf16[128,2048]{1,0:T(8,128)(2,1)S(1)}, u32[]{:S(2)}, u32[]{:S(2)}) collective-permute-start(bf16[128,2048]{1,0:T(8,128)(2,1)S(1)} %slice.181), channel_id=1, source_target_pairs={{0,16},{8,24},{16,0},{24,8},{1,17},{9,25},{17,1},{25,9},{2,18},{10... | collective-permute-start | bytes 1572872 | tf_op jit(solution)/shard_map/cond/branch_1_fun/ppermute | solution.py:42
  169.4 17.3 %collective-permute-start.17 = (bf16[128,2048]{1,0:T(8,128)(2,1)S(1)}, bf16[128,2048]{1,0:T(8,128)(2,1)S(1)}, u32[]{:S(2)}, u32[]{:S(2)}) collective-permute-start(bf16[128,2048]{1,0:T(8,128)(2,1)S(1)} %get-tuple-element.397), channel_id=1, source_target_pairs={{0,1},{1,0},{2,3},{3,2},{4,5},{5,4},{6,7},{7,6},{8,9},{9,8},{10,11... | collective-permute-start | bytes 1572872 | tf_op jit(solution)/shard_map/cond/branch_1_fun/ppermute | solution.py:46
  170.4 16.9 %collective-permute-start.19 = (bf16[128,2048]{1,0:T(8,128)(2,1)S(1)}, bf16[128,2048]{1,0:T(8,128)(2,1)S(1)}, u32[]{:S(2)}, u32[]{:S(2)}) collective-permute-start(bf16[128,2048]{1,0:T(8,128)(2,1)S(1)} %get-tuple-element.396), channel_id=1, source_target_pairs={{0,16},{8,24},{16,0},{24,8},{1,17},{9,25},{17,1},{25,9},{2,18},{10... | collective-permute-start | bytes 1572872 | tf_op jit(solution)/shard_map/cond/branch_1_fun/ppermute | solution.py:42
  177.1 40.3 %collective-permute-start.25 = (bf16[768,2048]{1,0:T(8,128)(2,1)}, bf16[768,2048]{1,0:T(8,128)(2,1)}, u32[]{:S(2)}, u32[]{:S(2)}) collective-permute-start(bf16[768,2048]{1,0:T(8,128)(2,1)} %constant_dynamic-update-slice_fusion.4), channel_id=1, source_target_pairs={{0,8},{8,0},{16,24},{24,16},{1,9},{9,1},{17,25},{25,17},{2,10},{10... | collective-permute-start | bytes 9437192 | tf_op jit(solution)/shard_map/cond/branch_1_fun/ppermute | solution.py:38
  187.7 23.7 %collective-permute-start.18 = (bf16[256,2048]{1,0:T(8,128)(2,1)S(1)}, bf16[256,2048]{1,0:T(8,128)(2,1)S(1)}, u32[]{:S(2)}, u32[]{:S(2)}) collective-permute-start(bf16[256,2048]{1,0:T(8,128)(2,1)S(1)} %pad_maximum_fusion.1), channel_id=1, source_target_pairs={{0,16},{8,24},{16,0},{24,8},{1,17},{9,25},{17,1},{25,9},{2,18},{10... | collective-permute-start | bytes 3145736 | tf_op jit(solution)/shard_map/cond/branch_1_fun/ppermute | solution.py:42
  189.1 23.5 %collective-permute-start.20 = (bf16[256,2048]{1,0:T(8,128)(2,1)S(1)}, bf16[256,2048]{1,0:T(8,128)(2,1)S(1)}, u32[]{:S(2)}, u32[]{:S(2)}) collective-permute-start(bf16[256,2048]{1,0:T(8,128)(2,1)S(1)} %pad_maximum_fusion.2), channel_id=1, source_target_pairs={{0,1},{1,0},{2,3},{3,2},{4,5},{5,4},{6,7},{7,6},{8,9},{9,8},{10,11... | collective-permute-start | bytes 3145736 | tf_op jit(solution)/shard_map/cond/branch_1_fun/ppermute | solution.py:46
  189.7 27.7 %collective-permute-start.24 = (bf16[256,2048]{1,0:T(8,128)(2,1)S(1)}, bf16[256,2048]{1,0:T(8,128)(2,1)}, u32[]{:S(2)}, u32[]{:S(2)}) collective-permute-start(bf16[256,2048]{1,0:T(8,128)(2,1)S(1)} %copy-done.10), channel_id=1, source_target_pairs={{0,8},{8,0},{16,24},{24,16},{1,9},{9,1},{17,25},{25,17},{2,10},{10... | collective-permute-start | bytes 3145736 | tf_op jit(solution)/shard_map/cond/branch_1_fun/ppermute | solution.py:38
  217.4 22.9 %collective-permute-start.26 = (bf16[256,2048]{1,0:T(8,128)(2,1)}, bf16[256,2048]{1,0:T(8,128)(2,1)S(1)}, u32[]{:S(2)}, u32[]{:S(2)}) collective-permute-start(bf16[256,2048]{1,0:T(8,128)(2,1)} %multiply_convert_fusion), channel_id=1, source_target_pairs={{0,16},{8,24},{16,0},{24,8},{1,17},{9,25},{17,1},{25,9},{2,18},{10... | collective-permute-start | bytes 3145736 | tf_op jit(solution)/shard_map/cond/branch_1_fun/ppermute | solution.py:42
  217.5 22.7 %collective-permute-start.27 = (bf16[256,2048]{1,0:T(8,128)(2,1)}, bf16[256,2048]{1,0:T(8,128)(2,1)S(1)}, u32[]{:S(2)}, u32[]{:S(2)}) collective-permute-start(bf16[256,2048]{1,0:T(8,128)(2,1)} %multiply_convert_fusion), channel_id=1, source_target_pairs={{0,1},{1,0},{2,3},{3,2},{4,5},{5,4},{6,7},{7,6},{8,9},{9,8},{10,11... | collective-permute-start | bytes 3145736 | tf_op jit(solution)/shard_map/cond/branch_1_fun/ppermute | solution.py:46
  252.5 21.9 %collective-permute-start.31 = (bf16[768,2048]{1,0:T(8,128)(2,1)}, bf16[768,2048]{1,0:T(8,128)(2,1)}, u32[]{:S(2)}, u32[]{:S(2)}) collective-permute-start(bf16[768,2048]{1,0:T(8,128)(2,1)} %constant_dynamic-update-slice_fusion.8), channel_id=1, source_target_pairs={{0,8},{8,0},{16,24},{24,16},{1,9},{9,1},{17,25},{25,17},{2,10},{10... | collective-permute-start | bytes 9437192 | tf_op jit(solution)/shard_map/cond/branch_1_fun/ppermute | solution.py:38
  257.7 14.4 %collective-permute-start.21 = (bf16[256,2048]{1,0:T(8,128)(2,1)S(1)}, bf16[256,2048]{1,0:T(8,128)(2,1)}, u32[]{:S(2)}, u32[]{:S(2)}) collective-permute-start(bf16[256,2048]{1,0:T(8,128)(2,1)S(1)} %dynamic-slice_bitcast_fusion), channel_id=1, source_target_pairs={{0,1},{2,3},{5,4},{7,6},{8,9},{11,10},{13,12},{14,15},{17,16},{19,... | collective-permute-start | bytes 3145736 | tf_op jit(solution)/shard_map/cond/branch_1_fun/ppermute | solution.py:667
  261.4 13.1 %collective-permute-start.30 = (bf16[256,2048]{1,0:T(8,128)(2,1)}, bf16[256,2048]{1,0:T(8,128)(2,1)}, u32[]{:S(2)}, u32[]{:S(2)}) collective-permute-start(bf16[256,2048]{1,0:T(8,128)(2,1)} %multiply_convert_fusion), channel_id=1, source_target_pairs={{0,8},{8,0},{16,24},{24,16},{1,9},{9,1},{17,25},{25,17},{2,10},{10... | collective-permute-start | bytes 3145736 | tf_op jit(solution)/shard_map/cond/branch_1_fun/ppermute | solution.py:38
  274.7 185.8 %reduce-scatter.4.cloned.1.call-start = ((), (), s32[]{:S(2)}) async-start(), calls=%async_computation.9 | async-start | bytes 5242880 | tf_op jit(solution)/shard_map/reduce_scatter | solution.py:110
  318.6 298.0 %reduce-scatter.6.cloned.1.call-start = ((), (), s32[]{:S(2)}) async-start(), calls=%async_computation.11 | async-start | bytes 10485760 | tf_op jit(solution)/shard_map/reduce_scatter | solution.py:110
  414.6 13.3 %collective-permute-start.33 = (bf16[128,2048]{1,0:T(8,128)(2,1)S(1)}, bf16[128,2048]{1,0:T(8,128)(2,1)S(1)}, u32[]{:S(2)}, u32[]{:S(2)}) collective-permute-start(bf16[128,2048]{1,0:T(8,128)(2,1)S(1)} %get-tuple-element.375), channel_id=1, source_target_pairs={{0,1},{1,0},{2,3},{3,2},{4,5},{5,4},{6,7},{7,6},{8,9},{9,8},{10,11... | collective-permute-start | bytes 1572872 | tf_op jit(solution)/shard_map/cond/branch_1_fun/ppermute | solution.py:46
  415.7 12.9 %collective-permute-start.35 = (bf16[128,2048]{1,0:T(8,128)(2,1)S(1)}, bf16[128,2048]{1,0:T(8,128)(2,1)S(1)}, u32[]{:S(2)}, u32[]{:S(2)}) collective-permute-start(bf16[128,2048]{1,0:T(8,128)(2,1)S(1)} %get-tuple-element.374), channel_id=1, source_target_pairs={{0,16},{8,24},{16,0},{24,8},{1,17},{9,25},{17,1},{25,9},{2,18},{10... | collective-permute-start | bytes 1572872 | tf_op jit(solution)/shard_map/cond/branch_1_fun/ppermute | solution.py:42
  429.2 24.5 %collective-permute-start.34 = (bf16[256,2048]{1,0:T(8,128)(2,1)S(1)}, bf16[256,2048]{1,0:T(8,128)(2,1)S(1)}, u32[]{:S(2)}, u32[]{:S(2)}) collective-permute-start(bf16[256,2048]{1,0:T(8,128)(2,1)S(1)} %pad_maximum_fusion.3), channel_id=1, source_target_pairs={{0,16},{8,24},{16,0},{24,8},{1,17},{9,25},{17,1},{25,9},{2,18},{10... | collective-permute-start | bytes 3145736 | tf_op jit(solution)/shard_map/cond/branch_1_fun/ppermute | solution.py:42
  429.6 24.1 %collective-permute-start.36 = (bf16[256,2048]{1,0:T(8,128)(2,1)S(1)}, bf16[256,2048]{1,0:T(8,128)(2,1)S(1)}, u32[]{:S(2)}, u32[]{:S(2)}) collective-permute-start(bf16[256,2048]{1,0:T(8,128)(2,1)S(1)} %pad_maximum_fusion.4), channel_id=1, source_target_pairs={{0,1},{1,0},{2,3},{3,2},{4,5},{5,4},{6,7},{7,6},{8,9},{9,8},{10,11... | collective-permute-start | bytes 3145736 | tf_op jit(solution)/shard_map/cond/branch_1_fun/ppermute | solution.py:46
  460.4 245.4 %reduce-scatter.8.cloned.1.call-start = ((), (), s32[]{:S(2)}) async-start(), calls=%async_computation.12 | async-start | bytes 3276800 | tf_op jit(solution)/shard_map/reduce_scatter | solution.py:110
  462.6 23.1 %collective-permute-start.37 = (bf16[256,2048]{1,0:T(8,128)(2,1)S(1)}, bf16[256,2048]{1,0:T(8,128)(2,1)S(1)}, u32[]{:S(2)}, u32[]{:S(2)}) collective-permute-start(bf16[256,2048]{1,0:T(8,128)(2,1)S(1)} %convert_element_type.202.refs_0_), channel_id=1, source_target_pairs={{0,16},{8,24},{16,0},{24,8},{1,17},{9,25},{17,1},{25,9},{2,18},{10... | collective-permute-start | bytes 3145736 | tf_op jit(solution)/shard_map/cond/branch_1_fun/ppermute | solution.py:42
  463.9 22.4 %collective-permute-start.38 = (bf16[256,2048]{1,0:T(8,128)(2,1)S(1)}, bf16[256,2048]{1,0:T(8,128)(2,1)S(1)}, u32[]{:S(2)}, u32[]{:S(2)}) collective-permute-start(bf16[256,2048]{1,0:T(8,128)(2,1)S(1)} %convert_element_type.202.refs_0_), channel_id=1, source_target_pairs={{0,1},{1,0},{2,3},{3,2},{4,5},{5,4},{6,7},{7,6},{8,9},{9,8},{10,11... | collective-permute-start | bytes 3145736 | tf_op jit(solution)/shard_map/cond/branch_1_fun/ppermute | solution.py:46
  569.8 13.3 %collective-permute-start.44 = (bf16[128,2048]{1,0:T(8,128)(2,1)S(1)}, bf16[128,2048]{1,0:T(8,128)(2,1)S(1)}, u32[]{:S(2)}, u32[]{:S(2)}) collective-permute-start(bf16[128,2048]{1,0:T(8,128)(2,1)S(1)} %get-tuple-element.391), channel_id=1, source_target_pairs={{0,1},{1,0},{2,3},{3,2},{4,5},{5,4},{6,7},{7,6},{8,9},{9,8},{10,11... | collective-permute-start | bytes 1572872 | tf_op jit(solution)/shard_map/cond/branch_1_fun/ppermute | solution.py:46
  585.1 23.6 %collective-permute-start.45 = (bf16[256,2048]{1,0:T(8,128)(2,1)}, bf16[256,2048]{1,0:T(8,128)(2,1)}, u32[]{:S(2)}, u32[]{:S(2)}) collective-permute-start(bf16[256,2048]{1,0:T(8,128)(2,1)} %pad_maximum_fusion.11), channel_id=1, source_target_pairs={{0,16},{8,24},{16,0},{24,8},{1,17},{9,25},{17,1},{25,9},{2,18},{10... | collective-permute-start | bytes 3145736 | tf_op jit(solution)/shard_map/cond/branch_1_fun/ppermute | solution.py:42
  586.5 23.3 %collective-permute-start.47 = (bf16[256,2048]{1,0:T(8,128)(2,1)}, bf16[256,2048]{1,0:T(8,128)(2,1)}, u32[]{:S(2)}, u32[]{:S(2)}) collective-permute-start(bf16[256,2048]{1,0:T(8,128)(2,1)} %pad_maximum_fusion.12), channel_id=1, source_target_pairs={{0,1},{1,0},{2,3},{3,2},{4,5},{5,4},{6,7},{7,6},{8,9},{9,8},{10,11... | collective-permute-start | bytes 3145736 | tf_op jit(solution)/shard_map/cond/branch_1_fun/ppermute | solution.py:46
  643.1 13.4 %collective-permute-start.10 = (bf16[128,2048]{1,0:T(8,128)(2,1)}, bf16[128,2048]{1,0:T(8,128)(2,1)}, u32[]{:S(2)}, u32[]{:S(2)}) collective-permute-start(bf16[128,2048]{1,0:T(8,128)(2,1)} %get-tuple-element.381), channel_id=1, source_target_pairs={{0,1},{1,0},{2,3},{3,2},{4,5},{5,4},{6,7},{7,6},{8,9},{9,8},{10,11... | collective-permute-start | bytes 1572872 | tf_op jit(solution)/shard_map/cond/branch_1_fun/ppermute | solution.py:46
  643.9 13.1 %collective-permute-start.12 = (bf16[128,2048]{1,0:T(8,128)(2,1)}, bf16[128,2048]{1,0:T(8,128)(2,1)}, u32[]{:S(2)}, u32[]{:S(2)}) collective-permute-start(bf16[128,2048]{1,0:T(8,128)(2,1)} %get-tuple-element.380), channel_id=1, source_target_pairs={{0,16},{8,24},{16,0},{24,8},{1,17},{9,25},{17,1},{25,9},{2,18},{10... | collective-permute-start | bytes 1572872 | tf_op jit(solution)/shard_map/cond/branch_1_fun/ppermute | solution.py:42
  645.0 35.6 %all-to-all-start.1 = ((bf16[8,64,2048]{2,1,0:T(8,128)(2,1)}), bf16[8,64,2048]{2,1,0:T(8,128)(2,1)S(1)}, u32[]{:S(2)}, u32[]{:S(2)}) async-start(bf16[8,64,2048]{2,1,0:T(8,128)(2,1)} %bitcast.87), calls=%async_computation.1 | async-start | bytes 4194304 | tf_op jit(solution)/shard_map/cond/branch_1_fun/all_to_all | solution.py:817
  649.7 13.2 %collective-permute-start.8 = (bf16[256,2048]{1,0:T(8,128)(2,1)}, bf16[256,2048]{1,0:T(8,128)(2,1)S(1)}, u32[]{:S(2)}, u32[]{:S(2)}) collective-permute-start(bf16[256,2048]{1,0:T(8,128)(2,1)} %get-tuple-element.151), channel_id=1, source_target_pairs={{0,0},{1,1},{2,10},{3,11},{4,20},{5,21},{6,30},{7,31},{8,24},{9,25... | collective-permute-start | bytes 3145736 | tf_op jit(solution)/shard_map/cond/branch_1_fun/ppermute | solution.py:789
  660.0 42.0 %collective-permute-start.11 = (bf16[256,2048]{1,0:T(8,128)(2,1)}, bf16[256,2048]{1,0:T(8,128)(2,1)}, u32[]{:S(2)}, u32[]{:S(2)}) collective-permute-start(bf16[256,2048]{1,0:T(8,128)(2,1)} %pad_maximum_fusion.6), channel_id=1, source_target_pairs={{0,16},{8,24},{16,0},{24,8},{1,17},{9,25},{17,1},{25,9},{2,18},{10... | collective-permute-start | bytes 3145736 | tf_op jit(solution)/shard_map/cond/branch_1_fun/ppermute | solution.py:42
  662.2 39.9 %collective-permute-start.13 = (bf16[256,2048]{1,0:T(8,128)(2,1)}, bf16[256,2048]{1,0:T(8,128)(2,1)S(1)}, u32[]{:S(2)}, u32[]{:S(2)}) collective-permute-start(bf16[256,2048]{1,0:T(8,128)(2,1)} %pad_maximum_fusion.7), channel_id=1, source_target_pairs={{0,1},{1,0},{2,3},{3,2},{4,5},{5,4},{6,7},{7,6},{8,9},{9,8},{10,11... | collective-permute-start | bytes 3145736 | tf_op jit(solution)/shard_map/cond/branch_1_fun/ppermute | solution.py:46
  706.6 33.5 %all-to-all-start.2 = ((f32[32,1,128]{2,1,0:T(1,128)}), f32[32,1,128]{2,1,0:T(1,128)S(1)}, u32[]{:S(2)}, u32[]{:S(2)}) async-start(f32[32,1,128]{2,1,0:T(1,128)} %reshape.218), calls=%async_computation.5 | async-start | bytes 32768 | tf_op jit(solution)/shard_map/all_to_all | solution.py:858
  740.1 22.0 %all-to-all-start.3 = ((bf16[8,64,384]{2,1,0:T(8,128)(2,1)}), bf16[8,64,384]{2,1,0:T(8,128)(2,1)S(1)}, u32[]{:S(2)}, u32[]{:S(2)}) async-start(bf16[8,64,384]{2,1,0:T(8,128)(2,1)} %bitcast.44), calls=%async_computation.6 | async-start | bytes 786432 | tf_op jit(solution)/shard_map/all_to_all | solution.py:817
  746.3 15.0 %collective-permute-start.50 = (bf16[64,2048]{1,0:T(8,128)(2,1)S(1)}, bf16[64,2048]{1,0:T(8,128)(2,1)S(1)}, u32[]{:S(2)}, u32[]{:S(2)}) collective-permute-start(bf16[64,2048]{1,0:T(8,128)(2,1)S(1)} %reshape.215), channel_id=1, source_target_pairs={{0,0},{1,4},{2,1},{3,5},{4,2},{5,6},{6,3},{7,7},{8,8},{9,12},{10,9... | collective-permute-start | bytes 786440 | tf_op jit(solution)/shard_map/ppermute | solution.py:789
  (32 other events, 382.1 us)
Sparse Core Ops, SparseCore 0:
  29.0 54.2 all-gather.3
  105.5 147.9 all-gather.5
  274.8 92.0 all-gather.7
  369.1 77.7 reduce-scatter.3
  460.5 146.2 reduce-scatter.5
  616.8 53.3 reduce-scatter.7

commit v4 on v3

--- a/solution.py
+++ b/solution.py
@@ -46,20 +46,36 @@
     return lax.ppermute(value, "fsdp", [(i, i ^ 1) for i in range(lax.axis_size("fsdp"))])
 
 
+def move(value, pairs):
+    kept = [source for source, target in pairs if source == target]
+    sent = lax.ppermute(value, ("seq", "fsdp"), [p for p in pairs if p[0] != p[1]])
+    if not kept:
+        return sent
+    here = lax.axis_index("seq") * lax.axis_size("fsdp") + lax.axis_index("fsdp")
+    own = functools.reduce(jnp.logical_or, [here == device for device in kept])
+    return jnp.where(own, value, sent)
+
+
+def swap_xy(value):
+    n_seq, n_fsdp = lax.axis_size("seq"), lax.axis_size("fsdp")
+    pairs = [(i * n_fsdp + j, (i ^ 2) * n_fsdp + (j ^ 1)) for i in range(n_seq) for j in range(n_fsdp)]
+    return move(value, pairs)
+
+
 def after(value, *others):
     return lax.optimization_barrier((value, *others))[0]
 
 
-def gather_plane(own, *others, x_part=None):
+def gather_rest(own, x_part, y_part, corner, *before_core):
+    others = jnp.concatenate([x_part, y_part, *corner])
+    others = after(others, *before_core) if before_core else others
+    return own, others, swap_core(own), swap_core(others)
+
+
+def gather_plane(own, *others):
     half = own.shape[0] // 2
-    x_part = swap_x(own) if x_part is None else x_part
-    y_part = swap_y(own)
-    core = swap_core(own)
-    x_part, y_part = lax.optimization_barrier((x_part, y_part, *others))[:2]
-    xy_up = swap_y(x_part[:half])
-    xy_low = swap_x(y_part[half:])
-    others = jnp.concatenate([x_part, y_part, xy_up, xy_low])
-    return y_part, (own, others, core, swap_core(others))
+    x_part, y_part = lax.optimization_barrier((swap_x(own), swap_y(own), *others))[:2]
+    return gather_rest(own, x_part, y_part, (swap_y(x_part[:half]), swap_x(y_part[half:])))
 
 
 def halve_core(make):
@@ -67,12 +83,12 @@
     return (make(0) + sent.astype(F32)).astype(BF16)
 
 
-def fold_corner(mine):
+def fold_corner(mine, *others):
     rows = mine.shape[0] // 4
     half = rows // 2
     own, x_part, y_part, corner = (mine[i * rows : (i + 1) * rows] for i in range(4))
-    from_x = swap_x(corner[:half]).astype(F32)
-    from_y = swap_y(corner[half:]).astype(F32)
+    from_x, from_y = lax.optimization_barrier((swap_x(corner[:half]), swap_y(corner[half:]), *others))[:2]
+    from_x, from_y = from_x.astype(F32), from_y.astype(F32)
     x_sum = jnp.concatenate([x_part[:half], (x_part[half:].astype(F32) + from_y).astype(BF16)])
     y_sum = jnp.concatenate([(y_part[:half].astype(F32) + from_x).astype(BF16), y_part[half:]])
     return own, x_sum, y_sum
@@ -125,11 +141,11 @@
     return values * jnp.tile(cosine, (1, repeats)) + partner * jnp.tile(sine, (1, repeats))
 
 
-def load_heads(blocks, cos_ref, sin_ref, q_at, k_at, v_at):
+def load_heads(blocks, cos_refs, sin_refs, q_at, k_at, v_at):
     rows = blocks[0].shape[0]
     for j, block in enumerate(blocks):
         at = pl.ds(j * rows, rows)
-        cosine, sine = cos_ref[at, :], sin_ref[at, :]
+        cosine, sine = cos_refs[j][...], sin_refs[j][...]
         q_width = q_at.shape[1]
         turned = turn_lanes(block[:, :q_width], cosine, sine).astype(BF16)
         q_at[at, :] = (turned.astype(F32) * (1.0 / math.sqrt(HD))).astype(BF16)
@@ -165,14 +181,14 @@
 
 
 def attend_kernel(n_parts, member, *refs):
-    blocks = refs[:n_parts]
-    cos_ref, sin_ref, o_ref, lse_ref, q_at, k_at, v_at, o_at, lse_at = refs[n_parts:]
+    blocks, cos_refs, sin_refs = (refs[i * n_parts : (i + 1) * n_parts] for i in range(3))
+    o_ref, lse_ref, q_at, k_at, v_at, o_at, lse_at = refs[3 * n_parts :]
     rows = blocks[0].shape[0]
     step = pl.program_id(1)
 
     @pl.when(step == 0)
     def _():
-        load_heads(blocks, cos_ref, sin_ref, q_at, k_at, v_at)
+        load_heads(blocks, cos_refs, sin_refs, q_at, k_at, v_at)
         o_at[...] = jnp.zeros_like(o_at)
         lse_at[...] = jnp.zeros_like(lse_at)
 
@@ -211,15 +227,17 @@
 
 
 def attend_back_kernel(n_parts, member, *refs):
-    blocks, d_blocks, l_blocks = refs[:n_parts], refs[n_parts : 2 * n_parts], refs[2 * n_parts : 3 * n_parts]
-    cos_ref, sin_ref, g_ref, q_at, k_at, v_at, dq_at, dk_at, dv_at = refs[3 * n_parts :]
+    blocks, d_blocks, l_blocks, cos_refs, sin_refs = (
+        refs[i * n_parts : (i + 1) * n_parts] for i in range(5)
+    )
+    cos_ref, sin_ref, g_ref, q_at, k_at, v_at, dq_at, dk_at, dv_at = refs[5 * n_parts :]
     rows = blocks[0].shape[0]
     width = q_at.shape[1]
     step = pl.program_id(1)
 
     @pl.when(step == 0)
     def _():
-        load_heads(blocks, cos_ref, sin_ref, q_at, k_at, v_at)
+        load_heads(blocks, cos_refs, sin_refs, q_at, k_at, v_at)
         dq_at[...] = jnp.zeros_like(dq_at)
         dk_at[...] = jnp.zeros_like(dk_at)
         dv_at[...] = jnp.zeros_like(dv_at)
@@ -254,7 +272,7 @@
         lax.fori_loop(0, width // HD, one_head, 0)
 
     here = pl.ds(pl.multiple_of(step * rows, rows), rows)
-    cosine, sine = cos_ref[here, :], -sin_ref[here, :]
+    cosine, sine = cos_ref[...], -sin_ref[...]
     dq = turn_lanes(dq_at[here, :] * (1.0 / math.sqrt(HD)), cosine, sine)
     span = cos_ref.shape[1]
 
@@ -291,7 +309,7 @@
     def own_spec(width):
         return pl.BlockSpec((rows, width), lambda y, i, member: (place_of(member, y, i), 0))
 
-    table = pl.BlockSpec((length, span), lambda y, i, member: (y, 0))
+    tables = [part_spec(span, j) for j in range(n_parts)]
     tiles = NY * (q_width // HD) * length * length
     return pl.pallas_call(
         functools.partial(attend_kernel, n_parts),
@@ -302,7 +320,7 @@
         grid_spec=pltpu.PrefetchScalarGridSpec(
             num_scalar_prefetch=1,
             grid=(NY, n_parts),
-            in_specs=[part_spec(qkv.shape[1], j) for j in range(n_parts)] + [table, table],
+            in_specs=[part_spec(qkv.shape[1], j) for j in range(n_parts)] + tables + tables,
             out_specs=(own_spec(q_width), own_spec(span)),
             scratch_shapes=[pltpu.VMEM((length, q_width), BF16)] * 3
             + [pltpu.VMEM((length, q_width), F32), pltpu.VMEM((length, span), F32)],
@@ -312,7 +330,7 @@
             flops=8 * tiles * HD, bytes_accessed=8 * qkv.size, transcendentals=tiles // 2
         ),
         name="attend",
-    )(member, *([qkv] * n_parts), cosine, sine)
+    )(member, *([qkv] * n_parts), *([cosine] * n_parts), *([sine] * n_parts))
 
 
 def attend_back(member, qkv, d_out, log_sums, cosine, sine, n_parts):
@@ -324,7 +342,10 @@
     def part_spec(width, part):
         return pl.BlockSpec((rows, width), lambda y, i, member: (place_of(member, y, part), 0))
 
-    table = pl.BlockSpec((length, span), lambda y, i, member: (y, 0))
+    def own_spec(width):
+        return pl.BlockSpec((rows, width), lambda y, i, member: (place_of(member, y, i), 0))
+
+    tables = [part_spec(span, j) for j in range(n_parts)]
     tiles = NY * (q_width // HD) * length * length
     return pl.pallas_call(
         functools.partial(attend_back_kernel, n_parts),
@@ -335,17 +356,24 @@
             in_specs=[part_spec(qkv.shape[1], j) for j in range(n_parts)]
             + [part_spec(q_width, j) for j in range(n_parts)]
             + [part_spec(span, j) for j in range(n_parts)]
-            + [table, table],
-            out_specs=pl.BlockSpec((rows, qkv.shape[1]), lambda y, i, member: (place_of(member, y, i), 0)),
+            + tables
+            + tables
+            + [own_spec(span)] * 2,
+            out_specs=own_spec(qkv.shape[1]),
             scratch_shapes=[pltpu.VMEM((length, q_width), BF16)] * 3
             + [pltpu.VMEM((length, q_width), F32)] * 3,
         ),
         compiler_params=pltpu.CompilerParams(vmem_limit_bytes=VMEM_BYTES),
         cost_estimate=pl.CostEstimate(
-            flops=20 * tiles * HD, bytes_accessed=10 * qkv.size, transcendentals=tiles // 2
+            flops=tiles, bytes_accessed=qkv.size // 8, transcendentals=0
         ),
         name="attend_back",
-    )(member, *([qkv] * n_parts), *([d_out] * n_parts), *([log_sums] * n_parts), cosine, sine)
+    )(
+        member,
+        *(value for value in (qkv, d_out, log_sums, cosine, sine) for _ in range(n_parts)),
+        cosine,
+        sine,
+    )
 
 def piece_specs(pieces):
     rows, width = pieces[0].shape
@@ -362,7 +390,7 @@
     return specs, first
 
 
-def pieces_call(name, body, pieces, fixed, by_rows, outs, flops):
+def pieces_call(name, body, pieces, fixed, by_rows, outs, flops, light=False):
     specs, blocks = piece_specs(pieces[0])
     specs = specs * len(pieces)
     rows = pieces[0][0].shape[0]
@@ -383,7 +411,10 @@
         return pl.BlockSpec((rows, width), lambda i: (i, 0))
 
     fixed_specs = [
-        pl.BlockSpec(shape, lambda i: (0, 0), pipeline_mode=pl.Buffered(1)) for _, shape in fixed
+        pl.BlockSpec(memory_space=pltpu.SMEM)
+        if shape is None
+        else pl.BlockSpec(shape, functools.partial(lambda i, n: (0,) * n, n=len(shape)), pipeline_mode=pl.Buffered(1))
+        for _, shape in fixed
     ]
     moved = sum(a.size * a.dtype.itemsize for a in (*pieces, *by_rows, *(f for f, _ in fixed)))
     moved += sum(blocks * rows * w * jnp.dtype(t).itemsize for w, t in outs)
@@ -394,101 +425,86 @@
         in_specs=specs + fixed_specs + [row_spec(a.shape[1]) for a in by_rows],
         out_specs=tuple(row_spec(w) for w, _ in outs),
         compiler_params=pltpu.CompilerParams(vmem_limit_bytes=VMEM_BYTES),
-        cost_estimate=pl.CostEstimate(flops=flops, bytes_accessed=moved, transcendentals=0),
+        cost_estimate=pl.CostEstimate(
+            flops=flops, bytes_accessed=moved // 64 if light else moved, transcendentals=0
+        ),
         name=name,
     )(*pieces, *(f for f, _ in fixed), *by_rows)
 
 
-def project(pieces, gain, weight, cols):
-    width = pieces[0].shape[1]
+def project(pieces, gain, weight, block):
+    width, cols = pieces[0].shape[1], block[-1]
 
     def body(x_ref, gain_ref, w_ref, xn_ref, out_ref):
         x = x_ref[...].astype(F32)
         inv = lax.rsqrt(jnp.mean(x * x, axis=-1, keepdims=True) + EPSILON)
         xn = (x * inv * gain_ref[...]).astype(BF16)
         xn_ref[...] = xn
-        out_ref[...] = dot(xn, w_ref[...])
+        out_ref[...] = dot(xn, w_ref[...].reshape(width, cols))
 
     rows = sum(p.shape[0] for p in pieces)
     return pieces_call(
         "project",
         body,
         [pieces],
-        [(gain, (1, width)), (weight, (width, cols))],
+        [(gain, gain.shape), (weight, block)],
         [],
         [(width, BF16), (cols, F32)],
         2 * rows * width * cols,
     )
 
 
-def feed(pieces, cot_pieces, w_both):
+def down_back(pieces, w_down, places):
+    cols, width = w_down.shape
+    chunk = cols // places.shape[0]
+
+    def body(c_ref, places_ref, w_ref, cot_ref, grad_ref):
+        cot = c_ref[...]
+        cot_ref[...] = cot
+        for q in range(places.shape[0]):
+            rows = pl.ds(pl.multiple_of(places_ref[q] * chunk, chunk), chunk)
+            grad_ref[:, q * chunk : (q + 1) * chunk] = dot_nt(cot, w_ref[rows, :])
+
+    rows = sum(p.shape[0] for p in pieces)
+    return pieces_call(
+        "down_back",
+        body,
+        [pieces],
+        [(places, None), (w_down, w_down.shape)],
+        [],
+        [(width, BF16), (cols, F32)],
+        2 * rows * width * cols,
+    )
+
+
+def feed(pieces, w_both, grad_mid):
     width, cols = w_both.shape[0], w_both.shape[1] // 2
 
-    def body(h_ref, c_ref, w_ref, hn_ref, cot_ref, mid_ref, by_gate_ref, by_up_ref):
+    def body(h_ref, w_ref, gm_ref, hn_ref, mid_ref, grad_ref):
         hn = h_ref[...]
         hn_ref[...] = hn
-        cot_ref[...] = c_ref[...]
         chunk = min(256, cols)
         for at in range(0, cols, chunk):
-            gate = dot(hn, w_ref[:, at : at + chunk])
-            up = dot(hn, w_ref[:, cols + at : cols + at + chunk])
+            here, there = slice(at, at + chunk), slice(cols + at, cols + at + chunk)
+            gate = dot(hn, w_ref[:, here])
+            up = dot(hn, w_ref[:, there])
             sigma = jax.nn.sigmoid(gate)
             active = gate * sigma
-            mid_ref[:, at : at + chunk] = (active * up).astype(BF16)
-            by_up_ref[:, at : at + chunk] = active.astype(BF16)
-            by_gate_ref[:, at : at + chunk] = (up * sigma * (1.0 + gate * (1.0 - sigma))).astype(BF16)
+            grad = gm_ref[:, here]
+            mid_ref[:, here] = (active * up).astype(BF16)
+            grad_ref[:, here] = (grad * up * sigma * (1.0 + gate * (1.0 - sigma))).astype(BF16)
+            grad_ref[:, there] = (grad * active).astype(BF16)
 
     rows = sum(p.shape[0] for p in pieces)
     return pieces_call(
         "feed",
         body,
-        [pieces, cot_pieces],
+        [pieces],
         [(w_both, w_both.shape)],
-        [],
-        [(width, BF16)] * 2 + [(cols, BF16)] * 3,
+        [grad_mid],
+        [(width, BF16), (cols, BF16), (2 * cols, BF16)],
         4 * rows * width * cols,
     )
-
-
-def feed_back(cot, w_down, by_gate, by_up, places):
-    cols, width = w_down.shape
-    chunk = cols // places.shape[0]
-
-    def body(places_ref, c_ref, w_ref, by_gate_ref, by_up_ref, grad_ref):
-        cot = c_ref[...]
-        for q in range(places.shape[0]):
-            at = q * chunk
-            grad = dot_nt(cot, w_ref[pl.ds(pl.multiple_of(places_ref[q] * chunk, chunk), chunk), :])
-            here = slice(at, at + chunk)
-            grad_ref[:, here] = (grad * by_gate_ref[:, here].astype(F32)).astype(BF16)
-            grad_ref[:, cols + at : cols + at + chunk] = (grad * by_up_ref[:, here].astype(F32)).astype(BF16)
-
-    rows = cot.shape[0]
-    block = rows // 8
-
-    def row_spec(width):
-        return pl.BlockSpec((block, width), lambda i: (i, 0))
-
-    return pl.pallas_call(
-        body,
-        out_shape=jax.ShapeDtypeStruct((rows, 2 * cols), BF16),
-        grid=(rows // block,),
-        in_specs=[
-            pl.BlockSpec(memory_space=pltpu.SMEM),
-            row_spec(width),
-            pl.BlockSpec(w_down.shape, lambda i: (0, 0), pipeline_mode=pl.Buffered(1)),
-            row_spec(cols),
-            row_spec(cols),
-        ],
-        out_specs=row_spec(2 * cols),
-        compiler_params=pltpu.CompilerParams(vmem_limit_bytes=VMEM_BYTES),
-        cost_estimate=pl.CostEstimate(
-            flops=2 * rows * width * cols,
-            bytes_accessed=2 * (rows * width + 4 * rows * cols + cols * width),
-            transcendentals=0,
-        ),
-        name="feed_back",
-    )(places, cot, w_down, by_gate, by_up)
 
 
 def out_back(pieces, w_o):
@@ -507,7 +523,8 @@
         [(w_o, w_o.shape)],
         [],
         [(width, BF16), (cols, BF16)],
-        2 * rows * width * cols,
+        rows * cols,
+        light=True,
     )
 
 
@@ -622,7 +639,7 @@
 
     x_own = tokens.reshape(part_len, width)
     cot_own = cotangent.reshape(part_len, width)
-    def cols_qkv(y_of):
+    def cols_qkv(y_of, w_q, w_k, w_v):
         team = s * NY + y_of
         return jnp.concatenate(
             [
@@ -674,14 +691,16 @@
 
     def rows_o():
         sub = w_o.shape[0] // n_seq
-        mine = lax.dynamic_slice_in_dim(w_o, s * sub, sub, 0)
+        mine, *later = lax.optimization_barrier(
+            (lax.dynamic_slice_in_dim(w_o, s * sub, sub, 0), w_q, w_k, w_v)
+        )
         pairs = []
         for block in range(n_all):
             team, z_to = block // n_z, block % n_z
             source = (block % n_seq) * n_fsdp + block // n_seq
             target = (team // NY) * n_fsdp + z_to * NY + team % NY
             pairs.append((source, target))
-        return lax.ppermute(mine, ("seq", "fsdp"), pairs)
+        return move(mine, pairs), *later
 
     head_cols = q_cols + 2 * kv_cols
     side = NY * n_seq * part_len // 2
@@ -704,78 +723,102 @@
         inv = lax.rsqrt(jnp.mean(rows * rows, axis=-1, keepdims=True) + EPSILON)
         return rows * inv, inv
 
-    def with_gains(rows, gains):
-        extra = jnp.pad(gains, ((0, 16 - gains.shape[0]), (0, rows.shape[1] - gains.shape[1])))
+    def with_rows(rows, extra):
+        extra = jnp.pad(extra, ((0, 16 - extra.shape[0]), (0, rows.shape[1] - extra.shape[1])))
         return jnp.concatenate([rows, extra])
 
+    rows_of_o, w_q, w_k, w_v = rows_o()
+    coded = positions.reshape(part_len)
+    coded = jnp.stack([coded // 64, coded % 64]).astype(BF16)
     gains_own = jnp.stack([attn_gain, mlp_gain])
-    mine, others = with_gains(cols_qkv(y), gains_own), with_gains(cols_qkv(1 - y), gains_own)
+    n_gains = w_rows
+
+    def with_small(rows):
+        extra = jnp.zeros((4, rows.shape[1]), BF16)
+        extra = lax.dynamic_update_slice(extra, gains_own, (0, 0))
+        return with_rows(rows, lax.dynamic_update_slice(extra, coded, (2, 0)))
+
+    mine, others = with_small(cols_qkv(y, w_q, w_k, w_v)), with_small(cols_qkv(1 - y, w_q, w_k, w_v))
     others = swap_y(others)
     first = jnp.where(y == 0, mine, others)
     second = jnp.where(y == 0, others, mine)
-    gains_both = jnp.concatenate([first[w_rows : w_rows + 2, :w_rows], second[w_rows : w_rows + 2, :w_rows]])
+    gains_both = jnp.concatenate([first[w_rows : w_rows + 2, :n_gains], second[w_rows : w_rows + 2, :n_gains]])
+    coded = jnp.stack([coded, others[w_rows + 2 : w_rows + 4, :part_len]]).astype(jnp.int32)
+    places = coded[:, 0] * 64 + coded[:, 1]
     head_rows = jnp.concatenate(
-        [jnp.concatenate([first[:w_rows], second[:w_rows]]), rows_o().reshape(NY * w_rows, -1)], axis=1
-    )
-    w_heads = gather_z(with_gains(head_rows, gains_both)).reshape(n_z, -1, head_rows.shape[1])
-
-    def first_moves(x_own, w_gate, w_up, positions, ready):
-        ours, theirs = cols_ff(w_gate, w_up)
-        both = both_rows(ours, theirs)
-        places = lax.all_to_all(
-            jnp.broadcast_to(positions.reshape(part_len), (n_seq, part_len)),
-            "seq",
-            split_axis=0,
-            concat_axis=0,
-            tiled=True,
-        ).reshape(length)
-        x_pieces = gather_plane(after(x_own, theirs), places)[1]
-        places = jnp.concatenate([places, swap_y(places)])
+        [jnp.concatenate([first[:w_rows], second[:w_rows]]), rows_of_o.reshape(NY * w_rows, -1)], axis=1
+    )
+    places = jnp.stack([places, swap_x(places)], axis=1)
+    places = jnp.stack([places, swap_core(places)]).reshape(-1)
+    w_heads = gather_z(after(with_rows(head_rows, gains_both), places))
+    w_heads = w_heads.reshape(n_z, -1, head_rows.shape[1])
+    down_places = jnp.stack([hidden_plane(q, s) for q in range(n_z)]).astype(jnp.int32)
+
+    def first_moves(x_own, w_down, places, ready):
+        x_part, y_part = lax.optimization_barrier((swap_x(x_own), swap_y(x_own)))
+        down_own = rows_down(w_down)
+        x_pieces = gather_rest(x_own, x_part, y_part, (swap_x(y_part),), down_own)
         freqs = jnp.exp(jnp.arange(HD // 2).astype(F32) * (-2.0 * math.log(ROPE_BASE) / HD))
         angles = places.astype(F32)[:, None] * freqs
         cosine, sine = jnp.cos(angles), jnp.sin(angles)
         cosine = jnp.tile(cosine, (1, 4))
         sine = jnp.concatenate([-sine, sine, -sine, sine], axis=1)
-        return both, x_pieces, cosine, sine
-
-    both, x_pieces, cosine, sine = stage(first_moves, x_own, w_gate, w_up, positions, head_rows)
-    w_both = gather_z(after(both, w_heads))
-
-    def attention(x_own, x_pieces, cot_own, w_heads, w_down, cosine, sine):
-        gains = w_heads[:, NY * w_rows : NY * w_rows + 4, :w_rows].reshape(n_z, NY, 2, w_rows)
+        return x_pieces, down_own, cosine, sine
+
+    x_pieces, down_own, cosine, sine = stage(first_moves, x_own, w_down, places, head_rows)
+    wd = gather_z(after(down_own, w_heads))
+
+    def attention(x_pieces, w_heads, cosine, sine, w_gate, w_up):
+        gains = w_heads[:, NY * w_rows : NY * w_rows + 4, :n_gains].reshape(n_z, NY, 2, n_gains)
         gains = gains.transpose(2, 0, 1, 3).reshape(2, width).astype(F32)
         gain_one, gain_two = gains[:1], gains[1:]
         wqkv = w_heads[:, : NY * w_rows, :head_cols].reshape(width, head_cols)
         wo = w_heads[:, : NY * w_rows, head_cols:].reshape(q_cols, width)
-        cot_hop, cot_pieces = gather_plane(cot_own)
-        xn, qkv = project(x_pieces, gain_one, wqkv, head_cols)
-        attn_rows, log_sums = attend(member, after(qkv, cot_hop), cosine, sine, q_cols, n_seq)
-        residual = x_own.astype(F32) + scatter_plane(halves(attn_rows, wo, False))
+        both = both_rows(*cols_ff(w_gate, w_up))
+        xn, qkv = project(x_pieces, gain_one, w_heads, (n_z, NY * w_rows, head_cols))
+        attn_rows, log_sums = attend(member, qkv, cosine, sine, q_cols, n_seq)
+        attn_rows = after(attn_rows, both)
+        sums = fold_corner(halve_core(halves(attn_rows, wo, False)))
+        return xn, qkv, attn_rows, log_sums, wqkv, wo, gain_one, gain_two, both, sums
+
+    xn, qkv, attn_rows, log_sums, wqkv, wo, gain_one, gain_two, both, sums = stage(
+        attention, x_pieces, w_heads, cosine, sine, w_gate, w_up
+    )
+    w_both = gather_z(after(both, wd, sums[0]))
+
+    def through_attention(x_own, sums, gain_two, cot_own, wd):
+        residual = x_own.astype(F32) + fold_sides(*sums)
         hn_own = (normed(residual)[0] * gain_two).astype(BF16)
-        hn_pieces = gather_plane(after(hn_own, *cot_pieces))[1]
-        return xn, qkv, attn_rows, log_sums, wqkv, wo, gain_one, gain_two, residual, rows_down(w_down), hn_pieces, cot_pieces
-
-    xn, qkv, attn_rows, log_sums, wqkv, wo, gain_one, gain_two, residual, down_own, hn_pieces, cot_pieces = stage(
-        attention, x_own, x_pieces, cot_own, w_heads, w_down, cosine, sine
-    )
-    wd = gather_z(down_own)
-    down_places = jnp.stack([hidden_plane(q, s) for q in range(n_z)]).astype(jnp.int32)
-
-    hn, cot_all, mid, by_gate, by_up = feed(hn_pieces, cot_pieces, w_both)
+        hn_pieces = gather_plane(hn_own)
+        cot_pieces = gather_plane(after(cot_own, hn_own))
+        return residual, hn_pieces, down_back(cot_pieces, wd, down_places)
+
+    residual, hn_pieces, (cot_all, grad_mid) = stage(
+        through_attention, x_own, sums, gain_two, cot_own, wd
+    )
+
+    hn, mid, grad_both = feed(hn_pieces, w_both, grad_mid)
     down_summed = scatter_z(dot_rows(mid, cot_all).astype(BF16))
 
-    def feed_backward(cot_all, cot_own, wd, by_gate, by_up, hn, w_both, residual, gain_two):
+    def feed_backward(grad_both, cot_own, hn, w_both, residual, gain_two, mid, wd):
         z_two, inv_two = normed(residual)
-        grad_both = feed_back(cot_all, wd, by_gate, by_up, down_places)
-        grad_hn = scatter_plane(halves(grad_both, w_both, True))
+        sums = halve_core(halves(grad_both, w_both, True))
+        blocks = [
+            lax.dynamic_slice_in_dim(wd, down_places[q] * ff_block, ff_block, 0) for q in range(n_z)
+        ]
+        branch_of = halves(after(mid, sums), jnp.concatenate(blocks), False)
+        branch_sent = branch_of(1).astype(BF16)
+        grad_hn = fold_sides(*fold_corner(sums, branch_sent))
+        branch = (branch_of(0) + swap_core(branch_sent).astype(F32)).astype(BF16)
         grad_z2 = grad_hn * gain_two
         grad_res = cot_own.astype(F32) + inv_two * (
             grad_z2 - z_two * jnp.mean(grad_z2 * z_two, axis=-1, keepdims=True)
         )
-        return row_terms(hn, grad_both, n_seq, n_z), grad_res, jnp.sum(grad_hn * z_two, axis=0)
-
-    both_terms, grad_res, gain_two_terms = stage(
-        feed_backward, cot_all, cot_own, wd, by_gate, by_up, hn, w_both, residual, gain_two
+        gain_terms = jnp.sum(grad_hn * z_two, axis=0)
+        return row_terms(hn, grad_both, n_seq, n_z), grad_res, gain_terms, branch
+
+    both_terms, grad_res, gain_two_terms, branch = stage(
+        feed_backward, grad_both, cot_own, hn, w_both, residual, gain_two, mid, wd
     )
     both_summed = scatter_z(both_terms)
 
@@ -786,11 +829,19 @@
             for zi in range(n_z)
             for yi in range(NY)
         ]
-        return lax.ppermute(summed, ("seq", "fsdp"), pairs).astype(F32)
-
-    def attention_backward(grad_res, wo, wqkv, xn, qkv, cosine, sine, attn_rows, log_sums, x_own, gain_one):
-        da, d_out = out_back(gather_plane(grad_res.astype(BF16))[1], wo)
+        return move(summed, pairs).astype(F32)
+
+    def attention_backward(
+        grad_res, wo, wqkv, xn, qkv, cosine, sine, attn_rows, log_sums, x_own, gain_one, residual, branch
+    ):
+        da_pieces = gather_plane(grad_res.astype(BF16))
+        own, x_part, y_part, corner = jnp.split(branch, 4)
+        x_part, y_part, corner = lax.optimization_barrier((x_part, y_part, corner, *da_pieces))[:3]
+        x_part, y_part, corner = swap_x(x_part), swap_y(y_part), swap_xy(corner)
+        da, d_out = out_back(da_pieces, wo)
         grad_qkv = attend_back(member, qkv, d_out, log_sums, cosine, sine, n_seq)
+        grad_qkv, x_part, y_part, corner = lax.optimization_barrier((grad_qkv, x_part, y_part, corner))
+        output = residual + sum(part.astype(F32) for part in (own, x_part, y_part, corner))
         z_one, inv_one = normed(x_own)
         grad_xn = scatter_plane(halves(grad_qkv, wqkv, True))
         grad_z1 = grad_xn * gain_one
@@ -804,12 +855,14 @@
             ],
             axis=1,
         )
-        return head_terms, grad_x.astype(BF16), jnp.sum(grad_xn * z_one, axis=0)
-
-    head_terms, grad_x, gain_one_terms = stage(
+        return head_terms, grad_x.astype(BF16), jnp.sum(grad_xn * z_one, axis=0), output.astype(BF16)
+
+    head_terms, grad_x, gain_one_terms, output = stage(
         attention_backward,
-        *(after(grad_res, down_summed), wo, wqkv, xn, qkv, cosine, sine, attn_rows, log_sums, x_own, gain_one),
-    )
+        *(after(grad_res, down_summed), wo, wqkv, xn, qkv, cosine, sine, attn_rows, log_sums, x_own),
+        *(gain_one, residual, branch),
+    )
+    output = output.reshape(tokens.shape)
     tokens_grad = grad_x.reshape(tokens.shape)
     head_summed = scatter_z(after(head_terms, both_summed))
 
@@ -827,22 +880,15 @@
             ((turn - plane // lines) % n_seq * NY + rest % NY, plane % lines * n_seq + turn)
         )
 
-    def outputs(mid, wd, residual, down_summed, both_summed):
+    def rows_to_owners(down_summed, both_summed):
         spread = to_team(both_summed)
-        blocks = [
-            lax.dynamic_slice_in_dim(wd, down_places[q] * ff_block, ff_block, 0) for q in range(n_z)
-        ]
-        branch = scatter_plane(halves(mid, jnp.concatenate(blocks), False))
-        output = (residual + branch).astype(BF16)
         w_down_grad = to_owner(
             down_summed, lambda si, zi, yi: (zi - si) % n_seq * n_fsdp + zi * NY + yi
         )
-        return output, w_down_grad, *deal(spread, places_of, ff_block)
-
-    output, w_down_grad, w_gate_grad, w_up_grad = stage(
-        outputs, mid, wd, residual, down_summed, both_summed
-    )
-    output = output.reshape(tokens.shape)
+        return w_down_grad, *deal(spread, places_of, ff_block)
+
+    w_down_grad, w_gate_grad, w_up_grad = stage(rows_to_owners, down_summed, both_summed)
+    head_summed = after(head_summed, w_gate_grad)
 
     w_o_grad = to_owner(
         head_summed[:, head_cols:].reshape(-1, width), lambda si, zi, yi: (si * NY + yi) * n_z + zi

time: 781 us -> 723 us (0.926)
  blocking collectives: 25 us -> 0 us
  waiting for transfers between devices: 293 us -> 279 us
  local copies, waits for them, and re-layouts: 68 us -> 57.2 us
  starting transfers between devices: 96 us -> 86.2 us
    ppermute x16, waiting for transfers between devices: 87.4 us -> 38.7 us  [swap_x(): lax.ppermute(value, 'seq', [(i, i ^ 2) for i in range(lax.axis_size('seq'...]
    ppermute x19 -> x16, waiting for transfers between devices: 85.5 us -> 119 us  [swap_y(): lax.ppermute(value, 'fsdp', [(i, i ^ 1) for i in range(lax.axis_size('fsd...]
    all_to_all x1 -> x0, blocking collectives: 25 us -> none  [first_moves(): lax.all_to_all(jnp.broadcast_to(positions.reshape(part_len), (n_seq, part...]
    all_gather x3, waiting for transfers between devices: 48.2 us -> 24.8 us  [gather_z(): lax.all_gather(own, 'fsdp', axis=0, tiled=True, axis_index_groups=z_group...]
    all_to_all x1, starting transfers between devices: 28.8 us -> 8.93 us  [shards(): lax.all_to_all(gain_terms, ('seq', 'fsdp'), split_axis=0, concat_axis=0,...]
    reduce_scatter x3, waiting for transfers between devices: 0.04 us -> 19.2 us  [scatter_z(): lax.psum_scatter(terms, 'fsdp', scatter_dimension=0, tiled=True, axis_ind...]
    pallas_call x1 -> x0, Pallas kernels: 17.4 us -> none  [feed_back(): pl.pallas_call(body, out_shape=jax.ShapeDtypeStruct((rows, 2 * cols), BF1...]
    pallas_call x3 -> x4, Pallas kernels: 52.5 us -> 66.4 us  [pieces_call(): pl.pallas_call(kernel, out_shape=tuple((jax.ShapeDtypeStruct((blocks * ro...]
  transfers between devices with their start and end apart: 60 -> 59, of which waited for: 35 -> 40; matrix products, arithmetic and copies ran while one was open for 21% -> 19% of each run, Pallas kernels for 21% -> 19%
where the time goes in v4:
time: 723 us; the launch traced here: 713 us
  waiting for transfers between devices  279 us (39%)
  Pallas kernels  160 us (22%)
  starting transfers between devices  86.2 us (12%)
  matrix products  68.2 us (9%)
  local copies, waits for them, and re-layouts  57.2 us (8%)
  other arithmetic  44 us (6%)
  between operations  15.5 us (2%)
    ppermute x16, waiting for transfers between devices, swap_y(): lax.ppermute(value, 'fsdp', [(i, i ^ 1) for i in range(lax.axis_size('fsd...  119 us
    pallas_call x4, Pallas kernels, pieces_call(): pl.pallas_call(kernel, out_shape=tuple((jax.ShapeDtypeStruct((blocks * ro...  66.4 us
    ppermute x16, waiting for transfers between devices, swap_x(): lax.ppermute(value, 'seq', [(i, i ^ 2) for i in range(lax.axis_size('seq'...  38.7 us
    dot_general x4, matrix products, dot_cols(): lax.dot_general(left, right, (((1,), (1,)), ((), ())), preferred_element_...  35.4 us
    pallas_call x1, Pallas kernels, attend_back(): pl.pallas_call(functools.partial(attend_back_kernel, n_parts), out_shape=...  34 us
    ppermute x13, waiting for transfers between devices, swap_core(): lax.ppermute(value, 'seq', [(i, i ^ 1) for i in range(lax.axis_size('seq'...  33.9 us
    pallas_call x2, Pallas kernels, row_terms(): pl.pallas_call(kernel, out_shape=jax.ShapeDtypeStruct((n_planes, n_blocks...  31.1 us
    ppermute x13, starting transfers between devices, swap_core(): lax.ppermute(value, 'seq', [(i, i ^ 1) for i in range(lax.axis_size('seq'...  25.2 us
  transfers between devices with their start and end apart: 59, of which 40 were waited for; matrix products, arithmetic and copies ran while one was open for 19% of the time, Pallas kernels for 19%

profile of v4, /device:TPU:11, one launch (start us, length us, event | category | flops | bytes accessed | tf_op | source)
XLA Modules:
  0.0 713.1 jit_solution(1446895865484411095)
XLA Ops:
  24.0 4.5 collective-permute-done.46
  30.9 58.9 %conditional.6 = (bf16[256,2048]{1,0:T(8,128)(2,1)}, bf16[768,2048]{1,0:T(8,128)(2,1)}, bf16[256,2048]{1,0:T(8,128)(2,1)}, bf16[768,2048]{1,0:T(8,128)(2,1)}, bf...) conditional(s32[]{:T(128)} %bitcast.30, () %tuple.91, ...), branch_computations={%region_0.1_spmd, %region_1.2_spmd} | conditional | flops 10881148 | bytes 50881672 | solution.py:713
  35.7 17.7 %collective-permute-done.1 = bf16[256,2048]{1,0:T(8,128)(2,1)} collective-permute-done((bf16[256,2048]{1,0:T(8,128)(2,1)S(1)}, bf16[256,2048]{1,0:T(8,128)(2,1)}, u32[]{:S(2)}, u32[]{:S(2)}) %collective-permute-start.1) | collective-permute-done | bytes 1048608 | tf_op jit(solution)/shard_map/cond/branch_1_fun/ppermute | solution.py:46
  53.6 11.8 %collective-permute-done.3 = bf16[256,2048]{1,0:T(8,128)(2,1)S(1)} collective-permute-done((bf16[256,2048]{1,0:T(8,128)(2,1)S(1)}, bf16[256,2048]{1,0:T(8,128)(2,1)S(1)}, u32[]{:S(2)}, u32[]{:S(2)}) %collective-permute-start.3) | collective-permute-done | bytes 1048608 | tf_op jit(solution)/shard_map/cond/branch_1_fun/ppermute | solution.py:684
  67.7 6.8 collective-permute-done.2
  77.6 4.9 collective-permute-start.5
  84.6 4.7 collective-permute-done.4
  91.0 81.4 %conditional.7 = (bf16[2048,2048]{1,0:T(8,128)(2,1)}, f32[2048,384]{1,0:T(8,128)}, bf16[2048,256]{1,0:T(8,128)(2,1)S(1)}, f32[2048,128]{1,0:T(8,128)}, bf16[2048...) conditional(s32[]{:T(128)} %bitcast.30, () %tuple.88, ...), branch_computations={%region_2.3_spmd, %region_3.4_spmd} | conditional | flops 9681506304 | bytes 147965088 | solution.py:713
  103.5 13.7 %project.1 = (bf16[2048,2048]{1,0:T(8,128)(2,1)}, f32[2048,384]{1,0:T(8,128)}) custom-call(bf16[256,2048]{1,0:T(8,128)(2,1)} %get-tuple-element.121.refs_0_, bf16[768,2048]{1,0:T(8,128)(2,1)} %get-tuple-element.122.refs_1_, bf16[256,2048]{1,0:T(8,128)(2,1)} %get-tuple-element.123.refs_2_, bf16[768,2048]{1,0:T(8,128)(2,1)} %get-tuple-element.124.refs_3_, ...), custom_call_target="tpu_custom_call" | custom-call | flops 3221225472 | bytes 22634496 | tf_op jit(solution)/shard_map/cond/branch_1_fun/project/pallas_call | solution.py:421
  117.2 23.3 %attend.1 = (bf16[2048,256]{1,0:T(8,128)(2,1)S(1)}, f32[2048,128]{1,0:T(8,128)}) custom-call(s32[1]{0:T(128)} %get-tuple-element.128.member, f32[2048,384]{1,0:T(8,128)} %get-tuple-element.483.refs_0_.refs_1_.refs_2_.refs_3_, f32[2048,384]{1,0:T(8,128)} %get-tuple-element.483.refs_0_.refs_1_.refs_2_.refs_3_, ...), custom_call_target="tpu_custom_call" | custom-call | flops 4294967296 | bytes 6291456 | tf_op jit(solution)/shard_map/cond/branch_1_fun/attend/pallas_call | solution.py:314
  146.0 6.8 collective-permute-done.22
  161.3 7.4 %collective-permute-done.24 = bf16[128,2048]{1,0:T(8,128)(2,1)S(1)} collective-permute-done((bf16[128,2048]{1,0:T(8,128)(2,1)}, bf16[128,2048]{1,0:T(8,128)(2,1)S(1)}, u32[]{:S(2)}, u32[]{:S(2)}) %collective-permute-start.24) | collective-permute-done | bytes 524320 | tf_op jit(solution)/shard_map/cond/branch_1_fun/ppermute | solution.py:46
  173.5 125.3 %conditional.8 = (f32[256,2048]{1,0:T(8,128)S(1)}, bf16[256,2048]{1,0:T(8,128)(2,1)}, bf16[768,2048]{1,0:T(8,128)(2,1)}, bf16[256,2048]{1,0:T(8,128)(2,1)}, bf16...) conditional(s32[]{:T(128)} %bitcast.30, () %tuple.87, ...), branch_computations={%region_4.5_spmd, %region_5.7_spmd} | conditional | flops 8596226048 | bytes 173028096 | solution.py:713
  175.1 22.2 %collective-permute-done.7 = bf16[256,2048]{1,0:T(8,128)(2,1)S(1)} collective-permute-done((bf16[256,2048]{1,0:T(8,128)(2,1)}, bf16[256,2048]{1,0:T(8,128)(2,1)S(1)}, u32[]{:S(2)}, u32[]{:S(2)}) %collective-permute-start.7) | collective-permute-done | bytes 1048608 | tf_op jit(solution)/shard_map/cond/branch_1_fun/ppermute | solution.py:42
  204.6 19.3 %collective-permute-done.16 = bf16[256,2048]{1,0:T(8,128)(2,1)S(1)} collective-permute-done((bf16[256,2048]{1,0:T(8,128)(2,1)S(1)}, bf16[256,2048]{1,0:T(8,128)(2,1)S(1)}, u32[]{:S(2)}, u32[]{:S(2)}) %collective-permute-start.16) | collective-permute-done | bytes 1048608 | tf_op jit(solution)/shard_map/cond/branch_1_fun/ppermute | solution.py:46
  226.6 19.7 %collective-permute-done.10 = bf16[256,2048]{1,0:T(8,128)(2,1)S(1)} collective-permute-done((bf16[256,2048]{1,0:T(8,128)(2,1)}, bf16[256,2048]{1,0:T(8,128)(2,1)S(1)}, u32[]{:S(2)}, u32[]{:S(2)}) %collective-permute-start.10) | collective-permute-done | bytes 1048608 | tf_op jit(solution)/shard_map/cond/branch_1_fun/ppermute | solution.py:46
  249.0 8.5 %collective-permute-done.17 = bf16[128,2048]{1,0:T(8,128)(2,1)S(1)} collective-permute-done((bf16[128,2048]{1,0:T(8,128)(2,1)S(1)}, bf16[128,2048]{1,0:T(8,128)(2,1)S(1)}, u32[]{:S(2)}, u32[]{:S(2)}) %collective-permute-start.17) | collective-permute-done | bytes 524320 | tf_op jit(solution)/shard_map/cond/branch_1_fun/ppermute | solution.py:46
  258.5 6.9 collective-permute-start.20
  274.6 7.6 %collective-permute-done.19.refs_2_ = bf16[256,2048]{1,0:T(8,128)(2,1)S(1)} collective-permute-done((bf16[256,2048]{1,0:T(8,128)(2,1)S(1)}, bf16[256,2048]{1,0:T(8,128)(2,1)S(1)}, u32[]{:S(2)}, u32[]{:S(2)}) %collective-permute-start.19) | collective-permute-done | bytes 1048608 | tf_op jit(solution)/shard_map/cond/branch_1_fun/ppermute | solution.py:38
  284.0 14.3 %down_back.1 = (bf16[2048,2048]{1,0:T(8,128)(2,1)}, f32[2048,1024]{1,0:T(8,128)}) custom-call(bf16[256,2048]{1,0:T(8,128)(2,1)S(1)} %copy-done.31, bf16[768,2048]{1,0:T(8,128)(2,1)S(1)} %constant_dynamic-update-slice_fusion.4.refs_1_, bf16[256,2048]{1,0:T(8,128)(2,1)S(1)} %collective-permute-done.19.refs_2_, bf16[768,2048]{1,0:T(8,128)(2,1)} %copy-done.36, ...), custom_call_target="tpu_custom_call" | custom-call | flops 8589934592 | bytes 29360144 | tf_op jit(solution)/shard_map/cond/branch_1_fun/down_back/pallas_call | solution.py:421
  298.8 24.7 %all-gather.8.cloned.1.call-done.refs_4_ = bf16[2048,2048]{1,0:T(8,128)(2,1)} async-done(((bf16[512,2048]{1,0:T(8,128)(2,1)}), bf16[2048,2048]{1,0:T(8,128)(2,1)}) %all-gather.8.cloned.1.call-update) | async-done | bytes 8388624 | tf_op jit(solution)/shard_map/all_gather | solution.py:122
  323.5 28.0 %feed.1 = (bf16[2048,2048]{1,0:T(8,128)(2,1)}, bf16[2048,1024]{1,0:T(8,128)(2,1)S(1)}, bf16[2048,2048]{1,0:T(8,128)(2,1)}) custom-call(bf16[256,2048]{1,0:T(8,128)(2,1)} %get-tuple-element.282.refs_0_, bf16[768,2048]{1,0:T(8,128)(2,1)} %get-tuple-element.283.refs_1_, bf16[256,2048]{1,0:T(8,128)(2,1)} %get-tuple-element.284.refs_2_, ...), custom_call_target="tpu_custom_call" | custom-call | flops 17179869184 | bytes 46137344 | tf_op jit(solution)/shard_map/feed/pallas_call | solution.py:421
  353.4 13.0 %convolution_convert_fusion.4 = bf16[1024,2048]{1,0:T(8,128)(2,1)} fusion(bf16[2048,1024]{1,0:T(8,128)(2,1)S(1)} %get-tuple-element.292, bf16[2048,2048]{1,0:T(8,128)(2,1)} %get-tuple-element.294), kind=kOutput, calls=%fused_computation.98 | convolution fusion | flops 8592031744 | bytes 16777216 | tf_op jit(solution)/shard_map/dot_general | solution.py:26
  366.5 86.7 %conditional.9 = (bf16[2048,2048]{1,0:T(8,128)(2,1)}, f32[256,2048]{1,0:T(8,128)}, bf16[1024,2048]{1,0:T(8,128)(2,1)}, f32[1,2048]{1,0:T(1,128)S(1)}) conditional(s32[]{:T(128)} %bitcast.30, () %tuple.86, (bf16[2048,2048]{1,0:T(8,128)(2,1)}, bf16[2048,2048]{1,0:T(8,128)(2,1)}, bf16[256,2048]{1,0:T(8,128)(2,1)}, f32[256,2048]{1,0:T(8,128)S(1)}, ...), branch_computations={%region_7.8_spmd, %region_8.12_spmd} | conditional | flops 43019399168 | bytes 207652480 | solution.py:713
  366.5 14.1 %fusion.10 = bf16[1024,2048]{1,0:T(8,128)(2,1)} fusion(bf16[2048,2048]{1,0:T(8,128)(2,1)} %get-tuple-element.161, bf16[2048,2048]{1,0:T(8,128)(2,1)} %get-tuple-element.158.right_ref), kind=kOutput, calls=%fused_computation.42 | convolution fusion | flops 8592031744 | bytes 16777216 | tf_op jit(solution)/shard_map/cond/branch_1_fun/dot_general | solution.py:30
  384.2 4.3 collective-permute-done.25
  388.5 13.2 %add_convert_fusion.4 = bf16[1024,2048]{1,0:T(8,128)(2,1)S(1)} fusion(bf16[1024,2048]{1,0:T(8,128)(2,1)} %collective-permute-done.25, bf16[2048,2048]{1,0:T(8,128)(2,1)} %get-tuple-element.161, bf16[2048,2048]{1,0:T(8,128)(2,1)} %get-tuple-element.158.right_ref), kind=kOutput, calls=%fused_computation.36 | convolution fusion | flops 8596226048 | bytes 20971520 | tf_op jit(solution)/shard_map/cond/branch_1_fun/dot_general | solution.py:30
  403.9 6.1 convolution_convert_fusion.1
  410.7 4.5 collective-permute-done.27
  417.4 23.7 %row_terms.2 = bf16[4,4,128,2048]{3,2,1,0:T(8,128)(2,1)} custom-call(bf16[2048,2048]{1,0:T(8,128)(2,1)} %get-tuple-element.157.left_ref, bf16[2048,2048]{1,0:T(8,128)(2,1)} %get-tuple-element.158.right_ref), custom_call_target="tpu_custom_call" | custom-call | flops 17179869184 | bytes 25165824 | tf_op jit(solution)/shard_map/cond/branch_1_fun/row_terms/pallas_call | solution.py:544
  445.0 7.7 %add_convert_fusion.3 = bf16[1024,2048]{1,0:T(8,128)(2,1)} fusion(bf16[1024,2048]{1,0:T(8,128)(2,1)} %collective-permute-done.30, bf16[2048,1024]{1,0:T(8,128)(2,1)S(1)} %copy-done.39, bf16[256,2048]{1,0:T(8,128)(2,1)S(1)} %get-tuple-element.428, bf16[256,2048]{1,0:T(8,128)(2,1)S(1)} %get-tuple-element.429, bf16[256,2048]{1,0:T(8,128)(2,1)S(1)} %get-tuple-element.430, ...), kind=kOutput, calls=%fused_computation.35 | convolution fusion | flops 4318035968 | bytes 14680064 | tf_op jit(solution)/shard_map/cond/branch_1_fun/dot_general | solution.py:34
  453.3 164.5 %conditional.10 = (bf16[2048,640]{1,0:T(8,128)(2,1)}, bf16[1,256,2048]{2,1,0:T(8,128)(2,1)}, f32[1,2048]{1,0:T(1,128)S(1)}, bf16[1,256,2048]{2,1,0:T(8,128)(2,1)}) conditional(s32[]{:T(128)} %bitcast.30, () %tuple.85, (f32[256,2048]{1,0:T(8,128)}, bf16[256,2048]{1,0:T(8,128)(2,1)}, s32[1]{0:T(128)}, f32[2048,384]{1,0:T(8,128)}, ...), branch_computations={%region_13.14_spmd, %region_14.18_spmd} | conditional | flops 8639215616 | bytes 312379392 | solution.py:713
  458.5 20.0 %collective-permute-done.32 = bf16[256,2048]{1,0:T(8,128)(2,1)S(1)} collective-permute-done((bf16[256,2048]{1,0:T(8,128)(2,1)S(1)}, bf16[256,2048]{1,0:T(8,128)(2,1)S(1)}, u32[]{:S(2)}, u32[]{:S(2)}) %collective-permute-start.32) | collective-permute-done | bytes 1048608 | tf_op jit(solution)/shard_map/cond/branch_1_fun/ppermute | solution.py:46
  482.1 7.7 %collective-permute-done.33 = bf16[128,2048]{1,0:T(8,128)(2,1)S(1)} collective-permute-done((bf16[128,2048]{1,0:T(8,128)(2,1)S(1)}, bf16[128,2048]{1,0:T(8,128)(2,1)S(1)}, u32[]{:S(2)}, u32[]{:S(2)}) %collective-permute-start.33) | collective-permute-done | bytes 524320 | tf_op jit(solution)/shard_map/cond/branch_1_fun/ppermute | solution.py:46
  508.5 10.4 %out_back.1 = (bf16[2048,2048]{1,0:T(8,128)(2,1)}, bf16[2048,256]{1,0:T(8,128)(2,1)S(1)}) custom-call(bf16[256,2048]{1,0:T(8,128)(2,1)S(1)} %convert_element_type.185.refs_0_, bf16[768,2048]{1,0:T(8,128)(2,1)} %copy-done.20, bf16[256,2048]{1,0:T(8,128)(2,1)S(1)} %copy-done.5, bf16[768,2048]{1,0:T(8,128)(2,1)} %copy-done.26, ...), custom_call_target="tpu_custom_call" | custom-call | flops 524288 | bytes 294912 | tf_op jit(solution)/shard_map/cond/branch_1_fun/out_back/pallas_call | solution.py:421
  518.9 34.0 %attend_back.1.right_ref = bf16[2048,384]{1,0:T(8,128)(2,1)S(1)} custom-call(s32[1]{0:T(128)} %get-tuple-element.173.member, f32[2048,384]{1,0:T(8,128)} %get-tuple-element.174.refs_0_.refs_1_.refs_2_.refs_3_, f32[2048,384]{1,0:T(8,128)} %get-tuple-element.174.refs_0_.refs_1_.refs_2_.refs_3_, f32[2048,384]{1,0:T(8,128)} %get-tuple-element.174.refs_0_.refs_1_.refs_2_.refs_3_, ...), custom_call_target="tpu_custom_call" | custom-call | flops 8388608 | bytes 98304 | tf_op jit(solution)/shard_map/cond/branch_1_fun/attend_back/pallas_call | solution.py:350
  553.0 4.3 convolution_convert_fusion.2
  558.8 6.5 collective-permute-done.40
  580.8 5.1 collective-permute-done.42
  591.0 7.4 %row_terms.3 = bf16[4,4,128,384]{3,2,1,0:T(8,128)(2,1)S(1)} custom-call(bf16[2048,2048]{1,0:T(8,128)(2,1)} %get-tuple-element.172.left_ref, bf16[2048,384]{1,0:T(8,128)(2,1)S(1)} %copy-done.3), custom_call_target="tpu_custom_call" | custom-call | flops 3221225472 | bytes 11534336 | tf_op jit(solution)/shard_map/cond/branch_1_fun/row_terms/pallas_call | solution.py:544
  600.9 4.1 fusion.33
  605.1 7.6 %collective-permute-done.44 = bf16[256,2048]{1,0:T(8,128)(2,1)S(1)} collective-permute-done((bf16[256,2048]{1,0:T(8,128)(2,1)S(1)}, bf16[256,2048]{1,0:T(8,128)(2,1)S(1)}, u32[]{:S(2)}, u32[]{:S(2)}) %collective-permute-start.44) | collective-permute-done | bytes 1048608 | tf_op jit(solution)/shard_map/cond/branch_1_fun/ppermute | solution.py:46
  617.8 34.8 %conditional.11 = (f32[256,2048]{1,0:T(8,128)}, f32[64,8192]{1,0:T(8,128)}, f32[64,8192]{1,0:T(8,128)}) conditional(s32[]{:T(128)} %bitcast.30, () %tuple.101, (bf16[256,2048]{1,0:T(8,128)(2,1)}, bf16[512,2048]{1,0:T(8,128)(2,1)}) %tuple.102), branch_computations={%region_20.21_spmd, %region_21.22_spmd} | conditional | flops 1048598 | bytes 24117542 | solution.py:713
  617.9 7.2 %all-to-all-start = ((bf16[8,64,2048]{2,1,0:T(8,128)(2,1)}), bf16[8,64,2048]{2,1,0:T(8,128)(2,1)S(1)}, u32[]{:S(2)}, u32[]{:S(2)}) async-start(bf16[8,64,2048]{2,1,0:T(8,128)(2,1)} %bitcast.89), calls=%async_computation | async-start | bytes 4194304 | tf_op jit(solution)/shard_map/cond/branch_1_fun/all_to_all | solution.py:870
  632.5 17.8 %all-to-all-done.in_ref = bf16[8,64,2048]{2,1,0:T(8,128)(2,1)S(1)} async-done(((bf16[8,64,2048]{2,1,0:T(8,128)(2,1)}), bf16[8,64,2048]{2,1,0:T(8,128)(2,1)S(1)}, u32[]{:S(2)}, u32[]{:S(2)}) %all-to-all-start) | async-done | bytes 2097184 | tf_op jit(solution)/shard_map/cond/branch_1_fun/all_to_all | solution.py:870
  652.6 19.2 %reduce-scatter.8.cloned.1.call-done = bf16[512,640]{1,0:T(8,128)(2,1)} async-done(((bf16[2048,640]{1,0:T(8,128)(2,1)}), bf16[512,640]{1,0:T(8,128)(2,1)}) %reduce-scatter.8.cloned.1.call-update) | async-done | bytes 655376 | tf_op jit(solution)/shard_map/reduce_scatter | solution.py:126
  677.6 8.9 %all-to-all-start.1 = ((f32[32,1,128]{2,1,0:T(1,128)}), f32[32,1,128]{2,1,0:T(1,128)S(1)}, u32[]{:S(2)}, u32[]{:S(2)}) async-start(f32[32,1,128]{2,1,0:T(1,128)} %reshape.225), calls=%async_computation.4 | async-start | bytes 32768 | tf_op jit(solution)/shard_map/all_to_all | solution.py:904
  691.2 5.0 all-to-all-start.2
  (315 shorter events, 190.7 us)
Async XLA Ops:
  7.2 82.6 %all-gather.4.cloned.1.call-start = ((), (), s32[]{:S(2)}) async-start(), calls=%async_computation.6 | async-start | bytes 3379200 | tf_op jit(solution)/shard_map/all_gather | solution.py:122
  13.1 15.4 %collective-permute-start.46 = (bf16[64,2048]{1,0:T(8,128)(2,1)S(1)}, bf16[64,2048]{1,0:T(8,128)(2,1)S(1)}, u32[]{:S(2)}, u32[]{:S(2)}) collective-permute-start(bf16[64,2048]{1,0:T(8,128)(2,1)S(1)} %constant_dynamic-slice_fusion.10), channel_id=1, source_target_pairs={{8,2},{16,4},{24,6},{9,3},{17,5},{25,7},{2,8},{18,12},{26,14},{3,9... | collective-permute-start | bytes 786440 | tf_op jit(solution)/shard_map/ppermute | solution.py:51
  29.6 142.9 %all-gather.6.cloned.1.call-start = ((), (), s32[]{:S(2)}) async-start(), calls=%async_computation.7 | async-start | bytes 5242880 | tf_op jit(solution)/shard_map/all_gather | solution.py:122
  30.9 22.5 %collective-permute-start.1 = (bf16[256,2048]{1,0:T(8,128)(2,1)S(1)}, bf16[256,2048]{1,0:T(8,128)(2,1)}, u32[]{:S(2)}, u32[]{:S(2)}) collective-permute-start(bf16[256,2048]{1,0:T(8,128)(2,1)S(1)} %get-tuple-element.463), channel_id=1, source_target_pairs={{0,1},{1,0},{2,3},{3,2},{4,5},{5,4},{6,7},{7,6},{8,9},{9,8},{10,11... | collective-permute-start | bytes 3145736 | tf_op jit(solution)/shard_map/cond/branch_1_fun/ppermute | solution.py:46
  31.2 22.2 %collective-permute-start = (bf16[256,2048]{1,0:T(8,128)(2,1)S(1)}, bf16[256,2048]{1,0:T(8,128)(2,1)}, u32[]{:S(2)}, u32[]{:S(2)}) collective-permute-start(bf16[256,2048]{1,0:T(8,128)(2,1)S(1)} %get-tuple-element.463), channel_id=1, source_target_pairs={{0,16},{8,24},{16,0},{24,8},{1,17},{9,25},{17,1},{25,9},{2,18},{10... | collective-permute-start | bytes 3145736 | tf_op jit(solution)/shard_map/cond/branch_1_fun/ppermute | solution.py:42
  32.5 32.9 %collective-permute-start.3 = (bf16[256,2048]{1,0:T(8,128)(2,1)S(1)}, bf16[256,2048]{1,0:T(8,128)(2,1)S(1)}, u32[]{:S(2)}, u32[]{:S(2)}) collective-permute-start(bf16[256,2048]{1,0:T(8,128)(2,1)S(1)} %dynamic-slice_bitcast_fusion), channel_id=1, source_target_pairs={{0,1},{2,3},{5,4},{7,6},{8,9},{11,10},{13,12},{14,15},{17,16},{19,... | collective-permute-start | bytes 3145736 | tf_op jit(solution)/shard_map/cond/branch_1_fun/ppermute | solution.py:684
  53.4 21.1 %collective-permute-start.2 = (bf16[256,2048]{1,0:T(8,128)(2,1)}, bf16[256,2048]{1,0:T(8,128)(2,1)}, u32[]{:S(2)}, u32[]{:S(2)}) collective-permute-start(bf16[256,2048]{1,0:T(8,128)(2,1)} %collective-permute-done.1), channel_id=1, source_target_pairs={{0,16},{8,24},{16,0},{24,8},{1,17},{9,25},{17,1},{25,9},{2,18},{10... | collective-permute-start | bytes 3145736 | tf_op jit(solution)/shard_map/cond/branch_1_fun/ppermute | solution.py:42
  77.6 12.0 %collective-permute-start.5 = (bf16[768,2048]{1,0:T(8,128)(2,1)}, bf16[768,2048]{1,0:T(8,128)(2,1)}, u32[]{:S(2)}, u32[]{:S(2)}) collective-permute-start(bf16[768,2048]{1,0:T(8,128)(2,1)} %pad_maximum_fusion), channel_id=1, source_target_pairs={{0,8},{8,0},{16,24},{24,16},{1,9},{9,1},{17,25},{25,17},{2,10},{10... | collective-permute-start | bytes 9437192 | tf_op jit(solution)/shard_map/cond/branch_1_fun/ppermute | solution.py:38
  89.8 233.7 %all-gather.8.cloned.1.call-start = ((), (), s32[]{:S(2)}) async-start(), calls=%async_computation.8 | async-start | bytes 10485760 | tf_op jit(solution)/shard_map/all_gather | solution.py:122
  94.7 45.8 %collective-permute-start.21 = (bf16[256,2048]{1,0:T(8,128)(2,1)}, bf16[256,2048]{1,0:T(8,128)(2,1)}, u32[]{:S(2)}, u32[]{:S(2)}) collective-permute-start(bf16[256,2048]{1,0:T(8,128)(2,1)} %get-tuple-element.137), channel_id=1, source_target_pairs={{0,1},{1,0},{2,3},{3,2},{4,5},{5,4},{6,7},{7,6},{8,9},{9,8},{10,11... | collective-permute-start | bytes 3145736 | tf_op jit(solution)/shard_map/cond/branch_1_fun/ppermute | solution.py:46
  155.2 13.4 %collective-permute-start.24 = (bf16[128,2048]{1,0:T(8,128)(2,1)}, bf16[128,2048]{1,0:T(8,128)(2,1)S(1)}, u32[]{:S(2)}, u32[]{:S(2)}) collective-permute-start(bf16[128,2048]{1,0:T(8,128)(2,1)} %get-tuple-element.414), channel_id=1, source_target_pairs={{0,1},{1,0},{2,3},{3,2},{4,5},{5,4},{6,7},{7,6},{8,9},{9,8},{10,11... | collective-permute-start | bytes 1572872 | tf_op jit(solution)/shard_map/cond/branch_1_fun/ppermute | solution.py:46
  155.6 13.1 %collective-permute-start.23 = (bf16[128,2048]{1,0:T(8,128)(2,1)}, bf16[128,2048]{1,0:T(8,128)(2,1)S(1)}, u32[]{:S(2)}, u32[]{:S(2)}) collective-permute-start(bf16[128,2048]{1,0:T(8,128)(2,1)} %get-tuple-element.415), channel_id=1, source_target_pairs={{0,16},{8,24},{16,0},{24,8},{1,17},{9,25},{17,1},{25,9},{2,18},{10... | collective-permute-start | bytes 1572872 | tf_op jit(solution)/shard_map/cond/branch_1_fun/ppermute | solution.py:42
  172.5 280.7 %reduce-scatter.4.cloned.1.call-start = ((), (), s32[]{:S(2)}) async-start(), calls=%async_computation.9 | async-start | bytes 5242880 | tf_op jit(solution)/shard_map/reduce_scatter | solution.py:126
  173.7 23.6 %collective-permute-start.7 = (bf16[256,2048]{1,0:T(8,128)(2,1)}, bf16[256,2048]{1,0:T(8,128)(2,1)S(1)}, u32[]{:S(2)}, u32[]{:S(2)}) collective-permute-start(bf16[256,2048]{1,0:T(8,128)(2,1)} %get-tuple-element.144), channel_id=1, source_target_pairs={{0,16},{8,24},{16,0},{24,8},{1,17},{9,25},{17,1},{25,9},{2,18},{10... | collective-permute-start | bytes 3145736 | tf_op jit(solution)/shard_map/cond/branch_1_fun/ppermute | solution.py:42
  174.0 23.4 %collective-permute-start.8 = (bf16[256,2048]{1,0:T(8,128)(2,1)}, bf16[256,2048]{1,0:T(8,128)(2,1)S(1)}, u32[]{:S(2)}, u32[]{:S(2)}) collective-permute-start(bf16[256,2048]{1,0:T(8,128)(2,1)} %get-tuple-element.145), channel_id=1, source_target_pairs={{0,1},{1,0},{2,3},{3,2},{4,5},{5,4},{6,7},{7,6},{8,9},{9,8},{10,11... | collective-permute-start | bytes 3145736 | tf_op jit(solution)/shard_map/cond/branch_1_fun/ppermute | solution.py:46
  201.6 22.2 %collective-permute-start.16 = (bf16[256,2048]{1,0:T(8,128)(2,1)S(1)}, bf16[256,2048]{1,0:T(8,128)(2,1)S(1)}, u32[]{:S(2)}, u32[]{:S(2)}) collective-permute-start(bf16[256,2048]{1,0:T(8,128)(2,1)S(1)} %copy-done.31), channel_id=1, source_target_pairs={{0,1},{1,0},{2,3},{3,2},{4,5},{5,4},{6,7},{7,6},{8,9},{9,8},{10,11... | collective-permute-start | bytes 3145736 | tf_op jit(solution)/shard_map/cond/branch_1_fun/ppermute | solution.py:46
  202.7 22.0 %collective-permute-start.15 = (bf16[256,2048]{1,0:T(8,128)(2,1)S(1)}, bf16[256,2048]{1,0:T(8,128)(2,1)S(1)}, u32[]{:S(2)}, u32[]{:S(2)}) collective-permute-start(bf16[256,2048]{1,0:T(8,128)(2,1)S(1)} %copy-done.31), channel_id=1, source_target_pairs={{0,16},{8,24},{16,0},{24,8},{1,17},{9,25},{17,1},{25,9},{2,18},{10... | collective-permute-start | bytes 3145736 | tf_op jit(solution)/shard_map/cond/branch_1_fun/ppermute | solution.py:42
  203.9 42.3 %collective-permute-start.10 = (bf16[256,2048]{1,0:T(8,128)(2,1)}, bf16[256,2048]{1,0:T(8,128)(2,1)S(1)}, u32[]{:S(2)}, u32[]{:S(2)}) collective-permute-start(bf16[256,2048]{1,0:T(8,128)(2,1)} %multiply_convert_fusion), channel_id=1, source_target_pairs={{0,1},{1,0},{2,3},{3,2},{4,5},{5,4},{6,7},{7,6},{8,9},{9,8},{10,11... | collective-permute-start | bytes 3145736 | tf_op jit(solution)/shard_map/cond/branch_1_fun/ppermute | solution.py:46
  204.3 42.9 %collective-permute-start.9 = (bf16[256,2048]{1,0:T(8,128)(2,1)}, bf16[256,2048]{1,0:T(8,128)(2,1)S(1)}, u32[]{:S(2)}, u32[]{:S(2)}) collective-permute-start(bf16[256,2048]{1,0:T(8,128)(2,1)} %multiply_convert_fusion), channel_id=1, source_target_pairs={{0,16},{8,24},{16,0},{24,8},{1,17},{9,25},{17,1},{25,9},{2,18},{10... | collective-permute-start | bytes 3145736 | tf_op jit(solution)/shard_map/cond/branch_1_fun/ppermute | solution.py:42
  224.8 32.7 %collective-permute-start.17 = (bf16[128,2048]{1,0:T(8,128)(2,1)S(1)}, bf16[128,2048]{1,0:T(8,128)(2,1)S(1)}, u32[]{:S(2)}, u32[]{:S(2)}) collective-permute-start(bf16[128,2048]{1,0:T(8,128)(2,1)S(1)} %slice.159), channel_id=1, source_target_pairs={{0,1},{1,0},{2,3},{3,2},{4,5},{5,4},{6,7},{7,6},{8,9},{9,8},{10,11... | collective-permute-start | bytes 1572872 | tf_op jit(solution)/shard_map/cond/branch_1_fun/ppermute | solution.py:46
  225.1 33.3 %collective-permute-start.18 = (bf16[128,2048]{1,0:T(8,128)(2,1)S(1)}, bf16[128,2048]{1,0:T(8,128)(2,1)S(1)}, u32[]{:S(2)}, u32[]{:S(2)}) collective-permute-start(bf16[128,2048]{1,0:T(8,128)(2,1)S(1)} %slice.160), channel_id=1, source_target_pairs={{0,16},{8,24},{16,0},{24,8},{1,17},{9,25},{17,1},{25,9},{2,18},{10... | collective-permute-start | bytes 1572872 | tf_op jit(solution)/shard_map/cond/branch_1_fun/ppermute | solution.py:42
  247.3 22.4 %collective-permute-start.12 = (bf16[128,2048]{1,0:T(8,128)(2,1)S(1)}, bf16[128,2048]{1,0:T(8,128)(2,1)S(1)}, u32[]{:S(2)}, u32[]{:S(2)}) collective-permute-start(bf16[128,2048]{1,0:T(8,128)(2,1)S(1)} %slice.158), channel_id=1, source_target_pairs={{0,16},{8,24},{16,0},{24,8},{1,17},{9,25},{17,1},{25,9},{2,18},{10... | collective-permute-start | bytes 1572872 | tf_op jit(solution)/shard_map/cond/branch_1_fun/ppermute | solution.py:42
  248.6 20.2 %collective-permute-start.11 = (bf16[128,2048]{1,0:T(8,128)(2,1)S(1)}, bf16[128,2048]{1,0:T(8,128)(2,1)S(1)}, u32[]{:S(2)}, u32[]{:S(2)}) collective-permute-start(bf16[128,2048]{1,0:T(8,128)(2,1)S(1)} %slice.157), channel_id=1, source_target_pairs={{0,1},{1,0},{2,3},{3,2},{4,5},{5,4},{6,7},{7,6},{8,9},{9,8},{10,11... | collective-permute-start | bytes 1572872 | tf_op jit(solution)/shard_map/cond/branch_1_fun/ppermute | solution.py:46
  258.5 23.7 %collective-permute-start.20 = (bf16[768,2048]{1,0:T(8,128)(2,1)S(1)}, bf16[768,2048]{1,0:T(8,128)(2,1)S(1)}, u32[]{:S(2)}, u32[]{:S(2)}) collective-permute-start(bf16[768,2048]{1,0:T(8,128)(2,1)S(1)} %constant_dynamic-update-slice_fusion.4.refs_1_), channel_id=1, source_target_pairs={{0,8},{8,0},{16,24},{24,16},{1,9},{9,1},{17,25},{25,17},{2,10},{10... | collective-permute-start | bytes 9437192 | tf_op jit(solution)/shard_map/cond/branch_1_fun/ppermute | solution.py:38
  270.5 27.8 %collective-permute-start.14 = (bf16[768,2048]{1,0:T(8,128)(2,1)}, bf16[768,2048]{1,0:T(8,128)(2,1)}, u32[]{:S(2)}, u32[]{:S(2)}) collective-permute-start(bf16[768,2048]{1,0:T(8,128)(2,1)} %constant_dynamic-update-slice_fusion), channel_id=1, source_target_pairs={{0,8},{8,0},{16,24},{24,16},{1,9},{9,1},{17,25},{25,17},{2,10},{10... | collective-permute-start | bytes 9437192 | tf_op jit(solution)/shard_map/cond/branch_1_fun/ppermute | solution.py:38
  274.1 24.2 %collective-permute-start.13 = (bf16[256,2048]{1,0:T(8,128)(2,1)}, bf16[256,2048]{1,0:T(8,128)(2,1)}, u32[]{:S(2)}, u32[]{:S(2)}) collective-permute-start(bf16[256,2048]{1,0:T(8,128)(2,1)} %multiply_convert_fusion), channel_id=1, source_target_pairs={{0,8},{8,0},{16,24},{24,16},{1,9},{9,1},{17,25},{25,17},{2,10},{10... | collective-permute-start | bytes 3145736 | tf_op jit(solution)/shard_map/cond/branch_1_fun/ppermute | solution.py:38
  366.4 251.4 %reduce-scatter.6.cloned.1.call-start = ((), (), s32[]{:S(2)}) async-start(), calls=%async_computation.10 | async-start | bytes 10485760 | tf_op jit(solution)/shard_map/reduce_scatter | solution.py:126
  401.9 13.3 %collective-permute-start.27 = (bf16[128,2048]{1,0:T(8,128)(2,1)S(1)}, bf16[128,2048]{1,0:T(8,128)(2,1)S(1)}, u32[]{:S(2)}, u32[]{:S(2)}) collective-permute-start(bf16[128,2048]{1,0:T(8,128)(2,1)S(1)} %get-tuple-element.423), channel_id=1, source_target_pairs={{0,1},{1,0},{2,3},{3,2},{4,5},{5,4},{6,7},{7,6},{8,9},{9,8},{10,11... | collective-permute-start | bytes 1572872 | tf_op jit(solution)/shard_map/cond/branch_1_fun/ppermute | solution.py:46
  403.2 12.9 %collective-permute-start.26 = (bf16[128,2048]{1,0:T(8,128)(2,1)S(1)}, bf16[128,2048]{1,0:T(8,128)(2,1)S(1)}, u32[]{:S(2)}, u32[]{:S(2)}) collective-permute-start(bf16[128,2048]{1,0:T(8,128)(2,1)S(1)} %get-tuple-element.424), channel_id=1, source_target_pairs={{0,16},{8,24},{16,0},{24,8},{1,17},{9,25},{17,1},{25,9},{2,18},{10... | collective-permute-start | bytes 1572872 | tf_op jit(solution)/shard_map/cond/branch_1_fun/ppermute | solution.py:42
  410.0 34.7 %collective-permute-start.30 = (bf16[1024,2048]{1,0:T(8,128)(2,1)}, bf16[1024,2048]{1,0:T(8,128)(2,1)}, u32[]{:S(2)}, u32[]{:S(2)}) collective-permute-start(bf16[1024,2048]{1,0:T(8,128)(2,1)} %convolution_convert_fusion.1), channel_id=1, source_target_pairs={{0,8},{8,0},{16,24},{24,16},{1,9},{9,1},{17,25},{25,17},{2,10},{10... | collective-permute-start | bytes 12582920 | tf_op jit(solution)/shard_map/cond/branch_1_fun/ppermute | solution.py:38
  416.6 24.5 %collective-permute-start.29 = (bf16[256,2048]{1,0:T(8,128)(2,1)S(1)}, bf16[256,2048]{1,0:T(8,128)(2,1)S(1)}, u32[]{:S(2)}, u32[]{:S(2)}) collective-permute-start(bf16[256,2048]{1,0:T(8,128)(2,1)S(1)} %pad_maximum_fusion.6), channel_id=1, source_target_pairs={{0,1},{1,0},{2,3},{3,2},{4,5},{5,4},{6,7},{7,6},{8,9},{9,8},{10,11... | collective-permute-start | bytes 3145736 | tf_op jit(solution)/shard_map/cond/branch_1_fun/ppermute | solution.py:46
  417.0 24.1 %collective-permute-start.28 = (bf16[256,2048]{1,0:T(8,128)(2,1)S(1)}, bf16[256,2048]{1,0:T(8,128)(2,1)S(1)}, u32[]{:S(2)}, u32[]{:S(2)}) collective-permute-start(bf16[256,2048]{1,0:T(8,128)(2,1)S(1)} %pad_maximum_fusion.5), channel_id=1, source_target_pairs={{0,16},{8,24},{16,0},{24,8},{1,17},{9,25},{17,1},{25,9},{2,18},{10... | collective-permute-start | bytes 3145736 | tf_op jit(solution)/shard_map/cond/branch_1_fun/ppermute | solution.py:42
  453.2 218.6 %reduce-scatter.8.cloned.1.call-start = ((), (), s32[]{:S(2)}) async-start(), calls=%async_computation.11 | async-start | bytes 3276800 | tf_op jit(solution)/shard_map/reduce_scatter | solution.py:126
  455.8 22.7 %collective-permute-start.32 = (bf16[256,2048]{1,0:T(8,128)(2,1)S(1)}, bf16[256,2048]{1,0:T(8,128)(2,1)S(1)}, u32[]{:S(2)}, u32[]{:S(2)}) collective-permute-start(bf16[256,2048]{1,0:T(8,128)(2,1)S(1)} %convert_element_type.185.refs_0_), channel_id=1, source_target_pairs={{0,1},{1,0},{2,3},{3,2},{4,5},{5,4},{6,7},{7,6},{8,9},{9,8},{10,11... | collective-permute-start | bytes 3145736 | tf_op jit(solution)/shard_map/cond/branch_1_fun/ppermute | solution.py:46
  457.0 22.4 %collective-permute-start.31 = (bf16[256,2048]{1,0:T(8,128)(2,1)S(1)}, bf16[256,2048]{1,0:T(8,128)(2,1)S(1)}, u32[]{:S(2)}, u32[]{:S(2)}) collective-permute-start(bf16[256,2048]{1,0:T(8,128)(2,1)S(1)} %convert_element_type.185.refs_0_), channel_id=1, source_target_pairs={{0,16},{8,24},{16,0},{24,8},{1,17},{9,25},{17,1},{25,9},{2,18},{10... | collective-permute-start | bytes 3145736 | tf_op jit(solution)/shard_map/cond/branch_1_fun/ppermute | solution.py:42
  480.0 10.9 %collective-permute-start.34 = (bf16[128,2048]{1,0:T(8,128)(2,1)S(1)}, bf16[128,2048]{1,0:T(8,128)(2,1)S(1)}, u32[]{:S(2)}, u32[]{:S(2)}) collective-permute-start(bf16[128,2048]{1,0:T(8,128)(2,1)S(1)} %slice.173), channel_id=1, source_target_pairs={{0,16},{8,24},{16,0},{24,8},{1,17},{9,25},{17,1},{25,9},{2,18},{10... | collective-permute-start | bytes 1572872 | tf_op jit(solution)/shard_map/cond/branch_1_fun/ppermute | solution.py:42
  491.0 11.7 %collective-permute-start.36 = (bf16[768,2048]{1,0:T(8,128)(2,1)S(1)}, bf16[768,2048]{1,0:T(8,128)(2,1)S(1)}, u32[]{:S(2)}, u32[]{:S(2)}) collective-permute-start(bf16[768,2048]{1,0:T(8,128)(2,1)S(1)} %constant_dynamic-update-slice_fusion.8.refs_1_), channel_id=1, source_target_pairs={{0,8},{8,0},{16,24},{24,16},{1,9},{9,1},{17,25},{25,17},{2,10},{10... | collective-permute-start | bytes 9437192 | tf_op jit(solution)/shard_map/cond/branch_1_fun/ppermute | solution.py:38
  502.6 50.3 %collective-permute-start.37 = (bf16[256,2048]{1,0:T(8,128)(2,1)}, bf16[256,2048]{1,0:T(8,128)(2,1)}, u32[]{:S(2)}, u32[]{:S(2)}) collective-permute-start(bf16[256,2048]{1,0:T(8,128)(2,1)} %get-tuple-element.184), channel_id=1, source_target_pairs={{0,16},{8,24},{16,0},{24,8},{1,17},{9,25},{17,1},{25,9},{2,18},{10... | collective-permute-start | bytes 3145736 | tf_op jit(solution)/shard_map/cond/branch_1_fun/ppermute | solution.py:42
  504.1 48.8 %collective-permute-start.38 = (bf16[256,2048]{1,0:T(8,128)(2,1)}, bf16[256,2048]{1,0:T(8,128)(2,1)}, u32[]{:S(2)}, u32[]{:S(2)}) collective-permute-start(bf16[256,2048]{1,0:T(8,128)(2,1)} %get-tuple-element.185), channel_id=1, source_target_pairs={{0,1},{1,0},{2,3},{3,2},{4,5},{5,4},{6,7},{7,6},{8,9},{9,8},{10,11... | collective-permute-start | bytes 3145736 | tf_op jit(solution)/shard_map/cond/branch_1_fun/ppermute | solution.py:46
  505.2 47.7 %collective-permute-start.39 = (bf16[256,2048]{1,0:T(8,128)(2,1)}, bf16[256,2048]{1,0:T(8,128)(2,1)}, u32[]{:S(2)}, u32[]{:S(2)}) collective-permute-start(bf16[256,2048]{1,0:T(8,128)(2,1)} %get-tuple-element.186), channel_id=1, source_target_pairs={{0,17},{1,16},{2,19},{3,18},{4,21},{5,20},{6,23},{7,22},{8,25},{9,... | collective-permute-start | bytes 3145736 | tf_op jit(solution)/shard_map/cond/branch_1_fun/ppermute | solution.py:51
  572.5 13.5 %collective-permute-start.42 = (bf16[128,2048]{1,0:T(8,128)(2,1)}, bf16[128,2048]{1,0:T(8,128)(2,1)}, u32[]{:S(2)}, u32[]{:S(2)}) collective-permute-start(bf16[128,2048]{1,0:T(8,128)(2,1)} %get-tuple-element.433), channel_id=1, source_target_pairs={{0,1},{1,0},{2,3},{3,2},{4,5},{5,4},{6,7},{7,6},{8,9},{9,8},{10,11... | collective-permute-start | bytes 1572872 | tf_op jit(solution)/shard_map/cond/branch_1_fun/ppermute | solution.py:46
  573.6 13.6 %collective-permute-start.41 = (bf16[128,2048]{1,0:T(8,128)(2,1)}, bf16[128,2048]{1,0:T(8,128)(2,1)}, u32[]{:S(2)}, u32[]{:S(2)}) collective-permute-start(bf16[128,2048]{1,0:T(8,128)(2,1)} %get-tuple-element.434), channel_id=1, source_target_pairs={{0,16},{8,24},{16,0},{24,8},{1,17},{9,25},{17,1},{25,9},{2,18},{10... | collective-permute-start | bytes 1572872 | tf_op jit(solution)/shard_map/cond/branch_1_fun/ppermute | solution.py:42
  589.3 23.4 %collective-permute-start.44 = (bf16[256,2048]{1,0:T(8,128)(2,1)S(1)}, bf16[256,2048]{1,0:T(8,128)(2,1)S(1)}, u32[]{:S(2)}, u32[]{:S(2)}) collective-permute-start(bf16[256,2048]{1,0:T(8,128)(2,1)S(1)} %pad_maximum_fusion.11), channel_id=1, source_target_pairs={{0,1},{1,0},{2,3},{3,2},{4,5},{5,4},{6,7},{7,6},{8,9},{9,8},{10,11... | collective-permute-start | bytes 3145736 | tf_op jit(solution)/shard_map/cond/branch_1_fun/ppermute | solution.py:46
  589.8 23.2 %collective-permute-start.43 = (bf16[256,2048]{1,0:T(8,128)(2,1)S(1)}, bf16[256,2048]{1,0:T(8,128)(2,1)S(1)}, u32[]{:S(2)}, u32[]{:S(2)}) collective-permute-start(bf16[256,2048]{1,0:T(8,128)(2,1)S(1)} %pad_maximum_fusion.10), channel_id=1, source_target_pairs={{0,16},{8,24},{16,0},{24,8},{1,17},{9,25},{17,1},{25,9},{2,18},{10... | collective-permute-start | bytes 3145736 | tf_op jit(solution)/shard_map/cond/branch_1_fun/ppermute | solution.py:42
  617.9 32.4 %all-to-all-start = ((bf16[8,64,2048]{2,1,0:T(8,128)(2,1)}), bf16[8,64,2048]{2,1,0:T(8,128)(2,1)S(1)}, u32[]{:S(2)}, u32[]{:S(2)}) async-start(bf16[8,64,2048]{2,1,0:T(8,128)(2,1)} %bitcast.89), calls=%async_computation | async-start | bytes 4194304 | tf_op jit(solution)/shard_map/cond/branch_1_fun/all_to_all | solution.py:870
  672.9 25.2 %collective-permute-start.49 = (bf16[64,2048]{1,0:T(8,128)(2,1)S(1)}, bf16[64,2048]{1,0:T(8,128)(2,1)S(1)}, u32[]{:S(2)}, u32[]{:S(2)}) collective-permute-start(bf16[64,2048]{1,0:T(8,128)(2,1)S(1)} %reshape.222), channel_id=1, source_target_pairs={{1,4},{2,1},{3,5},{4,2},{5,6},{6,3},{9,12},{10,9},{11,13},{12,10},... | collective-permute-start | bytes 786440 | tf_op jit(solution)/shard_map/ppermute | solution.py:51
  677.6 13.6 %all-to-all-start.1 = ((f32[32,1,128]{2,1,0:T(1,128)}), f32[32,1,128]{2,1,0:T(1,128)S(1)}, u32[]{:S(2)}, u32[]{:S(2)}) async-start(f32[32,1,128]{2,1,0:T(1,128)} %reshape.225), calls=%async_computation.4 | async-start | bytes 32768 | tf_op jit(solution)/shard_map/all_to_all | solution.py:904
  691.2 11.8 %all-to-all-start.2 = ((bf16[8,64,384]{2,1,0:T(8,128)(2,1)}), bf16[8,64,384]{2,1,0:T(8,128)(2,1)S(1)}, u32[]{:S(2)}, u32[]{:S(2)}) async-start(bf16[8,64,384]{2,1,0:T(8,128)(2,1)} %bitcast.46), calls=%async_computation.5 | async-start | bytes 786432 | tf_op jit(solution)/shard_map/all_to_all | solution.py:870
  (53 other events, 416.7 us)
Sparse Core Ops, SparseCore 0:
  29.7 54.2 all-gather.3
  89.9 81.3 all-gather.5
  173.5 150.0 all-gather.7
  366.6 77.7 reduce-scatter.3
  453.3 146.4 reduce-scatter.5
  617.9 53.7 reduce-scatter.7

commit v5 on v4

--- a/solution.py
+++ b/solution.py
@@ -78,8 +78,8 @@
     return gather_rest(own, x_part, y_part, (swap_y(x_part[:half]), swap_x(y_part[half:])))
 
 
-def halve_core(make):
-    sent = swap_core(make(1).astype(BF16))
+def halve_core(make, *others):
+    sent = lax.optimization_barrier((swap_core(make(1).astype(BF16)), *others))[0]
     return (make(0) + sent.astype(F32)).astype(BF16)
 
 
@@ -192,34 +192,27 @@
         o_at[...] = jnp.zeros_like(o_at)
         lse_at[...] = jnp.zeros_like(lse_at)
 
-        def one_head(h, carry):
+        def one_head(h):
             for i in range(n_parts):
                 at = slice(i * rows, (i + 1) * rows)
                 mask = lanes_of((rows, q_at.shape[1])) // HD == h
                 q_head = jnp.where(mask, q_at[at, :], 0)
                 scores = scores_at(q_head, k_at, i, rows)
-                top = scores[0].max(axis=-1, keepdims=True)
-                for part in scores[1:]:
-                    top = jnp.maximum(top, part.max(axis=-1, keepdims=True))
+                top = functools.reduce(jnp.maximum, scores).max(axis=-1, keepdims=True)
                 terms = [jnp.exp(part - top) for part in scores]
-                total = terms[0].sum(axis=-1, keepdims=True)
-                for part in terms[1:]:
-                    total = total + part.sum(axis=-1, keepdims=True)
+                total = sum(terms).sum(axis=-1, keepdims=True)
                 scale = 1.0 / total
-                mixed = jnp.zeros((rows, q_at.shape[1]), F32)
-                for j, part in enumerate(terms):
-                    mixed = mixed + jnp.dot(
-                        (part * scale).astype(BF16),
-                        v_at[j * rows : (j + 1) * rows, :],
-                        preferred_element_type=F32,
-                    )
+                mixed = sum(
+                    dot((part * scale).astype(BF16), v_at[j * rows : (j + 1) * rows, :])
+                    for j, part in enumerate(terms)
+                )
                 o_at[at, :] = jnp.where(mask, mixed, o_at[at, :])
                 lse_at[at, :] = jnp.where(
                     lanes_of((rows, lse_at.shape[1])) == h, top + jnp.log(total), lse_at[at, :]
                 )
-            return carry
-
-        lax.fori_loop(0, q_at.shape[1] // HD, one_head, 0)
+
+        for h in range(q_at.shape[1] // HD):
+            one_head(h)
 
     here = pl.ds(pl.multiple_of(step * rows, rows), rows)
     o_ref[...] = o_at[here, :].astype(BF16)
@@ -242,7 +235,7 @@
         dk_at[...] = jnp.zeros_like(dk_at)
         dv_at[...] = jnp.zeros_like(dv_at)
 
-        def one_head(h, carry):
+        def one_head(h):
             for i in range(n_parts):
                 at = slice(i * rows, (i + 1) * rows)
                 mask = lanes_of((rows, width)) // HD == h
@@ -256,9 +249,7 @@
                 scores = scores_at(q_head, k_at, i, rows)
                 probs = [jnp.exp(part - lse) for part in scores]
                 grads = [dot_nt(d_head, v_at[j * rows : (j + 1) * rows, :]) for j in range(i + 1)]
-                inner = jnp.zeros((rows, 1), F32)
-                for prob, grad in zip(probs, grads):
-                    inner = inner + jnp.sum(prob * grad, axis=-1, keepdims=True)
+                inner = sum(prob * grad for prob, grad in zip(probs, grads)).sum(axis=-1, keepdims=True)
                 dq = jnp.zeros((rows, width), F32)
                 for j, (prob, grad) in enumerate(zip(probs, grads)):
                     there = slice(j * rows, (j + 1) * rows)
@@ -267,9 +258,9 @@
                     dk_at[there, :] += dot_tn(d_score, q_head)
                     dv_at[there, :] += dot_tn(prob.astype(BF16), d_head)
                 dq_at[at, :] = jnp.where(mask, dq, dq_at[at, :])
-            return carry
-
-        lax.fori_loop(0, width // HD, one_head, 0)
+
+        for h in range(width // HD):
+            one_head(h)
 
     here = pl.ds(pl.multiple_of(step * rows, rows), rows)
     cosine, sine = cos_ref[...], -sin_ref[...]
@@ -599,6 +590,25 @@
     )(firsts, *weights)
 
 
+def deal_heads(spread, rows, q_cols, kv_cols):
+    team = spread.shape[0]
+    starts, widths = (0, q_cols, q_cols + kv_cols), (q_cols, kv_cols, kv_cols)
+
+    def kernel(in_ref, *out_refs):
+        for member in range(team):
+            values = in_ref[member, :rows, :].astype(F32)
+            for start, width, out_ref in zip(starts, widths, out_refs):
+                out_ref[:, member * width : (member + 1) * width] = values[:, start : start + width]
+
+    return pl.pallas_call(
+        kernel,
+        out_shape=tuple(jax.ShapeDtypeStruct((rows, team * width), F32) for width in widths),
+        compiler_params=pltpu.CompilerParams(vmem_limit_bytes=VMEM_BYTES),
+        cost_estimate=pl.CostEstimate(flops=0, bytes_accessed=6 * spread.size, transcendentals=0),
+        name="deal_heads",
+    )(spread)
+
+
 def deal(spread, places, block):
     _, rows, cols = spread.shape
     width = len(places) * block
@@ -652,8 +662,11 @@
 
     lines = n_z // n_seq
 
+    def turned(value, s_of):
+        return value ^ (s_of // 2 + s_of % 2 * 2)
+
     def hidden_plane(q, s_of):
-        return lax.rem(q % n_seq - s_of + n_seq, n_seq) * lines + q // n_seq
+        return turned(q % n_seq, s_of) * lines + q // n_seq
 
     def cols_ff(w_gate, w_up):
         firsts = [
@@ -671,14 +684,14 @@
         ]
 
     def rows_down(w_down):
-        turn = lax.rem(f // NY // lines + s, n_seq)
+        turn = turned(f // NY // lines, s)
         blocks = w_down.reshape(n_seq, ff_block, width)
         mine = lax.dynamic_index_in_dim(blocks, lax.rem(NY * turn + y, n_seq), 0, keepdims=False)
         theirs = lax.dynamic_index_in_dim(blocks, lax.rem(NY * turn + 1 - y, n_seq), 0, keepdims=False)
         pairs = []
         for si in range(n_seq):
             for zi in range(n_z):
-                holder = NY * ((zi // lines + si) % n_seq) // n_seq
+                holder = NY * turned(zi // lines, si) // n_seq
                 base = si * n_fsdp + zi * NY
                 pairs.append((base + holder, base + 1 - holder))
         sent = lax.ppermute(theirs, ("seq", "fsdp"), pairs)
@@ -809,15 +822,15 @@
         branch_of = halves(after(mid, sums), jnp.concatenate(blocks), False)
         branch_sent = branch_of(1).astype(BF16)
         grad_hn = fold_sides(*fold_corner(sums, branch_sent))
-        branch = (branch_of(0) + swap_core(branch_sent).astype(F32)).astype(BF16)
         grad_z2 = grad_hn * gain_two
         grad_res = cot_own.astype(F32) + inv_two * (
             grad_z2 - z_two * jnp.mean(grad_z2 * z_two, axis=-1, keepdims=True)
         )
         gain_terms = jnp.sum(grad_hn * z_two, axis=0)
-        return row_terms(hn, grad_both, n_seq, n_z), grad_res, gain_terms, branch
-
-    both_terms, grad_res, gain_two_terms, branch = stage(
+        terms = row_terms(hn, grad_both, n_seq, n_z)
+        return terms, grad_res, grad_res.astype(BF16), gain_terms, jnp.concatenate(blocks), branch_sent
+
+    both_terms, grad_res, da_own, gain_two_terms, wd, branch_sent = stage(
         feed_backward, grad_both, cot_own, hn, w_both, residual, gain_two, mid, wd
     )
     both_summed = scatter_z(both_terms)
@@ -829,80 +842,82 @@
             for zi in range(n_z)
             for yi in range(NY)
         ]
-        return move(summed, pairs).astype(F32)
+        return move(summed, pairs)
 
     def attention_backward(
-        grad_res, wo, wqkv, xn, qkv, cosine, sine, attn_rows, log_sums, x_own, gain_one, residual, branch
+        da_own, wo, wqkv, xn, qkv, cosine, sine, attn_rows, log_sums, mid, wd, branch_sent, down_summed
     ):
-        da_pieces = gather_plane(grad_res.astype(BF16))
+        branch = (dot(mid[:side], wd) + swap_core(branch_sent).astype(F32)).astype(BF16)
+        da_pieces = gather_plane(da_own, branch)
         own, x_part, y_part, corner = jnp.split(branch, 4)
         x_part, y_part, corner = lax.optimization_barrier((x_part, y_part, corner, *da_pieces))[:3]
         x_part, y_part, corner = swap_x(x_part), swap_y(y_part), swap_xy(corner)
         da, d_out = out_back(da_pieces, wo)
         grad_qkv = attend_back(member, qkv, d_out, log_sums, cosine, sine, n_seq)
         grad_qkv, x_part, y_part, corner = lax.optimization_barrier((grad_qkv, x_part, y_part, corner))
-        output = residual + sum(part.astype(F32) for part in (own, x_part, y_part, corner))
+        down_rows = to_owner(
+            after(down_summed, da), lambda si, zi, yi: turned(zi % n_seq, si) * n_fsdp + zi * NY + yi
+        )
+        out_terms = dot_rows(attn_rows, da).astype(BF16).reshape(w_rows * n_fsdp, -1)
+        sums = halve_core(halves(grad_qkv, wqkv, True), out_terms)
+        head_terms = jnp.concatenate([row_terms(xn, after(grad_qkv, sums), n_seq, n_z), out_terms], axis=1)
+        return head_terms, fold_corner(sums, head_terms), (own, x_part, y_part, corner), down_rows
+
+    head_terms, sums, branch, down_rows = stage(
+        attention_backward,
+        *(after(da_own, down_summed), wo, wqkv, xn, qkv, cosine, sine, attn_rows, log_sums),
+        *(mid, wd, branch_sent, down_summed),
+    )
+    head_summed = scatter_z(after(head_terms, both_summed))
+
+    def to_team(summed):
+        spread = lax.all_to_all(
+            summed, ("seq", "fsdp"), split_axis=0, concat_axis=0, tiled=True, axis_index_groups=plane_groups()
+        )
+        return spread.reshape(n_team, -1, spread.shape[-1])
+
+    places_of = []
+    for block in range(n_all):
+        plane, rest = divmod(block, n_team)
+        turn = rest // NY
+        member_of = next(si for si in range(n_seq) if turned(plane // lines, si) == turn)
+        places_of.append((member_of * NY + rest % NY, plane % lines * n_seq + turn))
+
+    def last_moves(sums, x_own, grad_res, gain_one, gain_two_terms, both_summed, residual, branch, down_rows):
         z_one, inv_one = normed(x_own)
-        grad_xn = scatter_plane(halves(grad_qkv, wqkv, True))
+        grad_xn = fold_sides(*sums)
+        spread = to_team(after(both_summed, inv_one))
         grad_z1 = grad_xn * gain_one
         grad_x = grad_res + inv_one * (
             grad_z1 - z_one * jnp.mean(grad_z1 * z_one, axis=-1, keepdims=True)
         )
-        head_terms = jnp.concatenate(
-            [
-                row_terms(xn, grad_qkv, n_seq, n_z),
-                dot_rows(attn_rows, da).astype(BF16).reshape(w_rows * n_fsdp, -1),
-            ],
-            axis=1,
-        )
-        return head_terms, grad_x.astype(BF16), jnp.sum(grad_xn * z_one, axis=0), output.astype(BF16)
-
-    head_terms, grad_x, gain_one_terms, output = stage(
-        attention_backward,
-        *(after(grad_res, down_summed), wo, wqkv, xn, qkv, cosine, sine, attn_rows, log_sums, x_own),
-        *(gain_one, residual, branch),
+        gain_terms = jnp.stack([jnp.sum(grad_xn * z_one, axis=0), gain_two_terms])
+        gain_terms = gain_terms.reshape(2, n_seq, n_z, NY, out_rows).transpose(2, 1, 3, 0, 4)
+        gain_terms = gain_terms.reshape(n_z, n_team, 2 * out_rows)
+        output = (residual + sum(part.astype(F32) for part in branch)).astype(BF16)
+        w_both_grad = deal(spread, places_of, ff_block)
+        return grad_x.astype(BF16), gain_terms, output, down_rows.astype(F32), *w_both_grad
+
+    grad_x, gain_terms, output, w_down_grad, w_gate_grad, w_up_grad = stage(
+        last_moves, sums, x_own, grad_res, gain_one, gain_two_terms, both_summed, residual, branch, down_rows
     )
     output = output.reshape(tokens.shape)
     tokens_grad = grad_x.reshape(tokens.shape)
-    head_summed = scatter_z(after(head_terms, both_summed))
-
-    def to_team(summed):
-        spread = lax.all_to_all(
-            summed, ("seq", "fsdp"), split_axis=0, concat_axis=0, tiled=True, axis_index_groups=plane_groups()
-        )
-        return spread.reshape(n_team, out_rows, -1)
-
-    places_of = []
-    for block in range(n_all):
-        plane, rest = divmod(block, n_team)
-        turn = rest // NY
-        places_of.append(
-            ((turn - plane // lines) % n_seq * NY + rest % NY, plane % lines * n_seq + turn)
-        )
-
-    def rows_to_owners(down_summed, both_summed):
-        spread = to_team(both_summed)
-        w_down_grad = to_owner(
-            down_summed, lambda si, zi, yi: (zi - si) % n_seq * n_fsdp + zi * NY + yi
-        )
-        return w_down_grad, *deal(spread, places_of, ff_block)
-
-    w_down_grad, w_gate_grad, w_up_grad = stage(rows_to_owners, down_summed, both_summed)
-    head_summed = after(head_summed, w_gate_grad)
-
+    z = f // NY
+    gain_sums = lax.dynamic_index_in_dim(gain_terms, z, 0, keepdims=False)
+    for hop in range(1, n_z):
+        term = lax.dynamic_index_in_dim(gain_terms, lax.rem(z + hop, n_z), 0, keepdims=False)
+        pairs = [(i, (i + hop * NY) % n_fsdp) for i in range(n_fsdp)]
+        gain_sums = gain_sums + lax.ppermute(term, "fsdp", pairs)
+    head_summed, gain_sums = lax.optimization_barrier((head_summed, gain_sums))
     w_o_grad = to_owner(
         head_summed[:, head_cols:].reshape(-1, width), lambda si, zi, yi: (si * NY + yi) * n_z + zi
-    )
-    spread = to_team(head_summed[:, :head_cols]).astype(F32).transpose(1, 0, 2)
-    w_q_grad = spread[..., :q_cols].reshape(out_rows, q_width)
-    w_k_grad = spread[..., q_cols : q_cols + kv_cols].reshape(out_rows, kv_width)
-    w_v_grad = spread[..., q_cols + kv_cols :].reshape(out_rows, kv_width)
-
-    gain_terms = after(jnp.stack([gain_one_terms, gain_two_terms]), head_summed)
-    gain_terms = gain_terms.reshape(2, n_all, out_rows).transpose(1, 0, 2)
-    gain_sums = jnp.sum(
-        lax.all_to_all(gain_terms, ("seq", "fsdp"), split_axis=0, concat_axis=0, tiled=True), axis=0
-    )
+    ).astype(F32)
+    gain_sums = jnp.pad(gain_sums[:, None].astype(BF16), ((0, 0), (0, 15), (0, head_cols - 2 * out_rows)))
+    head_summed = head_summed[:, :head_cols].reshape(n_team, out_rows, head_cols)
+    spread = to_team(jnp.concatenate([head_summed, gain_sums], axis=1).reshape(-1, head_cols))
+    gain_sums = jnp.sum(spread[:, out_rows, : 2 * out_rows].astype(F32), axis=0).reshape(2, out_rows)
+    w_q_grad, w_k_grad, w_v_grad = deal_heads(spread, out_rows, q_cols, kv_cols)
     return (
         output,
         tokens_grad,

time: 723 us -> 696 us (0.963)
  waiting for transfers between devices: 279 us -> 250 us
  other arithmetic: 44 us -> 59 us
  matrix products: 68.2 us -> 76.7 us
    ppermute x16, waiting for transfers between devices: 119 us -> 25.8 us  [swap_y(): lax.ppermute(value, 'fsdp', [(i, i ^ 1) for i in range(lax.axis_size('fsd...]
    ppermute x16, waiting for transfers between devices: 38.7 us -> 119 us  [swap_x(): lax.ppermute(value, 'seq', [(i, i ^ 2) for i in range(lax.axis_size('seq'...]
    reduce_scatter x3, waiting for transfers between devices: 19.2 us -> 0.3 us  [scatter_z(): lax.psum_scatter(terms, 'fsdp', scatter_dimension=0, tiled=True, axis_ind...]
    convert_element_type x3 -> x5, other arithmetic: 6.01 us -> 16.3 us  [the longest x2 9.81 us: halve_core(): return (make(0) + sent.astype(F32)).astype(BF16)]
    all_to_all x1 -> x0, starting transfers between devices: 8.93 us -> none  [shards(): lax.all_to_all(gain_terms, ('seq', 'fsdp'), split_axis=0, concat_axis=0,...]
    ppermute x4, waiting for transfers between devices: 6.85 us -> 15.5 us  [move(): lax.ppermute(value, ('seq', 'fsdp'), [p for p in pairs if p[0] != p[1]])]
    cond x78 -> x64, local copies, waits for them, and re-layouts: 15.1 us -> 13.5 us
  transfers between devices with their start and end apart: 59 -> 61, of which waited for: 40 -> 40; matrix products, arithmetic and copies ran while one was open for 19% -> 22% of each run, Pallas kernels for 19% -> 18%
where the time goes in v5:
time: 696 us; the launch traced here: 689 us
  waiting for transfers between devices  250 us (36%)
  Pallas kernels  154 us (22%)
  starting transfers between devices  80.1 us (12%)
  matrix products  76.7 us (11%)
  other arithmetic  59 us (8%)
  local copies, waits for them, and re-layouts  50.7 us (7%)
  between operations  15.7 us (2%)
    ppermute x16, waiting for transfers between devices, swap_x(): lax.ppermute(value, 'seq', [(i, i ^ 2) for i in range(lax.axis_size('seq'...  119 us
    pallas_call x4, Pallas kernels, pieces_call(): pl.pallas_call(kernel, out_shape=tuple((jax.ShapeDtypeStruct((blocks * ro...  65.3 us
    dot_general x4, matrix products, dot_cols(): lax.dot_general(left, right, (((1,), (1,)), ((), ())), preferred_element_...  36.1 us
    pallas_call x2, Pallas kernels, row_terms(): pl.pallas_call(kernel, out_shape=jax.ShapeDtypeStruct((n_planes, n_blocks...  30.9 us
    pallas_call x1, Pallas kernels, attend_back(): pl.pallas_call(functools.partial(attend_back_kernel, n_parts), out_shape=...  30.6 us
    ppermute x13, waiting for transfers between devices, swap_core(): lax.ppermute(value, 'seq', [(i, i ^ 1) for i in range(lax.axis_size('seq'...  28.9 us
    ppermute x13, starting transfers between devices, swap_core(): lax.ppermute(value, 'seq', [(i, i ^ 1) for i in range(lax.axis_size('seq'...  27.3 us
    ppermute x16, waiting for transfers between devices, swap_y(): lax.ppermute(value, 'fsdp', [(i, i ^ 1) for i in range(lax.axis_size('fsd...  25.8 us
  transfers between devices with their start and end apart: 61, of which 40 were waited for; matrix products, arithmetic and copies ran while one was open for 22% of the time, Pallas kernels for 18%

profile of v5, /device:TPU:11, one launch (start us, length us, event | category | flops | bytes accessed | tf_op | source)
XLA Modules:
  0.0 688.7 jit_solution(12589588723070339672)
XLA Ops:
  14.1 4.2 collective-permute-start.46
  25.1 4.5 collective-permute-done.46
  31.9 58.9 %conditional.6 = (bf16[256,2048]{1,0:T(8,128)(2,1)}, bf16[768,2048]{1,0:T(8,128)(2,1)}, bf16[256,2048]{1,0:T(8,128)(2,1)}, bf16[768,2048]{1,0:T(8,128)(2,1)}, bf...) conditional(s32[]{:T(128)} %bitcast.29, () %tuple.91, ...), branch_computations={%region_0.1_spmd, %region_1.2_spmd} | conditional | flops 10881163 | bytes 50881816 | solution.py:726
  34.9 19.5 %collective-permute-done = bf16[256,2048]{1,0:T(8,128)(2,1)} collective-permute-done((bf16[256,2048]{1,0:T(8,128)(2,1)S(1)}, bf16[256,2048]{1,0:T(8,128)(2,1)}, u32[]{:S(2)}, u32[]{:S(2)}) %collective-permute-start) | collective-permute-done | bytes 1048608 | tf_op jit(solution)/shard_map/cond/branch_1_fun/ppermute | solution.py:42
  55.6 13.0 %collective-permute-done.3 = bf16[256,2048]{1,0:T(8,128)(2,1)S(1)} collective-permute-done((bf16[256,2048]{1,0:T(8,128)(2,1)S(1)}, bf16[256,2048]{1,0:T(8,128)(2,1)S(1)}, u32[]{:S(2)}, u32[]{:S(2)}) %collective-permute-start.3) | collective-permute-done | bytes 1048608 | tf_op jit(solution)/shard_map/cond/branch_1_fun/ppermute | solution.py:697
  76.5 7.0 %collective-permute-start.5 = (bf16[768,2048]{1,0:T(8,128)(2,1)}, bf16[768,2048]{1,0:T(8,128)(2,1)}, u32[]{:S(2)}, u32[]{:S(2)}) collective-permute-start(bf16[768,2048]{1,0:T(8,128)(2,1)} %pad_maximum_fusion), channel_id=1, source_target_pairs={{0,8},{8,0},{16,24},{24,16},{1,9},{9,1},{17,25},{25,17},{2,10},{10... | collective-permute-start | bytes 9437192 | tf_op jit(solution)/shard_map/cond/branch_1_fun/ppermute | solution.py:38
  85.6 4.7 collective-permute-done.4
  92.1 83.1 %conditional.7 = (bf16[2048,2048]{1,0:T(8,128)(2,1)}, f32[2048,384]{1,0:T(8,128)}, bf16[2048,256]{1,0:T(8,128)(2,1)}, f32[2048,128]{1,0:T(8,128)S(1)}, bf16[2048...) conditional(s32[]{:T(128)} %bitcast.29, () %tuple.88, ...), branch_computations={%region_2.3_spmd, %region_3.4_spmd} | conditional | flops 9681506304 | bytes 158417984 | solution.py:726
  103.4 13.9 %project.1 = (bf16[2048,2048]{1,0:T(8,128)(2,1)}, f32[2048,384]{1,0:T(8,128)}) custom-call(bf16[256,2048]{1,0:T(8,128)(2,1)} %get-tuple-element.143.refs_0_, bf16[768,2048]{1,0:T(8,128)(2,1)} %get-tuple-element.144.refs_1_, bf16[256,2048]{1,0:T(8,128)(2,1)} %get-tuple-element.145.refs_2_, bf16[768,2048]{1,0:T(8,128)(2,1)} %get-tuple-element.146.refs_3_, ...), custom_call_target="tpu_custom_call" | custom-call | flops 3221225472 | bytes 22634496 | tf_op jit(solution)/shard_map/cond/branch_1_fun/project/pallas_call | solution.py:412
  117.3 20.9 %attend.1 = (bf16[2048,256]{1,0:T(8,128)(2,1)}, f32[2048,128]{1,0:T(8,128)}) custom-call(s32[1]{0:T(128)} %get-tuple-element.150.member, f32[2048,384]{1,0:T(8,128)} %get-tuple-element.526.refs_0_.refs_1_.refs_2_.refs_3_, f32[2048,384]{1,0:T(8,128)} %get-tuple-element.526.refs_0_.refs_1_.refs_2_.refs_3_, ...), custom_call_target="tpu_custom_call" | custom-call | flops 4294967296 | bytes 6291456 | tf_op jit(solution)/shard_map/cond/branch_1_fun/attend/pallas_call | solution.py:305
  147.4 4.3 collective-permute-done.23
  162.9 7.1 %collective-permute-done.24 = bf16[128,2048]{1,0:T(8,128)(2,1)} collective-permute-done((bf16[128,2048]{1,0:T(8,128)(2,1)}, bf16[128,2048]{1,0:T(8,128)(2,1)}, u32[]{:S(2)}, u32[]{:S(2)}) %collective-permute-start.24) | collective-permute-done | bytes 524320 | tf_op jit(solution)/shard_map/cond/branch_1_fun/ppermute | solution.py:42
  176.2 125.5 %conditional.8 = (f32[256,2048]{1,0:T(8,128)S(1)}, bf16[256,2048]{1,0:T(8,128)(2,1)}, bf16[768,2048]{1,0:T(8,128)(2,1)}, bf16[256,2048]{1,0:T(8,128)(2,1)}, bf16...) conditional(s32[]{:T(128)} %bitcast.29, () %tuple.87, ...), branch_computations={%region_4.5_spmd, %region_5.7_spmd} | conditional | flops 8596226048 | bytes 173028096 | solution.py:726
  177.9 21.7 %collective-permute-done.8 = bf16[256,2048]{1,0:T(8,128)(2,1)S(1)} collective-permute-done((bf16[256,2048]{1,0:T(8,128)(2,1)}, bf16[256,2048]{1,0:T(8,128)(2,1)S(1)}, u32[]{:S(2)}, u32[]{:S(2)}) %collective-permute-start.8) | collective-permute-done | bytes 1048608 | tf_op jit(solution)/shard_map/cond/branch_1_fun/ppermute | solution.py:42
  207.1 19.1 %collective-permute-done.16 = bf16[256,2048]{1,0:T(8,128)(2,1)S(1)} collective-permute-done((bf16[256,2048]{1,0:T(8,128)(2,1)S(1)}, bf16[256,2048]{1,0:T(8,128)(2,1)S(1)}, u32[]{:S(2)}, u32[]{:S(2)}) %collective-permute-start.16) | collective-permute-done | bytes 1048608 | tf_op jit(solution)/shard_map/cond/branch_1_fun/ppermute | solution.py:42
  228.9 19.7 %collective-permute-done.10 = bf16[256,2048]{1,0:T(8,128)(2,1)S(1)} collective-permute-done((bf16[256,2048]{1,0:T(8,128)(2,1)}, bf16[256,2048]{1,0:T(8,128)(2,1)S(1)}, u32[]{:S(2)}, u32[]{:S(2)}) %collective-permute-start.10) | collective-permute-done | bytes 1048608 | tf_op jit(solution)/shard_map/cond/branch_1_fun/ppermute | solution.py:42
  251.4 9.3 %collective-permute-done.18 = bf16[128,2048]{1,0:T(8,128)(2,1)S(1)} collective-permute-done((bf16[128,2048]{1,0:T(8,128)(2,1)S(1)}, bf16[128,2048]{1,0:T(8,128)(2,1)S(1)}, u32[]{:S(2)}, u32[]{:S(2)}) %collective-permute-start.18) | collective-permute-done | bytes 524320 | tf_op jit(solution)/shard_map/cond/branch_1_fun/ppermute | solution.py:46
  260.8 7.2 %collective-permute-start.21 = (bf16[768,2048]{1,0:T(8,128)(2,1)S(1)}, bf16[768,2048]{1,0:T(8,128)(2,1)S(1)}, u32[]{:S(2)}, u32[]{:S(2)}) collective-permute-start(bf16[768,2048]{1,0:T(8,128)(2,1)S(1)} %constant_dynamic-update-slice_fusion.4.refs_1_), channel_id=1, source_target_pairs={{0,8},{8,0},{16,24},{24,16},{1,9},{9,1},{17,25},{25,17},{2,10},{10... | collective-permute-start | bytes 9437192 | tf_op jit(solution)/shard_map/cond/branch_1_fun/ppermute | solution.py:38
  277.9 7.6 %collective-permute-done.20.refs_2_ = bf16[256,2048]{1,0:T(8,128)(2,1)S(1)} collective-permute-done((bf16[256,2048]{1,0:T(8,128)(2,1)S(1)}, bf16[256,2048]{1,0:T(8,128)(2,1)S(1)}, u32[]{:S(2)}, u32[]{:S(2)}) %collective-permute-start.20) | collective-permute-done | bytes 1048608 | tf_op jit(solution)/shard_map/cond/branch_1_fun/ppermute | solution.py:38
  287.2 14.3 %down_back.1 = (bf16[2048,2048]{1,0:T(8,128)(2,1)}, f32[2048,1024]{1,0:T(8,128)}) custom-call(bf16[256,2048]{1,0:T(8,128)(2,1)S(1)} %copy-done.27, bf16[768,2048]{1,0:T(8,128)(2,1)S(1)} %constant_dynamic-update-slice_fusion.4.refs_1_, bf16[256,2048]{1,0:T(8,128)(2,1)S(1)} %collective-permute-done.20.refs_2_, bf16[768,2048]{1,0:T(8,128)(2,1)} %copy-done.32, ...), custom_call_target="tpu_custom_call" | custom-call | flops 8589934592 | bytes 29360144 | tf_op jit(solution)/shard_map/cond/branch_1_fun/down_back/pallas_call | solution.py:412
  301.7 25.0 %all-gather.8.cloned.1.call-done.refs_4_ = bf16[2048,2048]{1,0:T(8,128)(2,1)} async-done(((bf16[512,2048]{1,0:T(8,128)(2,1)}), bf16[2048,2048]{1,0:T(8,128)(2,1)}) %all-gather.8.cloned.1.call-update) | async-done | bytes 8388624 | tf_op jit(solution)/shard_map/all_gather | solution.py:122
  326.7 27.9 %feed.1 = (bf16[2048,2048]{1,0:T(8,128)(2,1)}, bf16[2048,1024]{1,0:T(8,128)(2,1)S(1)}, bf16[2048,2048]{1,0:T(8,128)(2,1)}) custom-call(bf16[256,2048]{1,0:T(8,128)(2,1)} %get-tuple-element.332.refs_0_, bf16[768,2048]{1,0:T(8,128)(2,1)} %get-tuple-element.333.refs_1_, bf16[256,2048]{1,0:T(8,128)(2,1)} %get-tuple-element.334.refs_2_, ...), custom_call_target="tpu_custom_call" | custom-call | flops 17179869184 | bytes 46137344 | tf_op jit(solution)/shard_map/feed/pallas_call | solution.py:412
  356.7 12.9 %convolution_convert_fusion.4 = bf16[1024,2048]{1,0:T(8,128)(2,1)} fusion(bf16[2048,1024]{1,0:T(8,128)(2,1)S(1)} %get-tuple-element.342, bf16[2048,2048]{1,0:T(8,128)(2,1)} %get-tuple-element.344), kind=kOutput, calls=%fused_computation.97 | convolution fusion | flops 8592031744 | bytes 16777216 | tf_op jit(solution)/shard_map/dot_general | solution.py:26
  369.7 86.0 %conditional.9 = (bf16[2048,2048]{1,0:T(8,128)(2,1)}, f32[256,2048]{1,0:T(8,128)}, bf16[256,2048]{1,0:T(8,128)(2,1)}, f32[2048]{0:T(1024)S(1)}, bf16[1024,2048]{1,0:T(8,128)(2,1)}, /*index=5*/bf16[1024,2048]{1,0:T(8,128)(2,1)}) conditional(s32[]{:T(128)} %bitcast.29, () %tuple.86, (bf16[2048,2048]{1,0:T(8,128)(2,1)}, bf16[2048,2048]{1,0:T(8,128)(2,1)}, ...), branch_computations={%region_7.8_spmd, %region_8.12_spmd} | conditional | flops 38701887488 | bytes 244352624 | solution.py:726
  369.8 14.2 %fusion.8 = bf16[1024,2048]{1,0:T(8,128)(2,1)} fusion(bf16[2048,2048]{1,0:T(8,128)(2,1)} %get-tuple-element.183, bf16[2048,2048]{1,0:T(8,128)(2,1)} %get-tuple-element.180.right_ref), kind=kOutput, calls=%fused_computation.41 | convolution fusion | flops 8592031744 | bytes 16777216 | tf_op jit(solution)/shard_map/cond/branch_1_fun/dot_general | solution.py:30
  393.9 11.0 %fusion.6 = f32[1024,2048]{1,0:T(8,128)} fusion(bf16[2048,2048]{1,0:T(8,128)(2,1)S(1)} %bitcast.115, bf16[2048,2048]{1,0:T(8,128)(2,1)S(1)} %copy-done.35), kind=kOutput, calls=%fused_computation.39 | convolution fusion | flops 8589934592 | bytes 20971520 | tf_op jit(solution)/shard_map/cond/branch_1_fun/dot_general | solution.py:30
  404.9 6.1 add_convert_fusion.3
  413.3 8.7 %convolution_convert_fusion.1 = bf16[1024,2048]{1,0:T(8,128)(2,1)} fusion(bf16[1024,2048]{1,0:T(8,128)(2,1)} %pad_maximum_fusion.4, bf16[2048,1024]{1,0:T(8,128)(2,1)S(1)} %copy-done.34), kind=kOutput, calls=%fused_computation.42 | convolution fusion | flops 4297064448 | bytes 10485760 | tf_op jit(solution)/shard_map/cond/branch_1_fun/dot_general | solution.py:34
  428.0 23.6 %row_terms.2 = bf16[4,4,128,2048]{3,2,1,0:T(8,128)(2,1)} custom-call(bf16[2048,2048]{1,0:T(8,128)(2,1)} %get-tuple-element.179.left_ref, bf16[2048,2048]{1,0:T(8,128)(2,1)} %get-tuple-element.180.right_ref), custom_call_target="tpu_custom_call" | custom-call | flops 17179869184 | bytes 25165824 | tf_op jit(solution)/shard_map/cond/branch_1_fun/row_terms/pallas_call | solution.py:535
  457.0 143.7 %conditional.10 = (bf16[2048,640]{1,0:T(8,128)(2,1)}, bf16[256,2048]{1,0:T(8,128)(2,1)S(1)}, bf16[256,2048]{1,0:T(8,128)(2,1)}, bf16[256,2048]{1,0:T(8,128)(2,1)...) conditional(s32[]{:T(128)} %bitcast.29, () %tuple.85, ...), branch_computations={%region_13.14_spmd, %region_14.15_spmd} | conditional | flops 12921077760 | bytes 244188128 | solution.py:726
  458.9 6.6 collective-permute-done.33
  465.5 7.3 %add_convert_fusion.7 = bf16[1024,2048]{1,0:T(8,128)(2,1)S(1)} fusion(bf16[1024,2048]{1,0:T(8,128)(2,1)S(1)} %collective-permute-done.33, bf16[1024,2048]{1,0:T(8,128)(2,1)} %get-tuple-element.199, bf16[2048,1024]{1,0:T(8,128)(2,1)} %get-tuple-element.198), kind=kOutput, calls=%fused_computation.60 | convolution fusion | flops 4301258752 | bytes 14680064 | tf_op jit(solution)/shard_map/cond/branch_1_fun/dot_general | solution.py:34
  472.9 10.8 %collective-permute-done.31 = bf16[256,2048]{1,0:T(8,128)(2,1)S(1)} collective-permute-done((bf16[256,2048]{1,0:T(8,128)(2,1)}, bf16[256,2048]{1,0:T(8,128)(2,1)S(1)}, u32[]{:S(2)}, u32[]{:S(2)}) %collective-permute-start.31) | collective-permute-done | bytes 1048608 | tf_op jit(solution)/shard_map/cond/branch_1_fun/ppermute | solution.py:42
  485.5 10.8 %collective-permute-done.34 = bf16[128,2048]{1,0:T(8,128)(2,1)S(1)} collective-permute-done((bf16[128,2048]{1,0:T(8,128)(2,1)S(1)}, bf16[128,2048]{1,0:T(8,128)(2,1)S(1)}, u32[]{:S(2)}, u32[]{:S(2)}) %collective-permute-start.34) | collective-permute-done | bytes 524320 | tf_op jit(solution)/shard_map/cond/branch_1_fun/ppermute | solution.py:46
  500.8 4.6 collective-permute-done.36.refs_2_
  511.9 9.2 %out_back.1 = (bf16[2048,2048]{1,0:T(8,128)(2,1)}, bf16[2048,256]{1,0:T(8,128)(2,1)S(1)}) custom-call(bf16[256,2048]{1,0:T(8,128)(2,1)} %get-tuple-element.197.refs_0_, bf16[768,2048]{1,0:T(8,128)(2,1)S(1)} %copy-done.3, bf16[256,2048]{1,0:T(8,128)(2,1)S(1)} %collective-permute-done.36.refs_2_, bf16[768,2048]{1,0:T(8,128)(2,1)} %copy-done.24, ...), custom_call_target="tpu_custom_call" | custom-call | flops 524288 | bytes 294912 | tf_op jit(solution)/shard_map/cond/branch_1_fun/out_back/pallas_call | solution.py:412
  521.1 30.6 %attend_back.1.right_ref = bf16[2048,384]{1,0:T(8,128)(2,1)S(1)} custom-call(s32[1]{0:T(128)} %get-tuple-element.195.member, f32[2048,384]{1,0:T(8,128)} %get-tuple-element.196.refs_0_.refs_1_.refs_2_.refs_3_, f32[2048,384]{1,0:T(8,128)} %get-tuple-element.196.refs_0_.refs_1_.refs_2_.refs_3_, f32[2048,384]{1,0:T(8,128)} %get-tuple-element.196.refs_0_.refs_1_.refs_2_.refs_3_, ...), custom_call_target="tpu_custom_call" | custom-call | flops 8388608 | bytes 98304 | tf_op jit(solution)/shard_map/cond/branch_1_fun/attend_back/pallas_call | solution.py:341
  553.7 5.8 convolution_convert_fusion.2
  562.8 6.2 fusion.12
  571.0 6.0 collective-permute-done.44
  579.3 5.0 add_convert_fusion.6
  586.0 7.3 %row_terms.3 = bf16[4,4,128,384]{3,2,1,0:T(8,128)(2,1)S(1)} custom-call(bf16[2048,2048]{1,0:T(8,128)(2,1)} %get-tuple-element.194.left_ref, bf16[2048,384]{1,0:T(8,128)(2,1)S(1)} %copy-done.5), custom_call_target="tpu_custom_call" | custom-call | flops 3221225472 | bytes 11534336 | tf_op jit(solution)/shard_map/cond/branch_1_fun/row_terms/pallas_call | solution.py:535
  601.0 51.5 %conditional.11 = (f32[4,8,128]{2,1,0:T(8,128)S(1)}, f32[256,2048]{1,0:T(8,128)}, f32[64,8192]{1,0:T(8,128)}, f32[64,8192]{1,0:T(8,128)}, bf16[1,256,2048]{2,1,0:T(8,128)(2,1)}, /*index=5*/bf16[1,256,2048]{2,1,0:T(8,128)(2,1)}) conditional(s32[]{:T(128)} %bitcast.29, () %tuple.84, (bf16[256,2048]{1,0:T(8,128)(2,1)S(1)}, ...), branch_computations={%region_16.17_spmd, %region_17.21_spmd} | conditional | flops 19925248 | bytes 64128272 | solution.py:726
  603.7 4.8 all-to-all-start
  615.9 9.6 %collective-permute-done.6 = bf16[256,2048]{1,0:T(8,128)(2,1)} collective-permute-done((bf16[256,2048]{1,0:T(8,128)(2,1)}, bf16[256,2048]{1,0:T(8,128)(2,1)}, u32[]{:S(2)}, u32[]{:S(2)}) %collective-permute-start.6) | collective-permute-done | bytes 1048608 | tf_op jit(solution)/shard_map/cond/branch_1_fun/ppermute | solution.py:42
  629.0 4.6 fusion.30
  633.6 16.6 %all-to-all-done.in_ref = bf16[8,64,2048]{2,1,0:T(8,128)(2,1)S(1)} async-done(((bf16[8,64,2048]{2,1,0:T(8,128)(2,1)}), bf16[8,64,2048]{2,1,0:T(8,128)(2,1)S(1)}, u32[]{:S(2)}, u32[]{:S(2)}) %all-to-all-start) | async-done | bytes 2097184 | tf_op jit(solution)/shard_map/cond/branch_1_fun/all_to_all | solution.py:874
  664.5 7.5 %all-to-all-start.1 = ((bf16[8,80,384]{2,1,0:T(8,128)(2,1)}), bf16[8,80,384]{2,1,0:T(8,128)(2,1)S(1)}, u32[]{:S(2)}, u32[]{:S(2)}) async-start(bf16[8,80,384]{2,1,0:T(8,128)(2,1)} %fusion.32), calls=%async_computation.4 | async-start | bytes 983040 | tf_op jit(solution)/shard_map/all_to_all | solution.py:874
  (309 shorter events, 189.9 us)
Async XLA Ops:
  7.2 83.6 %all-gather.4.cloned.1.call-start = ((), (), s32[]{:S(2)}) async-start(), calls=%async_computation.5 | async-start | bytes 3379200 | tf_op jit(solution)/shard_map/all_gather | solution.py:122
  14.1 15.5 %collective-permute-start.46 = (bf16[64,2048]{1,0:T(8,128)(2,1)S(1)}, bf16[64,2048]{1,0:T(8,128)(2,1)S(1)}, u32[]{:S(2)}, u32[]{:S(2)}) collective-permute-start(bf16[64,2048]{1,0:T(8,128)(2,1)S(1)} %constant_dynamic-slice_fusion.10), channel_id=1, source_target_pairs={{8,2},{16,4},{24,6},{9,3},{17,5},{25,7},{2,8},{18,12},{26,14},{3,9... | collective-permute-start | bytes 786440 | tf_op jit(solution)/shard_map/ppermute | solution.py:51
  30.7 144.6 %all-gather.6.cloned.1.call-start = ((), (), s32[]{:S(2)}) async-start(), calls=%async_computation.6 | async-start | bytes 5242880 | tf_op jit(solution)/shard_map/all_gather | solution.py:122
  31.9 22.5 %collective-permute-start = (bf16[256,2048]{1,0:T(8,128)(2,1)S(1)}, bf16[256,2048]{1,0:T(8,128)(2,1)}, u32[]{:S(2)}, u32[]{:S(2)}) collective-permute-start(bf16[256,2048]{1,0:T(8,128)(2,1)S(1)} %get-tuple-element.506), channel_id=1, source_target_pairs={{0,16},{8,24},{16,0},{24,8},{1,17},{9,25},{17,1},{25,9},{2,18},{10... | collective-permute-start | bytes 3145736 | tf_op jit(solution)/shard_map/cond/branch_1_fun/ppermute | solution.py:42
  32.0 22.5 %collective-permute-start.1 = (bf16[256,2048]{1,0:T(8,128)(2,1)S(1)}, bf16[256,2048]{1,0:T(8,128)(2,1)}, u32[]{:S(2)}, u32[]{:S(2)}) collective-permute-start(bf16[256,2048]{1,0:T(8,128)(2,1)S(1)} %get-tuple-element.506), channel_id=1, source_target_pairs={{0,1},{1,0},{2,3},{3,2},{4,5},{5,4},{6,7},{7,6},{8,9},{9,8},{10,11... | collective-permute-start | bytes 3145736 | tf_op jit(solution)/shard_map/cond/branch_1_fun/ppermute | solution.py:46
  33.6 35.0 %collective-permute-start.3 = (bf16[256,2048]{1,0:T(8,128)(2,1)S(1)}, bf16[256,2048]{1,0:T(8,128)(2,1)S(1)}, u32[]{:S(2)}, u32[]{:S(2)}) collective-permute-start(bf16[256,2048]{1,0:T(8,128)(2,1)S(1)} %dynamic-slice_bitcast_fusion), channel_id=1, source_target_pairs={{0,1},{2,3},{5,4},{7,6},{9,8},{11,10},{12,13},{14,15},{16,17},{18,... | collective-permute-start | bytes 3145736 | tf_op jit(solution)/shard_map/cond/branch_1_fun/ppermute | solution.py:697
  54.5 18.9 %collective-permute-start.2 = (bf16[256,2048]{1,0:T(8,128)(2,1)}, bf16[256,2048]{1,0:T(8,128)(2,1)}, u32[]{:S(2)}, u32[]{:S(2)}) collective-permute-start(bf16[256,2048]{1,0:T(8,128)(2,1)} %collective-permute-done.1), channel_id=1, source_target_pairs={{0,16},{8,24},{16,0},{24,8},{1,17},{9,25},{17,1},{25,9},{2,18},{10... | collective-permute-start | bytes 3145736 | tf_op jit(solution)/shard_map/cond/branch_1_fun/ppermute | solution.py:42
  76.5 14.2 %collective-permute-start.5 = (bf16[768,2048]{1,0:T(8,128)(2,1)}, bf16[768,2048]{1,0:T(8,128)(2,1)}, u32[]{:S(2)}, u32[]{:S(2)}) collective-permute-start(bf16[768,2048]{1,0:T(8,128)(2,1)} %pad_maximum_fusion), channel_id=1, source_target_pairs={{0,8},{8,0},{16,24},{24,16},{1,9},{9,1},{17,25},{25,17},{2,10},{10... | collective-permute-start | bytes 9437192 | tf_op jit(solution)/shard_map/cond/branch_1_fun/ppermute | solution.py:38
  90.8 235.8 %all-gather.8.cloned.1.call-start = ((), (), s32[]{:S(2)}) async-start(), calls=%async_computation.7 | async-start | bytes 10485760 | tf_op jit(solution)/shard_map/all_gather | solution.py:122
  95.7 42.5 %collective-permute-start.22 = (bf16[256,2048]{1,0:T(8,128)(2,1)}, bf16[256,2048]{1,0:T(8,128)(2,1)}, u32[]{:S(2)}, u32[]{:S(2)}) collective-permute-start(bf16[256,2048]{1,0:T(8,128)(2,1)} %get-tuple-element.159), channel_id=1, source_target_pairs={{0,1},{1,0},{2,3},{3,2},{4,5},{5,4},{6,7},{7,6},{8,9},{9,8},{10,11... | collective-permute-start | bytes 3145736 | tf_op jit(solution)/shard_map/cond/branch_1_fun/ppermute | solution.py:46
  156.6 13.4 %collective-permute-start.24 = (bf16[128,2048]{1,0:T(8,128)(2,1)}, bf16[128,2048]{1,0:T(8,128)(2,1)}, u32[]{:S(2)}, u32[]{:S(2)}) collective-permute-start(bf16[128,2048]{1,0:T(8,128)(2,1)} %get-tuple-element.454), channel_id=1, source_target_pairs={{0,16},{8,24},{16,0},{24,8},{1,17},{9,25},{17,1},{25,9},{2,18},{10... | collective-permute-start | bytes 1572872 | tf_op jit(solution)/shard_map/cond/branch_1_fun/ppermute | solution.py:42
  157.6 13.1 %collective-permute-start.25 = (bf16[128,2048]{1,0:T(8,128)(2,1)}, bf16[128,2048]{1,0:T(8,128)(2,1)}, u32[]{:S(2)}, u32[]{:S(2)}) collective-permute-start(bf16[128,2048]{1,0:T(8,128)(2,1)} %get-tuple-element.453), channel_id=1, source_target_pairs={{0,1},{1,0},{2,3},{3,2},{4,5},{5,4},{6,7},{7,6},{8,9},{9,8},{10,11... | collective-permute-start | bytes 1572872 | tf_op jit(solution)/shard_map/cond/branch_1_fun/ppermute | solution.py:46
  175.3 280.5 %reduce-scatter.4.cloned.1.call-start = ((), (), s32[]{:S(2)}) async-start(), calls=%async_computation.8 | async-start | bytes 5242880 | tf_op jit(solution)/shard_map/reduce_scatter | solution.py:126
  176.2 23.4 %collective-permute-start.8 = (bf16[256,2048]{1,0:T(8,128)(2,1)}, bf16[256,2048]{1,0:T(8,128)(2,1)S(1)}, u32[]{:S(2)}, u32[]{:S(2)}) collective-permute-start(bf16[256,2048]{1,0:T(8,128)(2,1)} %get-tuple-element.166), channel_id=1, source_target_pairs={{0,16},{8,24},{16,0},{24,8},{1,17},{9,25},{17,1},{25,9},{2,18},{10... | collective-permute-start | bytes 3145736 | tf_op jit(solution)/shard_map/cond/branch_1_fun/ppermute | solution.py:42
  176.7 23.2 %collective-permute-start.9 = (bf16[256,2048]{1,0:T(8,128)(2,1)}, bf16[256,2048]{1,0:T(8,128)(2,1)S(1)}, u32[]{:S(2)}, u32[]{:S(2)}) collective-permute-start(bf16[256,2048]{1,0:T(8,128)(2,1)} %get-tuple-element.167), channel_id=1, source_target_pairs={{0,1},{1,0},{2,3},{3,2},{4,5},{5,4},{6,7},{7,6},{8,9},{9,8},{10,11... | collective-permute-start | bytes 3145736 | tf_op jit(solution)/shard_map/cond/branch_1_fun/ppermute | solution.py:46
  204.1 22.0 %collective-permute-start.16 = (bf16[256,2048]{1,0:T(8,128)(2,1)S(1)}, bf16[256,2048]{1,0:T(8,128)(2,1)S(1)}, u32[]{:S(2)}, u32[]{:S(2)}) collective-permute-start(bf16[256,2048]{1,0:T(8,128)(2,1)S(1)} %copy-done.27), channel_id=1, source_target_pairs={{0,16},{8,24},{16,0},{24,8},{1,17},{9,25},{17,1},{25,9},{2,18},{10... | collective-permute-start | bytes 3145736 | tf_op jit(solution)/shard_map/cond/branch_1_fun/ppermute | solution.py:42
  205.2 21.8 %collective-permute-start.17 = (bf16[256,2048]{1,0:T(8,128)(2,1)S(1)}, bf16[256,2048]{1,0:T(8,128)(2,1)S(1)}, u32[]{:S(2)}, u32[]{:S(2)}) collective-permute-start(bf16[256,2048]{1,0:T(8,128)(2,1)S(1)} %copy-done.27), channel_id=1, source_target_pairs={{0,1},{1,0},{2,3},{3,2},{4,5},{5,4},{6,7},{7,6},{8,9},{9,8},{10,11... | collective-permute-start | bytes 3145736 | tf_op jit(solution)/shard_map/cond/branch_1_fun/ppermute | solution.py:46
  206.4 42.2 %collective-permute-start.10 = (bf16[256,2048]{1,0:T(8,128)(2,1)}, bf16[256,2048]{1,0:T(8,128)(2,1)S(1)}, u32[]{:S(2)}, u32[]{:S(2)}) collective-permute-start(bf16[256,2048]{1,0:T(8,128)(2,1)} %multiply_convert_fusion), channel_id=1, source_target_pairs={{0,16},{8,24},{16,0},{24,8},{1,17},{9,25},{17,1},{25,9},{2,18},{10... | collective-permute-start | bytes 3145736 | tf_op jit(solution)/shard_map/cond/branch_1_fun/ppermute | solution.py:42
  206.8 42.6 %collective-permute-start.11 = (bf16[256,2048]{1,0:T(8,128)(2,1)}, bf16[256,2048]{1,0:T(8,128)(2,1)S(1)}, u32[]{:S(2)}, u32[]{:S(2)}) collective-permute-start(bf16[256,2048]{1,0:T(8,128)(2,1)} %multiply_convert_fusion), channel_id=1, source_target_pairs={{0,1},{1,0},{2,3},{3,2},{4,5},{5,4},{6,7},{7,6},{8,9},{9,8},{10,11... | collective-permute-start | bytes 3145736 | tf_op jit(solution)/shard_map/cond/branch_1_fun/ppermute | solution.py:46
  227.0 33.7 %collective-permute-start.18 = (bf16[128,2048]{1,0:T(8,128)(2,1)S(1)}, bf16[128,2048]{1,0:T(8,128)(2,1)S(1)}, u32[]{:S(2)}, u32[]{:S(2)}) collective-permute-start(bf16[128,2048]{1,0:T(8,128)(2,1)S(1)} %slice.157), channel_id=1, source_target_pairs={{0,1},{1,0},{2,3},{3,2},{4,5},{5,4},{6,7},{7,6},{8,9},{9,8},{10,11... | collective-permute-start | bytes 1572872 | tf_op jit(solution)/shard_map/cond/branch_1_fun/ppermute | solution.py:46
  228.3 32.4 %collective-permute-start.19 = (bf16[128,2048]{1,0:T(8,128)(2,1)S(1)}, bf16[128,2048]{1,0:T(8,128)(2,1)S(1)}, u32[]{:S(2)}, u32[]{:S(2)}) collective-permute-start(bf16[128,2048]{1,0:T(8,128)(2,1)S(1)} %slice.158), channel_id=1, source_target_pairs={{0,16},{8,24},{16,0},{24,8},{1,17},{9,25},{17,1},{25,9},{2,18},{10... | collective-permute-start | bytes 1572872 | tf_op jit(solution)/shard_map/cond/branch_1_fun/ppermute | solution.py:42
  249.5 22.4 %collective-permute-start.12 = (bf16[128,2048]{1,0:T(8,128)(2,1)S(1)}, bf16[128,2048]{1,0:T(8,128)(2,1)S(1)}, u32[]{:S(2)}, u32[]{:S(2)}) collective-permute-start(bf16[128,2048]{1,0:T(8,128)(2,1)S(1)} %slice.155), channel_id=1, source_target_pairs={{0,1},{1,0},{2,3},{3,2},{4,5},{5,4},{6,7},{7,6},{8,9},{9,8},{10,11... | collective-permute-start | bytes 1572872 | tf_op jit(solution)/shard_map/cond/branch_1_fun/ppermute | solution.py:46
  250.8 22.0 %collective-permute-start.13 = (bf16[128,2048]{1,0:T(8,128)(2,1)S(1)}, bf16[128,2048]{1,0:T(8,128)(2,1)S(1)}, u32[]{:S(2)}, u32[]{:S(2)}) collective-permute-start(bf16[128,2048]{1,0:T(8,128)(2,1)S(1)} %slice.156), channel_id=1, source_target_pairs={{0,16},{8,24},{16,0},{24,8},{1,17},{9,25},{17,1},{25,9},{2,18},{10... | collective-permute-start | bytes 1572872 | tf_op jit(solution)/shard_map/cond/branch_1_fun/ppermute | solution.py:42
  260.8 24.8 %collective-permute-start.21 = (bf16[768,2048]{1,0:T(8,128)(2,1)S(1)}, bf16[768,2048]{1,0:T(8,128)(2,1)S(1)}, u32[]{:S(2)}, u32[]{:S(2)}) collective-permute-start(bf16[768,2048]{1,0:T(8,128)(2,1)S(1)} %constant_dynamic-update-slice_fusion.4.refs_1_), channel_id=1, source_target_pairs={{0,8},{8,0},{16,24},{24,16},{1,9},{9,1},{17,25},{25,17},{2,10},{10... | collective-permute-start | bytes 9437192 | tf_op jit(solution)/shard_map/cond/branch_1_fun/ppermute | solution.py:38
  273.6 27.9 %collective-permute-start.15 = (bf16[768,2048]{1,0:T(8,128)(2,1)}, bf16[768,2048]{1,0:T(8,128)(2,1)}, u32[]{:S(2)}, u32[]{:S(2)}) collective-permute-start(bf16[768,2048]{1,0:T(8,128)(2,1)} %constant_dynamic-update-slice_fusion), channel_id=1, source_target_pairs={{0,8},{8,0},{16,24},{24,16},{1,9},{9,1},{17,25},{25,17},{2,10},{10... | collective-permute-start | bytes 9437192 | tf_op jit(solution)/shard_map/cond/branch_1_fun/ppermute | solution.py:38
  277.4 24.1 %collective-permute-start.14 = (bf16[256,2048]{1,0:T(8,128)(2,1)}, bf16[256,2048]{1,0:T(8,128)(2,1)}, u32[]{:S(2)}, u32[]{:S(2)}) collective-permute-start(bf16[256,2048]{1,0:T(8,128)(2,1)} %multiply_convert_fusion), channel_id=1, source_target_pairs={{0,8},{8,0},{16,24},{24,16},{1,9},{9,1},{17,25},{25,17},{2,10},{10... | collective-permute-start | bytes 3145736 | tf_op jit(solution)/shard_map/cond/branch_1_fun/ppermute | solution.py:38
  369.7 231.2 %reduce-scatter.6.cloned.1.call-start = ((), (), s32[]{:S(2)}) async-start(), calls=%async_computation.9 | async-start | bytes 10485760 | tf_op jit(solution)/shard_map/reduce_scatter | solution.py:126
  384.0 20.9 %collective-permute-start.26 = (bf16[1024,2048]{1,0:T(8,128)(2,1)}, bf16[1024,2048]{1,0:T(8,128)(2,1)}, u32[]{:S(2)}, u32[]{:S(2)}) collective-permute-start(bf16[1024,2048]{1,0:T(8,128)(2,1)} %fusion.8), channel_id=1, source_target_pairs={{0,8},{8,0},{16,24},{24,16},{1,9},{9,1},{17,25},{25,17},{2,10},{10... | collective-permute-start | bytes 12582920 | tf_op jit(solution)/shard_map/cond/branch_1_fun/ppermute | solution.py:38
  411.3 13.7 %collective-permute-start.27 = (bf16[128,2048]{1,0:T(8,128)(2,1)S(1)}, bf16[128,2048]{1,0:T(8,128)(2,1)S(1)}, u32[]{:S(2)}, u32[]{:S(2)}) collective-permute-start(bf16[128,2048]{1,0:T(8,128)(2,1)S(1)} %get-tuple-element.475), channel_id=1, source_target_pairs={{0,16},{8,24},{16,0},{24,8},{1,17},{9,25},{17,1},{25,9},{2,18},{10... | collective-permute-start | bytes 1572872 | tf_op jit(solution)/shard_map/cond/branch_1_fun/ppermute | solution.py:42
  411.4 13.6 %collective-permute-start.28 = (bf16[128,2048]{1,0:T(8,128)(2,1)S(1)}, bf16[128,2048]{1,0:T(8,128)(2,1)S(1)}, u32[]{:S(2)}, u32[]{:S(2)}) collective-permute-start(bf16[128,2048]{1,0:T(8,128)(2,1)S(1)} %get-tuple-element.474), channel_id=1, source_target_pairs={{0,1},{1,0},{2,3},{3,2},{4,5},{5,4},{6,7},{7,6},{8,9},{9,8},{10,11... | collective-permute-start | bytes 1572872 | tf_op jit(solution)/shard_map/cond/branch_1_fun/ppermute | solution.py:46
  425.5 26.1 %collective-permute-start.29 = (bf16[256,2048]{1,0:T(8,128)(2,1)S(1)}, bf16[256,2048]{1,0:T(8,128)(2,1)S(1)}, u32[]{:S(2)}, u32[]{:S(2)}) collective-permute-start(bf16[256,2048]{1,0:T(8,128)(2,1)S(1)} %pad_maximum_fusion.5), channel_id=1, source_target_pairs={{0,16},{8,24},{16,0},{24,8},{1,17},{9,25},{17,1},{25,9},{2,18},{10... | collective-permute-start | bytes 3145736 | tf_op jit(solution)/shard_map/cond/branch_1_fun/ppermute | solution.py:42
  426.8 24.8 %collective-permute-start.30 = (bf16[256,2048]{1,0:T(8,128)(2,1)S(1)}, bf16[256,2048]{1,0:T(8,128)(2,1)S(1)}, u32[]{:S(2)}, u32[]{:S(2)}) collective-permute-start(bf16[256,2048]{1,0:T(8,128)(2,1)S(1)} %pad_maximum_fusion.6), channel_id=1, source_target_pairs={{0,1},{1,0},{2,3},{3,2},{4,5},{5,4},{6,7},{7,6},{8,9},{9,8},{10,11... | collective-permute-start | bytes 3145736 | tf_op jit(solution)/shard_map/cond/branch_1_fun/ppermute | solution.py:46
  455.8 203.8 %reduce-scatter.8.cloned.1.call-start = ((), (), s32[]{:S(2)}) async-start(), calls=%async_computation.10 | async-start | bytes 3276800 | tf_op jit(solution)/shard_map/reduce_scatter | solution.py:126
  458.5 25.1 %collective-permute-start.31 = (bf16[256,2048]{1,0:T(8,128)(2,1)}, bf16[256,2048]{1,0:T(8,128)(2,1)S(1)}, u32[]{:S(2)}, u32[]{:S(2)}) collective-permute-start(bf16[256,2048]{1,0:T(8,128)(2,1)} %get-tuple-element.197.refs_0_), channel_id=1, source_target_pairs={{0,16},{8,24},{16,0},{24,8},{1,17},{9,25},{17,1},{25,9},{2,18},{10... | collective-permute-start | bytes 3145736 | tf_op jit(solution)/shard_map/cond/branch_1_fun/ppermute | solution.py:42
  458.8 24.8 %collective-permute-start.32 = (bf16[256,2048]{1,0:T(8,128)(2,1)}, bf16[256,2048]{1,0:T(8,128)(2,1)S(1)}, u32[]{:S(2)}, u32[]{:S(2)}) collective-permute-start(bf16[256,2048]{1,0:T(8,128)(2,1)} %get-tuple-element.197.refs_0_), channel_id=1, source_target_pairs={{0,1},{1,0},{2,3},{3,2},{4,5},{5,4},{6,7},{7,6},{8,9},{9,8},{10,11... | collective-permute-start | bytes 3145736 | tf_op jit(solution)/shard_map/cond/branch_1_fun/ppermute | solution.py:46
  483.7 12.6 %collective-permute-start.34 = (bf16[128,2048]{1,0:T(8,128)(2,1)S(1)}, bf16[128,2048]{1,0:T(8,128)(2,1)S(1)}, u32[]{:S(2)}, u32[]{:S(2)}) collective-permute-start(bf16[128,2048]{1,0:T(8,128)(2,1)S(1)} %slice.170), channel_id=1, source_target_pairs={{0,1},{1,0},{2,3},{3,2},{4,5},{5,4},{6,7},{7,6},{8,9},{9,8},{10,11... | collective-permute-start | bytes 1572872 | tf_op jit(solution)/shard_map/cond/branch_1_fun/ppermute | solution.py:46
  505.5 46.3 %collective-permute-start.38 = (bf16[256,2048]{1,0:T(8,128)(2,1)}, bf16[256,2048]{1,0:T(8,128)(2,1)}, u32[]{:S(2)}, u32[]{:S(2)}) collective-permute-start(bf16[256,2048]{1,0:T(8,128)(2,1)} %get-tuple-element.208), channel_id=1, source_target_pairs={{0,16},{8,24},{16,0},{24,8},{1,17},{9,25},{17,1},{25,9},{2,18},{10... | collective-permute-start | bytes 3145736 | tf_op jit(solution)/shard_map/cond/branch_1_fun/ppermute | solution.py:42
  506.6 45.2 %collective-permute-start.39 = (bf16[256,2048]{1,0:T(8,128)(2,1)}, bf16[256,2048]{1,0:T(8,128)(2,1)}, u32[]{:S(2)}, u32[]{:S(2)}) collective-permute-start(bf16[256,2048]{1,0:T(8,128)(2,1)} %get-tuple-element.209), channel_id=1, source_target_pairs={{0,1},{1,0},{2,3},{3,2},{4,5},{5,4},{6,7},{7,6},{8,9},{9,8},{10,11... | collective-permute-start | bytes 3145736 | tf_op jit(solution)/shard_map/cond/branch_1_fun/ppermute | solution.py:46
  507.8 45.9 %collective-permute-start.40 = (bf16[256,2048]{1,0:T(8,128)(2,1)}, bf16[256,2048]{1,0:T(8,128)(2,1)}, u32[]{:S(2)}, u32[]{:S(2)}) collective-permute-start(bf16[256,2048]{1,0:T(8,128)(2,1)} %get-tuple-element.210), channel_id=1, source_target_pairs={{0,17},{1,16},{2,19},{3,18},{4,21},{5,20},{6,23},{7,22},{8,25},{9,... | collective-permute-start | bytes 3145736 | tf_op jit(solution)/shard_map/cond/branch_1_fun/ppermute | solution.py:51
  559.5 19.8 %collective-permute-start.41 = (bf16[1024,2048]{1,0:T(8,128)(2,1)}, bf16[1024,2048]{1,0:T(8,128)(2,1)}, u32[]{:S(2)}, u32[]{:S(2)}) collective-permute-start(bf16[1024,2048]{1,0:T(8,128)(2,1)} %convolution_convert_fusion.2), channel_id=1, source_target_pairs={{0,8},{8,0},{16,24},{24,16},{1,9},{9,1},{17,25},{25,17},{2,10},{10... | collective-permute-start | bytes 12582920 | tf_op jit(solution)/shard_map/cond/branch_1_fun/ppermute | solution.py:38
  560.8 16.1 %collective-permute-start.44 = (bf16[256,2048]{1,0:T(8,128)(2,1)}, bf16[256,2048]{1,0:T(8,128)(2,1)}, u32[]{:S(2)}, u32[]{:S(2)}) collective-permute-start(bf16[256,2048]{1,0:T(8,128)(2,1)} %get-tuple-element.223), channel_id=1, source_target_pairs={{2,10},{3,11},{4,20},{5,21},{6,30},{7,31},{8,16},{9,17},{10,26},{1... | collective-permute-start | bytes 3145736 | tf_op jit(solution)/shard_map/cond/branch_1_fun/ppermute | solution.py:51
  584.7 13.7 %collective-permute-start.42 = (bf16[128,2048]{1,0:T(8,128)(2,1)S(1)}, bf16[128,2048]{1,0:T(8,128)(2,1)S(1)}, u32[]{:S(2)}, u32[]{:S(2)}) collective-permute-start(bf16[128,2048]{1,0:T(8,128)(2,1)S(1)} %get-tuple-element.468), channel_id=1, source_target_pairs={{0,16},{8,24},{16,0},{24,8},{1,17},{9,25},{17,1},{25,9},{2,18},{10... | collective-permute-start | bytes 1572872 | tf_op jit(solution)/shard_map/cond/branch_1_fun/ppermute | solution.py:42
  584.8 13.6 %collective-permute-start.43 = (bf16[128,2048]{1,0:T(8,128)(2,1)S(1)}, bf16[128,2048]{1,0:T(8,128)(2,1)S(1)}, u32[]{:S(2)}, u32[]{:S(2)}) collective-permute-start(bf16[128,2048]{1,0:T(8,128)(2,1)S(1)} %get-tuple-element.467), channel_id=1, source_target_pairs={{0,1},{1,0},{2,3},{3,2},{4,5},{5,4},{6,7},{7,6},{8,9},{9,8},{10,11... | collective-permute-start | bytes 1572872 | tf_op jit(solution)/shard_map/cond/branch_1_fun/ppermute | solution.py:46
  601.0 24.5 %collective-permute-start.6 = (bf16[256,2048]{1,0:T(8,128)(2,1)}, bf16[256,2048]{1,0:T(8,128)(2,1)}, u32[]{:S(2)}, u32[]{:S(2)}) collective-permute-start(bf16[256,2048]{1,0:T(8,128)(2,1)} %get-tuple-element.225), channel_id=1, source_target_pairs={{0,16},{8,24},{16,0},{24,8},{1,17},{9,25},{17,1},{25,9},{2,18},{10... | collective-permute-start | bytes 3145736 | tf_op jit(solution)/shard_map/cond/branch_1_fun/ppermute | solution.py:42
  601.9 24.4 %collective-permute-start.7 = (bf16[256,2048]{1,0:T(8,128)(2,1)}, bf16[256,2048]{1,0:T(8,128)(2,1)}, u32[]{:S(2)}, u32[]{:S(2)}) collective-permute-start(bf16[256,2048]{1,0:T(8,128)(2,1)} %get-tuple-element.226), channel_id=1, source_target_pairs={{0,1},{1,0},{2,3},{3,2},{4,5},{5,4},{6,7},{7,6},{8,9},{9,8},{10,11... | collective-permute-start | bytes 3145736 | tf_op jit(solution)/shard_map/cond/branch_1_fun/ppermute | solution.py:46
  603.7 46.5 %all-to-all-start = ((bf16[8,64,2048]{2,1,0:T(8,128)(2,1)}), bf16[8,64,2048]{2,1,0:T(8,128)(2,1)S(1)}, u32[]{:S(2)}, u32[]{:S(2)}) async-start(bf16[8,64,2048]{2,1,0:T(8,128)(2,1)} %bitcast.96), calls=%async_computation | async-start | bytes 4194304 | tf_op jit(solution)/shard_map/cond/branch_1_fun/all_to_all | solution.py:874
  660.6 14.5 %collective-permute-start.52 = (bf16[64,2048]{1,0:T(8,128)(2,1)S(1)}, bf16[64,2048]{1,0:T(8,128)(2,1)S(1)}, u32[]{:S(2)}, u32[]{:S(2)}) collective-permute-start(bf16[64,2048]{1,0:T(8,128)(2,1)S(1)} %reshape.227), channel_id=1, source_target_pairs={{1,4},{2,1},{3,5},{4,2},{5,6},{6,3},{9,12},{10,9},{11,13},{12,10},... | collective-permute-start | bytes 786440 | tf_op jit(solution)/shard_map/ppermute | solution.py:51
  664.5 15.3 %all-to-all-start.1 = ((bf16[8,80,384]{2,1,0:T(8,128)(2,1)}), bf16[8,80,384]{2,1,0:T(8,128)(2,1)S(1)}, u32[]{:S(2)}, u32[]{:S(2)}) async-start(bf16[8,80,384]{2,1,0:T(8,128)(2,1)} %fusion.32), calls=%async_computation.4 | async-start | bytes 983040 | tf_op jit(solution)/shard_map/all_to_all | solution.py:874
  (51 other events, 575.9 us)
Sparse Core Ops, SparseCore 0:
  30.8 54.2 all-gather.3
  91.0 81.3 all-gather.5
  175.4 151.2 all-gather.7
  369.8 77.7 reduce-scatter.3
  455.9 144.9 reduce-scatter.5
  603.1 52.1 reduce-scatter.7

commit v6 on v5

--- a/solution.py
+++ b/solution.py
@@ -79,7 +79,8 @@
 
 
 def halve_core(make, *others):
-    sent = lax.optimization_barrier((swap_core(make(1).astype(BF16)), *others))[0]
+    sent = swap_core(make(1).astype(BF16))
+    sent = after(sent, *others) if others else sent
     return (make(0) + sent.astype(F32)).astype(BF16)
 
 
@@ -850,7 +851,7 @@
         branch = (dot(mid[:side], wd) + swap_core(branch_sent).astype(F32)).astype(BF16)
         da_pieces = gather_plane(da_own, branch)
         own, x_part, y_part, corner = jnp.split(branch, 4)
-        x_part, y_part, corner = lax.optimization_barrier((x_part, y_part, corner, *da_pieces))[:3]
+        x_part, y_part, corner = lax.optimization_barrier((x_part, y_part, corner, da_pieces[1]))[:3]
         x_part, y_part, corner = swap_x(x_part), swap_y(y_part), swap_xy(corner)
         da, d_out = out_back(da_pieces, wo)
         grad_qkv = attend_back(member, qkv, d_out, log_sums, cosine, sine, n_seq)

time: 696 us -> 686 us (0.986)
  other arithmetic: 59 us -> 48.8 us
    convert_element_type x2 -> x0, other arithmetic: 9.81 us -> none  [halve_core(): return (make(0) + sent.astype(F32)).astype(BF16)]
  transfers between devices with their start and end apart: 61 -> 61, of which waited for: 40 -> 39; matrix products, arithmetic and copies ran while one was open for 22% -> 21% of each run, Pallas kernels for 18% -> 19%
where the time goes in v6:
time: 686 us; the launch traced here: 679 us
  waiting for transfers between devices  252 us (37%)
  Pallas kernels  156 us (23%)
  starting transfers between devices  80.3 us (12%)
  matrix products  76.3 us (11%)
  other arithmetic  48.8 us (7%)
  local copies, waits for them, and re-layouts  48.6 us (7%)
  between operations  15.7 us (2%)
    ppermute x16, waiting for transfers between devices, swap_x(): lax.ppermute(value, 'seq', [(i, i ^ 2) for i in range(lax.axis_size('seq'...  120 us
    pallas_call x4, Pallas kernels, pieces_call(): pl.pallas_call(kernel, out_shape=tuple((jax.ShapeDtypeStruct((blocks * ro...  66.8 us
    dot_general x4, matrix products, dot_cols(): lax.dot_general(left, right, (((1,), (1,)), ((), ())), preferred_element_...  36.3 us
    pallas_call x2, Pallas kernels, row_terms(): pl.pallas_call(kernel, out_shape=jax.ShapeDtypeStruct((n_planes, n_blocks...  31.2 us
    pallas_call x1, Pallas kernels, attend_back(): pl.pallas_call(functools.partial(attend_back_kernel, n_parts), out_shape=...  30.5 us
    ppermute x13, waiting for transfers between devices, swap_core(): lax.ppermute(value, 'seq', [(i, i ^ 1) for i in range(lax.axis_size('seq'...  28.7 us
    ppermute x13, starting transfers between devices, swap_core(): lax.ppermute(value, 'seq', [(i, i ^ 1) for i in range(lax.axis_size('seq'...  28.1 us
    all_gather x3, waiting for transfers between devices, gather_z(): lax.all_gather(own, 'fsdp', axis=0, tiled=True, axis_index_groups=z_group...  24.8 us
  transfers between devices with their start and end apart: 61, of which 39 were waited for; matrix products, arithmetic and copies ran while one was open for 21% of the time, Pallas kernels for 19%

profile of v6, /device:TPU:11, one launch (start us, length us, event | category | flops | bytes accessed | tf_op | source)
XLA Modules:
  0.0 679.4 jit_solution(11370060778210211060)
XLA Ops:
  25.1 4.5 collective-permute-done.46
  31.9 58.9 %conditional.6 = (bf16[256,2048]{1,0:T(8,128)(2,1)}, bf16[768,2048]{1,0:T(8,128)(2,1)}, bf16[256,2048]{1,0:T(8,128)(2,1)}, bf16[768,2048]{1,0:T(8,128)(2,1)}, bf...) conditional(s32[]{:T(128)} %bitcast.29, () %tuple.91, ...), branch_computations={%region_0.1_spmd, %region_1.2_spmd} | conditional | flops 10881163 | bytes 50881816 | solution.py:727
  34.9 19.5 %collective-permute-done = bf16[256,2048]{1,0:T(8,128)(2,1)} collective-permute-done((bf16[256,2048]{1,0:T(8,128)(2,1)S(1)}, bf16[256,2048]{1,0:T(8,128)(2,1)}, u32[]{:S(2)}, u32[]{:S(2)}) %collective-permute-start) | collective-permute-done | bytes 1048608 | tf_op jit(solution)/shard_map/cond/branch_1_fun/ppermute | solution.py:42
  55.6 13.0 %collective-permute-done.3 = bf16[256,2048]{1,0:T(8,128)(2,1)S(1)} collective-permute-done((bf16[256,2048]{1,0:T(8,128)(2,1)S(1)}, bf16[256,2048]{1,0:T(8,128)(2,1)S(1)}, u32[]{:S(2)}, u32[]{:S(2)}) %collective-permute-start.3) | collective-permute-done | bytes 1048608 | tf_op jit(solution)/shard_map/cond/branch_1_fun/ppermute | solution.py:698
  76.5 7.0 %collective-permute-start.5 = (bf16[768,2048]{1,0:T(8,128)(2,1)}, bf16[768,2048]{1,0:T(8,128)(2,1)}, u32[]{:S(2)}, u32[]{:S(2)}) collective-permute-start(bf16[768,2048]{1,0:T(8,128)(2,1)} %pad_maximum_fusion), channel_id=1, source_target_pairs={{0,8},{8,0},{16,24},{24,16},{1,9},{9,1},{17,25},{25,17},{2,10},{10... | collective-permute-start | bytes 9437192 | tf_op jit(solution)/shard_map/cond/branch_1_fun/ppermute | solution.py:38
  85.6 4.7 collective-permute-done.4
  92.1 81.6 %conditional.7 = (bf16[2048,2048]{1,0:T(8,128)(2,1)}, f32[2048,384]{1,0:T(8,128)}, bf16[2048,256]{1,0:T(8,128)(2,1)}, f32[2048,128]{1,0:T(8,128)S(1)}, bf16[2048...) conditional(s32[]{:T(128)} %bitcast.29, () %tuple.88, ...), branch_computations={%region_2.3_spmd, %region_3.4_spmd} | conditional | flops 9681506304 | bytes 139543584 | solution.py:727
  103.4 13.9 %project.1 = (bf16[2048,2048]{1,0:T(8,128)(2,1)}, f32[2048,384]{1,0:T(8,128)}) custom-call(bf16[256,2048]{1,0:T(8,128)(2,1)} %get-tuple-element.143.refs_0_, bf16[768,2048]{1,0:T(8,128)(2,1)} %get-tuple-element.144.refs_1_, bf16[256,2048]{1,0:T(8,128)(2,1)} %get-tuple-element.145.refs_2_, bf16[768,2048]{1,0:T(8,128)(2,1)} %get-tuple-element.146.refs_3_, ...), custom_call_target="tpu_custom_call" | custom-call | flops 3221225472 | bytes 22634496 | tf_op jit(solution)/shard_map/cond/branch_1_fun/project/pallas_call | solution.py:413
  117.3 20.8 %attend.1 = (bf16[2048,256]{1,0:T(8,128)(2,1)}, f32[2048,128]{1,0:T(8,128)}) custom-call(s32[1]{0:T(128)} %get-tuple-element.150.member, f32[2048,384]{1,0:T(8,128)} %get-tuple-element.526.refs_0_.refs_1_.refs_2_.refs_3_, f32[2048,384]{1,0:T(8,128)} %get-tuple-element.526.refs_0_.refs_1_.refs_2_.refs_3_, ...), custom_call_target="tpu_custom_call" | custom-call | flops 4294967296 | bytes 6291456 | tf_op jit(solution)/shard_map/cond/branch_1_fun/attend/pallas_call | solution.py:306
  144.7 6.8 collective-permute-done.23
  161.5 7.2 %collective-permute-done.24 = bf16[128,2048]{1,0:T(8,128)(2,1)S(1)} collective-permute-done((bf16[128,2048]{1,0:T(8,128)(2,1)}, bf16[128,2048]{1,0:T(8,128)(2,1)S(1)}, u32[]{:S(2)}, u32[]{:S(2)}) %collective-permute-start.24) | collective-permute-done | bytes 524320 | tf_op jit(solution)/shard_map/cond/branch_1_fun/ppermute | solution.py:42
  174.7 125.6 %conditional.8 = (f32[256,2048]{1,0:T(8,128)S(1)}, bf16[256,2048]{1,0:T(8,128)(2,1)}, bf16[768,2048]{1,0:T(8,128)(2,1)}, bf16[256,2048]{1,0:T(8,128)(2,1)}, bf16...) conditional(s32[]{:T(128)} %bitcast.29, () %tuple.87, ...), branch_computations={%region_4.5_spmd, %region_5.7_spmd} | conditional | flops 8596226048 | bytes 173028096 | solution.py:727
  176.4 21.8 %collective-permute-done.8 = bf16[256,2048]{1,0:T(8,128)(2,1)S(1)} collective-permute-done((bf16[256,2048]{1,0:T(8,128)(2,1)}, bf16[256,2048]{1,0:T(8,128)(2,1)S(1)}, u32[]{:S(2)}, u32[]{:S(2)}) %collective-permute-start.8) | collective-permute-done | bytes 1048608 | tf_op jit(solution)/shard_map/cond/branch_1_fun/ppermute | solution.py:42
  205.6 19.2 %collective-permute-done.16 = bf16[256,2048]{1,0:T(8,128)(2,1)S(1)} collective-permute-done((bf16[256,2048]{1,0:T(8,128)(2,1)S(1)}, bf16[256,2048]{1,0:T(8,128)(2,1)S(1)}, u32[]{:S(2)}, u32[]{:S(2)}) %collective-permute-start.16) | collective-permute-done | bytes 1048608 | tf_op jit(solution)/shard_map/cond/branch_1_fun/ppermute | solution.py:42
  227.6 19.6 %collective-permute-done.10 = bf16[256,2048]{1,0:T(8,128)(2,1)S(1)} collective-permute-done((bf16[256,2048]{1,0:T(8,128)(2,1)}, bf16[256,2048]{1,0:T(8,128)(2,1)S(1)}, u32[]{:S(2)}, u32[]{:S(2)}) %collective-permute-start.10) | collective-permute-done | bytes 1048608 | tf_op jit(solution)/shard_map/cond/branch_1_fun/ppermute | solution.py:42
  250.1 9.2 %collective-permute-done.18 = bf16[128,2048]{1,0:T(8,128)(2,1)S(1)} collective-permute-done((bf16[128,2048]{1,0:T(8,128)(2,1)S(1)}, bf16[128,2048]{1,0:T(8,128)(2,1)S(1)}, u32[]{:S(2)}, u32[]{:S(2)}) %collective-permute-start.18) | collective-permute-done | bytes 524320 | tf_op jit(solution)/shard_map/cond/branch_1_fun/ppermute | solution.py:46
  259.3 7.1 %collective-permute-start.21 = (bf16[768,2048]{1,0:T(8,128)(2,1)S(1)}, bf16[768,2048]{1,0:T(8,128)(2,1)S(1)}, u32[]{:S(2)}, u32[]{:S(2)}) collective-permute-start(bf16[768,2048]{1,0:T(8,128)(2,1)S(1)} %constant_dynamic-update-slice_fusion.4.refs_1_), channel_id=1, source_target_pairs={{0,8},{8,0},{16,24},{24,16},{1,9},{9,1},{17,25},{25,17},{2,10},{10... | collective-permute-start | bytes 9437192 | tf_op jit(solution)/shard_map/cond/branch_1_fun/ppermute | solution.py:38
  276.4 7.6 %collective-permute-done.20.refs_2_ = bf16[256,2048]{1,0:T(8,128)(2,1)S(1)} collective-permute-done((bf16[256,2048]{1,0:T(8,128)(2,1)S(1)}, bf16[256,2048]{1,0:T(8,128)(2,1)S(1)}, u32[]{:S(2)}, u32[]{:S(2)}) %collective-permute-start.20) | collective-permute-done | bytes 1048608 | tf_op jit(solution)/shard_map/cond/branch_1_fun/ppermute | solution.py:38
  285.8 14.3 %down_back.1 = (bf16[2048,2048]{1,0:T(8,128)(2,1)}, f32[2048,1024]{1,0:T(8,128)}) custom-call(bf16[256,2048]{1,0:T(8,128)(2,1)S(1)} %copy-done.23, bf16[768,2048]{1,0:T(8,128)(2,1)S(1)} %constant_dynamic-update-slice_fusion.4.refs_1_, bf16[256,2048]{1,0:T(8,128)(2,1)S(1)} %collective-permute-done.20.refs_2_, bf16[768,2048]{1,0:T(8,128)(2,1)} %copy-done.28, ...), custom_call_target="tpu_custom_call" | custom-call | flops 8589934592 | bytes 29360144 | tf_op jit(solution)/shard_map/cond/branch_1_fun/down_back/pallas_call | solution.py:413
  300.3 24.7 %all-gather.8.cloned.1.call-done.refs_4_ = bf16[2048,2048]{1,0:T(8,128)(2,1)} async-done(((bf16[512,2048]{1,0:T(8,128)(2,1)}), bf16[2048,2048]{1,0:T(8,128)(2,1)}) %all-gather.8.cloned.1.call-update) | async-done | bytes 8388624 | tf_op jit(solution)/shard_map/all_gather | solution.py:123
  325.0 27.9 %feed.1 = (bf16[2048,2048]{1,0:T(8,128)(2,1)}, bf16[2048,1024]{1,0:T(8,128)(2,1)S(1)}, bf16[2048,2048]{1,0:T(8,128)(2,1)}) custom-call(bf16[256,2048]{1,0:T(8,128)(2,1)} %get-tuple-element.332.refs_0_, bf16[768,2048]{1,0:T(8,128)(2,1)} %get-tuple-element.333.refs_1_, bf16[256,2048]{1,0:T(8,128)(2,1)} %get-tuple-element.334.refs_2_, ...), custom_call_target="tpu_custom_call" | custom-call | flops 17179869184 | bytes 46137344 | tf_op jit(solution)/shard_map/feed/pallas_call | solution.py:413
  355.0 13.0 %convolution_convert_fusion.4 = bf16[1024,2048]{1,0:T(8,128)(2,1)} fusion(bf16[2048,1024]{1,0:T(8,128)(2,1)S(1)} %get-tuple-element.342, bf16[2048,2048]{1,0:T(8,128)(2,1)} %get-tuple-element.344), kind=kOutput, calls=%fused_computation.97 | convolution fusion | flops 8592031744 | bytes 16777216 | tf_op jit(solution)/shard_map/dot_general | solution.py:26
  368.1 78.1 %conditional.9 = (bf16[2048,2048]{1,0:T(8,128)(2,1)}, f32[256,2048]{1,0:T(8,128)}, bf16[256,2048]{1,0:T(8,128)(2,1)}, f32[2048]{0:T(1024)S(1)}, bf16[1024,2048]{1,0:T(8,128)(2,1)}, /*index=5*/bf16[1024,2048]{1,0:T(8,128)(2,1)}) conditional(s32[]{:T(128)} %bitcast.29, () %tuple.86, (bf16[2048,2048]{1,0:T(8,128)(2,1)}, bf16[2048,2048]{1,0:T(8,128)(2,1)}, ...), branch_computations={%region_7.8_spmd, %region_8.12_spmd} | conditional | flops 38701887488 | bytes 194020976 | solution.py:727
  368.1 14.2 %fusion.10 = bf16[1024,2048]{1,0:T(8,128)(2,1)} fusion(bf16[2048,2048]{1,0:T(8,128)(2,1)} %get-tuple-element.183, bf16[2048,2048]{1,0:T(8,128)(2,1)} %get-tuple-element.180.right_ref), kind=kOutput, calls=%fused_computation.41 | convolution fusion | flops 8592031744 | bytes 16777216 | tf_op jit(solution)/shard_map/cond/branch_1_fun/dot_general | solution.py:30
  390.1 11.3 %add_convert_fusion.3 = bf16[1024,2048]{1,0:T(8,128)(2,1)S(1)} fusion(bf16[1024,2048]{1,0:T(8,128)(2,1)} %collective-permute-done.26, bf16[2048,2048]{1,0:T(8,128)(2,1)S(1)} %bitcast.115, bf16[2048,2048]{1,0:T(8,128)(2,1)} %get-tuple-element.180.right_ref), kind=kOutput, calls=%fused_computation.35 | convolution fusion | flops 8596226048 | bytes 20971520 | tf_op jit(solution)/shard_map/cond/branch_1_fun/dot_general | solution.py:30
  403.6 8.3 %convolution_convert_fusion.1 = bf16[1024,2048]{1,0:T(8,128)(2,1)} fusion(bf16[1024,2048]{1,0:T(8,128)(2,1)} %pad_maximum_fusion.4, bf16[2048,1024]{1,0:T(8,128)(2,1)S(1)} %copy-done.30), kind=kOutput, calls=%fused_computation.42 | convolution fusion | flops 4297064448 | bytes 10485760 | tf_op jit(solution)/shard_map/cond/branch_1_fun/dot_general | solution.py:34
  418.0 24.0 %row_terms.2 = bf16[4,4,128,2048]{3,2,1,0:T(8,128)(2,1)} custom-call(bf16[2048,2048]{1,0:T(8,128)(2,1)} %get-tuple-element.179.left_ref, bf16[2048,2048]{1,0:T(8,128)(2,1)} %get-tuple-element.180.right_ref), custom_call_target="tpu_custom_call" | custom-call | flops 17179869184 | bytes 25165824 | tf_op jit(solution)/shard_map/cond/branch_1_fun/row_terms/pallas_call | solution.py:536
  447.4 141.1 %conditional.10 = (bf16[2048,640]{1,0:T(8,128)(2,1)}, bf16[256,2048]{1,0:T(8,128)(2,1)S(1)}, bf16[256,2048]{1,0:T(8,128)(2,1)}, bf16[256,2048]{1,0:T(8,128)(2,1)...) conditional(s32[]{:T(128)} %bitcast.29, () %tuple.85, ...), branch_computations={%region_13.14_spmd, %region_14.15_spmd} | conditional | flops 12921077760 | bytes 206439328 | solution.py:727
  449.8 6.6 collective-permute-done.33
  456.5 7.3 %add_convert_fusion.7 = bf16[1024,2048]{1,0:T(8,128)(2,1)S(1)} fusion(bf16[1024,2048]{1,0:T(8,128)(2,1)S(1)} %collective-permute-done.33, bf16[1024,2048]{1,0:T(8,128)(2,1)} %get-tuple-element.199, bf16[2048,1024]{1,0:T(8,128)(2,1)} %get-tuple-element.198), kind=kOutput, calls=%fused_computation.60 | convolution fusion | flops 4301258752 | bytes 14680064 | tf_op jit(solution)/shard_map/cond/branch_1_fun/dot_general | solution.py:34
  463.8 10.8 %collective-permute-done.31 = bf16[256,2048]{1,0:T(8,128)(2,1)S(1)} collective-permute-done((bf16[256,2048]{1,0:T(8,128)(2,1)}, bf16[256,2048]{1,0:T(8,128)(2,1)S(1)}, u32[]{:S(2)}, u32[]{:S(2)}) %collective-permute-start.31) | collective-permute-done | bytes 1048608 | tf_op jit(solution)/shard_map/cond/branch_1_fun/ppermute | solution.py:42
  478.4 8.9 %collective-permute-done.34 = bf16[128,2048]{1,0:T(8,128)(2,1)S(1)} collective-permute-done((bf16[128,2048]{1,0:T(8,128)(2,1)S(1)}, bf16[128,2048]{1,0:T(8,128)(2,1)S(1)}, u32[]{:S(2)}, u32[]{:S(2)}) %collective-permute-start.34) | collective-permute-done | bytes 524320 | tf_op jit(solution)/shard_map/cond/branch_1_fun/ppermute | solution.py:46
  497.9 10.7 %out_back.1 = (bf16[2048,2048]{1,0:T(8,128)(2,1)}, bf16[2048,256]{1,0:T(8,128)(2,1)S(1)}) custom-call(bf16[256,2048]{1,0:T(8,128)(2,1)} %get-tuple-element.197.refs_0_, bf16[768,2048]{1,0:T(8,128)(2,1)} %constant_dynamic-update-slice_fusion.8.refs_1_, bf16[256,2048]{1,0:T(8,128)(2,1)S(1)} %collective-permute-done.36.refs_2_, ...), custom_call_target="tpu_custom_call" | custom-call | flops 524288 | bytes 294912 | tf_op jit(solution)/shard_map/cond/branch_1_fun/out_back/pallas_call | solution.py:413
  508.5 30.5 %attend_back.1.right_ref = bf16[2048,384]{1,0:T(8,128)(2,1)S(1)} custom-call(s32[1]{0:T(128)} %get-tuple-element.195.member, f32[2048,384]{1,0:T(8,128)} %get-tuple-element.196.refs_0_.refs_1_.refs_2_.refs_3_, f32[2048,384]{1,0:T(8,128)} %get-tuple-element.196.refs_0_.refs_1_.refs_2_.refs_3_, f32[2048,384]{1,0:T(8,128)} %get-tuple-element.196.refs_0_.refs_1_.refs_2_.refs_3_, ...), custom_call_target="tpu_custom_call" | custom-call | flops 8388608 | bytes 98304 | tf_op jit(solution)/shard_map/cond/branch_1_fun/attend_back/pallas_call | solution.py:342
  540.4 5.8 convolution_convert_fusion.2
  550.2 6.1 fusion.16
  558.3 6.1 collective-permute-done.44
  566.8 5.0 add_convert_fusion.6
  573.0 7.3 %row_terms.3 = bf16[4,4,128,384]{3,2,1,0:T(8,128)(2,1)S(1)} custom-call(bf16[2048,2048]{1,0:T(8,128)(2,1)} %get-tuple-element.194.left_ref, bf16[2048,384]{1,0:T(8,128)(2,1)S(1)} %copy-done.3), custom_call_target="tpu_custom_call" | custom-call | flops 3221225472 | bytes 11534336 | tf_op jit(solution)/shard_map/cond/branch_1_fun/row_terms/pallas_call | solution.py:536
  582.0 4.2 collective-permute-done.42
  588.5 4.5 reduce-scatter.6.cloned.1.call-done
  593.1 50.7 %conditional.11 = (f32[4,8,128]{2,1,0:T(8,128)S(1)}, f32[256,2048]{1,0:T(8,128)}, f32[64,8192]{1,0:T(8,128)}, f32[64,8192]{1,0:T(8,128)}, bf16[1,256,2048]{2,1,0:T(8,128)(2,1)}, /*index=5*/bf16[1,256,2048]{2,1,0:T(8,128)(2,1)}) conditional(s32[]{:T(128)} %bitcast.29, () %tuple.84, (bf16[256,2048]{1,0:T(8,128)(2,1)S(1)}, ...), branch_computations={%region_16.17_spmd, %region_17.21_spmd} | conditional | flops 19925248 | bytes 64128272 | solution.py:727
  594.7 5.9 all-to-all-start
  608.0 9.5 %collective-permute-done.6 = bf16[256,2048]{1,0:T(8,128)(2,1)} collective-permute-done((bf16[256,2048]{1,0:T(8,128)(2,1)}, bf16[256,2048]{1,0:T(8,128)(2,1)}, u32[]{:S(2)}, u32[]{:S(2)}) %collective-permute-start.6) | collective-permute-done | bytes 1048608 | tf_op jit(solution)/shard_map/cond/branch_1_fun/ppermute | solution.py:42
  620.3 4.6 fusion.34
  624.9 16.6 %all-to-all-done.in_ref = bf16[8,64,2048]{2,1,0:T(8,128)(2,1)S(1)} async-done(((bf16[8,64,2048]{2,1,0:T(8,128)(2,1)}), bf16[8,64,2048]{2,1,0:T(8,128)(2,1)S(1)}, u32[]{:S(2)}, u32[]{:S(2)}) %all-to-all-start) | async-done | bytes 2097184 | tf_op jit(solution)/shard_map/cond/branch_1_fun/all_to_all | solution.py:875
  654.9 7.8 %all-to-all-start.1 = ((bf16[8,80,384]{2,1,0:T(8,128)(2,1)}), bf16[8,80,384]{2,1,0:T(8,128)(2,1)S(1)}, u32[]{:S(2)}, u32[]{:S(2)}) async-start(bf16[8,80,384]{2,1,0:T(8,128)(2,1)} %fusion.36), calls=%async_computation.4 | async-start | bytes 983040 | tf_op jit(solution)/shard_map/all_to_all | solution.py:875
  665.2 5.2 all-to-all-done.1.in_ref
  (297 shorter events, 178.5 us)
Async XLA Ops:
  7.2 83.6 %all-gather.4.cloned.1.call-start = ((), (), s32[]{:S(2)}) async-start(), calls=%async_computation.5 | async-start | bytes 3379200 | tf_op jit(solution)/shard_map/all_gather | solution.py:123
  14.1 15.5 %collective-permute-start.46 = (bf16[64,2048]{1,0:T(8,128)(2,1)S(1)}, bf16[64,2048]{1,0:T(8,128)(2,1)S(1)}, u32[]{:S(2)}, u32[]{:S(2)}) collective-permute-start(bf16[64,2048]{1,0:T(8,128)(2,1)S(1)} %constant_dynamic-slice_fusion.10), channel_id=1, source_target_pairs={{8,2},{16,4},{24,6},{9,3},{17,5},{25,7},{2,8},{18,12},{26,14},{3,9... | collective-permute-start | bytes 786440 | tf_op jit(solution)/shard_map/ppermute | solution.py:51
  30.7 143.1 %all-gather.6.cloned.1.call-start = ((), (), s32[]{:S(2)}) async-start(), calls=%async_computation.6 | async-start | bytes 5242880 | tf_op jit(solution)/shard_map/all_gather | solution.py:123
  31.9 22.5 %collective-permute-start = (bf16[256,2048]{1,0:T(8,128)(2,1)S(1)}, bf16[256,2048]{1,0:T(8,128)(2,1)}, u32[]{:S(2)}, u32[]{:S(2)}) collective-permute-start(bf16[256,2048]{1,0:T(8,128)(2,1)S(1)} %get-tuple-element.506), channel_id=1, source_target_pairs={{0,16},{8,24},{16,0},{24,8},{1,17},{9,25},{17,1},{25,9},{2,18},{10... | collective-permute-start | bytes 3145736 | tf_op jit(solution)/shard_map/cond/branch_1_fun/ppermute | solution.py:42
  32.0 22.5 %collective-permute-start.1 = (bf16[256,2048]{1,0:T(8,128)(2,1)S(1)}, bf16[256,2048]{1,0:T(8,128)(2,1)}, u32[]{:S(2)}, u32[]{:S(2)}) collective-permute-start(bf16[256,2048]{1,0:T(8,128)(2,1)S(1)} %get-tuple-element.506), channel_id=1, source_target_pairs={{0,1},{1,0},{2,3},{3,2},{4,5},{5,4},{6,7},{7,6},{8,9},{9,8},{10,11... | collective-permute-start | bytes 3145736 | tf_op jit(solution)/shard_map/cond/branch_1_fun/ppermute | solution.py:46
  33.6 35.0 %collective-permute-start.3 = (bf16[256,2048]{1,0:T(8,128)(2,1)S(1)}, bf16[256,2048]{1,0:T(8,128)(2,1)S(1)}, u32[]{:S(2)}, u32[]{:S(2)}) collective-permute-start(bf16[256,2048]{1,0:T(8,128)(2,1)S(1)} %dynamic-slice_bitcast_fusion), channel_id=1, source_target_pairs={{0,1},{2,3},{5,4},{7,6},{9,8},{11,10},{12,13},{14,15},{16,17},{18,... | collective-permute-start | bytes 3145736 | tf_op jit(solution)/shard_map/cond/branch_1_fun/ppermute | solution.py:698
  54.5 18.9 %collective-permute-start.2 = (bf16[256,2048]{1,0:T(8,128)(2,1)}, bf16[256,2048]{1,0:T(8,128)(2,1)}, u32[]{:S(2)}, u32[]{:S(2)}) collective-permute-start(bf16[256,2048]{1,0:T(8,128)(2,1)} %collective-permute-done.1), channel_id=1, source_target_pairs={{0,16},{8,24},{16,0},{24,8},{1,17},{9,25},{17,1},{25,9},{2,18},{10... | collective-permute-start | bytes 3145736 | tf_op jit(solution)/shard_map/cond/branch_1_fun/ppermute | solution.py:42
  76.5 14.2 %collective-permute-start.5 = (bf16[768,2048]{1,0:T(8,128)(2,1)}, bf16[768,2048]{1,0:T(8,128)(2,1)}, u32[]{:S(2)}, u32[]{:S(2)}) collective-permute-start(bf16[768,2048]{1,0:T(8,128)(2,1)} %pad_maximum_fusion), channel_id=1, source_target_pairs={{0,8},{8,0},{16,24},{24,16},{1,9},{9,1},{17,25},{25,17},{2,10},{10... | collective-permute-start | bytes 9437192 | tf_op jit(solution)/shard_map/cond/branch_1_fun/ppermute | solution.py:38
  90.8 234.2 %all-gather.8.cloned.1.call-start = ((), (), s32[]{:S(2)}) async-start(), calls=%async_computation.7 | async-start | bytes 10485760 | tf_op jit(solution)/shard_map/all_gather | solution.py:123
  95.7 42.4 %collective-permute-start.22 = (bf16[256,2048]{1,0:T(8,128)(2,1)}, bf16[256,2048]{1,0:T(8,128)(2,1)}, u32[]{:S(2)}, u32[]{:S(2)}) collective-permute-start(bf16[256,2048]{1,0:T(8,128)(2,1)} %get-tuple-element.159), channel_id=1, source_target_pairs={{0,1},{1,0},{2,3},{3,2},{4,5},{5,4},{6,7},{7,6},{8,9},{9,8},{10,11... | collective-permute-start | bytes 3145736 | tf_op jit(solution)/shard_map/cond/branch_1_fun/ppermute | solution.py:46
  155.3 13.3 %collective-permute-start.24 = (bf16[128,2048]{1,0:T(8,128)(2,1)}, bf16[128,2048]{1,0:T(8,128)(2,1)S(1)}, u32[]{:S(2)}, u32[]{:S(2)}) collective-permute-start(bf16[128,2048]{1,0:T(8,128)(2,1)} %get-tuple-element.454), channel_id=1, source_target_pairs={{0,16},{8,24},{16,0},{24,8},{1,17},{9,25},{17,1},{25,9},{2,18},{10... | collective-permute-start | bytes 1572872 | tf_op jit(solution)/shard_map/cond/branch_1_fun/ppermute | solution.py:42
  156.3 13.1 %collective-permute-start.25 = (bf16[128,2048]{1,0:T(8,128)(2,1)}, bf16[128,2048]{1,0:T(8,128)(2,1)S(1)}, u32[]{:S(2)}, u32[]{:S(2)}) collective-permute-start(bf16[128,2048]{1,0:T(8,128)(2,1)} %get-tuple-element.453), channel_id=1, source_target_pairs={{0,1},{1,0},{2,3},{3,2},{4,5},{5,4},{6,7},{7,6},{8,9},{9,8},{10,11... | collective-permute-start | bytes 1572872 | tf_op jit(solution)/shard_map/cond/branch_1_fun/ppermute | solution.py:46
  173.7 272.5 %reduce-scatter.4.cloned.1.call-start = ((), (), s32[]{:S(2)}) async-start(), calls=%async_computation.8 | async-start | bytes 5242880 | tf_op jit(solution)/shard_map/reduce_scatter | solution.py:127
  174.7 23.5 %collective-permute-start.8 = (bf16[256,2048]{1,0:T(8,128)(2,1)}, bf16[256,2048]{1,0:T(8,128)(2,1)S(1)}, u32[]{:S(2)}, u32[]{:S(2)}) collective-permute-start(bf16[256,2048]{1,0:T(8,128)(2,1)} %get-tuple-element.166), channel_id=1, source_target_pairs={{0,16},{8,24},{16,0},{24,8},{1,17},{9,25},{17,1},{25,9},{2,18},{10... | collective-permute-start | bytes 3145736 | tf_op jit(solution)/shard_map/cond/branch_1_fun/ppermute | solution.py:42
  175.1 23.3 %collective-permute-start.9 = (bf16[256,2048]{1,0:T(8,128)(2,1)}, bf16[256,2048]{1,0:T(8,128)(2,1)S(1)}, u32[]{:S(2)}, u32[]{:S(2)}) collective-permute-start(bf16[256,2048]{1,0:T(8,128)(2,1)} %get-tuple-element.167), channel_id=1, source_target_pairs={{0,1},{1,0},{2,3},{3,2},{4,5},{5,4},{6,7},{7,6},{8,9},{9,8},{10,11... | collective-permute-start | bytes 3145736 | tf_op jit(solution)/shard_map/cond/branch_1_fun/ppermute | solution.py:46
  202.7 22.1 %collective-permute-start.16 = (bf16[256,2048]{1,0:T(8,128)(2,1)S(1)}, bf16[256,2048]{1,0:T(8,128)(2,1)S(1)}, u32[]{:S(2)}, u32[]{:S(2)}) collective-permute-start(bf16[256,2048]{1,0:T(8,128)(2,1)S(1)} %copy-done.23), channel_id=1, source_target_pairs={{0,16},{8,24},{16,0},{24,8},{1,17},{9,25},{17,1},{25,9},{2,18},{10... | collective-permute-start | bytes 3145736 | tf_op jit(solution)/shard_map/cond/branch_1_fun/ppermute | solution.py:42
  203.7 21.9 %collective-permute-start.17 = (bf16[256,2048]{1,0:T(8,128)(2,1)S(1)}, bf16[256,2048]{1,0:T(8,128)(2,1)S(1)}, u32[]{:S(2)}, u32[]{:S(2)}) collective-permute-start(bf16[256,2048]{1,0:T(8,128)(2,1)S(1)} %copy-done.23), channel_id=1, source_target_pairs={{0,1},{1,0},{2,3},{3,2},{4,5},{5,4},{6,7},{7,6},{8,9},{9,8},{10,11... | collective-permute-start | bytes 3145736 | tf_op jit(solution)/shard_map/cond/branch_1_fun/ppermute | solution.py:46
  204.9 42.3 %collective-permute-start.10 = (bf16[256,2048]{1,0:T(8,128)(2,1)}, bf16[256,2048]{1,0:T(8,128)(2,1)S(1)}, u32[]{:S(2)}, u32[]{:S(2)}) collective-permute-start(bf16[256,2048]{1,0:T(8,128)(2,1)} %multiply_convert_fusion), channel_id=1, source_target_pairs={{0,16},{8,24},{16,0},{24,8},{1,17},{9,25},{17,1},{25,9},{2,18},{10... | collective-permute-start | bytes 3145736 | tf_op jit(solution)/shard_map/cond/branch_1_fun/ppermute | solution.py:42
  205.4 42.6 %collective-permute-start.11 = (bf16[256,2048]{1,0:T(8,128)(2,1)}, bf16[256,2048]{1,0:T(8,128)(2,1)S(1)}, u32[]{:S(2)}, u32[]{:S(2)}) collective-permute-start(bf16[256,2048]{1,0:T(8,128)(2,1)} %multiply_convert_fusion), channel_id=1, source_target_pairs={{0,1},{1,0},{2,3},{3,2},{4,5},{5,4},{6,7},{7,6},{8,9},{9,8},{10,11... | collective-permute-start | bytes 3145736 | tf_op jit(solution)/shard_map/cond/branch_1_fun/ppermute | solution.py:46
  225.6 33.7 %collective-permute-start.18 = (bf16[128,2048]{1,0:T(8,128)(2,1)S(1)}, bf16[128,2048]{1,0:T(8,128)(2,1)S(1)}, u32[]{:S(2)}, u32[]{:S(2)}) collective-permute-start(bf16[128,2048]{1,0:T(8,128)(2,1)S(1)} %slice.157), channel_id=1, source_target_pairs={{0,1},{1,0},{2,3},{3,2},{4,5},{5,4},{6,7},{7,6},{8,9},{9,8},{10,11... | collective-permute-start | bytes 1572872 | tf_op jit(solution)/shard_map/cond/branch_1_fun/ppermute | solution.py:46
  226.9 32.3 %collective-permute-start.19 = (bf16[128,2048]{1,0:T(8,128)(2,1)S(1)}, bf16[128,2048]{1,0:T(8,128)(2,1)S(1)}, u32[]{:S(2)}, u32[]{:S(2)}) collective-permute-start(bf16[128,2048]{1,0:T(8,128)(2,1)S(1)} %slice.158), channel_id=1, source_target_pairs={{0,16},{8,24},{16,0},{24,8},{1,17},{9,25},{17,1},{25,9},{2,18},{10... | collective-permute-start | bytes 1572872 | tf_op jit(solution)/shard_map/cond/branch_1_fun/ppermute | solution.py:42
  248.0 22.4 %collective-permute-start.12 = (bf16[128,2048]{1,0:T(8,128)(2,1)S(1)}, bf16[128,2048]{1,0:T(8,128)(2,1)S(1)}, u32[]{:S(2)}, u32[]{:S(2)}) collective-permute-start(bf16[128,2048]{1,0:T(8,128)(2,1)S(1)} %slice.155), channel_id=1, source_target_pairs={{0,1},{1,0},{2,3},{3,2},{4,5},{5,4},{6,7},{7,6},{8,9},{9,8},{10,11... | collective-permute-start | bytes 1572872 | tf_op jit(solution)/shard_map/cond/branch_1_fun/ppermute | solution.py:46
  249.4 21.9 %collective-permute-start.13 = (bf16[128,2048]{1,0:T(8,128)(2,1)S(1)}, bf16[128,2048]{1,0:T(8,128)(2,1)S(1)}, u32[]{:S(2)}, u32[]{:S(2)}) collective-permute-start(bf16[128,2048]{1,0:T(8,128)(2,1)S(1)} %slice.156), channel_id=1, source_target_pairs={{0,16},{8,24},{16,0},{24,8},{1,17},{9,25},{17,1},{25,9},{2,18},{10... | collective-permute-start | bytes 1572872 | tf_op jit(solution)/shard_map/cond/branch_1_fun/ppermute | solution.py:42
  259.3 24.7 %collective-permute-start.21 = (bf16[768,2048]{1,0:T(8,128)(2,1)S(1)}, bf16[768,2048]{1,0:T(8,128)(2,1)S(1)}, u32[]{:S(2)}, u32[]{:S(2)}) collective-permute-start(bf16[768,2048]{1,0:T(8,128)(2,1)S(1)} %constant_dynamic-update-slice_fusion.4.refs_1_), channel_id=1, source_target_pairs={{0,8},{8,0},{16,24},{24,16},{1,9},{9,1},{17,25},{25,17},{2,10},{10... | collective-permute-start | bytes 9437192 | tf_op jit(solution)/shard_map/cond/branch_1_fun/ppermute | solution.py:38
  272.2 27.9 %collective-permute-start.15 = (bf16[768,2048]{1,0:T(8,128)(2,1)}, bf16[768,2048]{1,0:T(8,128)(2,1)}, u32[]{:S(2)}, u32[]{:S(2)}) collective-permute-start(bf16[768,2048]{1,0:T(8,128)(2,1)} %constant_dynamic-update-slice_fusion), channel_id=1, source_target_pairs={{0,8},{8,0},{16,24},{24,16},{1,9},{9,1},{17,25},{25,17},{2,10},{10... | collective-permute-start | bytes 9437192 | tf_op jit(solution)/shard_map/cond/branch_1_fun/ppermute | solution.py:38
  275.9 24.2 %collective-permute-start.14 = (bf16[256,2048]{1,0:T(8,128)(2,1)}, bf16[256,2048]{1,0:T(8,128)(2,1)}, u32[]{:S(2)}, u32[]{:S(2)}) collective-permute-start(bf16[256,2048]{1,0:T(8,128)(2,1)} %multiply_convert_fusion), channel_id=1, source_target_pairs={{0,8},{8,0},{16,24},{24,16},{1,9},{9,1},{17,25},{25,17},{2,10},{10... | collective-permute-start | bytes 3145736 | tf_op jit(solution)/shard_map/cond/branch_1_fun/ppermute | solution.py:38
  368.0 225.0 %reduce-scatter.6.cloned.1.call-start = ((), (), s32[]{:S(2)}) async-start(), calls=%async_computation.9 | async-start | bytes 10485760 | tf_op jit(solution)/shard_map/reduce_scatter | solution.py:127
  401.7 13.3 %collective-permute-start.27 = (bf16[128,2048]{1,0:T(8,128)(2,1)S(1)}, bf16[128,2048]{1,0:T(8,128)(2,1)S(1)}, u32[]{:S(2)}, u32[]{:S(2)}) collective-permute-start(bf16[128,2048]{1,0:T(8,128)(2,1)S(1)} %get-tuple-element.475), channel_id=1, source_target_pairs={{0,16},{8,24},{16,0},{24,8},{1,17},{9,25},{17,1},{25,9},{2,18},{10... | collective-permute-start | bytes 1572872 | tf_op jit(solution)/shard_map/cond/branch_1_fun/ppermute | solution.py:42
  401.8 13.2 %collective-permute-start.28 = (bf16[128,2048]{1,0:T(8,128)(2,1)S(1)}, bf16[128,2048]{1,0:T(8,128)(2,1)S(1)}, u32[]{:S(2)}, u32[]{:S(2)}) collective-permute-start(bf16[128,2048]{1,0:T(8,128)(2,1)S(1)} %get-tuple-element.474), channel_id=1, source_target_pairs={{0,1},{1,0},{2,3},{3,2},{4,5},{5,4},{6,7},{7,6},{8,9},{9,8},{10,11... | collective-permute-start | bytes 1572872 | tf_op jit(solution)/shard_map/cond/branch_1_fun/ppermute | solution.py:46
  415.4 26.5 %collective-permute-start.29 = (bf16[256,2048]{1,0:T(8,128)(2,1)S(1)}, bf16[256,2048]{1,0:T(8,128)(2,1)S(1)}, u32[]{:S(2)}, u32[]{:S(2)}) collective-permute-start(bf16[256,2048]{1,0:T(8,128)(2,1)S(1)} %pad_maximum_fusion.5), channel_id=1, source_target_pairs={{0,16},{8,24},{16,0},{24,8},{1,17},{9,25},{17,1},{25,9},{2,18},{10... | collective-permute-start | bytes 3145736 | tf_op jit(solution)/shard_map/cond/branch_1_fun/ppermute | solution.py:42
  416.8 25.2 %collective-permute-start.30 = (bf16[256,2048]{1,0:T(8,128)(2,1)S(1)}, bf16[256,2048]{1,0:T(8,128)(2,1)S(1)}, u32[]{:S(2)}, u32[]{:S(2)}) collective-permute-start(bf16[256,2048]{1,0:T(8,128)(2,1)S(1)} %pad_maximum_fusion.6), channel_id=1, source_target_pairs={{0,1},{1,0},{2,3},{3,2},{4,5},{5,4},{6,7},{7,6},{8,9},{9,8},{10,11... | collective-permute-start | bytes 3145736 | tf_op jit(solution)/shard_map/cond/branch_1_fun/ppermute | solution.py:46
  446.2 203.2 %reduce-scatter.8.cloned.1.call-start = ((), (), s32[]{:S(2)}) async-start(), calls=%async_computation.10 | async-start | bytes 3276800 | tf_op jit(solution)/shard_map/reduce_scatter | solution.py:127
  449.5 25.1 %collective-permute-start.31 = (bf16[256,2048]{1,0:T(8,128)(2,1)}, bf16[256,2048]{1,0:T(8,128)(2,1)S(1)}, u32[]{:S(2)}, u32[]{:S(2)}) collective-permute-start(bf16[256,2048]{1,0:T(8,128)(2,1)} %get-tuple-element.197.refs_0_), channel_id=1, source_target_pairs={{0,16},{8,24},{16,0},{24,8},{1,17},{9,25},{17,1},{25,9},{2,18},{10... | collective-permute-start | bytes 3145736 | tf_op jit(solution)/shard_map/cond/branch_1_fun/ppermute | solution.py:42
  449.8 24.8 %collective-permute-start.32 = (bf16[256,2048]{1,0:T(8,128)(2,1)}, bf16[256,2048]{1,0:T(8,128)(2,1)S(1)}, u32[]{:S(2)}, u32[]{:S(2)}) collective-permute-start(bf16[256,2048]{1,0:T(8,128)(2,1)} %get-tuple-element.197.refs_0_), channel_id=1, source_target_pairs={{0,1},{1,0},{2,3},{3,2},{4,5},{5,4},{6,7},{7,6},{8,9},{9,8},{10,11... | collective-permute-start | bytes 3145736 | tf_op jit(solution)/shard_map/cond/branch_1_fun/ppermute | solution.py:46
  474.6 12.6 %collective-permute-start.34 = (bf16[128,2048]{1,0:T(8,128)(2,1)S(1)}, bf16[128,2048]{1,0:T(8,128)(2,1)S(1)}, u32[]{:S(2)}, u32[]{:S(2)}) collective-permute-start(bf16[128,2048]{1,0:T(8,128)(2,1)S(1)} %slice.170), channel_id=1, source_target_pairs={{0,1},{1,0},{2,3},{3,2},{4,5},{5,4},{6,7},{7,6},{8,9},{9,8},{10,11... | collective-permute-start | bytes 1572872 | tf_op jit(solution)/shard_map/cond/branch_1_fun/ppermute | solution.py:46
  475.0 13.1 %collective-permute-start.35 = (bf16[128,2048]{1,0:T(8,128)(2,1)S(1)}, bf16[128,2048]{1,0:T(8,128)(2,1)S(1)}, u32[]{:S(2)}, u32[]{:S(2)}) collective-permute-start(bf16[128,2048]{1,0:T(8,128)(2,1)S(1)} %slice.171), channel_id=1, source_target_pairs={{0,16},{8,24},{16,0},{24,8},{1,17},{9,25},{17,1},{25,9},{2,18},{10... | collective-permute-start | bytes 1572872 | tf_op jit(solution)/shard_map/cond/branch_1_fun/ppermute | solution.py:42
  492.9 46.2 %collective-permute-start.38 = (bf16[256,2048]{1,0:T(8,128)(2,1)}, bf16[256,2048]{1,0:T(8,128)(2,1)}, u32[]{:S(2)}, u32[]{:S(2)}) collective-permute-start(bf16[256,2048]{1,0:T(8,128)(2,1)} %get-tuple-element.208), channel_id=1, source_target_pairs={{0,16},{8,24},{16,0},{24,8},{1,17},{9,25},{17,1},{25,9},{2,18},{10... | collective-permute-start | bytes 3145736 | tf_op jit(solution)/shard_map/cond/branch_1_fun/ppermute | solution.py:42
  494.0 45.0 %collective-permute-start.39 = (bf16[256,2048]{1,0:T(8,128)(2,1)}, bf16[256,2048]{1,0:T(8,128)(2,1)}, u32[]{:S(2)}, u32[]{:S(2)}) collective-permute-start(bf16[256,2048]{1,0:T(8,128)(2,1)} %get-tuple-element.209), channel_id=1, source_target_pairs={{0,1},{1,0},{2,3},{3,2},{4,5},{5,4},{6,7},{7,6},{8,9},{9,8},{10,11... | collective-permute-start | bytes 3145736 | tf_op jit(solution)/shard_map/cond/branch_1_fun/ppermute | solution.py:46
  494.8 45.6 %collective-permute-start.40 = (bf16[256,2048]{1,0:T(8,128)(2,1)}, bf16[256,2048]{1,0:T(8,128)(2,1)}, u32[]{:S(2)}, u32[]{:S(2)}) collective-permute-start(bf16[256,2048]{1,0:T(8,128)(2,1)} %get-tuple-element.210), channel_id=1, source_target_pairs={{0,17},{1,16},{2,19},{3,18},{4,21},{5,20},{6,23},{7,22},{8,25},{9,... | collective-permute-start | bytes 3145736 | tf_op jit(solution)/shard_map/cond/branch_1_fun/ppermute | solution.py:51
  546.2 20.6 %collective-permute-start.41 = (bf16[1024,2048]{1,0:T(8,128)(2,1)}, bf16[1024,2048]{1,0:T(8,128)(2,1)}, u32[]{:S(2)}, u32[]{:S(2)}) collective-permute-start(bf16[1024,2048]{1,0:T(8,128)(2,1)} %convolution_convert_fusion.2), channel_id=1, source_target_pairs={{0,8},{8,0},{16,24},{24,16},{1,9},{9,1},{17,25},{25,17},{2,10},{10... | collective-permute-start | bytes 12582920 | tf_op jit(solution)/shard_map/cond/branch_1_fun/ppermute | solution.py:38
  548.3 16.1 %collective-permute-start.44 = (bf16[256,2048]{1,0:T(8,128)(2,1)}, bf16[256,2048]{1,0:T(8,128)(2,1)}, u32[]{:S(2)}, u32[]{:S(2)}) collective-permute-start(bf16[256,2048]{1,0:T(8,128)(2,1)} %get-tuple-element.223), channel_id=1, source_target_pairs={{2,10},{3,11},{4,20},{5,21},{6,30},{7,31},{8,16},{9,17},{10,26},{1... | collective-permute-start | bytes 3145736 | tf_op jit(solution)/shard_map/cond/branch_1_fun/ppermute | solution.py:51
  572.2 14.1 %collective-permute-start.42 = (bf16[128,2048]{1,0:T(8,128)(2,1)S(1)}, bf16[128,2048]{1,0:T(8,128)(2,1)S(1)}, u32[]{:S(2)}, u32[]{:S(2)}) collective-permute-start(bf16[128,2048]{1,0:T(8,128)(2,1)S(1)} %get-tuple-element.468), channel_id=1, source_target_pairs={{0,16},{8,24},{16,0},{24,8},{1,17},{9,25},{17,1},{25,9},{2,18},{10... | collective-permute-start | bytes 1572872 | tf_op jit(solution)/shard_map/cond/branch_1_fun/ppermute | solution.py:42
  572.2 14.0 %collective-permute-start.43 = (bf16[128,2048]{1,0:T(8,128)(2,1)S(1)}, bf16[128,2048]{1,0:T(8,128)(2,1)S(1)}, u32[]{:S(2)}, u32[]{:S(2)}) collective-permute-start(bf16[128,2048]{1,0:T(8,128)(2,1)S(1)} %get-tuple-element.467), channel_id=1, source_target_pairs={{0,1},{1,0},{2,3},{3,2},{4,5},{5,4},{6,7},{7,6},{8,9},{9,8},{10,11... | collective-permute-start | bytes 1572872 | tf_op jit(solution)/shard_map/cond/branch_1_fun/ppermute | solution.py:46
  593.1 24.5 %collective-permute-start.6 = (bf16[256,2048]{1,0:T(8,128)(2,1)}, bf16[256,2048]{1,0:T(8,128)(2,1)}, u32[]{:S(2)}, u32[]{:S(2)}) collective-permute-start(bf16[256,2048]{1,0:T(8,128)(2,1)} %get-tuple-element.225), channel_id=1, source_target_pairs={{0,16},{8,24},{16,0},{24,8},{1,17},{9,25},{17,1},{25,9},{2,18},{10... | collective-permute-start | bytes 3145736 | tf_op jit(solution)/shard_map/cond/branch_1_fun/ppermute | solution.py:42
  593.5 24.1 %collective-permute-start.7 = (bf16[256,2048]{1,0:T(8,128)(2,1)}, bf16[256,2048]{1,0:T(8,128)(2,1)}, u32[]{:S(2)}, u32[]{:S(2)}) collective-permute-start(bf16[256,2048]{1,0:T(8,128)(2,1)} %get-tuple-element.226), channel_id=1, source_target_pairs={{0,1},{1,0},{2,3},{3,2},{4,5},{5,4},{6,7},{7,6},{8,9},{9,8},{10,11... | collective-permute-start | bytes 3145736 | tf_op jit(solution)/shard_map/cond/branch_1_fun/ppermute | solution.py:46
  594.7 46.8 %all-to-all-start = ((bf16[8,64,2048]{2,1,0:T(8,128)(2,1)}), bf16[8,64,2048]{2,1,0:T(8,128)(2,1)S(1)}, u32[]{:S(2)}, u32[]{:S(2)}) async-start(bf16[8,64,2048]{2,1,0:T(8,128)(2,1)} %bitcast.96), calls=%async_computation | async-start | bytes 4194304 | tf_op jit(solution)/shard_map/cond/branch_1_fun/all_to_all | solution.py:875
  650.5 13.9 %collective-permute-start.52 = (bf16[64,2048]{1,0:T(8,128)(2,1)S(1)}, bf16[64,2048]{1,0:T(8,128)(2,1)S(1)}, u32[]{:S(2)}, u32[]{:S(2)}) collective-permute-start(bf16[64,2048]{1,0:T(8,128)(2,1)S(1)} %reshape.227), channel_id=1, source_target_pairs={{1,4},{2,1},{3,5},{4,2},{5,6},{6,3},{9,12},{10,9},{11,13},{12,10},... | collective-permute-start | bytes 786440 | tf_op jit(solution)/shard_map/ppermute | solution.py:51
  654.9 15.6 %all-to-all-start.1 = ((bf16[8,80,384]{2,1,0:T(8,128)(2,1)}), bf16[8,80,384]{2,1,0:T(8,128)(2,1)S(1)}, u32[]{:S(2)}, u32[]{:S(2)}) async-start(bf16[8,80,384]{2,1,0:T(8,128)(2,1)} %fusion.36), calls=%async_computation.4 | async-start | bytes 983040 | tf_op jit(solution)/shard_map/all_to_all | solution.py:875
  (46 other events, 542.6 us)
Sparse Core Ops, SparseCore 0:
  30.8 54.2 all-gather.3
  91.0 81.3 all-gather.5
  174.5 150.4 all-gather.7
  368.1 77.7 reduce-scatter.3
  448.3 144.6 reduce-scatter.5
  595.3 52.1 reduce-scatter.7

commit v7 on v6

--- a/solution.py
+++ b/solution.py
@@ -860,7 +860,7 @@
             after(down_summed, da), lambda si, zi, yi: turned(zi % n_seq, si) * n_fsdp + zi * NY + yi
         )
         out_terms = dot_rows(attn_rows, da).astype(BF16).reshape(w_rows * n_fsdp, -1)
-        sums = halve_core(halves(grad_qkv, wqkv, True), out_terms)
+        sums = halve_core(halves(grad_qkv, wqkv, True))
         head_terms = jnp.concatenate([row_terms(xn, after(grad_qkv, sums), n_seq, n_z), out_terms], axis=1)
         return head_terms, fold_corner(sums, head_terms), (own, x_part, y_part, corner), down_rows
 

time: 686 us -> 686 us (level)
  no operation moved by 1% of the time
where the time goes in v7:
time: 686 us; the launch traced here: 679 us
  waiting for transfers between devices  252 us (37%)
  Pallas kernels  156 us (23%)
  starting transfers between devices  80.3 us (12%)
  matrix products  76.3 us (11%)
  other arithmetic  48.8 us (7%)
  local copies, waits for them, and re-layouts  48.6 us (7%)
  between operations  15.7 us (2%)
    ppermute x16, waiting for transfers between devices, swap_x(): lax.ppermute(value, 'seq', [(i, i ^ 2) for i in range(lax.axis_size('seq'...  120 us
    pallas_call x4, Pallas kernels, pieces_call(): pl.pallas_call(kernel, out_shape=tuple((jax.ShapeDtypeStruct((blocks * ro...  66.8 us
    dot_general x4, matrix products, dot_cols(): lax.dot_general(left, right, (((1,), (1,)), ((), ())), preferred_element_...  36.3 us
    pallas_call x2, Pallas kernels, row_terms(): pl.pallas_call(kernel, out_shape=jax.ShapeDtypeStruct((n_planes, n_blocks...  31.2 us
    pallas_call x1, Pallas kernels, attend_back(): pl.pallas_call(functools.partial(attend_back_kernel, n_parts), out_shape=...  30.5 us
    ppermute x13, waiting for transfers between devices, swap_core(): lax.ppermute(value, 'seq', [(i, i ^ 1) for i in range(lax.axis_size('seq'...  28.7 us
    ppermute x13, starting transfers between devices, swap_core(): lax.ppermute(value, 'seq', [(i, i ^ 1) for i in range(lax.axis_size('seq'...  28.1 us
    all_gather x3, waiting for transfers between devices, gather_z(): lax.all_gather(own, 'fsdp', axis=0, tiled=True, axis_index_groups=z_group...  24.8 us
  transfers between devices with their start and end apart: 61, of which 39 were waited for; matrix products, arithmetic and copies ran while one was open for 21% of the time, Pallas kernels for 19%

profile of v7, /device:TPU:11, one launch (start us, length us, event | category | flops | bytes accessed | tf_op | source)
XLA Modules:
  0.0 679.4 jit_solution(11370060778210211060)
XLA Ops:
  25.1 4.5 collective-permute-done.46
  31.9 58.9 %conditional.6 = (bf16[256,2048]{1,0:T(8,128)(2,1)}, bf16[768,2048]{1,0:T(8,128)(2,1)}, bf16[256,2048]{1,0:T(8,128)(2,1)}, bf16[768,2048]{1,0:T(8,128)(2,1)}, bf...) conditional(s32[]{:T(128)} %bitcast.29, () %tuple.90, ...), branch_computations={%region_0.1_spmd, %region_1.2_spmd} | conditional | flops 10881163 | bytes 50881816 | solution.py:727
  34.9 19.5 %collective-permute-done = bf16[256,2048]{1,0:T(8,128)(2,1)} collective-permute-done((bf16[256,2048]{1,0:T(8,128)(2,1)S(1)}, bf16[256,2048]{1,0:T(8,128)(2,1)}, u32[]{:S(2)}, u32[]{:S(2)}) %collective-permute-start) | collective-permute-done | bytes 1048608 | tf_op jit(solution)/shard_map/cond/branch_1_fun/ppermute | solution.py:42
  55.6 13.0 %collective-permute-done.3 = bf16[256,2048]{1,0:T(8,128)(2,1)S(1)} collective-permute-done((bf16[256,2048]{1,0:T(8,128)(2,1)S(1)}, bf16[256,2048]{1,0:T(8,128)(2,1)S(1)}, u32[]{:S(2)}, u32[]{:S(2)}) %collective-permute-start.3) | collective-permute-done | bytes 1048608 | tf_op jit(solution)/shard_map/cond/branch_1_fun/ppermute | solution.py:698
  76.5 7.0 %collective-permute-start.5 = (bf16[768,2048]{1,0:T(8,128)(2,1)}, bf16[768,2048]{1,0:T(8,128)(2,1)}, u32[]{:S(2)}, u32[]{:S(2)}) collective-permute-start(bf16[768,2048]{1,0:T(8,128)(2,1)} %pad_maximum_fusion), channel_id=1, source_target_pairs={{0,8},{8,0},{16,24},{24,16},{1,9},{9,1},{17,25},{25,17},{2,10},{10... | collective-permute-start | bytes 9437192 | tf_op jit(solution)/shard_map/cond/branch_1_fun/ppermute | solution.py:38
  85.6 4.7 collective-permute-done.4
  92.1 81.6 %conditional.7 = (bf16[2048,2048]{1,0:T(8,128)(2,1)}, f32[2048,384]{1,0:T(8,128)}, bf16[2048,256]{1,0:T(8,128)(2,1)}, f32[2048,128]{1,0:T(8,128)S(1)}, bf16[2048...) conditional(s32[]{:T(128)} %bitcast.29, () %tuple.87, ...), branch_computations={%region_2.3_spmd, %region_3.4_spmd} | conditional | flops 9681506304 | bytes 139543584 | solution.py:727
  103.4 13.9 %project.1 = (bf16[2048,2048]{1,0:T(8,128)(2,1)}, f32[2048,384]{1,0:T(8,128)}) custom-call(bf16[256,2048]{1,0:T(8,128)(2,1)} %get-tuple-element.143.refs_0_, bf16[768,2048]{1,0:T(8,128)(2,1)} %get-tuple-element.144.refs_1_, bf16[256,2048]{1,0:T(8,128)(2,1)} %get-tuple-element.145.refs_2_, bf16[768,2048]{1,0:T(8,128)(2,1)} %get-tuple-element.146.refs_3_, ...), custom_call_target="tpu_custom_call" | custom-call | flops 3221225472 | bytes 22634496 | tf_op jit(solution)/shard_map/cond/branch_1_fun/project/pallas_call | solution.py:413
  117.3 20.8 %attend.1 = (bf16[2048,256]{1,0:T(8,128)(2,1)}, f32[2048,128]{1,0:T(8,128)}) custom-call(s32[1]{0:T(128)} %get-tuple-element.150.member, f32[2048,384]{1,0:T(8,128)} %get-tuple-element.525.refs_0_.refs_1_.refs_2_.refs_3_, f32[2048,384]{1,0:T(8,128)} %get-tuple-element.525.refs_0_.refs_1_.refs_2_.refs_3_, ...), custom_call_target="tpu_custom_call" | custom-call | flops 4294967296 | bytes 6291456 | tf_op jit(solution)/shard_map/cond/branch_1_fun/attend/pallas_call | solution.py:306
  144.7 6.8 collective-permute-done.23
  161.5 7.2 %collective-permute-done.24 = bf16[128,2048]{1,0:T(8,128)(2,1)S(1)} collective-permute-done((bf16[128,2048]{1,0:T(8,128)(2,1)}, bf16[128,2048]{1,0:T(8,128)(2,1)S(1)}, u32[]{:S(2)}, u32[]{:S(2)}) %collective-permute-start.24) | collective-permute-done | bytes 524320 | tf_op jit(solution)/shard_map/cond/branch_1_fun/ppermute | solution.py:42
  174.7 125.6 %conditional.8 = (f32[256,2048]{1,0:T(8,128)S(1)}, bf16[256,2048]{1,0:T(8,128)(2,1)}, bf16[768,2048]{1,0:T(8,128)(2,1)}, bf16[256,2048]{1,0:T(8,128)(2,1)}, bf16...) conditional(s32[]{:T(128)} %bitcast.29, () %tuple.86, ...), branch_computations={%region_4.5_spmd, %region_5.7_spmd} | conditional | flops 8596226048 | bytes 173028096 | solution.py:727
  176.4 21.8 %collective-permute-done.8 = bf16[256,2048]{1,0:T(8,128)(2,1)S(1)} collective-permute-done((bf16[256,2048]{1,0:T(8,128)(2,1)}, bf16[256,2048]{1,0:T(8,128)(2,1)S(1)}, u32[]{:S(2)}, u32[]{:S(2)}) %collective-permute-start.8) | collective-permute-done | bytes 1048608 | tf_op jit(solution)/shard_map/cond/branch_1_fun/ppermute | solution.py:42
  205.6 19.2 %collective-permute-done.16 = bf16[256,2048]{1,0:T(8,128)(2,1)S(1)} collective-permute-done((bf16[256,2048]{1,0:T(8,128)(2,1)S(1)}, bf16[256,2048]{1,0:T(8,128)(2,1)S(1)}, u32[]{:S(2)}, u32[]{:S(2)}) %collective-permute-start.16) | collective-permute-done | bytes 1048608 | tf_op jit(solution)/shard_map/cond/branch_1_fun/ppermute | solution.py:42
  227.6 19.6 %collective-permute-done.10 = bf16[256,2048]{1,0:T(8,128)(2,1)S(1)} collective-permute-done((bf16[256,2048]{1,0:T(8,128)(2,1)}, bf16[256,2048]{1,0:T(8,128)(2,1)S(1)}, u32[]{:S(2)}, u32[]{:S(2)}) %collective-permute-start.10) | collective-permute-done | bytes 1048608 | tf_op jit(solution)/shard_map/cond/branch_1_fun/ppermute | solution.py:42
  250.1 9.2 %collective-permute-done.18 = bf16[128,2048]{1,0:T(8,128)(2,1)S(1)} collective-permute-done((bf16[128,2048]{1,0:T(8,128)(2,1)S(1)}, bf16[128,2048]{1,0:T(8,128)(2,1)S(1)}, u32[]{:S(2)}, u32[]{:S(2)}) %collective-permute-start.18) | collective-permute-done | bytes 524320 | tf_op jit(solution)/shard_map/cond/branch_1_fun/ppermute | solution.py:46
  259.3 7.1 %collective-permute-start.21 = (bf16[768,2048]{1,0:T(8,128)(2,1)S(1)}, bf16[768,2048]{1,0:T(8,128)(2,1)S(1)}, u32[]{:S(2)}, u32[]{:S(2)}) collective-permute-start(bf16[768,2048]{1,0:T(8,128)(2,1)S(1)} %constant_dynamic-update-slice_fusion.4.refs_1_), channel_id=1, source_target_pairs={{0,8},{8,0},{16,24},{24,16},{1,9},{9,1},{17,25},{25,17},{2,10},{10... | collective-permute-start | bytes 9437192 | tf_op jit(solution)/shard_map/cond/branch_1_fun/ppermute | solution.py:38
  276.4 7.6 %collective-permute-done.20.refs_2_ = bf16[256,2048]{1,0:T(8,128)(2,1)S(1)} collective-permute-done((bf16[256,2048]{1,0:T(8,128)(2,1)S(1)}, bf16[256,2048]{1,0:T(8,128)(2,1)S(1)}, u32[]{:S(2)}, u32[]{:S(2)}) %collective-permute-start.20) | collective-permute-done | bytes 1048608 | tf_op jit(solution)/shard_map/cond/branch_1_fun/ppermute | solution.py:38
  285.8 14.3 %down_back.1 = (bf16[2048,2048]{1,0:T(8,128)(2,1)}, f32[2048,1024]{1,0:T(8,128)}) custom-call(bf16[256,2048]{1,0:T(8,128)(2,1)S(1)} %copy-done.23, bf16[768,2048]{1,0:T(8,128)(2,1)S(1)} %constant_dynamic-update-slice_fusion.4.refs_1_, bf16[256,2048]{1,0:T(8,128)(2,1)S(1)} %collective-permute-done.20.refs_2_, bf16[768,2048]{1,0:T(8,128)(2,1)} %copy-done.28, ...), custom_call_target="tpu_custom_call" | custom-call | flops 8589934592 | bytes 29360144 | tf_op jit(solution)/shard_map/cond/branch_1_fun/down_back/pallas_call | solution.py:413
  300.3 24.7 %all-gather.8.cloned.1.call-done.refs_4_ = bf16[2048,2048]{1,0:T(8,128)(2,1)} async-done(((bf16[512,2048]{1,0:T(8,128)(2,1)}), bf16[2048,2048]{1,0:T(8,128)(2,1)}) %all-gather.8.cloned.1.call-update) | async-done | bytes 8388624 | tf_op jit(solution)/shard_map/all_gather | solution.py:123
  325.0 27.9 %feed.1 = (bf16[2048,2048]{1,0:T(8,128)(2,1)}, bf16[2048,1024]{1,0:T(8,128)(2,1)S(1)}, bf16[2048,2048]{1,0:T(8,128)(2,1)}) custom-call(bf16[256,2048]{1,0:T(8,128)(2,1)} %get-tuple-element.331.refs_0_, bf16[768,2048]{1,0:T(8,128)(2,1)} %get-tuple-element.332.refs_1_, bf16[256,2048]{1,0:T(8,128)(2,1)} %get-tuple-element.333.refs_2_, ...), custom_call_target="tpu_custom_call" | custom-call | flops 17179869184 | bytes 46137344 | tf_op jit(solution)/shard_map/feed/pallas_call | solution.py:413
  355.0 13.0 %convolution_convert_fusion.4 = bf16[1024,2048]{1,0:T(8,128)(2,1)} fusion(bf16[2048,1024]{1,0:T(8,128)(2,1)S(1)} %get-tuple-element.341, bf16[2048,2048]{1,0:T(8,128)(2,1)} %get-tuple-element.343), kind=kOutput, calls=%fused_computation.97 | convolution fusion | flops 8592031744 | bytes 16777216 | tf_op jit(solution)/shard_map/dot_general | solution.py:26
  368.1 78.1 %conditional.9 = (bf16[2048,2048]{1,0:T(8,128)(2,1)}, f32[256,2048]{1,0:T(8,128)}, bf16[256,2048]{1,0:T(8,128)(2,1)}, f32[2048]{0:T(1024)S(1)}, bf16[1024,2048]{1,0:T(8,128)(2,1)}, /*index=5*/bf16[1024,2048]{1,0:T(8,128)(2,1)}) conditional(s32[]{:T(128)} %bitcast.29, () %tuple.85, (bf16[2048,2048]{1,0:T(8,128)(2,1)}, bf16[2048,2048]{1,0:T(8,128)(2,1)}, ...), branch_computations={%region_7.8_spmd, %region_8.12_spmd} | conditional | flops 38701887488 | bytes 194020976 | solution.py:727
  368.1 14.2 %fusion.10 = bf16[1024,2048]{1,0:T(8,128)(2,1)} fusion(bf16[2048,2048]{1,0:T(8,128)(2,1)} %get-tuple-element.183, bf16[2048,2048]{1,0:T(8,128)(2,1)} %get-tuple-element.180.right_ref), kind=kOutput, calls=%fused_computation.41 | convolution fusion | flops 8592031744 | bytes 16777216 | tf_op jit(solution)/shard_map/cond/branch_1_fun/dot_general | solution.py:30
  390.1 11.3 %add_convert_fusion.3 = bf16[1024,2048]{1,0:T(8,128)(2,1)S(1)} fusion(bf16[1024,2048]{1,0:T(8,128)(2,1)} %collective-permute-done.26, bf16[2048,2048]{1,0:T(8,128)(2,1)S(1)} %bitcast.115, bf16[2048,2048]{1,0:T(8,128)(2,1)} %get-tuple-element.180.right_ref), kind=kOutput, calls=%fused_computation.35 | convolution fusion | flops 8596226048 | bytes 20971520 | tf_op jit(solution)/shard_map/cond/branch_1_fun/dot_general | solution.py:30
  403.6 8.3 %convolution_convert_fusion.1 = bf16[1024,2048]{1,0:T(8,128)(2,1)} fusion(bf16[1024,2048]{1,0:T(8,128)(2,1)} %pad_maximum_fusion.4, bf16[2048,1024]{1,0:T(8,128)(2,1)S(1)} %copy-done.30), kind=kOutput, calls=%fused_computation.42 | convolution fusion | flops 4297064448 | bytes 10485760 | tf_op jit(solution)/shard_map/cond/branch_1_fun/dot_general | solution.py:34
  418.0 24.0 %row_terms.2 = bf16[4,4,128,2048]{3,2,1,0:T(8,128)(2,1)} custom-call(bf16[2048,2048]{1,0:T(8,128)(2,1)} %get-tuple-element.179.left_ref, bf16[2048,2048]{1,0:T(8,128)(2,1)} %get-tuple-element.180.right_ref), custom_call_target="tpu_custom_call" | custom-call | flops 17179869184 | bytes 25165824 | tf_op jit(solution)/shard_map/cond/branch_1_fun/row_terms/pallas_call | solution.py:536
  447.4 141.1 %conditional.10 = (bf16[2048,640]{1,0:T(8,128)(2,1)}, bf16[256,2048]{1,0:T(8,128)(2,1)S(1)}, bf16[256,2048]{1,0:T(8,128)(2,1)}, bf16[256,2048]{1,0:T(8,128)(2,1)...) conditional(s32[]{:T(128)} %bitcast.29, () %tuple.84, ...), branch_computations={%region_13.14_spmd, %region_14.15_spmd} | conditional | flops 12921077760 | bytes 206439328 | solution.py:727
  449.8 6.6 collective-permute-done.33
  456.5 7.3 %add_convert_fusion.7 = bf16[1024,2048]{1,0:T(8,128)(2,1)S(1)} fusion(bf16[1024,2048]{1,0:T(8,128)(2,1)S(1)} %collective-permute-done.33, bf16[1024,2048]{1,0:T(8,128)(2,1)} %get-tuple-element.199, bf16[2048,1024]{1,0:T(8,128)(2,1)} %get-tuple-element.198), kind=kOutput, calls=%fused_computation.60 | convolution fusion | flops 4301258752 | bytes 14680064 | tf_op jit(solution)/shard_map/cond/branch_1_fun/dot_general | solution.py:34
  463.8 10.8 %collective-permute-done.31 = bf16[256,2048]{1,0:T(8,128)(2,1)S(1)} collective-permute-done((bf16[256,2048]{1,0:T(8,128)(2,1)}, bf16[256,2048]{1,0:T(8,128)(2,1)S(1)}, u32[]{:S(2)}, u32[]{:S(2)}) %collective-permute-start.31) | collective-permute-done | bytes 1048608 | tf_op jit(solution)/shard_map/cond/branch_1_fun/ppermute | solution.py:42
  478.4 8.9 %collective-permute-done.34 = bf16[128,2048]{1,0:T(8,128)(2,1)S(1)} collective-permute-done((bf16[128,2048]{1,0:T(8,128)(2,1)S(1)}, bf16[128,2048]{1,0:T(8,128)(2,1)S(1)}, u32[]{:S(2)}, u32[]{:S(2)}) %collective-permute-start.34) | collective-permute-done | bytes 524320 | tf_op jit(solution)/shard_map/cond/branch_1_fun/ppermute | solution.py:46
  497.9 10.7 %out_back.1 = (bf16[2048,2048]{1,0:T(8,128)(2,1)}, bf16[2048,256]{1,0:T(8,128)(2,1)S(1)}) custom-call(bf16[256,2048]{1,0:T(8,128)(2,1)} %get-tuple-element.197.refs_0_, bf16[768,2048]{1,0:T(8,128)(2,1)} %constant_dynamic-update-slice_fusion.8.refs_1_, bf16[256,2048]{1,0:T(8,128)(2,1)S(1)} %collective-permute-done.36.refs_2_, ...), custom_call_target="tpu_custom_call" | custom-call | flops 524288 | bytes 294912 | tf_op jit(solution)/shard_map/cond/branch_1_fun/out_back/pallas_call | solution.py:413
  508.5 30.5 %attend_back.1.right_ref = bf16[2048,384]{1,0:T(8,128)(2,1)S(1)} custom-call(s32[1]{0:T(128)} %get-tuple-element.195.member, f32[2048,384]{1,0:T(8,128)} %get-tuple-element.196.refs_0_.refs_1_.refs_2_.refs_3_, f32[2048,384]{1,0:T(8,128)} %get-tuple-element.196.refs_0_.refs_1_.refs_2_.refs_3_, f32[2048,384]{1,0:T(8,128)} %get-tuple-element.196.refs_0_.refs_1_.refs_2_.refs_3_, ...), custom_call_target="tpu_custom_call" | custom-call | flops 8388608 | bytes 98304 | tf_op jit(solution)/shard_map/cond/branch_1_fun/attend_back/pallas_call | solution.py:342
  540.4 5.8 convolution_convert_fusion.2
  550.2 6.1 fusion.16
  558.3 6.1 collective-permute-done.44
  566.8 5.0 add_convert_fusion.6
  573.0 7.3 %row_terms.3 = bf16[4,4,128,384]{3,2,1,0:T(8,128)(2,1)S(1)} custom-call(bf16[2048,2048]{1,0:T(8,128)(2,1)} %get-tuple-element.194.left_ref, bf16[2048,384]{1,0:T(8,128)(2,1)S(1)} %copy-done.3), custom_call_target="tpu_custom_call" | custom-call | flops 3221225472 | bytes 11534336 | tf_op jit(solution)/shard_map/cond/branch_1_fun/row_terms/pallas_call | solution.py:536
  582.0 4.2 collective-permute-done.42
  588.5 4.5 reduce-scatter.6.cloned.1.call-done
  593.1 50.7 %conditional.11 = (f32[4,8,128]{2,1,0:T(8,128)S(1)}, f32[256,2048]{1,0:T(8,128)}, f32[64,8192]{1,0:T(8,128)}, f32[64,8192]{1,0:T(8,128)}, bf16[1,256,2048]{2,1,0:T(8,128)(2,1)}, /*index=5*/bf16[1,256,2048]{2,1,0:T(8,128)(2,1)}) conditional(s32[]{:T(128)} %bitcast.29, () %tuple.83, (bf16[256,2048]{1,0:T(8,128)(2,1)S(1)}, ...), branch_computations={%region_16.17_spmd, %region_17.21_spmd} | conditional | flops 19925248 | bytes 64128272 | solution.py:727
  594.7 5.9 all-to-all-start
  608.0 9.5 %collective-permute-done.6 = bf16[256,2048]{1,0:T(8,128)(2,1)} collective-permute-done((bf16[256,2048]{1,0:T(8,128)(2,1)}, bf16[256,2048]{1,0:T(8,128)(2,1)}, u32[]{:S(2)}, u32[]{:S(2)}) %collective-permute-start.6) | collective-permute-done | bytes 1048608 | tf_op jit(solution)/shard_map/cond/branch_1_fun/ppermute | solution.py:42
  620.3 4.6 fusion.34
  624.9 16.6 %all-to-all-done.in_ref = bf16[8,64,2048]{2,1,0:T(8,128)(2,1)S(1)} async-done(((bf16[8,64,2048]{2,1,0:T(8,128)(2,1)}), bf16[8,64,2048]{2,1,0:T(8,128)(2,1)S(1)}, u32[]{:S(2)}, u32[]{:S(2)}) %all-to-all-start) | async-done | bytes 2097184 | tf_op jit(solution)/shard_map/cond/branch_1_fun/all_to_all | solution.py:875
  654.9 7.8 %all-to-all-start.1 = ((bf16[8,80,384]{2,1,0:T(8,128)(2,1)}), bf16[8,80,384]{2,1,0:T(8,128)(2,1)S(1)}, u32[]{:S(2)}, u32[]{:S(2)}) async-start(bf16[8,80,384]{2,1,0:T(8,128)(2,1)} %fusion.36), calls=%async_computation.4 | async-start | bytes 983040 | tf_op jit(solution)/shard_map/all_to_all | solution.py:875
  665.2 5.2 all-to-all-done.1.in_ref
  (297 shorter events, 178.5 us)
Async XLA Ops:
  7.2 83.6 %all-gather.4.cloned.1.call-start = ((), (), s32[]{:S(2)}) async-start(), calls=%async_computation.5 | async-start | bytes 3379200 | tf_op jit(solution)/shard_map/all_gather | solution.py:123
  14.1 15.5 %collective-permute-start.46 = (bf16[64,2048]{1,0:T(8,128)(2,1)S(1)}, bf16[64,2048]{1,0:T(8,128)(2,1)S(1)}, u32[]{:S(2)}, u32[]{:S(2)}) collective-permute-start(bf16[64,2048]{1,0:T(8,128)(2,1)S(1)} %constant_dynamic-slice_fusion.10), channel_id=1, source_target_pairs={{8,2},{16,4},{24,6},{9,3},{17,5},{25,7},{2,8},{18,12},{26,14},{3,9... | collective-permute-start | bytes 786440 | tf_op jit(solution)/shard_map/ppermute | solution.py:51
  30.7 143.1 %all-gather.6.cloned.1.call-start = ((), (), s32[]{:S(2)}) async-start(), calls=%async_computation.6 | async-start | bytes 5242880 | tf_op jit(solution)/shard_map/all_gather | solution.py:123
  31.9 22.5 %collective-permute-start = (bf16[256,2048]{1,0:T(8,128)(2,1)S(1)}, bf16[256,2048]{1,0:T(8,128)(2,1)}, u32[]{:S(2)}, u32[]{:S(2)}) collective-permute-start(bf16[256,2048]{1,0:T(8,128)(2,1)S(1)} %get-tuple-element.505), channel_id=1, source_target_pairs={{0,16},{8,24},{16,0},{24,8},{1,17},{9,25},{17,1},{25,9},{2,18},{10... | collective-permute-start | bytes 3145736 | tf_op jit(solution)/shard_map/cond/branch_1_fun/ppermute | solution.py:42
  32.0 22.5 %collective-permute-start.1 = (bf16[256,2048]{1,0:T(8,128)(2,1)S(1)}, bf16[256,2048]{1,0:T(8,128)(2,1)}, u32[]{:S(2)}, u32[]{:S(2)}) collective-permute-start(bf16[256,2048]{1,0:T(8,128)(2,1)S(1)} %get-tuple-element.505), channel_id=1, source_target_pairs={{0,1},{1,0},{2,3},{3,2},{4,5},{5,4},{6,7},{7,6},{8,9},{9,8},{10,11... | collective-permute-start | bytes 3145736 | tf_op jit(solution)/shard_map/cond/branch_1_fun/ppermute | solution.py:46
  33.6 35.0 %collective-permute-start.3 = (bf16[256,2048]{1,0:T(8,128)(2,1)S(1)}, bf16[256,2048]{1,0:T(8,128)(2,1)S(1)}, u32[]{:S(2)}, u32[]{:S(2)}) collective-permute-start(bf16[256,2048]{1,0:T(8,128)(2,1)S(1)} %dynamic-slice_bitcast_fusion), channel_id=1, source_target_pairs={{0,1},{2,3},{5,4},{7,6},{9,8},{11,10},{12,13},{14,15},{16,17},{18,... | collective-permute-start | bytes 3145736 | tf_op jit(solution)/shard_map/cond/branch_1_fun/ppermute | solution.py:698
  54.5 18.9 %collective-permute-start.2 = (bf16[256,2048]{1,0:T(8,128)(2,1)}, bf16[256,2048]{1,0:T(8,128)(2,1)}, u32[]{:S(2)}, u32[]{:S(2)}) collective-permute-start(bf16[256,2048]{1,0:T(8,128)(2,1)} %collective-permute-done.1), channel_id=1, source_target_pairs={{0,16},{8,24},{16,0},{24,8},{1,17},{9,25},{17,1},{25,9},{2,18},{10... | collective-permute-start | bytes 3145736 | tf_op jit(solution)/shard_map/cond/branch_1_fun/ppermute | solution.py:42
  76.5 14.2 %collective-permute-start.5 = (bf16[768,2048]{1,0:T(8,128)(2,1)}, bf16[768,2048]{1,0:T(8,128)(2,1)}, u32[]{:S(2)}, u32[]{:S(2)}) collective-permute-start(bf16[768,2048]{1,0:T(8,128)(2,1)} %pad_maximum_fusion), channel_id=1, source_target_pairs={{0,8},{8,0},{16,24},{24,16},{1,9},{9,1},{17,25},{25,17},{2,10},{10... | collective-permute-start | bytes 9437192 | tf_op jit(solution)/shard_map/cond/branch_1_fun/ppermute | solution.py:38
  90.8 234.2 %all-gather.8.cloned.1.call-start = ((), (), s32[]{:S(2)}) async-start(), calls=%async_computation.7 | async-start | bytes 10485760 | tf_op jit(solution)/shard_map/all_gather | solution.py:123
  95.7 42.4 %collective-permute-start.22 = (bf16[256,2048]{1,0:T(8,128)(2,1)}, bf16[256,2048]{1,0:T(8,128)(2,1)}, u32[]{:S(2)}, u32[]{:S(2)}) collective-permute-start(bf16[256,2048]{1,0:T(8,128)(2,1)} %get-tuple-element.159), channel_id=1, source_target_pairs={{0,1},{1,0},{2,3},{3,2},{4,5},{5,4},{6,7},{7,6},{8,9},{9,8},{10,11... | collective-permute-start | bytes 3145736 | tf_op jit(solution)/shard_map/cond/branch_1_fun/ppermute | solution.py:46
  155.3 13.3 %collective-permute-start.24 = (bf16[128,2048]{1,0:T(8,128)(2,1)}, bf16[128,2048]{1,0:T(8,128)(2,1)S(1)}, u32[]{:S(2)}, u32[]{:S(2)}) collective-permute-start(bf16[128,2048]{1,0:T(8,128)(2,1)} %get-tuple-element.453), channel_id=1, source_target_pairs={{0,16},{8,24},{16,0},{24,8},{1,17},{9,25},{17,1},{25,9},{2,18},{10... | collective-permute-start | bytes 1572872 | tf_op jit(solution)/shard_map/cond/branch_1_fun/ppermute | solution.py:42
  156.3 13.1 %collective-permute-start.25 = (bf16[128,2048]{1,0:T(8,128)(2,1)}, bf16[128,2048]{1,0:T(8,128)(2,1)S(1)}, u32[]{:S(2)}, u32[]{:S(2)}) collective-permute-start(bf16[128,2048]{1,0:T(8,128)(2,1)} %get-tuple-element.452), channel_id=1, source_target_pairs={{0,1},{1,0},{2,3},{3,2},{4,5},{5,4},{6,7},{7,6},{8,9},{9,8},{10,11... | collective-permute-start | bytes 1572872 | tf_op jit(solution)/shard_map/cond/branch_1_fun/ppermute | solution.py:46
  173.7 272.5 %reduce-scatter.4.cloned.1.call-start = ((), (), s32[]{:S(2)}) async-start(), calls=%async_computation.8 | async-start | bytes 5242880 | tf_op jit(solution)/shard_map/reduce_scatter | solution.py:127
  174.7 23.5 %collective-permute-start.8 = (bf16[256,2048]{1,0:T(8,128)(2,1)}, bf16[256,2048]{1,0:T(8,128)(2,1)S(1)}, u32[]{:S(2)}, u32[]{:S(2)}) collective-permute-start(bf16[256,2048]{1,0:T(8,128)(2,1)} %get-tuple-element.166), channel_id=1, source_target_pairs={{0,16},{8,24},{16,0},{24,8},{1,17},{9,25},{17,1},{25,9},{2,18},{10... | collective-permute-start | bytes 3145736 | tf_op jit(solution)/shard_map/cond/branch_1_fun/ppermute | solution.py:42
  175.1 23.3 %collective-permute-start.9 = (bf16[256,2048]{1,0:T(8,128)(2,1)}, bf16[256,2048]{1,0:T(8,128)(2,1)S(1)}, u32[]{:S(2)}, u32[]{:S(2)}) collective-permute-start(bf16[256,2048]{1,0:T(8,128)(2,1)} %get-tuple-element.167), channel_id=1, source_target_pairs={{0,1},{1,0},{2,3},{3,2},{4,5},{5,4},{6,7},{7,6},{8,9},{9,8},{10,11... | collective-permute-start | bytes 3145736 | tf_op jit(solution)/shard_map/cond/branch_1_fun/ppermute | solution.py:46
  202.7 22.1 %collective-permute-start.16 = (bf16[256,2048]{1,0:T(8,128)(2,1)S(1)}, bf16[256,2048]{1,0:T(8,128)(2,1)S(1)}, u32[]{:S(2)}, u32[]{:S(2)}) collective-permute-start(bf16[256,2048]{1,0:T(8,128)(2,1)S(1)} %copy-done.23), channel_id=1, source_target_pairs={{0,16},{8,24},{16,0},{24,8},{1,17},{9,25},{17,1},{25,9},{2,18},{10... | collective-permute-start | bytes 3145736 | tf_op jit(solution)/shard_map/cond/branch_1_fun/ppermute | solution.py:42
  203.7 21.9 %collective-permute-start.17 = (bf16[256,2048]{1,0:T(8,128)(2,1)S(1)}, bf16[256,2048]{1,0:T(8,128)(2,1)S(1)}, u32[]{:S(2)}, u32[]{:S(2)}) collective-permute-start(bf16[256,2048]{1,0:T(8,128)(2,1)S(1)} %copy-done.23), channel_id=1, source_target_pairs={{0,1},{1,0},{2,3},{3,2},{4,5},{5,4},{6,7},{7,6},{8,9},{9,8},{10,11... | collective-permute-start | bytes 3145736 | tf_op jit(solution)/shard_map/cond/branch_1_fun/ppermute | solution.py:46
  204.9 42.3 %collective-permute-start.10 = (bf16[256,2048]{1,0:T(8,128)(2,1)}, bf16[256,2048]{1,0:T(8,128)(2,1)S(1)}, u32[]{:S(2)}, u32[]{:S(2)}) collective-permute-start(bf16[256,2048]{1,0:T(8,128)(2,1)} %multiply_convert_fusion), channel_id=1, source_target_pairs={{0,16},{8,24},{16,0},{24,8},{1,17},{9,25},{17,1},{25,9},{2,18},{10... | collective-permute-start | bytes 3145736 | tf_op jit(solution)/shard_map/cond/branch_1_fun/ppermute | solution.py:42
  205.4 42.6 %collective-permute-start.11 = (bf16[256,2048]{1,0:T(8,128)(2,1)}, bf16[256,2048]{1,0:T(8,128)(2,1)S(1)}, u32[]{:S(2)}, u32[]{:S(2)}) collective-permute-start(bf16[256,2048]{1,0:T(8,128)(2,1)} %multiply_convert_fusion), channel_id=1, source_target_pairs={{0,1},{1,0},{2,3},{3,2},{4,5},{5,4},{6,7},{7,6},{8,9},{9,8},{10,11... | collective-permute-start | bytes 3145736 | tf_op jit(solution)/shard_map/cond/branch_1_fun/ppermute | solution.py:46
  225.6 33.7 %collective-permute-start.18 = (bf16[128,2048]{1,0:T(8,128)(2,1)S(1)}, bf16[128,2048]{1,0:T(8,128)(2,1)S(1)}, u32[]{:S(2)}, u32[]{:S(2)}) collective-permute-start(bf16[128,2048]{1,0:T(8,128)(2,1)S(1)} %slice.157), channel_id=1, source_target_pairs={{0,1},{1,0},{2,3},{3,2},{4,5},{5,4},{6,7},{7,6},{8,9},{9,8},{10,11... | collective-permute-start | bytes 1572872 | tf_op jit(solution)/shard_map/cond/branch_1_fun/ppermute | solution.py:46
  226.9 32.3 %collective-permute-start.19 = (bf16[128,2048]{1,0:T(8,128)(2,1)S(1)}, bf16[128,2048]{1,0:T(8,128)(2,1)S(1)}, u32[]{:S(2)}, u32[]{:S(2)}) collective-permute-start(bf16[128,2048]{1,0:T(8,128)(2,1)S(1)} %slice.158), channel_id=1, source_target_pairs={{0,16},{8,24},{16,0},{24,8},{1,17},{9,25},{17,1},{25,9},{2,18},{10... | collective-permute-start | bytes 1572872 | tf_op jit(solution)/shard_map/cond/branch_1_fun/ppermute | solution.py:42
  248.0 22.4 %collective-permute-start.12 = (bf16[128,2048]{1,0:T(8,128)(2,1)S(1)}, bf16[128,2048]{1,0:T(8,128)(2,1)S(1)}, u32[]{:S(2)}, u32[]{:S(2)}) collective-permute-start(bf16[128,2048]{1,0:T(8,128)(2,1)S(1)} %slice.155), channel_id=1, source_target_pairs={{0,1},{1,0},{2,3},{3,2},{4,5},{5,4},{6,7},{7,6},{8,9},{9,8},{10,11... | collective-permute-start | bytes 1572872 | tf_op jit(solution)/shard_map/cond/branch_1_fun/ppermute | solution.py:46
  249.4 21.9 %collective-permute-start.13 = (bf16[128,2048]{1,0:T(8,128)(2,1)S(1)}, bf16[128,2048]{1,0:T(8,128)(2,1)S(1)}, u32[]{:S(2)}, u32[]{:S(2)}) collective-permute-start(bf16[128,2048]{1,0:T(8,128)(2,1)S(1)} %slice.156), channel_id=1, source_target_pairs={{0,16},{8,24},{16,0},{24,8},{1,17},{9,25},{17,1},{25,9},{2,18},{10... | collective-permute-start | bytes 1572872 | tf_op jit(solution)/shard_map/cond/branch_1_fun/ppermute | solution.py:42
  259.3 24.7 %collective-permute-start.21 = (bf16[768,2048]{1,0:T(8,128)(2,1)S(1)}, bf16[768,2048]{1,0:T(8,128)(2,1)S(1)}, u32[]{:S(2)}, u32[]{:S(2)}) collective-permute-start(bf16[768,2048]{1,0:T(8,128)(2,1)S(1)} %constant_dynamic-update-slice_fusion.4.refs_1_), channel_id=1, source_target_pairs={{0,8},{8,0},{16,24},{24,16},{1,9},{9,1},{17,25},{25,17},{2,10},{10... | collective-permute-start | bytes 9437192 | tf_op jit(solution)/shard_map/cond/branch_1_fun/ppermute | solution.py:38
  272.2 27.9 %collective-permute-start.15 = (bf16[768,2048]{1,0:T(8,128)(2,1)}, bf16[768,2048]{1,0:T(8,128)(2,1)}, u32[]{:S(2)}, u32[]{:S(2)}) collective-permute-start(bf16[768,2048]{1,0:T(8,128)(2,1)} %constant_dynamic-update-slice_fusion), channel_id=1, source_target_pairs={{0,8},{8,0},{16,24},{24,16},{1,9},{9,1},{17,25},{25,17},{2,10},{10... | collective-permute-start | bytes 9437192 | tf_op jit(solution)/shard_map/cond/branch_1_fun/ppermute | solution.py:38
  275.9 24.2 %collective-permute-start.14 = (bf16[256,2048]{1,0:T(8,128)(2,1)}, bf16[256,2048]{1,0:T(8,128)(2,1)}, u32[]{:S(2)}, u32[]{:S(2)}) collective-permute-start(bf16[256,2048]{1,0:T(8,128)(2,1)} %multiply_convert_fusion), channel_id=1, source_target_pairs={{0,8},{8,0},{16,24},{24,16},{1,9},{9,1},{17,25},{25,17},{2,10},{10... | collective-permute-start | bytes 3145736 | tf_op jit(solution)/shard_map/cond/branch_1_fun/ppermute | solution.py:38
  368.0 225.0 %reduce-scatter.6.cloned.1.call-start = ((), (), s32[]{:S(2)}) async-start(), calls=%async_computation.9 | async-start | bytes 10485760 | tf_op jit(solution)/shard_map/reduce_scatter | solution.py:127
  401.7 13.3 %collective-permute-start.27 = (bf16[128,2048]{1,0:T(8,128)(2,1)S(1)}, bf16[128,2048]{1,0:T(8,128)(2,1)S(1)}, u32[]{:S(2)}, u32[]{:S(2)}) collective-permute-start(bf16[128,2048]{1,0:T(8,128)(2,1)S(1)} %get-tuple-element.474), channel_id=1, source_target_pairs={{0,16},{8,24},{16,0},{24,8},{1,17},{9,25},{17,1},{25,9},{2,18},{10... | collective-permute-start | bytes 1572872 | tf_op jit(solution)/shard_map/cond/branch_1_fun/ppermute | solution.py:42
  401.8 13.2 %collective-permute-start.28 = (bf16[128,2048]{1,0:T(8,128)(2,1)S(1)}, bf16[128,2048]{1,0:T(8,128)(2,1)S(1)}, u32[]{:S(2)}, u32[]{:S(2)}) collective-permute-start(bf16[128,2048]{1,0:T(8,128)(2,1)S(1)} %get-tuple-element.473), channel_id=1, source_target_pairs={{0,1},{1,0},{2,3},{3,2},{4,5},{5,4},{6,7},{7,6},{8,9},{9,8},{10,11... | collective-permute-start | bytes 1572872 | tf_op jit(solution)/shard_map/cond/branch_1_fun/ppermute | solution.py:46
  415.4 26.5 %collective-permute-start.29 = (bf16[256,2048]{1,0:T(8,128)(2,1)S(1)}, bf16[256,2048]{1,0:T(8,128)(2,1)S(1)}, u32[]{:S(2)}, u32[]{:S(2)}) collective-permute-start(bf16[256,2048]{1,0:T(8,128)(2,1)S(1)} %pad_maximum_fusion.5), channel_id=1, source_target_pairs={{0,16},{8,24},{16,0},{24,8},{1,17},{9,25},{17,1},{25,9},{2,18},{10... | collective-permute-start | bytes 3145736 | tf_op jit(solution)/shard_map/cond/branch_1_fun/ppermute | solution.py:42
  416.8 25.2 %collective-permute-start.30 = (bf16[256,2048]{1,0:T(8,128)(2,1)S(1)}, bf16[256,2048]{1,0:T(8,128)(2,1)S(1)}, u32[]{:S(2)}, u32[]{:S(2)}) collective-permute-start(bf16[256,2048]{1,0:T(8,128)(2,1)S(1)} %pad_maximum_fusion.6), channel_id=1, source_target_pairs={{0,1},{1,0},{2,3},{3,2},{4,5},{5,4},{6,7},{7,6},{8,9},{9,8},{10,11... | collective-permute-start | bytes 3145736 | tf_op jit(solution)/shard_map/cond/branch_1_fun/ppermute | solution.py:46
  446.2 203.2 %reduce-scatter.8.cloned.1.call-start = ((), (), s32[]{:S(2)}) async-start(), calls=%async_computation.10 | async-start | bytes 3276800 | tf_op jit(solution)/shard_map/reduce_scatter | solution.py:127
  449.5 25.1 %collective-permute-start.31 = (bf16[256,2048]{1,0:T(8,128)(2,1)}, bf16[256,2048]{1,0:T(8,128)(2,1)S(1)}, u32[]{:S(2)}, u32[]{:S(2)}) collective-permute-start(bf16[256,2048]{1,0:T(8,128)(2,1)} %get-tuple-element.197.refs_0_), channel_id=1, source_target_pairs={{0,16},{8,24},{16,0},{24,8},{1,17},{9,25},{17,1},{25,9},{2,18},{10... | collective-permute-start | bytes 3145736 | tf_op jit(solution)/shard_map/cond/branch_1_fun/ppermute | solution.py:42
  449.8 24.8 %collective-permute-start.32 = (bf16[256,2048]{1,0:T(8,128)(2,1)}, bf16[256,2048]{1,0:T(8,128)(2,1)S(1)}, u32[]{:S(2)}, u32[]{:S(2)}) collective-permute-start(bf16[256,2048]{1,0:T(8,128)(2,1)} %get-tuple-element.197.refs_0_), channel_id=1, source_target_pairs={{0,1},{1,0},{2,3},{3,2},{4,5},{5,4},{6,7},{7,6},{8,9},{9,8},{10,11... | collective-permute-start | bytes 3145736 | tf_op jit(solution)/shard_map/cond/branch_1_fun/ppermute | solution.py:46
  474.6 12.6 %collective-permute-start.34 = (bf16[128,2048]{1,0:T(8,128)(2,1)S(1)}, bf16[128,2048]{1,0:T(8,128)(2,1)S(1)}, u32[]{:S(2)}, u32[]{:S(2)}) collective-permute-start(bf16[128,2048]{1,0:T(8,128)(2,1)S(1)} %slice.170), channel_id=1, source_target_pairs={{0,1},{1,0},{2,3},{3,2},{4,5},{5,4},{6,7},{7,6},{8,9},{9,8},{10,11... | collective-permute-start | bytes 1572872 | tf_op jit(solution)/shard_map/cond/branch_1_fun/ppermute | solution.py:46
  475.0 13.1 %collective-permute-start.35 = (bf16[128,2048]{1,0:T(8,128)(2,1)S(1)}, bf16[128,2048]{1,0:T(8,128)(2,1)S(1)}, u32[]{:S(2)}, u32[]{:S(2)}) collective-permute-start(bf16[128,2048]{1,0:T(8,128)(2,1)S(1)} %slice.171), channel_id=1, source_target_pairs={{0,16},{8,24},{16,0},{24,8},{1,17},{9,25},{17,1},{25,9},{2,18},{10... | collective-permute-start | bytes 1572872 | tf_op jit(solution)/shard_map/cond/branch_1_fun/ppermute | solution.py:42
  492.9 46.2 %collective-permute-start.38 = (bf16[256,2048]{1,0:T(8,128)(2,1)}, bf16[256,2048]{1,0:T(8,128)(2,1)}, u32[]{:S(2)}, u32[]{:S(2)}) collective-permute-start(bf16[256,2048]{1,0:T(8,128)(2,1)} %get-tuple-element.208), channel_id=1, source_target_pairs={{0,16},{8,24},{16,0},{24,8},{1,17},{9,25},{17,1},{25,9},{2,18},{10... | collective-permute-start | bytes 3145736 | tf_op jit(solution)/shard_map/cond/branch_1_fun/ppermute | solution.py:42
  494.0 45.0 %collective-permute-start.39 = (bf16[256,2048]{1,0:T(8,128)(2,1)}, bf16[256,2048]{1,0:T(8,128)(2,1)}, u32[]{:S(2)}, u32[]{:S(2)}) collective-permute-start(bf16[256,2048]{1,0:T(8,128)(2,1)} %get-tuple-element.209), channel_id=1, source_target_pairs={{0,1},{1,0},{2,3},{3,2},{4,5},{5,4},{6,7},{7,6},{8,9},{9,8},{10,11... | collective-permute-start | bytes 3145736 | tf_op jit(solution)/shard_map/cond/branch_1_fun/ppermute | solution.py:46
  494.8 45.6 %collective-permute-start.40 = (bf16[256,2048]{1,0:T(8,128)(2,1)}, bf16[256,2048]{1,0:T(8,128)(2,1)}, u32[]{:S(2)}, u32[]{:S(2)}) collective-permute-start(bf16[256,2048]{1,0:T(8,128)(2,1)} %get-tuple-element.210), channel_id=1, source_target_pairs={{0,17},{1,16},{2,19},{3,18},{4,21},{5,20},{6,23},{7,22},{8,25},{9,... | collective-permute-start | bytes 3145736 | tf_op jit(solution)/shard_map/cond/branch_1_fun/ppermute | solution.py:51
  546.2 20.6 %collective-permute-start.41 = (bf16[1024,2048]{1,0:T(8,128)(2,1)}, bf16[1024,2048]{1,0:T(8,128)(2,1)}, u32[]{:S(2)}, u32[]{:S(2)}) collective-permute-start(bf16[1024,2048]{1,0:T(8,128)(2,1)} %convolution_convert_fusion.2), channel_id=1, source_target_pairs={{0,8},{8,0},{16,24},{24,16},{1,9},{9,1},{17,25},{25,17},{2,10},{10... | collective-permute-start | bytes 12582920 | tf_op jit(solution)/shard_map/cond/branch_1_fun/ppermute | solution.py:38
  548.3 16.1 %collective-permute-start.44 = (bf16[256,2048]{1,0:T(8,128)(2,1)}, bf16[256,2048]{1,0:T(8,128)(2,1)}, u32[]{:S(2)}, u32[]{:S(2)}) collective-permute-start(bf16[256,2048]{1,0:T(8,128)(2,1)} %get-tuple-element.222), channel_id=1, source_target_pairs={{2,10},{3,11},{4,20},{5,21},{6,30},{7,31},{8,16},{9,17},{10,26},{1... | collective-permute-start | bytes 3145736 | tf_op jit(solution)/shard_map/cond/branch_1_fun/ppermute | solution.py:51
  572.2 14.1 %collective-permute-start.42 = (bf16[128,2048]{1,0:T(8,128)(2,1)S(1)}, bf16[128,2048]{1,0:T(8,128)(2,1)S(1)}, u32[]{:S(2)}, u32[]{:S(2)}) collective-permute-start(bf16[128,2048]{1,0:T(8,128)(2,1)S(1)} %get-tuple-element.467), channel_id=1, source_target_pairs={{0,16},{8,24},{16,0},{24,8},{1,17},{9,25},{17,1},{25,9},{2,18},{10... | collective-permute-start | bytes 1572872 | tf_op jit(solution)/shard_map/cond/branch_1_fun/ppermute | solution.py:42
  572.2 14.0 %collective-permute-start.43 = (bf16[128,2048]{1,0:T(8,128)(2,1)S(1)}, bf16[128,2048]{1,0:T(8,128)(2,1)S(1)}, u32[]{:S(2)}, u32[]{:S(2)}) collective-permute-start(bf16[128,2048]{1,0:T(8,128)(2,1)S(1)} %get-tuple-element.466), channel_id=1, source_target_pairs={{0,1},{1,0},{2,3},{3,2},{4,5},{5,4},{6,7},{7,6},{8,9},{9,8},{10,11... | collective-permute-start | bytes 1572872 | tf_op jit(solution)/shard_map/cond/branch_1_fun/ppermute | solution.py:46
  593.1 24.5 %collective-permute-start.6 = (bf16[256,2048]{1,0:T(8,128)(2,1)}, bf16[256,2048]{1,0:T(8,128)(2,1)}, u32[]{:S(2)}, u32[]{:S(2)}) collective-permute-start(bf16[256,2048]{1,0:T(8,128)(2,1)} %get-tuple-element.224), channel_id=1, source_target_pairs={{0,16},{8,24},{16,0},{24,8},{1,17},{9,25},{17,1},{25,9},{2,18},{10... | collective-permute-start | bytes 3145736 | tf_op jit(solution)/shard_map/cond/branch_1_fun/ppermute | solution.py:42
  593.5 24.1 %collective-permute-start.7 = (bf16[256,2048]{1,0:T(8,128)(2,1)}, bf16[256,2048]{1,0:T(8,128)(2,1)}, u32[]{:S(2)}, u32[]{:S(2)}) collective-permute-start(bf16[256,2048]{1,0:T(8,128)(2,1)} %get-tuple-element.225), channel_id=1, source_target_pairs={{0,1},{1,0},{2,3},{3,2},{4,5},{5,4},{6,7},{7,6},{8,9},{9,8},{10,11... | collective-permute-start | bytes 3145736 | tf_op jit(solution)/shard_map/cond/branch_1_fun/ppermute | solution.py:46
  594.7 46.8 %all-to-all-start = ((bf16[8,64,2048]{2,1,0:T(8,128)(2,1)}), bf16[8,64,2048]{2,1,0:T(8,128)(2,1)S(1)}, u32[]{:S(2)}, u32[]{:S(2)}) async-start(bf16[8,64,2048]{2,1,0:T(8,128)(2,1)} %bitcast.96), calls=%async_computation | async-start | bytes 4194304 | tf_op jit(solution)/shard_map/cond/branch_1_fun/all_to_all | solution.py:875
  650.5 13.9 %collective-permute-start.52 = (bf16[64,2048]{1,0:T(8,128)(2,1)S(1)}, bf16[64,2048]{1,0:T(8,128)(2,1)S(1)}, u32[]{:S(2)}, u32[]{:S(2)}) collective-permute-start(bf16[64,2048]{1,0:T(8,128)(2,1)S(1)} %reshape.227), channel_id=1, source_target_pairs={{1,4},{2,1},{3,5},{4,2},{5,6},{6,3},{9,12},{10,9},{11,13},{12,10},... | collective-permute-start | bytes 786440 | tf_op jit(solution)/shard_map/ppermute | solution.py:51
  654.9 15.6 %all-to-all-start.1 = ((bf16[8,80,384]{2,1,0:T(8,128)(2,1)}), bf16[8,80,384]{2,1,0:T(8,128)(2,1)S(1)}, u32[]{:S(2)}, u32[]{:S(2)}) async-start(bf16[8,80,384]{2,1,0:T(8,128)(2,1)} %fusion.36), calls=%async_computation.4 | async-start | bytes 983040 | tf_op jit(solution)/shard_map/all_to_all | solution.py:875
  (46 other events, 542.6 us)
Sparse Core Ops, SparseCore 0:
  30.8 54.2 all-gather.3
  91.0 81.3 all-gather.5
  174.5 150.4 all-gather.7
  368.1 77.7 reduce-scatter.3
  448.3 144.6 reduce-scatter.5
  595.3 52.1 reduce-scatter.7
